TPU v7x, 256 devices: a whole 4x4x8 slice. The times are simulated.
256 devices in a mesh: slab: 64 (over z, x, core), view: 4 (over y).
Axes of the slice: x: 4, y: 4, z: 8, core: 2. Of those that a mesh axis runs over, the one named last changes fastest.
Arguments:
- activity: float32 [2048, 32, 1024], P('slab'), may hold values from 0.5 to 2
- sensitivity: float32 [2048, 32, 1024], P('slab'), may hold values from 1 to 8
- psf_width: float32 [2048], P('slab'), may hold values from 0.05 to 0.3
- measured: bfloat16 [4, 4096, 32, 128], P('view', 'slab'), may hold values from 0.25 to 4
- block_slab: int32 [4, 4096, 1], P('view', 'slab'), may hold values from 0 to 63; in each aligned block of 64 rows (0 to 63, 64 to 127, ..., all dimensions but the last counted through in order) at most 2 rows name the same one
- block_line: int32 [4, 4096], P('view', 'slab'), may hold values from 0 to 31
- block_angle: int32 [4, 4096], P('view', 'slab'), may hold values from 0 to 7
- subset_views: int32 [4, 8], P('view'), may hold values from 0 to 335
Outputs:
- updated: float32 [2048, 32, 1024], P('slab')
Inputs may be any that keep to these rules, and one draw needn't show every extreme that they name: `block_slab`: among the 64 blocks of one device (aligned blocks of 64 rows) no slab is named more than 2 times, a bound that some block reaches.
All inputs are finite; a program needn't handle non-finite values.
Results may differ from a plain program's by a relative error of at most 0.0014.
Values may be sent and summed in bfloat16 or wider, within the bound.
A program may use at most 64 MiB of HBM per device.

v0:
```python
import math

import jax
import jax.numpy as jnp
from jax import lax
from jax.sharding import PartitionSpec as P

VIEWS_ALL = 336


BACKGROUND = 0.05


def with_halo(value, sides, width):
    for axis, dim in sides:
        size, length = (lax.axis_size(axis), value.shape[dim])
        up = [(i, (i + 1) % size) for i in range(size - 1)]
        down = [(j, i) for i, j in up]
        last = lax.slice_in_dim(value, length - width, length, axis=dim)
        leading = lax.slice_in_dim(value, 0, width, axis=dim)
        before = lax.ppermute(last, axis, up)
        after = lax.ppermute(leading, axis, down)
        value = jnp.concatenate([before, value, after], axis=dim)
    return value


def kernels(angles, bins, length):
    view_angle = math.pi * angles.astype(jnp.float32) / VIEWS_ALL
    step_width = length / bins
    deviation = 0.25 * step_width
    spacing = step_width * (0.75 + 0.25 * jnp.cos(2.0 * view_angle))
    offset = 1.5 * step_width * jnp.sin(view_angle)
    centres = (jnp.arange(bins, dtype=jnp.float32) + 0.5 - bins / 2)[None, :] * spacing[
        :, None
    ] + offset[:, None]
    voxel_pos = jnp.arange(length, dtype=jnp.float32) + 0.5 - length / 2
    distance = voxel_pos[None, None, :] - centres[:, :, None]
    values = jnp.exp(-distance * distance / (2.0 * deviation * deviation)) / (
        deviation * math.sqrt(2.0 * math.pi)
    )
    return values.astype(jnp.bfloat16)


def on_device(
    activity, sensitivity, psf_width, measured, block_slab, block_line, block_angle, subset_views
):
    weight = psf_width[:, None, None]
    padded = with_halo(activity, (("slab", 0),), 1)
    blurred = ((1.0 - 2.0 * weight) * activity + weight * (padded[:-2] + padded[2:])).astype(
        jnp.bfloat16
    )
    planes, lines_here, length = activity.shape
    bins = measured.shape[3]
    tof_kernel = kernels(subset_views[0], bins, length)
    angle_count = tof_kernel.shape[0]
    projected = jnp.einsum("zlv,atv->alzt", blurred, tof_kernel, preferred_element_type=jnp.float32)
    projected = projected.reshape(angle_count * lines_here, planes, bins)
    slab_count = lax.axis_size("slab")
    block_total = measured.shape[1]
    capacity = 2 * block_total // slab_count
    targets = block_slab[0, :, 0]
    onehot = (targets[:, None] == jnp.arange(slab_count, dtype=jnp.int32)[None, :]).astype(
        jnp.int32
    )
    slot_pos = jnp.sum((jnp.cumsum(onehot, axis=0) - onehot) * onehot, axis=1)
    send_rows = (
        jnp.zeros((slab_count, capacity, planes, bins), jnp.bfloat16)
        .at[targets, slot_pos]
        .set(measured[0])
    )
    send_index = (
        jnp.zeros((slab_count, capacity), jnp.int32)
        .at[targets, slot_pos]
        .set(block_angle[0] * lines_here + block_line[0])
    )
    rows = lax.all_to_all(send_rows, "slab", split_axis=0, concat_axis=0, tiled=True)
    index = lax.all_to_all(send_index, "slab", split_axis=0, concat_axis=0, tiled=True)
    estimate = projected[index]
    ratios, index = (rows.astype(jnp.float32) / (estimate + BACKGROUND), index)
    sums = jnp.zeros((angle_count * lines_here, planes, bins), jnp.float32)
    sums = sums.at[index.reshape(-1)].add(ratios.reshape(-1, planes, bins))
    rounded = sums.astype(jnp.bfloat16).reshape(angle_count, lines_here, planes, bins)
    back = jnp.einsum("alzt,atv->zlv", rounded, tof_kernel, preferred_element_type=jnp.float32)
    total = lax.psum(back, "view")
    edges = with_halo(weight * total, (("slab", 0),), 1)
    smoothed = (1.0 - 2.0 * weight) * total + edges[:-2] + edges[2:]
    return activity * smoothed / sensitivity


def solution(mesh):
    in_specs = (
        P("slab", None, None),
        P("slab", None, None),
        P("slab"),
        P("view", "slab", None, None),
        P("view", "slab", None),
        P("view", "slab"),
        P("view", "slab"),
        P("view", None),
    )
    out_specs = P("slab", None, None)
    return jax.shard_map(
        on_device, mesh=mesh, in_specs=in_specs, out_specs=out_specs, check_vma=False
    )
```

profile of v0, /device:TPU:31, one launch (start us, length us, event | category | flops | bytes accessed | tf_op | source)
XLA Modules:
  0.0 245.7 jit_solution(8091599429287186392)
XLA Ops:
  6.5 0.0 copy-start.2
  6.5 0.7 fusion.23
  7.3 0.1 reduce_window_sum.11
  7.4 0.8 select_reduce_fusion
  8.2 0.7 fusion.26
  8.9 0.7 add_bitcast_fusion
  9.6 3.5 %scatter_fusion = s32[64,2]{0,1:T(2,128)S(1)} fusion(s32[64,2]{0,1:T(2,128)S(1)} %broadcast.188, s32[64]{0:T(128)S(1)} %fusion.26, s32[64]{0:T(128)S(1)} %add_bitcast_fusion), kind=kCustom, calls=%fused_computation.1 | custom fusion | bytes 1280 | tf_op jit(solution)/shard_map/scatter | solution.py:74
  13.1 0.7 copy.33
  13.8 12.3 %all-to-all-start = ((s32[64,1,2]{2,1,0:T(1,128)}), s32[64,1,2]{2,1,0:T(1,128)S(1)}, u32[]{:S(2)}, u32[]{:S(2)}) async-start(s32[64,1,2]{2,1,0:T(1,128)} %copy.33), calls=%async_computation | async-start | bytes 65536 | tf_op jit(solution)/shard_map/all_to_all | solution.py:77
  26.1 1.0 fusion.32
  27.1 0.1 copy.37
  27.2 2.3 collective-permute-start.1
  29.5 0.1 copy.35
  29.6 5.4 %collective-permute-start = (f32[1,32,1024]{2,0,1:T(1,128)S(1)}, f32[1,32,1024]{2,0,1:T(1,128)S(1)}, u32[]{:S(2)}, u32[]{:S(2)}) collective-permute-start(f32[1,32,1024]{2,0,1:T(1,128)S(1)} %copy.35), channel_id=1, source_target_pairs={{0,4},{4,8},{8,12},{12,16},{16,20},{20,24},{24,28},{28,32},{32,36}... | collective-permute-start | bytes 393224 | tf_op jit(solution)/shard_map/ppermute | solution.py:21
  35.0 0.7 multiply_bitcast_fusion
  35.8 0.1 multiply_add_fusion
  35.8 1.2 broadcast_in_dim.5
  37.1 8.0 %scatter_fusion.1 = bf16[64,2,32,128]{3,2,1,0:T(8,128)(2,1)} fusion(bf16[64,2,32,128]{3,2,1,0:T(8,128)(2,1)} %broadcast_in_dim.5, s32[64]{0:T(128)S(1)} %fusion.26, bf16[64,32,128]{2,1,0:T(8,128)(2,1)} %bitcast.57), kind=kCustom, calls=%fused_computation.2 | custom fusion | bytes 1573376 | tf_op jit(solution)/shard_map/scatter | solution.py:69
  45.1 0.0 all-to-all-done
  45.1 9.8 %all-to-all-start.1 = ((bf16[64,2,32,128]{3,2,1,0:T(8,128)(2,1)}), bf16[64,2,32,128]{3,2,1,0:T(8,128)(2,1)S(1)}, u32[]{:S(2)}, u32[]{:S(2)}) async-start(bf16[64,2,32,128]{3,2,1,0:T(8,128)(2,1)} %scatter_fusion.1), calls=%async_computation.1 | async-start | bytes 2097152 | tf_op jit(solution)/shard_map/all_to_all | solution.py:76
  54.9 0.0 all-reduce.2.cloned.1.call-start
  54.9 0.0 copy-done.2
  54.9 6.6 %copy.44 = f32[32,32,1024]{2,0,1:T(8,128)} copy(f32[32,32,1024]{2,1,0:T(8,128)} %param.8) | data formatting | bytes 8388608 | tf_op args[0]
  61.6 0.6 broadcast.255
  62.2 0.8 reduce.3
  62.9 0.1 reshape.197
  63.1 0.1 copy.41
  63.2 0.1 copy.42
  63.3 0.2 reshape.207
  63.4 0.0 collective-permute-done.1
  63.4 0.0 collective-permute-done
  63.4 6.8 %fusion.11 = bf16[32,32,1024]{2,0,1:T(8,128)(2,1)S(1)} fusion(f32[1,32,1024]{2,0,1:T(1,128)S(1)} %collective-permute-done.1, f32[32,32,1024]{2,0,1:T(8,128)} %copy.44, f32[1,32,1024]{2,0,1:T(1,128)S(1)} %collective-permute-done, f32[32]{0:T(128)S(1)} %copy-done.2, f32[32]{0:T(128)S(1)} %multiply_subtract_fusion), kind=kLoop, calls=%fused_computation.19 | loop fusion | flops 7340032 | bytes 6553856 | tf_op jit(solution)/shard_map/convert_element_type | solution.py:49
  70.2 3.3 %convolution_bitcast_fusion.1 = f32[8,32,32,128]{3,1,2,0:T(8,128)S(1)} fusion(bf16[32,32,1024]{2,0,1:T(8,128)(2,1)S(1)} %fusion.11, f32[8,128]{1,0:T(8,128)S(1)} %multiply_add_fusion, f32[1024]{0:T(1024)S(1)} %iota_add_fusion), kind=kOutput, calls=%fused_computation.22 | convolution fusion | flops 2153775104 | bytes 6299648 | tf_op jit(solution)/shard_map/zlv,atv->alzt/dot_general | solution.py:56
  73.6 4.4 %copy.40 = f32[8,32,32,128]{3,2,1,0:T(8,128)} copy(f32[8,32,32,128]{3,1,2,0:T(8,128)S(1)} %convolution_bitcast_fusion.1) | data formatting | bytes 8388608 | tf_op jit(solution)/shard_map/zlv,atv->alzt/transpose | solution.py:56
  77.9 2.9 %gather_fusion = f32[128,32,128]{2,1,0:T(8,128)S(1)} fusion(f32[256,32,128]{2,1,0:T(8,128)} %bitcast.53, s32[1024]{0:T(1024)S(1)} %pad_clamp_fusion), kind=kCustom, calls=%fused_computation | custom fusion | bytes 4194816 | tf_op jit(solution)/shard_map/gather | solution.py:78
  80.8 1.6 broadcast_add_fusion
  82.4 0.0 all-to-all-done.1
  82.4 2.0 convert_divide_fusion
  84.4 2.5 %broadcast_in_dim.4 = f32[256,32,128]{2,1,0:T(8,128)} broadcast(f32[]{:T(128)} %constant.17.clone.1), dimensions={} | broadcast | bytes 4194308 | tf_op jit(solution)/shard_map/broadcast_in_dim | solution.py:80
  86.9 18.1 %scatter_fusion.2 = f32[256,32,128]{2,1,0:T(8,128)} fusion(f32[256,32,128]{2,1,0:T(8,128)} %broadcast_in_dim.4, s32[128]{0:T(128)S(1)} %fusion.25, f32[128,32,128]{2,1,0:T(8,128)S(1)} %bitcast.54), kind=kCustom, calls=%fused_computation.3 | custom fusion | flops 524288 | bytes 6291968 | tf_op jit(solution)/shard_map/scatter-add | solution.py:81
  105.0 2.7 %convert_element_type.31 = bf16[256,32,128]{2,1,0:T(8,128)(2,1)S(1)} convert(f32[256,32,128]{2,1,0:T(8,128)} %scatter_fusion.2) | non-fusion elementwise | flops 1048576 | bytes 6291456 | tf_op jit(solution)/shard_map/convert_element_type | solution.py:82
  107.7 4.6 %convolution_bitcast_fusion = f32[32,32,1024]{2,0,1:T(8,128)} fusion(bf16[8,32,32,128]{3,2,1,0:T(8,128)(2,1)S(1)} %bitcast.56, f32[8,128]{1,0:T(8,128)S(1)} %multiply_add_fusion, f32[1024]{0:T(1024)S(1)} %iota_add_fusion), kind=kOutput, calls=%fused_computation.21 | convolution fusion | flops 2153775104 | bytes 6299648 | tf_op jit(solution)/shard_map/alzt,atv->zlv/dot_general | solution.py:83
  112.2 0.0 all-reduce.2.cloned.1.call-update
  112.3 97.2 %all-reduce.2.cloned.1.call-done = f32[32,32,1024]{2,0,1:T(8,128)} async-done(((f32[32,32,1024]{2,0,1:T(8,128)}), f32[32,32,1024]{2,0,1:T(8,128)}) %all-reduce.2.cloned.1.call-update) | async-done | bytes 4194320 | tf_op jit(solution)/shard_map/psum | solution.py:84
  209.4 0.0 copy-start
  209.4 0.0 copy-start.1
  209.4 3.1 %broadcast_multiply_fusion = f32[32,32,1024]{2,0,1:T(8,128)S(1)} fusion(f32[32,32,1024]{2,0,1:T(8,128)} %all-reduce.2.cloned.1.call-done, f32[32]{0:T(128)S(1)} %copy-done.2), kind=kLoop, calls=%fused_computation.26 | loop fusion | flops 1048576 | bytes 8388736 | tf_op jit(solution)/shard_map/mul | solution.py:85
  212.5 0.2 fusion.31
  212.7 3.9 %collective-permute-start.2 = (f32[1,32,1024]{2,0,1:T(1,128)S(1)}, f32[1,32,1024]{2,0,1:T(1,128)S(1)}, u32[]{:S(2)}, u32[]{:S(2)}) collective-permute-start(f32[1,32,1024]{2,0,1:T(1,128)S(1)} %get-tuple-element.5), channel_id=1, source_target_pairs={{0,4},{4,8},{8,12},{12,16},{16,20},{20,24},{24,28},{28,32},{32,36}... | collective-permute-start | bytes 393224 | tf_op jit(solution)/shard_map/ppermute | solution.py:21
  216.6 1.9 collective-permute-start.3
  218.5 0.0 collective-permute-done.2
  218.6 6.5 %collective-permute-done.3 = f32[1,32,1024]{2,0,1:T(1,128)S(1)} collective-permute-done((f32[1,32,1024]{2,0,1:T(1,128)S(1)}, f32[1,32,1024]{2,0,1:T(1,128)S(1)}, u32[]{:S(2)}, u32[]{:S(2)}) %collective-permute-start.3) | collective-permute-done | bytes 131104 | tf_op jit(solution)/shard_map/ppermute | solution.py:22
  225.0 0.0 copy-done
  225.0 0.0 copy-done.1
  225.0 9.4 %fusion.6 = f32[32,32,1024]{2,0,1:T(8,128)S(1)} fusion(f32[1,32,1024]{2,0,1:T(1,128)S(1)} %collective-permute-done.3, f32[32,32,1024]{2,0,1:T(8,128)S(1)} %broadcast_multiply_fusion, f32[1,32,1024]{2,0,1:T(1,128)S(1)} %collective-permute-done.2, f32[32,32,1024]{2,1,0:T(8,128)} %param.9, f32[32,32,1024]{2,0,1:T(8,128)S(1)} %copy-done.1, ...), kind=kLoop, calls=%fused_computation.12 | loop fusion | flops 7340032 | bytes 21233792 | tf_op jit(solution)/shard_map/div | solution.py:87
  234.4 4.4 %copy.46 = f32[32,32,1024]{2,1,0:T(8,128)} copy(f32[32,32,1024]{2,0,1:T(8,128)S(1)} %fusion.6) | data formatting | bytes 8388608 | tf_op jit(solution)/shard_map/div | solution.py:87
  (7 shorter events, 0.0 us)
Async XLA Ops:
  6.5 48.4 %copy-start.2 = (f32[32]{0:T(128)S(1)}, f32[32]{0:T(128)}, u32[]{:S(2)}) copy-start(f32[32]{0:T(128)} %param.10) | copy-start | bytes 388
  13.8 31.3 %all-to-all-start = ((s32[64,1,2]{2,1,0:T(1,128)}), s32[64,1,2]{2,1,0:T(1,128)S(1)}, u32[]{:S(2)}, u32[]{:S(2)}) async-start(s32[64,1,2]{2,1,0:T(1,128)} %copy.33), calls=%async_computation | async-start | bytes 65536 | tf_op jit(solution)/shard_map/all_to_all | solution.py:77
  27.2 36.2 %collective-permute-start.1 = (f32[1,32,1024]{2,0,1:T(1,128)S(1)}, f32[1,32,1024]{2,0,1:T(1,128)S(1)}, u32[]{:S(2)}, u32[]{:S(2)}) collective-permute-start(f32[1,32,1024]{2,0,1:T(1,128)S(1)} %copy.37), channel_id=1, source_target_pairs={{4,0},{8,4},{12,8},{16,12},{20,16},{24,20},{28,24},{32,28},{36,32}... | collective-permute-start | bytes 393224 | tf_op jit(solution)/shard_map/ppermute | solution.py:22
  29.6 33.8 %collective-permute-start = (f32[1,32,1024]{2,0,1:T(1,128)S(1)}, f32[1,32,1024]{2,0,1:T(1,128)S(1)}, u32[]{:S(2)}, u32[]{:S(2)}) collective-permute-start(f32[1,32,1024]{2,0,1:T(1,128)S(1)} %copy.35), channel_id=1, source_target_pairs={{0,4},{4,8},{8,12},{12,16},{16,20},{20,24},{24,28},{28,32},{32,36}... | collective-permute-start | bytes 393224 | tf_op jit(solution)/shard_map/ppermute | solution.py:21
  45.1 37.3 %all-to-all-start.1 = ((bf16[64,2,32,128]{3,2,1,0:T(8,128)(2,1)}), bf16[64,2,32,128]{3,2,1,0:T(8,128)(2,1)S(1)}, u32[]{:S(2)}, u32[]{:S(2)}) async-start(bf16[64,2,32,128]{3,2,1,0:T(8,128)(2,1)} %scatter_fusion.1), calls=%async_computation.1 | async-start | bytes 2097152 | tf_op jit(solution)/shard_map/all_to_all | solution.py:76
  54.9 154.6 %all-reduce.2.cloned.1.call-start = ((), (), s32[]{:S(2)}) async-start(), calls=%async_computation.2 | async-start | bytes 8388608 | tf_op jit(solution)/shard_map/psum | solution.py:84
  209.4 15.6 %copy-start = (f32[32,32,1024]{2,1,0:T(8,128)S(1)}, f32[32,32,1024]{2,1,0:T(8,128)}, u32[]{:S(2)}) copy-start(f32[32,32,1024]{2,1,0:T(8,128)} %param.8) | copy-start | bytes 12582916
  209.4 15.6 %copy-start.1 = (f32[32,32,1024]{2,0,1:T(8,128)S(1)}, f32[32,32,1024]{2,0,1:T(8,128)}, u32[]{:S(2)}) copy-start(f32[32,32,1024]{2,0,1:T(8,128)} %all-reduce.2.cloned.1.call-done) | copy-start | bytes 12582916
  212.7 5.8 %collective-permute-start.2 = (f32[1,32,1024]{2,0,1:T(1,128)S(1)}, f32[1,32,1024]{2,0,1:T(1,128)S(1)}, u32[]{:S(2)}, u32[]{:S(2)}) collective-permute-start(f32[1,32,1024]{2,0,1:T(1,128)S(1)} %get-tuple-element.5), channel_id=1, source_target_pairs={{0,4},{4,8},{8,12},{12,16},{16,20},{20,24},{24,28},{28,32},{32,36}... | collective-permute-start | bytes 393224 | tf_op jit(solution)/shard_map/ppermute | solution.py:21
  216.6 8.4 %collective-permute-start.3 = (f32[1,32,1024]{2,0,1:T(1,128)S(1)}, f32[1,32,1024]{2,0,1:T(1,128)S(1)}, u32[]{:S(2)}, u32[]{:S(2)}) collective-permute-start(f32[1,32,1024]{2,0,1:T(1,128)S(1)} %get-tuple-element.6), channel_id=1, source_target_pairs={{4,0},{8,4},{12,8},{16,12},{20,16},{24,20},{28,24},{32,28},{36,32}... | collective-permute-start | bytes 393224 | tf_op jit(solution)/shard_map/ppermute | solution.py:22
Sparse Core Ops, SparseCore 0:
  112.4 97.0 all-reduce.1
where the time goes:
time: 251 us; the launch traced here: 246 us
  waiting for transfers between devices  104 us (41%)
  other arithmetic  48.1 us (19%)
  local copies, waits for them, and re-layouts  36.9 us (15%)
  starting transfers between devices  35.5 us (14%)
  between operations  13.6 us (5%)
  matrix products  7.89 us (3%)
    psum x1, waiting for transfers between devices, on_device(): total = lax.psum(back, 'view')  97.2 us
    scatter-add x1, other arithmetic, on_device(): sums = sums.at[index.reshape(-1)].add(ratios.reshape(-1, planes, bins))  18.1 us
    all_to_all x1, starting transfers between devices, on_device(): lax.all_to_all(send_index, 'slab', split_axis=0, concat_axis=0, tiled=True)  12.3 us
    all_to_all x1, starting transfers between devices, on_device(): lax.all_to_all(send_rows, 'slab', split_axis=0, concat_axis=0, tiled=True)  9.77 us
    div x1, other arithmetic, on_device(): return activity * smoothed / sensitivity  9.36 us
    ppermute x2, starting transfers between devices, with_halo(): before = lax.ppermute(last, axis, up)  9.26 us
    scatter x1, local copies, waits for them, and re-layouts, on_device(): send_rows = jnp.zeros((slab_count, capacity, planes, bins), jnp.bfloat16)...  8 us
    convert_element_type x1, other arithmetic, on_device(): ((1.0 - 2.0 * weight) * activity + weight * (padded[:-2] + padded[2:])).a...  6.8 us
  transfers between devices with their start and end apart: 7, of which 2 were waited for; matrix products, arithmetic and copies ran while one was open for 16% of the time, Pallas kernels for 0%

commit v1 on v0

--- a/solution.py
+++ b/solution.py
@@ -51,37 +51,74 @@
     )
     planes, lines_here, length = activity.shape
     bins = measured.shape[3]
+    row = planes * bins
     tof_kernel = kernels(subset_views[0], bins, length)
     angle_count = tof_kernel.shape[0]
+    pairs = angle_count * lines_here
     projected = jnp.einsum("zlv,atv->alzt", blurred, tof_kernel, preferred_element_type=jnp.float32)
-    projected = projected.reshape(angle_count * lines_here, planes, bins)
+    projected = projected.reshape(pairs, planes, bins)
+
     slab_count = lax.axis_size("slab")
     block_total = measured.shape[1]
     capacity = 2 * block_total // slab_count
+    slots = slab_count * capacity
     targets = block_slab[0, :, 0]
     onehot = (targets[:, None] == jnp.arange(slab_count, dtype=jnp.int32)[None, :]).astype(
         jnp.int32
     )
     slot_pos = jnp.sum((jnp.cumsum(onehot, axis=0) - onehot) * onehot, axis=1)
-    send_rows = (
-        jnp.zeros((slab_count, capacity, planes, bins), jnp.bfloat16)
-        .at[targets, slot_pos]
-        .set(measured[0])
+    flat_slot = targets * capacity + slot_pos
+    place = (jnp.arange(slots, dtype=jnp.int32)[:, None] == flat_slot[None, :]).astype(
+        jnp.bfloat16
     )
-    send_index = (
-        jnp.zeros((slab_count, capacity), jnp.int32)
-        .at[targets, slot_pos]
-        .set(block_angle[0] * lines_here + block_line[0])
+    pair_id = block_angle[0] * lines_here + block_line[0]
+    extra = 128
+    tag = jnp.broadcast_to(pair_id.astype(jnp.bfloat16)[:, None], (block_total, extra))
+    outgoing = jnp.concatenate([measured[0].reshape(block_total, row), tag], axis=1)
+    send = jnp.dot(place, outgoing, preferred_element_type=jnp.float32).astype(jnp.bfloat16)
+    recv = lax.all_to_all(
+        send.reshape(slab_count, capacity, row + extra), "slab", 0, 0, tiled=True
+    ).reshape(slots, row + extra)
+    index = recv[:, row].astype(jnp.int32)
+    rows = recv[:, :row].reshape(slots, planes, bins)
+    estimate = projected[index]
+    ratios = (rows.astype(jnp.float32) / (estimate + BACKGROUND)).reshape(slots, row)
+
+    same = index[:, None] == index[None, :]
+    earlier = jnp.arange(slots)[None, :] < jnp.arange(slots)[:, None]
+    first = ~jnp.any(same & earlier, axis=1)
+    merge = (same & first[:, None]).astype(jnp.float32)
+    merged = jnp.dot(merge, ratios, precision=lax.Precision.HIGHEST).astype(jnp.bfloat16)
+
+    views = subset_views[0]
+    info = jnp.zeros((extra,), jnp.float32)
+    info = info.at[0:angle_count].set((views // 16).astype(jnp.float32))
+    info = info.at[angle_count : 2 * angle_count].set((views % 16).astype(jnp.float32))
+    info = jnp.broadcast_to(info[None, :], (slots, extra))
+    info = info.at[:, 2 * angle_count].set(index.astype(jnp.float32)).astype(jnp.bfloat16)
+    payload = jnp.concatenate([merged, info], axis=1)
+    everything = lax.all_gather(payload, "view", axis=0, tiled=False)
+    group_count = everything.shape[0]
+
+    dense = []
+    kernel_all = []
+    for group in range(group_count):
+        got = everything[group]
+        tail = got[0, row:].astype(jnp.int32)
+        views_k = tail[0:angle_count] * 16 + tail[angle_count : 2 * angle_count]
+        kernel_all.append(kernels(views_k, bins, length))
+        index_k = got[:, row + 2 * angle_count].astype(jnp.int32)
+        scatter = (jnp.arange(pairs, dtype=jnp.int32)[:, None] == index_k[None, :]).astype(
+            jnp.bfloat16
+        )
+        dense.append(
+            jnp.dot(scatter, got[:, :row], preferred_element_type=jnp.float32).astype(jnp.bfloat16)
+        )
+    dense = jnp.stack(dense).reshape(group_count, angle_count, lines_here, planes, bins)
+    kernel_all = jnp.stack(kernel_all)
+    total = jnp.einsum(
+        "kalzt,katv->zlv", dense, kernel_all, preferred_element_type=jnp.float32
     )
-    rows = lax.all_to_all(send_rows, "slab", split_axis=0, concat_axis=0, tiled=True)
-    index = lax.all_to_all(send_index, "slab", split_axis=0, concat_axis=0, tiled=True)
-    estimate = projected[index]
-    ratios, index = (rows.astype(jnp.float32) / (estimate + BACKGROUND), index)
-    sums = jnp.zeros((angle_count * lines_here, planes, bins), jnp.float32)
-    sums = sums.at[index.reshape(-1)].add(ratios.reshape(-1, planes, bins))
-    rounded = sums.astype(jnp.bfloat16).reshape(angle_count, lines_here, planes, bins)
-    back = jnp.einsum("alzt,atv->zlv", rounded, tof_kernel, preferred_element_type=jnp.float32)
-    total = lax.psum(back, "view")
     edges = with_halo(weight * total, (("slab", 0),), 1)
     smoothed = (1.0 - 2.0 * weight) * total + edges[:-2] + edges[2:]
     return activity * smoothed / sensitivity

time: 251 us -> 193 us (0.77)
  waiting for transfers between devices: 104 us -> 75.5 us
  other arithmetic: 48.1 us -> 26.9 us
  matrix products: 7.89 us -> 28 us
  local copies, waits for them, and re-layouts: 36.9 us -> 21.6 us
  starting transfers between devices: 35.5 us -> 23.5 us
    psum x1 -> x0, waiting for transfers between devices: 97.2 us -> none  [on_device(): total = lax.psum(back, 'view')]
    all_gather x0 -> x1, waiting for transfers between devices: none -> 49.8 us  [on_device(): everything = lax.all_gather(payload, 'view', axis=0, tiled=False)]
    scatter-add x1 -> x0, other arithmetic: 18.1 us -> none  [on_device(): sums = sums.at[index.reshape(-1)].add(ratios.reshape(-1, planes, bins))]
    dot_general x1 -> x7, matrix products: 4.59 us -> 20.9 us  [the longest x1 14 us: on_device(): jnp.einsum('kalzt,katv->zlv', dense, kernel_all, preferred_element_type=j...]
    ppermute x2, waiting for transfers between devices: 0.01 us -> 16.3 us  [with_halo(): before = lax.ppermute(last, axis, up)]
    scatter x2, local copies, waits for them, and re-layouts: 11.5 us -> 0.36 us  [the longest x1 0.36 us: on_device(): info.at[:, 2 * angle_count].set(index.astype(jnp.float32))]
    all_to_all x2 -> x1, starting transfers between devices: 22 us -> 12.3 us  [on_device(): lax.all_to_all(send.reshape(slab_count, capacity, row + extra), 'slab', 0...]
    dot_general x1, matrix products: 3.3 us -> 7.09 us  [on_device(): jnp.einsum('zlv,atv->alzt', blurred, tof_kernel, preferred_element_type=j...]
  transfers between devices with their start and end apart: 7 -> 6, of which waited for: 2 -> 4; matrix products, arithmetic and copies ran while one was open for 16% -> 7% of each run, Pallas kernels for 0% -> 0%
where the time goes in v1:
time: 193 us; the launch traced here: 189 us
  waiting for transfers between devices  75.5 us (39%)
  matrix products  28 us (15%)
  other arithmetic  26.9 us (14%)
  starting transfers between devices  23.5 us (12%)
  local copies, waits for them, and re-layouts  21.6 us (11%)
  between operations  13.7 us (7%)
    all_gather x1, waiting for transfers between devices, on_device(): everything = lax.all_gather(payload, 'view', axis=0, tiled=False)  49.8 us
    ppermute x2, waiting for transfers between devices, with_halo(): before = lax.ppermute(last, axis, up)  16.3 us
    dot_general x1, matrix products, on_device(): jnp.einsum('kalzt,katv->zlv', dense, kernel_all, preferred_element_type=j...  14 us
    all_to_all x1, starting transfers between devices, on_device(): lax.all_to_all(send.reshape(slab_count, capacity, row + extra), 'slab', 0...  12.3 us
    div x1, other arithmetic, on_device(): return activity * smoothed / sensitivity  11.1 us
    ppermute x2, waiting for transfers between devices, with_halo(): after = lax.ppermute(leading, axis, down)  9.37 us
    ppermute x2, starting transfers between devices, with_halo(): before = lax.ppermute(last, axis, up)  7.32 us
    dot_general x1, matrix products, on_device(): jnp.einsum('zlv,atv->alzt', blurred, tof_kernel, preferred_element_type=j...  7.09 us
  transfers between devices with their start and end apart: 6, of which 4 were waited for; matrix products, arithmetic and copies ran while one was open for 7% of the time, Pallas kernels for 0%

profile of v1, /device:TPU:31, one launch (start us, length us, event | category | flops | bytes accessed | tf_op | source)
XLA Modules:
  0.0 189.1 jit_solution(5127804948928661454)
XLA Ops:
  6.5 0.8 fusion.75
  7.3 0.1 reduce_window_sum.11
  7.4 0.8 select_reduce_fusion
  8.2 0.7 multiply_add_fusion.5
  8.9 1.3 copy.48
  10.1 0.7 convert_bitcast_fusion
  10.8 0.1 broadcast_in_dim.6
  10.9 0.4 convolution_convert_fusion
  11.3 1.2 reshape.516
  12.6 12.3 %all-to-all-start = ((bf16[64,2,4224]{2,1,0:T(2,128)(2,1)}), bf16[64,2,4224]{2,1,0:T(2,128)(2,1)S(1)}, u32[]{:S(2)}, u32[]{:S(2)}) async-start(bf16[64,2,4224]{2,1,0:T(2,128)(2,1)} %reshape.516), calls=%async_computation | async-start | bytes 2162688 | tf_op jit(solution)/shard_map/all_to_all | solution.py:79
  24.9 0.0 all-gather.3.cloned.1.call-start
  24.9 1.0 fusion.95
  25.9 3.3 %collective-permute-start = (f32[1,32,1024]{2,1,0:T(8,128)S(1)}, f32[1,32,1024]{2,1,0:T(8,128)S(1)}, u32[]{:S(2)}, u32[]{:S(2)}) collective-permute-start(f32[1,32,1024]{2,1,0:T(8,128)S(1)} %get-tuple-element.61), channel_id=1, source_target_pairs={{0,4},{4,8},{8,12},{12,16},{16,20},{20,24},{24,28},{28,32},{32,36}... | collective-permute-start | bytes 393224 | tf_op jit(solution)/shard_map/ppermute | solution.py:21
  29.3 1.9 %collective-permute-start.1 = (f32[1,32,1024]{2,1,0:T(8,128)S(1)}, f32[1,32,1024]{2,1,0:T(8,128)S(1)}, u32[]{:S(2)}, u32[]{:S(2)}) collective-permute-start(f32[1,32,1024]{2,1,0:T(8,128)S(1)} %get-tuple-element.62), channel_id=1, source_target_pairs={{4,0},{8,4},{12,8},{16,12},{20,16},{24,20},{28,24},{32,28},{36,32}... | collective-permute-start | bytes 393224 | tf_op jit(solution)/shard_map/ppermute | solution.py:22
  31.2 0.0 copy-done.4
  31.2 0.1 fusion.85
  31.3 0.1 multiply_add_fusion.4
  31.4 0.0 copy-done.3
  31.4 0.6 slice.160
  32.0 0.7 compare_reduce_fusion
  32.7 16.3 %collective-permute-done = f32[1,32,1024]{2,1,0:T(8,128)S(1)} collective-permute-done((f32[1,32,1024]{2,1,0:T(8,128)S(1)}, f32[1,32,1024]{2,1,0:T(8,128)S(1)}, u32[]{:S(2)}, u32[]{:S(2)}) %collective-permute-start) | collective-permute-done | bytes 131104 | tf_op jit(solution)/shard_map/ppermute | solution.py:21
  49.0 2.9 %collective-permute-done.1 = f32[1,32,1024]{2,1,0:T(8,128)S(1)} collective-permute-done((f32[1,32,1024]{2,1,0:T(8,128)S(1)}, f32[1,32,1024]{2,1,0:T(8,128)S(1)}, u32[]{:S(2)}, u32[]{:S(2)}) %collective-permute-start.1) | collective-permute-done | bytes 131104 | tf_op jit(solution)/shard_map/ppermute | solution.py:22
  51.9 7.1 %convolution_bitcast_fusion = f32[8,32,32,128]{3,1,2,0:T(8,128)S(1)} fusion(f32[8,128]{1,0:T(8,128)S(1)} %multiply_add_fusion.4, f32[1024]{0:T(1024)S(1)} %iota_add_fusion, f32[1,32,1024]{2,1,0:T(8,128)S(1)} %collective-permute-done.1, f32[32,32,1024]{2,1,0:T(8,128)} %param.14, f32[1,32,1024]{2,1,0:T(8,128)S(1)} %collective-permute-done, ...), kind=kOutput, calls=%fused_computation.63 | convolution fusion | flops 2161115136 | bytes 8659200 | tf_op jit(solution)/shard_map/zlv,atv->alzt/dot_general | solution.py:58
  59.0 4.4 %copy.24 = f32[8,32,32,128]{3,2,1,0:T(8,128)} copy(f32[8,32,32,128]{3,1,2,0:T(8,128)S(1)} %convolution_bitcast_fusion) | data formatting | bytes 8388608 | tf_op jit(solution)/shard_map/zlv,atv->alzt/transpose | solution.py:58
  63.4 0.0 all-to-all-done
  63.4 0.4 reshape.517
  63.8 0.1 convert_reduce_fusion
  63.9 0.2 fusion.72
  64.1 2.9 %gather_fusion = f32[128,32,128]{2,1,0:T(8,128)S(1)} fusion(f32[256,32,128]{2,1,0:T(8,128)} %bitcast.121, s32[1024]{0:T(1024)S(1)} %pad_clamp_fusion), kind=kCustom, calls=%fused_computation | custom fusion | bytes 4194816 | tf_op jit(solution)/shard_map/gather | solution.py:84
  67.0 0.2 broadcast_add_fusion
  67.3 1.3 fusion.66
  68.6 2.5 %convolution_convert_fusion.5 = bf16[128,4096]{1,0:T(8,128)(2,1)S(1)} fusion(f32[16,8,32,128]{3,2,1,0:T(8,128)S(1)} %bitcast.126, bf16[128,4224]{1,0:T(8,128)(2,1)S(1)} %reshape.517, s32[128]{0:T(128)S(1)} %get-tuple-element.45, pred[128]{0:T(512)(128)(4,1)S(1)} %not.7), kind=kOutput, calls=%fused_computation.26 | convolution fusion | flops 806912000 | bytes 4195840 | tf_op jit(solution)/shard_map/dot_general | solution.py:91
  71.1 0.4 scatter.14
  71.5 1.1 pad_maximum_fusion.4
  72.5 0.0 all-gather.3.cloned.1.call-update
  72.6 49.8 %all-gather.3.cloned.1.call-done = bf16[512,4224]{1,0:T(8,128)(2,1)} async-done(((bf16[128,4224]{1,0:T(8,128)(2,1)}), bf16[512,4224]{1,0:T(8,128)(2,1)}) %all-gather.3.cloned.1.call-update) | async-done | bytes 4325392 | tf_op jit(solution)/shard_map/all_gather | solution.py:100
  122.4 0.8 slice_convert_fusion.3
  123.2 0.1 multiply_bitcast_fusion.2
  123.4 0.1 multiply_bitcast_fusion
  123.7 1.1 convert_reduce_fusion.4
  124.7 1.9 %fusion.54 = bf16[32,8,32,128]{3,1,2,0:T(8,128)(2,1)S(1)} fusion(bf16[512,4224]{1,0:T(8,128)(2,1)} %all-gather.3.cloned.1.call-done, s32[128]{0:T(128)S(1)} %get-tuple-element.41), kind=kOutput, calls=%fused_computation.73 | convolution fusion | flops 269516800 | bytes 3146240 | tf_op jit(solution)/shard_map/dot_general | solution.py:115
  126.6 0.5 copy.37
  127.1 0.0 copy-done.1
  127.1 0.7 fusion.57
  127.8 0.5 copy.40
  128.3 0.7 fusion.55
  129.0 1.9 copy.38
  130.9 0.7 fusion.56
  131.6 1.8 copy.39
  133.4 0.1 multiply_add_fusion.3
  133.5 6.0 %fusion.21 = (bf16[1,8,128,1024]{3,2,0,1:T(8,128)(2,1)}, bf16[1,8,128,1024]{3,2,0,1:T(8,128)(2,1)}, bf16[1,8,128,1024]{3,2,0,1:T(8,128)(2,1)}, bf16[1,8,128,1024]{3,2,0,1:T(8,128)(2,1)}) fusion(f32[8,128]{1,0:T(8,128)S(1)} %get-tuple-element.67, f32[1024]{0:T(1024)S(1)} %iota_add_fusion, f32[8,128]{1,0:T(8,128)S(1)} %get-tuple-element.68, ...), kind=kLoop, calls=%fused_computation.34 | loop fusion | flops 25165824 | bytes 8409088 | tf_op jit(solution)/shard_map/convert_element_type | solution.py:41
  139.5 14.0 %fusion = f32[1024,32,32,1,1]{0,2,4,1,3:T(8,128)S(1)} fusion(bf16[1,8,128,1024]{3,2,0,1:T(8,128)(2,1)} %get-tuple-element.66, bf16[1,8,128,1024]{3,2,0,1:T(8,128)(2,1)} %get-tuple-element.65, bf16[1,8,128,1024]{3,2,0,1:T(8,128)(2,1)} %get-tuple-element.64, bf16[1,8,128,1024]{3,2,0,1:T(8,128)(2,1)} %get-tuple-element.63, ...), kind=kOutput, calls=%fused_computation.2 | convolution fusion | flops 8657043456 | bytes 20971520 | tf_op jit(solution)/shard_map/kalzt,katv->zlv/dot_general | solution.py:119
  153.4 0.0 copy-start
  153.5 0.0 copy-start.2
  153.5 0.6 fusion.43
  154.0 0.2 fusion.94
  154.3 4.0 %collective-permute-start.2 = (f32[1,32,1024]{2,0,1:T(1,128)S(1)}, f32[1,32,1024]{2,0,1:T(1,128)S(1)}, u32[]{:S(2)}, u32[]{:S(2)}) collective-permute-start(f32[1,32,1024]{2,0,1:T(1,128)S(1)} %get-tuple-element.59), channel_id=1, source_target_pairs={{0,4},{4,8},{8,12},{12,16},{16,20},{20,24},{24,28},{28,32},{32,36}... | collective-permute-start | bytes 393224 | tf_op jit(solution)/shard_map/ppermute | solution.py:21
  158.3 1.9 %collective-permute-start.3 = (f32[1,32,1024]{2,0,1:T(1,128)S(1)}, f32[1,32,1024]{2,0,1:T(1,128)S(1)}, u32[]{:S(2)}, u32[]{:S(2)}) collective-permute-start(f32[1,32,1024]{2,0,1:T(1,128)S(1)} %get-tuple-element.60), channel_id=1, source_target_pairs={{4,0},{8,4},{12,8},{16,12},{20,16},{24,20},{28,24},{32,28},{36,32}... | collective-permute-start | bytes 393224 | tf_op jit(solution)/shard_map/ppermute | solution.py:22
  160.2 0.0 collective-permute-done.2
  160.2 6.5 %collective-permute-done.3 = f32[1,32,1024]{2,0,1:T(1,128)S(1)} collective-permute-done((f32[1,32,1024]{2,0,1:T(1,128)S(1)}, f32[1,32,1024]{2,0,1:T(1,128)S(1)}, u32[]{:S(2)}, u32[]{:S(2)}) %collective-permute-start.3) | collective-permute-done | bytes 131104 | tf_op jit(solution)/shard_map/ppermute | solution.py:22
  166.7 0.0 copy-done
  166.7 0.0 copy-done.2
  166.7 11.1 %fusion.36 = f32[32,32,1024]{2,0,1:T(8,128)S(1)} fusion(f32[1,32,1024]{2,0,1:T(1,128)S(1)} %collective-permute-done.3, f32[32,32,1024]{2,0,1:T(8,128)S(1)} %fusion.43, f32[1,32,1024]{2,0,1:T(1,128)S(1)} %collective-permute-done.2, f32[1024,32,32,1,1]{0,2,4,1,3:T(8,128)S(1)} %fusion, f32[32,32,1024]{2,1,0:T(8,128)S(1)} %copy-done.2, ...), kind=kLoop, calls=%fused_computation.50 | loop fusion | flops 7340032 | bytes 21233792 | tf_op jit(solution)/shard_map/div | solution.py:124
  177.8 4.4 %copy.31 = f32[32,32,1024]{2,1,0:T(8,128)} copy(f32[32,32,1024]{2,0,1:T(8,128)S(1)} %fusion.36) | data formatting | bytes 8388608 | tf_op jit(solution)/shard_map/div | solution.py:124
  (15 shorter events, 0.2 us)
Async XLA Ops:
  6.5 24.7 %copy-start.4 = (s32[1,8]{1,0:T(1,128)S(1)}, s32[1,8]{1,0:T(1,128)}, u32[]{:S(2)}) copy-start(s32[1,8]{1,0:T(1,128)} %param.21) | copy-start | bytes 100
  6.5 24.9 %copy-start.3 = (f32[32]{0:T(128)S(1)}, f32[32]{0:T(128)}, u32[]{:S(2)}) copy-start(f32[32]{0:T(128)} %param.16) | copy-start | bytes 388
  12.6 50.8 %all-to-all-start = ((bf16[64,2,4224]{2,1,0:T(2,128)(2,1)}), bf16[64,2,4224]{2,1,0:T(2,128)(2,1)S(1)}, u32[]{:S(2)}, u32[]{:S(2)}) async-start(bf16[64,2,4224]{2,1,0:T(2,128)(2,1)} %reshape.516), calls=%async_computation | async-start | bytes 2162688 | tf_op jit(solution)/shard_map/all_to_all | solution.py:79
  24.9 97.5 %all-gather.3.cloned.1.call-start = ((), (), s32[]{:S(2)}) async-start(), calls=%async_computation.1 | async-start | bytes 5406720 | tf_op jit(solution)/shard_map/all_gather | solution.py:100
  25.9 23.1 %collective-permute-start = (f32[1,32,1024]{2,1,0:T(8,128)S(1)}, f32[1,32,1024]{2,1,0:T(8,128)S(1)}, u32[]{:S(2)}, u32[]{:S(2)}) collective-permute-start(f32[1,32,1024]{2,1,0:T(8,128)S(1)} %get-tuple-element.61), channel_id=1, source_target_pairs={{0,4},{4,8},{8,12},{12,16},{16,20},{20,24},{24,28},{28,32},{32,36}... | collective-permute-start | bytes 393224 | tf_op jit(solution)/shard_map/ppermute | solution.py:21
  29.3 22.6 %collective-permute-start.1 = (f32[1,32,1024]{2,1,0:T(8,128)S(1)}, f32[1,32,1024]{2,1,0:T(8,128)S(1)}, u32[]{:S(2)}, u32[]{:S(2)}) collective-permute-start(f32[1,32,1024]{2,1,0:T(8,128)S(1)} %get-tuple-element.62), channel_id=1, source_target_pairs={{4,0},{8,4},{12,8},{16,12},{20,16},{24,20},{28,24},{32,28},{36,32}... | collective-permute-start | bytes 393224 | tf_op jit(solution)/shard_map/ppermute | solution.py:22
  122.4 4.8 %copy-start.1 = (bf16[512,4224]{1,0:T(8,128)(2,1)S(1)}, bf16[512,4224]{1,0:T(8,128)(2,1)}, u32[]{:S(2)}) copy-start(bf16[512,4224]{1,0:T(8,128)(2,1)} %all-gather.3.cloned.1.call-done) | copy-start | bytes 12976132
  153.4 13.2 %copy-start = (f32[32,32,1024]{2,1,0:T(8,128)S(1)}, f32[32,32,1024]{2,1,0:T(8,128)}, u32[]{:S(2)}) copy-start(f32[32,32,1024]{2,1,0:T(8,128)} %param.14) | copy-start | bytes 12582916
  153.5 13.2 %copy-start.2 = (f32[32,32,1024]{2,1,0:T(8,128)S(1)}, f32[32,32,1024]{2,1,0:T(8,128)}, u32[]{:S(2)}) copy-start(f32[32,32,1024]{2,1,0:T(8,128)} %param.15) | copy-start | bytes 12582916
  154.3 5.9 %collective-permute-start.2 = (f32[1,32,1024]{2,0,1:T(1,128)S(1)}, f32[1,32,1024]{2,0,1:T(1,128)S(1)}, u32[]{:S(2)}, u32[]{:S(2)}) collective-permute-start(f32[1,32,1024]{2,0,1:T(1,128)S(1)} %get-tuple-element.59), channel_id=1, source_target_pairs={{0,4},{4,8},{8,12},{12,16},{16,20},{20,24},{24,28},{28,32},{32,36}... | collective-permute-start | bytes 393224 | tf_op jit(solution)/shard_map/ppermute | solution.py:21
  158.3 8.4 %collective-permute-start.3 = (f32[1,32,1024]{2,0,1:T(1,128)S(1)}, f32[1,32,1024]{2,0,1:T(1,128)S(1)}, u32[]{:S(2)}, u32[]{:S(2)}) collective-permute-start(f32[1,32,1024]{2,0,1:T(1,128)S(1)} %get-tuple-element.60), channel_id=1, source_target_pairs={{4,0},{8,4},{12,8},{16,12},{20,16},{24,20},{28,24},{32,28},{36,32}... | collective-permute-start | bytes 393224 | tf_op jit(solution)/shard_map/ppermute | solution.py:22
Sparse Core Ops, SparseCore 0:
  72.7 49.6 all-gather.2

commit v2 on v1

--- a/solution.py
+++ b/solution.py
@@ -3,7 +3,11 @@
 import jax
 import jax.numpy as jnp
 from jax import lax
+from jax.experimental import pallas as pl
+from jax.experimental.pallas import tpu as pltpu
 from jax.sharding import PartitionSpec as P
+
+MESH = pl.DeviceIdType.MESH
 
 VIEWS_ALL = 336
 
@@ -41,6 +45,62 @@
     return values.astype(jnp.bfloat16)
 
 
+def ring_gather_kernel(payload, out, send_sems, recv_sems):
+    count = lax.axis_size("view")
+    me = lax.axis_index("view")
+    slab = lax.axis_index("slab")
+    left = lax.rem(me + count - 1, count)
+    right = lax.rem(me + 1, count)
+    half = payload.shape[0] // 2
+
+    barrier = pltpu.get_barrier_semaphore()
+    for neighbour in (left, right):
+        pl.semaphore_signal(barrier, inc=1, device_id=(slab, neighbour), device_id_type=MESH)
+    pl.semaphore_wait(barrier, 2)
+
+    to_left = pltpu.make_async_remote_copy(
+        src_ref=payload, dst_ref=out.at[1], send_sem=send_sems.at[0], recv_sem=recv_sems.at[1],
+        device_id=(slab, left), device_id_type=MESH,
+    )
+    to_right = pltpu.make_async_remote_copy(
+        src_ref=payload, dst_ref=out.at[0], send_sem=send_sems.at[1], recv_sem=recv_sems.at[0],
+        device_id=(slab, right), device_id_type=MESH,
+    )
+    to_left.start()
+    to_right.start()
+    to_right.wait_recv()
+    onward_right = pltpu.make_async_remote_copy(
+        src_ref=out.at[0, pl.ds(0, half)], dst_ref=out.at[2, pl.ds(0, half)],
+        send_sem=send_sems.at[2], recv_sem=recv_sems.at[2],
+        device_id=(slab, right), device_id_type=MESH,
+    )
+    onward_right.start()
+    to_left.wait_recv()
+    onward_left = pltpu.make_async_remote_copy(
+        src_ref=out.at[1, pl.ds(half, half)], dst_ref=out.at[2, pl.ds(half, half)],
+        send_sem=send_sems.at[3], recv_sem=recv_sems.at[3],
+        device_id=(slab, left), device_id_type=MESH,
+    )
+    onward_left.start()
+    to_left.wait_send()
+    to_right.wait_send()
+    onward_right.wait_send()
+    onward_left.wait_send()
+    onward_right.wait_recv()
+    onward_left.wait_recv()
+
+
+def ring_gather(payload):
+    return pl.pallas_call(
+        ring_gather_kernel,
+        out_shape=jax.ShapeDtypeStruct((3,) + payload.shape, payload.dtype),
+        in_specs=[pl.BlockSpec(memory_space=pl.ANY)],
+        out_specs=pl.BlockSpec(memory_space=pl.ANY),
+        scratch_shapes=[pltpu.SemaphoreType.DMA((4,)), pltpu.SemaphoreType.DMA((4,))],
+        compiler_params=pltpu.CompilerParams(collective_id=0, has_side_effects=True),
+    )(payload)
+
+
 def on_device(
     activity, sensitivity, psf_width, measured, block_slab, block_line, block_angle, subset_views
 ):
@@ -97,7 +157,7 @@
     info = jnp.broadcast_to(info[None, :], (slots, extra))
     info = info.at[:, 2 * angle_count].set(index.astype(jnp.float32)).astype(jnp.bfloat16)
     payload = jnp.concatenate([merged, info], axis=1)
-    everything = lax.all_gather(payload, "view", axis=0, tiled=False)
+    everything = jnp.concatenate([payload[None], ring_gather(payload)], axis=0)
     group_count = everything.shape[0]
 
     dense = []

time: 193 us -> 170 us (0.88); the launches traced: 189 us -> 168 us
  waiting for transfers between devices: 75.5 us -> 26.5 us
  Pallas kernels: 0 us -> 36.1 us
  between operations: 13.7 us -> 0.36 us
  starting transfers between devices: 23.5 us -> 28.9 us
  local copies, waits for them, and re-layouts: 21.6 us -> 23.7 us
    all_gather x1 -> x0, waiting for transfers between devices: 49.8 us -> none  [on_device(): everything = lax.all_gather(payload, 'view', axis=0, tiled=False)]
    pallas_call x0 -> x1, Pallas kernels: none -> 36.1 us  [ring_gather(): pl.pallas_call(ring_gather_kernel, out_shape=jax.ShapeDtypeStruct((3,) +...]
    all_to_all x1, waiting for transfers between devices: 0.01 us -> 20.1 us  [on_device(): lax.all_to_all(send.reshape(slab_count, capacity, row + extra), 'slab', 0...]
    ppermute x2, waiting for transfers between devices: 16.3 us -> 0.01 us  [with_halo(): before = lax.ppermute(last, axis, up)]
    ppermute x2, starting transfers between devices: 7.32 us -> 12.8 us  [with_halo(): before = lax.ppermute(last, axis, up)]
    ppermute x2, waiting for transfers between devices: 9.37 us -> 6.46 us  [with_halo(): after = lax.ppermute(leading, axis, down)]
    squeeze x0 -> x1, local copies, waits for them, and re-layouts: none -> 2.11 us  [on_device(): got = everything[group]]
    unnamed x15 -> x13, local copies, waits for them, and re-layouts: 5.94 us -> 5.94 us
  transfers between devices with their start and end apart: 6 -> 5, of which waited for: 4 -> 2; matrix products, arithmetic and copies ran while one was open for 7% -> 3% of each run, Pallas kernels for 0% -> 0%
where the time goes in v2:
time: 170 us; the launch traced here: 168 us
  Pallas kernels  36.1 us (21%)
  starting transfers between devices  28.9 us (17%)
  matrix products  26.8 us (16%)
  waiting for transfers between devices  26.5 us (16%)
  other arithmetic  25.9 us (15%)
  local copies, waits for them, and re-layouts  23.7 us (14%)
    pallas_call x1, Pallas kernels, ring_gather(): pl.pallas_call(ring_gather_kernel, out_shape=jax.ShapeDtypeStruct((3,) +...  36.1 us
    all_to_all x1, waiting for transfers between devices, on_device(): lax.all_to_all(send.reshape(slab_count, capacity, row + extra), 'slab', 0...  20.1 us
    dot_general x1, matrix products, on_device(): jnp.einsum('kalzt,katv->zlv', dense, kernel_all, preferred_element_type=j...  14 us
    ppermute x2, starting transfers between devices, with_halo(): before = lax.ppermute(last, axis, up)  12.8 us
    all_to_all x1, starting transfers between devices, on_device(): lax.all_to_all(send.reshape(slab_count, capacity, row + extra), 'slab', 0...  12.3 us
    div x1, other arithmetic, on_device(): return activity * smoothed / sensitivity  11.1 us
    dot_general x1, matrix products, on_device(): jnp.einsum('zlv,atv->alzt', blurred, tof_kernel, preferred_element_type=j...  7.09 us
    ppermute x2, waiting for transfers between devices, with_halo(): after = lax.ppermute(leading, axis, down)  6.46 us
  transfers between devices with their start and end apart: 5, of which 2 were waited for; matrix products, arithmetic and copies ran while one was open for 3% of the time, Pallas kernels for 0%

profile of v2, /device:TPU:31, one launch (start us, length us, event | category | flops | bytes accessed | tf_op | source)
XLA Modules:
  0.0 168.2 jit_solution(16954019951760426)
XLA Ops:
  0.0 0.8 fusion.74
  0.8 0.1 reduce_window_sum.11
  0.9 0.8 select_reduce_fusion
  1.7 0.7 multiply_add_fusion.5
  2.4 1.3 copy.48
  3.6 0.7 convert_bitcast_fusion
  4.3 0.1 broadcast_in_dim.7
  4.4 0.4 convolution_convert_fusion
  4.8 1.2 reshape.516
  6.0 12.3 %all-to-all-start = ((bf16[64,2,4224]{2,1,0:T(2,128)(2,1)}), bf16[64,2,4224]{2,1,0:T(2,128)(2,1)S(1)}, u32[]{:S(2)}, u32[]{:S(2)}) async-start(bf16[64,2,4224]{2,1,0:T(2,128)(2,1)} %reshape.516), calls=%async_computation | async-start | bytes 2162688 | tf_op jit(solution)/shard_map/all_to_all | solution.py:139
  18.3 1.0 fusion.94
  19.3 3.3 %collective-permute-start = (f32[1,32,1024]{2,1,0:T(8,128)S(1)}, f32[1,32,1024]{2,1,0:T(8,128)S(1)}, u32[]{:S(2)}, u32[]{:S(2)}) collective-permute-start(f32[1,32,1024]{2,1,0:T(8,128)S(1)} %get-tuple-element.53), channel_id=1, source_target_pairs={{0,4},{4,8},{8,12},{12,16},{16,20},{20,24},{24,28},{28,32},{32,36}... | collective-permute-start | bytes 393224 | tf_op jit(solution)/shard_map/ppermute | solution.py:25
  22.7 1.9 %collective-permute-start.1 = (f32[1,32,1024]{2,1,0:T(8,128)S(1)}, f32[1,32,1024]{2,1,0:T(8,128)S(1)}, u32[]{:S(2)}, u32[]{:S(2)}) collective-permute-start(f32[1,32,1024]{2,1,0:T(8,128)S(1)} %get-tuple-element.54), channel_id=1, source_target_pairs={{4,0},{8,4},{12,8},{16,12},{20,16},{24,20},{28,24},{32,28},{36,32}... | collective-permute-start | bytes 393224 | tf_op jit(solution)/shard_map/ppermute | solution.py:26
  24.6 0.0 copy-done.3
  24.6 0.1 fusion.84
  24.7 0.7 slice.149
  25.4 0.6 compare_reduce_fusion
  26.0 0.0 copy-done.2
  26.1 20.1 %all-to-all-done = bf16[64,2,4224]{2,1,0:T(2,128)(2,1)S(1)} async-done(((bf16[64,2,4224]{2,1,0:T(2,128)(2,1)}), bf16[64,2,4224]{2,1,0:T(2,128)(2,1)S(1)}, u32[]{:S(2)}, u32[]{:S(2)}) %all-to-all-start) | async-done | bytes 1081376 | tf_op jit(solution)/shard_map/all_to_all | solution.py:139
  46.1 0.4 reshape.517
  46.6 0.1 convert_reduce_fusion
  46.7 0.2 fusion.71
  46.9 1.3 fusion.65
  48.2 0.4 scatter.14
  48.5 0.1 multiply_bitcast_fusion.3
  48.7 0.1 multiply_add_fusion.4
  48.8 0.2 convert_reduce_fusion.4
  49.0 0.0 collective-permute-done
  49.0 0.0 collective-permute-done.1
  49.0 7.1 %convolution_bitcast_fusion = f32[8,32,32,128]{3,1,2,0:T(8,128)S(1)} fusion(f32[8,128]{1,0:T(8,128)S(1)} %get-tuple-element.63, f32[1024]{0:T(1024)S(1)} %iota_add_fusion, f32[1,32,1024]{2,1,0:T(8,128)S(1)} %collective-permute-done.1, f32[32,32,1024]{2,1,0:T(8,128)} %param.14, f32[1,32,1024]{2,1,0:T(8,128)S(1)} %collective-permute-done, ...), kind=kOutput, calls=%fused_computation.63 | convolution fusion | flops 2161115136 | bytes 8659200 | tf_op jit(solution)/shard_map/zlv,atv->alzt/dot_general | solution.py:118
  56.1 4.4 %copy.24 = f32[8,32,32,128]{3,2,1,0:T(8,128)} copy(f32[8,32,32,128]{3,1,2,0:T(8,128)S(1)} %convolution_bitcast_fusion) | data formatting | bytes 8388608 | tf_op jit(solution)/shard_map/zlv,atv->alzt/transpose | solution.py:118
  60.5 2.9 %gather_fusion = f32[128,32,128]{2,1,0:T(8,128)S(1)} fusion(f32[256,32,128]{2,1,0:T(8,128)} %bitcast.128, s32[1024]{0:T(1024)S(1)} %pad_clamp_fusion), kind=kCustom, calls=%fused_computation | custom fusion | bytes 4194816 | tf_op jit(solution)/shard_map/gather | solution.py:144
  63.4 0.2 broadcast_add_fusion
  63.6 2.5 %convolution_convert_fusion.5 = bf16[128,4096]{1,0:T(8,128)(2,1)S(1)} fusion(f32[16,8,32,128]{3,2,1,0:T(8,128)S(1)} %bitcast.133, bf16[128,4224]{1,0:T(8,128)(2,1)S(1)} %reshape.517, s32[128]{0:T(128)S(1)} %get-tuple-element.41, pred[128]{0:T(512)(128)(4,1)S(1)} %not.7), kind=kOutput, calls=%fused_computation.26 | convolution fusion | flops 806912000 | bytes 4195840 | tf_op jit(solution)/shard_map/dot_general | solution.py:151
  66.1 1.1 pad_maximum_fusion.4.payload
  67.2 36.1 %shard_map.82 = bf16[3,128,4224]{2,1,0:T(8,128)(2,1)} custom-call(bf16[128,4224]{1,0:T(8,128)(2,1)} %pad_maximum_fusion.4.payload), custom_call_target="tpu_custom_call" | custom-call | tf_op jit(solution)/shard_map/pallas_call | solution.py:94
  103.3 2.1 %slice_bitcast_fusion.2 = (bf16[128,4224]{1,0:T(8,128)(2,1)S(1)}, bf16[128,4224]{1,0:T(8,128)(2,1)S(1)}, bf16[128,4224]{1,0:T(8,128)(2,1)S(1)}) fusion(bf16[3,128,4224]{2,1,0:T(8,128)(2,1)} %shard_map.82), kind=kLoop, calls=%fused_computation.80 | loop fusion | bytes 6488064 | tf_op jit(solution)/shard_map/squeeze | solution.py:166
  105.4 0.2 convert_reduce_fusion.3
  105.6 0.2 convert_reduce_fusion.1
  105.8 0.7 fusion.54
  106.5 0.5 copy.37
  107.0 0.1 multiply_bitcast_fusion.2
  107.1 0.1 multiply_bitcast_fusion
  107.3 0.1 multiply_bitcast_fusion.1
  107.5 0.7 fusion.56
  108.2 0.5 copy.39
  108.6 0.7 fusion.57
  109.3 1.8 %copy.40 = bf16[32,8,32,128]{3,2,1,0:T(8,128)(2,1)} copy(bf16[32,8,32,128]{3,1,2,0:T(8,128)(2,1)S(1)} %fusion.57) | data formatting | bytes 4194304
  111.2 0.7 fusion.55
  111.9 1.9 %copy.38 = bf16[32,8,32,128]{3,2,1,0:T(8,128)(2,1)} copy(bf16[32,8,32,128]{3,1,2,0:T(8,128)(2,1)S(1)} %fusion.55) | data formatting | bytes 4194304
  113.7 0.1 multiply_add_fusion.2
  113.8 6.2 %fusion.17 = (bf16[1,8,128,1024]{3,2,0,1:T(8,128)(2,1)}, bf16[1,8,128,1024]{3,2,0,1:T(8,128)(2,1)}, bf16[1,8,128,1024]{3,2,0,1:T(8,128)(2,1)}, bf16[1,8,128,1024]{3,2,0,1:T(8,128)(2,1)}) fusion(f32[8,128]{1,0:T(8,128)S(1)} %get-tuple-element.62, f32[1024]{0:T(1024)S(1)} %iota_add_fusion, f32[8,128]{1,0:T(8,128)S(1)} %get-tuple-element.64, ...), kind=kLoop, calls=%fused_computation.30 | loop fusion | flops 25165824 | bytes 8409088 | tf_op jit(solution)/shard_map/convert_element_type | solution.py:45
  120.0 14.0 %fusion = f32[1024,32,32,1,1]{0,2,4,1,3:T(8,128)S(1)} fusion(bf16[1,8,128,1024]{3,2,0,1:T(8,128)(2,1)} %get-tuple-element.61, bf16[1,8,128,1024]{3,2,0,1:T(8,128)(2,1)} %get-tuple-element.60, bf16[1,8,128,1024]{3,2,0,1:T(8,128)(2,1)} %get-tuple-element.59, bf16[1,8,128,1024]{3,2,0,1:T(8,128)(2,1)} %get-tuple-element.58, ...), kind=kOutput, calls=%fused_computation.2 | convolution fusion | flops 8657043456 | bytes 20971520 | tf_op jit(solution)/shard_map/kalzt,katv->zlv/dot_general | solution.py:179
  134.0 0.0 copy-start
  134.0 0.0 copy-start.1
  134.0 0.6 fusion.43
  134.6 0.2 fusion.93
  134.8 9.5 %collective-permute-start.2 = (f32[1,32,1024]{2,0,1:T(1,128)S(1)}, f32[1,32,1024]{2,0,1:T(1,128)S(1)}, u32[]{:S(2)}, u32[]{:S(2)}) collective-permute-start(f32[1,32,1024]{2,0,1:T(1,128)S(1)} %get-tuple-element.51), channel_id=1, source_target_pairs={{0,4},{4,8},{8,12},{12,16},{16,20},{20,24},{24,28},{28,32},{32,36}... | collective-permute-start | bytes 393224 | tf_op jit(solution)/shard_map/ppermute | solution.py:25
  144.3 1.9 %collective-permute-start.3 = (f32[1,32,1024]{2,0,1:T(1,128)S(1)}, f32[1,32,1024]{2,0,1:T(1,128)S(1)}, u32[]{:S(2)}, u32[]{:S(2)}) collective-permute-start(f32[1,32,1024]{2,0,1:T(1,128)S(1)} %get-tuple-element.52), channel_id=1, source_target_pairs={{4,0},{8,4},{12,8},{16,12},{20,16},{24,20},{28,24},{32,28},{36,32}... | collective-permute-start | bytes 393224 | tf_op jit(solution)/shard_map/ppermute | solution.py:26
  146.2 0.0 collective-permute-done.2
  146.2 6.5 %collective-permute-done.3 = f32[1,32,1024]{2,0,1:T(1,128)S(1)} collective-permute-done((f32[1,32,1024]{2,0,1:T(1,128)S(1)}, f32[1,32,1024]{2,0,1:T(1,128)S(1)}, u32[]{:S(2)}, u32[]{:S(2)}) %collective-permute-start.3) | collective-permute-done | bytes 131104 | tf_op jit(solution)/shard_map/ppermute | solution.py:26
  152.7 0.0 copy-done
  152.7 11.1 %fusion.36 = f32[32,32,1024]{2,0,1:T(8,128)S(1)} fusion(f32[1,32,1024]{2,0,1:T(1,128)S(1)} %collective-permute-done.3, f32[32,32,1024]{2,0,1:T(8,128)S(1)} %fusion.43, f32[1,32,1024]{2,0,1:T(1,128)S(1)} %collective-permute-done.2, f32[1024,32,32,1,1]{0,2,4,1,3:T(8,128)S(1)} %fusion, f32[32,32,1024]{2,1,0:T(8,128)S(1)} %copy-done.1, ...), kind=kLoop, calls=%fused_computation.50 | loop fusion | flops 7340032 | bytes 21233792 | tf_op jit(solution)/shard_map/div | solution.py:184
  163.8 4.4 %copy.31 = f32[32,32,1024]{2,1,0:T(8,128)} copy(f32[32,32,1024]{2,0,1:T(8,128)S(1)} %fusion.36) | data formatting | bytes 8388608 | tf_op jit(solution)/shard_map/div | solution.py:184
  (18 shorter events, 0.2 us)
Async XLA Ops:
  0.0 24.6 %copy-start.3 = (s32[1,8]{1,0:T(1,128)S(1)}, s32[1,8]{1,0:T(1,128)}, u32[]{:S(2)}) copy-start(s32[1,8]{1,0:T(1,128)} %param.21) | copy-start | bytes 100
  0.0 26.0 %copy-start.2 = (f32[32]{0:T(128)S(1)}, f32[32]{0:T(128)}, u32[]{:S(2)}) copy-start(f32[32]{0:T(128)} %param.16) | copy-start | bytes 388
  6.0 40.1 %all-to-all-start = ((bf16[64,2,4224]{2,1,0:T(2,128)(2,1)}), bf16[64,2,4224]{2,1,0:T(2,128)(2,1)S(1)}, u32[]{:S(2)}, u32[]{:S(2)}) async-start(bf16[64,2,4224]{2,1,0:T(2,128)(2,1)} %reshape.516), calls=%async_computation | async-start | bytes 2162688 | tf_op jit(solution)/shard_map/all_to_all | solution.py:139
  19.3 29.7 %collective-permute-start = (f32[1,32,1024]{2,1,0:T(8,128)S(1)}, f32[1,32,1024]{2,1,0:T(8,128)S(1)}, u32[]{:S(2)}, u32[]{:S(2)}) collective-permute-start(f32[1,32,1024]{2,1,0:T(8,128)S(1)} %get-tuple-element.53), channel_id=1, source_target_pairs={{0,4},{4,8},{8,12},{12,16},{16,20},{20,24},{24,28},{28,32},{32,36}... | collective-permute-start | bytes 393224 | tf_op jit(solution)/shard_map/ppermute | solution.py:25
  22.7 26.3 %collective-permute-start.1 = (f32[1,32,1024]{2,1,0:T(8,128)S(1)}, f32[1,32,1024]{2,1,0:T(8,128)S(1)}, u32[]{:S(2)}, u32[]{:S(2)}) collective-permute-start(f32[1,32,1024]{2,1,0:T(8,128)S(1)} %get-tuple-element.54), channel_id=1, source_target_pairs={{4,0},{8,4},{12,8},{16,12},{20,16},{24,20},{28,24},{32,28},{36,32}... | collective-permute-start | bytes 393224 | tf_op jit(solution)/shard_map/ppermute | solution.py:26
  134.0 18.7 %copy-start = (f32[32,32,1024]{2,1,0:T(8,128)S(1)}, f32[32,32,1024]{2,1,0:T(8,128)}, u32[]{:S(2)}) copy-start(f32[32,32,1024]{2,1,0:T(8,128)} %param.14) | copy-start | bytes 12582916
  134.0 18.7 %copy-start.1 = (f32[32,32,1024]{2,1,0:T(8,128)S(1)}, f32[32,32,1024]{2,1,0:T(8,128)}, u32[]{:S(2)}) copy-start(f32[32,32,1024]{2,1,0:T(8,128)} %param.15) | copy-start | bytes 12582916
  134.8 11.4 %collective-permute-start.2 = (f32[1,32,1024]{2,0,1:T(1,128)S(1)}, f32[1,32,1024]{2,0,1:T(1,128)S(1)}, u32[]{:S(2)}, u32[]{:S(2)}) collective-permute-start(f32[1,32,1024]{2,0,1:T(1,128)S(1)} %get-tuple-element.51), channel_id=1, source_target_pairs={{0,4},{4,8},{8,12},{12,16},{16,20},{20,24},{24,28},{28,32},{32,36}... | collective-permute-start | bytes 393224 | tf_op jit(solution)/shard_map/ppermute | solution.py:25
  144.3 8.4 %collective-permute-start.3 = (f32[1,32,1024]{2,0,1:T(1,128)S(1)}, f32[1,32,1024]{2,0,1:T(1,128)S(1)}, u32[]{:S(2)}, u32[]{:S(2)}) collective-permute-start(f32[1,32,1024]{2,0,1:T(1,128)S(1)} %get-tuple-element.52), channel_id=1, source_target_pairs={{4,0},{8,4},{12,8},{16,12},{20,16},{24,20},{28,24},{32,28},{36,32}... | collective-permute-start | bytes 393224 | tf_op jit(solution)/shard_map/ppermute | solution.py:26

commit v3 on v2

--- a/solution.py
+++ b/solution.py
@@ -52,6 +52,7 @@
     left = lax.rem(me + count - 1, count)
     right = lax.rem(me + 1, count)
     half = payload.shape[0] // 2
+    rest = payload.shape[0] - half
 
     barrier = pltpu.get_barrier_semaphore()
     for neighbour in (left, right):
@@ -77,7 +78,7 @@
     onward_right.start()
     to_left.wait_recv()
     onward_left = pltpu.make_async_remote_copy(
-        src_ref=out.at[1, pl.ds(half, half)], dst_ref=out.at[2, pl.ds(half, half)],
+        src_ref=out.at[1, pl.ds(half, rest)], dst_ref=out.at[2, pl.ds(half, rest)],
         send_sem=send_sems.at[3], recv_sem=recv_sems.at[3],
         device_id=(slab, left), device_id_type=MESH,
     )
@@ -115,8 +116,8 @@
     tof_kernel = kernels(subset_views[0], bins, length)
     angle_count = tof_kernel.shape[0]
     pairs = angle_count * lines_here
-    projected = jnp.einsum("zlv,atv->alzt", blurred, tof_kernel, preferred_element_type=jnp.float32)
-    projected = projected.reshape(pairs, planes, bins)
+    projected = jnp.einsum("zlv,atv->zlat", blurred, tof_kernel, preferred_element_type=jnp.float32)
+    projected = projected.reshape(planes, pairs, bins)
 
     slab_count = lax.axis_size("slab")
     block_total = measured.shape[1]
@@ -131,7 +132,7 @@
     place = (jnp.arange(slots, dtype=jnp.int32)[:, None] == flat_slot[None, :]).astype(
         jnp.bfloat16
     )
-    pair_id = block_angle[0] * lines_here + block_line[0]
+    pair_id = block_line[0] * angle_count + block_angle[0]
     extra = 128
     tag = jnp.broadcast_to(pair_id.astype(jnp.bfloat16)[:, None], (block_total, extra))
     outgoing = jnp.concatenate([measured[0].reshape(block_total, row), tag], axis=1)
@@ -140,45 +141,46 @@
         send.reshape(slab_count, capacity, row + extra), "slab", 0, 0, tiled=True
     ).reshape(slots, row + extra)
     index = recv[:, row].astype(jnp.int32)
-    rows = recv[:, :row].reshape(slots, planes, bins)
-    estimate = projected[index]
-    ratios = (rows.astype(jnp.float32) / (estimate + BACKGROUND)).reshape(slots, row)
+    rows = recv[:, :row].reshape(slots, planes, bins).transpose(1, 0, 2)
+    estimate = projected[:, index, :]
+    ratios = rows.astype(jnp.float32) / (estimate + BACKGROUND)
 
     same = index[:, None] == index[None, :]
     earlier = jnp.arange(slots)[None, :] < jnp.arange(slots)[:, None]
     first = ~jnp.any(same & earlier, axis=1)
-    merge = (same & first[:, None]).astype(jnp.float32)
-    merged = jnp.dot(merge, ratios, precision=lax.Precision.HIGHEST).astype(jnp.bfloat16)
+    merge = jnp.broadcast_to((same & first[:, None]).astype(jnp.float32)[None], (planes, slots, slots))
+    merged = jnp.einsum(
+        "zij,zjt->zit", merge, ratios, precision=lax.Precision.HIGHEST
+    ).astype(jnp.bfloat16)
 
     views = subset_views[0]
-    info = jnp.zeros((extra,), jnp.float32)
-    info = info.at[0:angle_count].set((views // 16).astype(jnp.float32))
-    info = info.at[angle_count : 2 * angle_count].set((views % 16).astype(jnp.float32))
-    info = jnp.broadcast_to(info[None, :], (slots, extra))
-    info = info.at[:, 2 * angle_count].set(index.astype(jnp.float32)).astype(jnp.bfloat16)
-    payload = jnp.concatenate([merged, info], axis=1)
+    info = jnp.zeros((slots, bins), jnp.float32)
+    info = info.at[:, 0].set(index.astype(jnp.float32))
+    info = info.at[:, 1 : 1 + angle_count].set((views // 16).astype(jnp.float32)[None, :])
+    info = info.at[:, 1 + angle_count : 1 + 2 * angle_count].set(
+        (views % 16).astype(jnp.float32)[None, :]
+    )
+    payload = jnp.concatenate([merged, info.astype(jnp.bfloat16)[None]], axis=0)
     everything = jnp.concatenate([payload[None], ring_gather(payload)], axis=0)
     group_count = everything.shape[0]
 
-    dense = []
-    kernel_all = []
+    total = None
     for group in range(group_count):
         got = everything[group]
-        tail = got[0, row:].astype(jnp.int32)
-        views_k = tail[0:angle_count] * 16 + tail[angle_count : 2 * angle_count]
-        kernel_all.append(kernels(views_k, bins, length))
-        index_k = got[:, row + 2 * angle_count].astype(jnp.int32)
+        tail = got[planes, 0].astype(jnp.int32)
+        views_k = tail[1 : 1 + angle_count] * 16 + tail[1 + angle_count : 1 + 2 * angle_count]
+        kernel_k = kernels(views_k, bins, length)
+        index_k = got[planes, :, 0].astype(jnp.int32)
         scatter = (jnp.arange(pairs, dtype=jnp.int32)[:, None] == index_k[None, :]).astype(
             jnp.bfloat16
         )
-        dense.append(
-            jnp.dot(scatter, got[:, :row], preferred_element_type=jnp.float32).astype(jnp.bfloat16)
-        )
-    dense = jnp.stack(dense).reshape(group_count, angle_count, lines_here, planes, bins)
-    kernel_all = jnp.stack(kernel_all)
-    total = jnp.einsum(
-        "kalzt,katv->zlv", dense, kernel_all, preferred_element_type=jnp.float32
-    )
+        scatter = jnp.broadcast_to(scatter[None], (planes, pairs, slots))
+        dense = jnp.einsum(
+            "zpi,zit->zpt", scatter, got[:planes], preferred_element_type=jnp.float32
+        ).astype(jnp.bfloat16)
+        dense = dense.reshape(planes, lines_here, angle_count, bins)
+        part = jnp.einsum("zlat,atv->zlv", dense, kernel_k, preferred_element_type=jnp.float32)
+        total = part if total is None else total + part
     edges = with_halo(weight * total, (("slab", 0),), 1)
     smoothed = (1.0 - 2.0 * weight) * total + edges[:-2] + edges[2:]
     return activity * smoothed / sensitivity

time: 170 us -> 148 us (0.87)
  waiting for transfers between devices: 26.5 us -> 15.8 us
  other arithmetic: 25.9 us -> 16.3 us
  local copies, waits for them, and re-layouts: 23.7 us -> 20.3 us
    all_to_all x1, waiting for transfers between devices: 20.1 us -> 9.35 us  [on_device(): lax.all_to_all(send.reshape(slab_count, capacity, row + extra), 'slab', 0...]
    div x1, other arithmetic: 11.1 us -> 4.26 us  [on_device(): return activity * smoothed / sensitivity]
    convert_element_type x8 -> x11, other arithmetic: 6.76 us -> 0.53 us  [the longest x3 0.32 us: on_device(): index_k = got[planes, :, 0].astype(jnp.int32)]
    reshape x0 -> x1, local copies, waits for them, and re-layouts: none -> 4.44 us  [on_device(): projected = projected.reshape(planes, pairs, bins)]
    div x1 -> x0, local copies, waits for them, and re-layouts: 4.44 us -> none  [on_device(): return activity * smoothed / sensitivity]
    transpose x1 -> x0, local copies, waits for them, and re-layouts: 4.39 us -> none  [on_device(): jnp.einsum('zlv,atv->alzt', blurred, tof_kernel, preferred_element_type=j...]
    unnamed x13 -> x12, local copies, waits for them, and re-layouts: 5.94 us -> 1.64 us
    dot_general x0 -> x1, local copies, waits for them, and re-layouts: none -> 3.79 us  [on_device(): jnp.einsum('zlv,atv->zlat', blurred, tof_kernel, preferred_element_type=j...]
  transfers between devices with their start and end apart: 5 -> 5, of which waited for: 2 -> 2; matrix products, arithmetic and copies ran while one was open for 3% -> 17% of each run, Pallas kernels for 0% -> 0%
where the time goes in v3:
time: 148 us; the launch traced here: 147 us
  Pallas kernels  36.6 us (25%)
  starting transfers between devices  29.2 us (20%)
  matrix products  28.3 us (19%)
  local copies, waits for them, and re-layouts  20.3 us (14%)
  other arithmetic  16.3 us (11%)
  waiting for transfers between devices  15.8 us (11%)
    pallas_call x1, Pallas kernels, ring_gather(): pl.pallas_call(ring_gather_kernel, out_shape=jax.ShapeDtypeStruct((3,) +...  36.6 us
    dot_general x4, matrix products, on_device(): jnp.einsum('zlat,atv->zlv', dense, kernel_k, preferred_element_type=jnp.f...  14.8 us
    all_to_all x1, starting transfers between devices, on_device(): lax.all_to_all(send.reshape(slab_count, capacity, row + extra), 'slab', 0...  12.8 us
    ppermute x2, starting transfers between devices, with_halo(): before = lax.ppermute(last, axis, up)  12.6 us
    all_to_all x1, waiting for transfers between devices, on_device(): lax.all_to_all(send.reshape(slab_count, capacity, row + extra), 'slab', 0...  9.35 us
    dot_general x1, matrix products, on_device(): jnp.einsum('zlv,atv->zlat', blurred, tof_kernel, preferred_element_type=j...  7.21 us
    ppermute x2, waiting for transfers between devices, with_halo(): after = lax.ppermute(leading, axis, down)  6.46 us
    reshape x1, local copies, waits for them, and re-layouts, on_device(): projected = projected.reshape(planes, pairs, bins)  4.44 us
  transfers between devices with their start and end apart: 5, of which 2 were waited for; matrix products, arithmetic and copies ran while one was open for 17% of the time, Pallas kernels for 0%

profile of v3, /device:TPU:31, one launch (start us, length us, event | category | flops | bytes accessed | tf_op | source)
XLA Modules:
  0.0 146.9 jit_solution(1184603619657607935)
XLA Ops:
  0.0 1.0 fusion.113
  1.0 4.0 %collective-permute-start = (f32[1,32,1024]{2,1,0:T(8,128)S(1)}, f32[1,32,1024]{2,1,0:T(8,128)S(1)}, u32[]{:S(2)}, u32[]{:S(2)}) collective-permute-start(f32[1,32,1024]{2,1,0:T(8,128)S(1)} %get-tuple-element.53), channel_id=1, source_target_pairs={{0,4},{4,8},{8,12},{12,16},{16,20},{20,24},{24,28},{28,32},{32,36}... | collective-permute-start | bytes 393224 | tf_op jit(solution)/shard_map/ppermute | solution.py:25
  5.0 1.9 %collective-permute-start.1 = (f32[1,32,1024]{2,1,0:T(8,128)S(1)}, f32[1,32,1024]{2,1,0:T(8,128)S(1)}, u32[]{:S(2)}, u32[]{:S(2)}) collective-permute-start(f32[1,32,1024]{2,1,0:T(8,128)S(1)} %get-tuple-element.54), channel_id=1, source_target_pairs={{4,0},{8,4},{12,8},{16,12},{20,16},{24,20},{28,24},{32,28},{36,32}... | collective-permute-start | bytes 393224 | tf_op jit(solution)/shard_map/ppermute | solution.py:26
  7.0 0.7 fusion.96
  7.7 0.1 reduce_window_sum.11
  7.8 0.8 select_reduce_fusion
  8.6 0.7 multiply_add_fusion.5
  9.3 1.3 copy.45
  10.6 0.7 convert_bitcast_fusion.6
  11.2 0.1 broadcast_in_dim.16
  11.3 0.4 convolution_convert_fusion
  11.8 1.2 reshape.574
  13.0 12.8 %all-to-all-start = ((bf16[64,2,4224]{2,1,0:T(2,128)(2,1)}), bf16[64,2,4224]{2,1,0:T(2,128)(2,1)S(1)}, u32[]{:S(2)}, u32[]{:S(2)}) async-start(bf16[64,2,4224]{2,1,0:T(2,128)(2,1)} %reshape.574), calls=%async_computation | async-start | bytes 2162688 | tf_op jit(solution)/shard_map/all_to_all | solution.py:140
  25.8 0.6 compare_reduce_fusion.1
  26.4 0.0 copy-done.4
  26.4 0.7 fusion.97
  27.1 0.1 multiply_bitcast_fusion.8
  27.1 0.1 multiply_add_fusion.4
  27.2 0.7 compare_reduce_fusion.2
  27.9 0.7 compare_reduce_fusion
  28.6 0.0 collective-permute-done
  28.6 0.0 collective-permute-done.1
  28.6 7.2 %fusion.33 = f32[32,32,8,128]{3,1,2,0:T(8,128)S(1)} fusion(f32[8,128]{1,0:T(8,128)S(1)} %multiply_add_fusion.4, f32[1024]{0:T(1024)S(1)} %iota_add_fusion, f32[1,32,1024]{2,1,0:T(8,128)S(1)} %collective-permute-done.1, f32[32,32,1024]{2,1,0:T(8,128)} %param.14, f32[1,32,1024]{2,1,0:T(8,128)S(1)} %collective-permute-done, f32[32]{0:T(128)S(1)} %copy-done.3, ...), kind=kOutput, calls=%fused_computation.48 | convolution fusion | flops 2161115136 | bytes 8659200 | tf_op jit(solution)/shard_map/zlv,atv->zlat/dot_general | solution.py:119
  35.8 3.8 %copy.44 = f32[32,32,8,128]{3,2,1,0:T(8,128)S(1)} copy(f32[32,32,8,128]{3,1,2,0:T(8,128)S(1)} %fusion.33) | data formatting | bytes 8388608 | tf_op jit(solution)/shard_map/zlv,atv->zlat/dot_general | solution.py:119
  39.6 4.4 %copy.15 = f32[32,256,128]{2,0,1:T(8,128)} copy(f32[32,256,128]{2,1,0:T(8,128)S(1)} %bitcast.106) | data formatting | bytes 8388608 | tf_op jit(solution)/shard_map/reshape | solution.py:120
  44.1 9.4 %all-to-all-done = bf16[64,2,4224]{2,1,0:T(2,128)(2,1)S(1)} async-done(((bf16[64,2,4224]{2,1,0:T(2,128)(2,1)}), bf16[64,2,4224]{2,1,0:T(2,128)(2,1)S(1)}, u32[]{:S(2)}, u32[]{:S(2)}) %all-to-all-start) | async-done | bytes 1081376 | tf_op jit(solution)/shard_map/all_to_all | solution.py:140
  53.4 0.4 reshape.575
  53.9 0.1 convert_reduce_fusion
  54.0 0.6 fusion.91
  54.7 0.4 scatter.11
  55.1 0.7 slice_select_fusion
  55.8 0.6 scatter.14
  56.4 0.1 convert_reduce_fusion.4
  56.5 0.2 convert_bitcast_fusion
  56.7 0.2 fusion.93
  56.9 0.1 fusion.94
  57.0 0.4 copy.27
  57.4 4.2 %gather_fusion = f32[128,32,128]{2,1,0:T(8,128)} fusion(f32[32,256,128]{2,0,1:T(8,128)} %copy.15, s32[1024]{0:T(1024)S(1)} %pad_clamp_fusion), kind=kCustom, calls=%fused_computation | custom fusion | bytes 4194816 | tf_op jit(solution)/shard_map/gather | solution.py:145
  61.6 2.1 %bitcast_divide_fusion = f32[128,32,128]{2,1,0:T(8,128)S(1)} fusion(f32[16,8,32,128]{3,2,1,0:T(8,128)S(1)} %copy.27, f32[128,32,128]{2,1,0:T(8,128)} %gather_fusion), kind=kLoop, calls=%fused_computation.52 | loop fusion | flops 1048576 | bytes 6291456 | tf_op jit(solution)/shard_map/div | solution.py:146
  63.7 3.1 %fusion.70 = bf16[32,128,128]{2,1,0:T(8,128)(2,1)S(1)} fusion(f32[32,128,128]{2,0,1:T(8,128)S(1)} %bitcast.107, f32[128,128]{1,0:T(8,128)S(1)} %fusion.94), kind=kOutput, calls=%fused_computation.86 | convolution fusion | flops 805830656 | bytes 3211264 | tf_op jit(solution)/shard_map/zij,zjt->zit/dot_general | solution.py:152
  66.9 1.1 pad_maximum_fusion.4.payload
  67.9 36.6 %shard_map.82 = bf16[3,33,128,128]{3,2,1,0:T(8,128)(2,1)} custom-call(bf16[33,128,128]{2,1,0:T(8,128)(2,1)} %pad_maximum_fusion.4.payload), custom_call_target="tpu_custom_call" | custom-call | tf_op jit(solution)/shard_map/pallas_call | solution.py:95
  104.6 2.4 %slice_bitcast_fusion = (bf16[33,128,128]{2,1,0:T(8,128)(2,1)S(1)}, bf16[33,128,128]{2,1,0:T(8,128)(2,1)S(1)}, bf16[33,128,128]{2,1,0:T(8,128)(2,1)S(1)}) fusion(bf16[3,33,128,128]{3,2,1,0:T(8,128)(2,1)} %shard_map.82), kind=kLoop, calls=%fused_computation.88 | loop fusion | bytes 6488064 | tf_op jit(solution)/shard_map/squeeze | solution.py:169
  107.0 0.1 convert_reduce_fusion.3
  107.1 0.1 convert_reduce_fusion.1
  107.3 0.7 convert_bitcast_fusion.4
  108.0 0.1 multiply_bitcast_fusion.2
  108.2 0.1 multiply_bitcast_fusion
  108.4 0.1 multiply_bitcast_fusion.1
  108.6 0.0 copy-done
  108.7 0.7 convert_bitcast_fusion.2
  109.4 0.7 convert_bitcast_fusion.3
  110.1 0.7 convert_bitcast_fusion.1
  110.8 0.1 multiply_add_fusion
  110.9 2.5 %fusion.37 = f32[32,32,1024,1]{2,1,3,0:T(8,128)S(1)} fusion(bf16[32,32,8,128]{3,2,1,0:T(8,128)(2,1)S(1)} %convert_bitcast_fusion.3, f32[8,128]{1,0:T(8,128)S(1)} %get-tuple-element.60, f32[1024]{0:T(1024)S(1)} %iota_add_fusion), kind=kOutput, calls=%fused_computation.50 | convolution fusion | flops 2153775104 | bytes 6299648 | tf_op jit(solution)/shard_map/zlat,atv->zlv/dot_general | solution.py:182
  113.4 2.8 %fusion.39 = f32[32,32,1024,1]{2,1,3,0:T(8,128)S(1)} fusion(bf16[32,32,8,128]{3,2,1,0:T(8,128)(2,1)S(1)} %convert_bitcast_fusion.2, f32[8,128]{1,0:T(8,128)S(1)} %get-tuple-element.61, f32[1024]{0:T(1024)S(1)} %iota_add_fusion), kind=kOutput, calls=%fused_computation.51 | convolution fusion | flops 2153775104 | bytes 6299648 | tf_op jit(solution)/shard_map/zlat,atv->zlv/dot_general | solution.py:182
  116.2 4.2 %fusion.35 = f32[32,32,1024,1]{2,1,3,0:T(8,128)} fusion(bf16[32,32,8,128]{3,2,1,0:T(8,128)(2,1)S(1)} %convert_bitcast_fusion.4, f32[8,128]{1,0:T(8,128)S(1)} %get-tuple-element.59, f32[1024]{0:T(1024)S(1)} %iota_add_fusion), kind=kOutput, calls=%fused_computation.49 | convolution fusion | flops 2153775104 | bytes 6299648 | tf_op jit(solution)/shard_map/zlat,atv->zlv/dot_general | solution.py:182
  120.4 5.2 %broadcast_multiply_fusion = (f32[32,32,1024]{2,1,0:T(8,128)S(1)}, f32[32,32,1024]{2,1,0:T(8,128)S(1)}) fusion(f32[32]{0:T(128)S(1)} %copy-done.3, f32[8,128]{1,0:T(8,128)S(1)} %get-tuple-element.58, f32[1024]{0:T(1024)S(1)} %iota_add_fusion, bf16[32,32,8,128]{3,2,1,0:T(8,128)(2,1)S(1)} %convert_bitcast_fusion.1, f32[32,32,1024,1]{2,1,3,0:T(8,128)S(1)} %fusion.39, ...), kind=kOutput, calls=%fused_computation.85 | convolution fusion | flops 2157969408 | bytes 23076992 | tf_op jit(solution)/shard_map/zlat,atv->zlv/dot_general | solution.py:182
  125.7 8.5 %collective-permute-start.2 = (f32[1,32,1024]{2,1,0:T(8,128)S(1)}, f32[1,32,1024]{2,1,0:T(8,128)S(1)}, u32[]{:S(2)}, u32[]{:S(2)}) collective-permute-start(f32[1,32,1024]{2,1,0:T(8,128)S(1)} %get-tuple-element.51), channel_id=1, source_target_pairs={{0,4},{4,8},{8,12},{12,16},{16,20},{20,24},{24,28},{28,32},{32,36}... | collective-permute-start | bytes 393224 | tf_op jit(solution)/shard_map/ppermute | solution.py:25
  134.2 1.9 %collective-permute-start.3 = (f32[1,32,1024]{2,1,0:T(8,128)S(1)}, f32[1,32,1024]{2,1,0:T(8,128)S(1)}, u32[]{:S(2)}, u32[]{:S(2)}) collective-permute-start(f32[1,32,1024]{2,1,0:T(8,128)S(1)} %get-tuple-element.52), channel_id=1, source_target_pairs={{4,0},{8,4},{12,8},{16,12},{20,16},{24,20},{28,24},{32,28},{36,32}... | collective-permute-start | bytes 393224 | tf_op jit(solution)/shard_map/ppermute | solution.py:26
  136.1 0.0 collective-permute-done.2
  136.2 6.5 %collective-permute-done.3 = f32[1,32,1024]{2,1,0:T(8,128)S(1)} collective-permute-done((f32[1,32,1024]{2,1,0:T(8,128)S(1)}, f32[1,32,1024]{2,1,0:T(8,128)S(1)}, u32[]{:S(2)}, u32[]{:S(2)}) %collective-permute-start.3) | collective-permute-done | bytes 131104 | tf_op jit(solution)/shard_map/ppermute | solution.py:26
  142.6 0.0 copy-done.2
  142.6 4.3 %fusion.22 = f32[32,32,1024]{2,1,0:T(8,128)} fusion(f32[32,32,1024]{2,1,0:T(8,128)S(1)} %copy-done.2, f32[32,32,1024]{2,1,0:T(8,128)S(1)} %copy-done.1, f32[1,32,1024]{2,1,0:T(8,128)S(1)} %collective-permute-done.3, f32[32,32,1024]{2,1,0:T(8,128)S(1)} %get-tuple-element.64, f32[1,32,1024]{2,1,0:T(8,128)S(1)} %collective-permute-done.2, ...), kind=kLoop, calls=%fused_computation.30 | loop fusion | flops 7340032 | bytes 21233792 | tf_op jit(solution)/shard_map/div | solution.py:186
  (27 shorter events, 0.4 us)
Async XLA Ops:
  0.0 26.4 %copy-start.4 = (s32[1,8]{1,0:T(1,128)S(1)}, s32[1,8]{1,0:T(1,128)}, u32[]{:S(2)}) copy-start(s32[1,8]{1,0:T(1,128)} %param.21) | copy-start | bytes 100
  0.0 27.2 %copy-start.3 = (f32[32]{0:T(128)S(1)}, f32[32]{0:T(128)}, u32[]{:S(2)}) copy-start(f32[32]{0:T(128)} %param.16) | copy-start | bytes 388
  1.0 27.6 %collective-permute-start = (f32[1,32,1024]{2,1,0:T(8,128)S(1)}, f32[1,32,1024]{2,1,0:T(8,128)S(1)}, u32[]{:S(2)}, u32[]{:S(2)}) collective-permute-start(f32[1,32,1024]{2,1,0:T(8,128)S(1)} %get-tuple-element.53), channel_id=1, source_target_pairs={{0,4},{4,8},{8,12},{12,16},{16,20},{20,24},{24,28},{28,32},{32,36}... | collective-permute-start | bytes 393224 | tf_op jit(solution)/shard_map/ppermute | solution.py:25
  5.0 23.6 %collective-permute-start.1 = (f32[1,32,1024]{2,1,0:T(8,128)S(1)}, f32[1,32,1024]{2,1,0:T(8,128)S(1)}, u32[]{:S(2)}, u32[]{:S(2)}) collective-permute-start(f32[1,32,1024]{2,1,0:T(8,128)S(1)} %get-tuple-element.54), channel_id=1, source_target_pairs={{4,0},{8,4},{12,8},{16,12},{20,16},{24,20},{28,24},{32,28},{36,32}... | collective-permute-start | bytes 393224 | tf_op jit(solution)/shard_map/ppermute | solution.py:26
  13.0 40.4 %all-to-all-start = ((bf16[64,2,4224]{2,1,0:T(2,128)(2,1)}), bf16[64,2,4224]{2,1,0:T(2,128)(2,1)S(1)}, u32[]{:S(2)}, u32[]{:S(2)}) async-start(bf16[64,2,4224]{2,1,0:T(2,128)(2,1)} %reshape.574), calls=%async_computation | async-start | bytes 2162688 | tf_op jit(solution)/shard_map/all_to_all | solution.py:140
  104.6 4.1 %copy-start = (bf16[3,33,128,128]{3,2,1,0:T(8,128)(2,1)S(1)}, bf16[3,33,128,128]{3,2,1,0:T(8,128)(2,1)}, u32[]{:S(2)}) copy-start(bf16[3,33,128,128]{3,2,1,0:T(8,128)(2,1)} %shard_map.82) | copy-start | bytes 9732100
  120.4 22.2 %copy-start.1 = (f32[32,32,1024]{2,1,0:T(8,128)S(1)}, f32[32,32,1024]{2,1,0:T(8,128)}, u32[]{:S(2)}) copy-start(f32[32,32,1024]{2,1,0:T(8,128)} %param.14) | copy-start | bytes 12582916
  120.4 22.2 %copy-start.2 = (f32[32,32,1024]{2,1,0:T(8,128)S(1)}, f32[32,32,1024]{2,1,0:T(8,128)}, u32[]{:S(2)}) copy-start(f32[32,32,1024]{2,1,0:T(8,128)} %param.15) | copy-start | bytes 12582916
  125.7 10.5 %collective-permute-start.2 = (f32[1,32,1024]{2,1,0:T(8,128)S(1)}, f32[1,32,1024]{2,1,0:T(8,128)S(1)}, u32[]{:S(2)}, u32[]{:S(2)}) collective-permute-start(f32[1,32,1024]{2,1,0:T(8,128)S(1)} %get-tuple-element.51), channel_id=1, source_target_pairs={{0,4},{4,8},{8,12},{12,16},{16,20},{20,24},{24,28},{28,32},{32,36}... | collective-permute-start | bytes 393224 | tf_op jit(solution)/shard_map/ppermute | solution.py:25
  134.2 8.4 %collective-permute-start.3 = (f32[1,32,1024]{2,1,0:T(8,128)S(1)}, f32[1,32,1024]{2,1,0:T(8,128)S(1)}, u32[]{:S(2)}, u32[]{:S(2)}) collective-permute-start(f32[1,32,1024]{2,1,0:T(8,128)S(1)} %get-tuple-element.52), channel_id=1, source_target_pairs={{4,0},{8,4},{12,8},{16,12},{20,16},{24,20},{28,24},{32,28},{36,32}... | collective-permute-start | bytes 393224 | tf_op jit(solution)/shard_map/ppermute | solution.py:26

commit v4 on v3

--- a/solution.py
+++ b/solution.py
@@ -116,7 +116,7 @@
     tof_kernel = kernels(subset_views[0], bins, length)
     angle_count = tof_kernel.shape[0]
     pairs = angle_count * lines_here
-    projected = jnp.einsum("zlv,atv->zlat", blurred, tof_kernel, preferred_element_type=jnp.float32)
+    projected = jnp.einsum("zlv,atv->zalt", blurred, tof_kernel, preferred_element_type=jnp.float32)
     projected = projected.reshape(planes, pairs, bins)
 
     slab_count = lax.axis_size("slab")
@@ -132,7 +132,7 @@
     place = (jnp.arange(slots, dtype=jnp.int32)[:, None] == flat_slot[None, :]).astype(
         jnp.bfloat16
     )
-    pair_id = block_line[0] * angle_count + block_angle[0]
+    pair_id = block_angle[0] * lines_here + block_line[0]
     extra = 128
     tag = jnp.broadcast_to(pair_id.astype(jnp.bfloat16)[:, None], (block_total, extra))
     outgoing = jnp.concatenate([measured[0].reshape(block_total, row), tag], axis=1)
@@ -142,7 +142,9 @@
     ).reshape(slots, row + extra)
     index = recv[:, row].astype(jnp.int32)
     rows = recv[:, :row].reshape(slots, planes, bins).transpose(1, 0, 2)
-    estimate = projected[:, index, :]
+    pick = (index[:, None] == jnp.arange(pairs, dtype=jnp.int32)[None, :]).astype(jnp.float32)
+    pick = jnp.broadcast_to(pick[None], (planes, slots, pairs))
+    estimate = jnp.einsum("zjp,zpt->zjt", pick, projected, precision=lax.Precision.HIGH)
     ratios = rows.astype(jnp.float32) / (estimate + BACKGROUND)
 
     same = index[:, None] == index[None, :]
@@ -150,7 +152,7 @@
     first = ~jnp.any(same & earlier, axis=1)
     merge = jnp.broadcast_to((same & first[:, None]).astype(jnp.float32)[None], (planes, slots, slots))
     merged = jnp.einsum(
-        "zij,zjt->zit", merge, ratios, precision=lax.Precision.HIGHEST
+        "zij,zjt->zit", merge, ratios, precision=lax.Precision.HIGH
     ).astype(jnp.bfloat16)
 
     views = subset_views[0]
@@ -171,18 +173,30 @@
         views_k = tail[1 : 1 + angle_count] * 16 + tail[1 + angle_count : 1 + 2 * angle_count]
         kernel_k = kernels(views_k, bins, length)
         index_k = got[planes, :, 0].astype(jnp.int32)
-        scatter = (jnp.arange(pairs, dtype=jnp.int32)[:, None] == index_k[None, :]).astype(
-            jnp.bfloat16
-        )
+        order = jnp.arange(pairs, dtype=jnp.int32)
+        wanted = (order % angle_count) * lines_here + order // angle_count
+        scatter = (wanted[:, None] == index_k[None, :]).astype(jnp.bfloat16)
         scatter = jnp.broadcast_to(scatter[None], (planes, pairs, slots))
         dense = jnp.einsum(
             "zpi,zit->zpt", scatter, got[:planes], preferred_element_type=jnp.float32
         ).astype(jnp.bfloat16)
         dense = dense.reshape(planes, lines_here, angle_count, bins)
-        part = jnp.einsum("zlat,atv->zlv", dense, kernel_k, preferred_element_type=jnp.float32)
-        total = part if total is None else total + part
-    edges = with_halo(weight * total, (("slab", 0),), 1)
-    smoothed = (1.0 - 2.0 * weight) * total + edges[:-2] + edges[2:]
+        parts = [
+            jnp.einsum("zlat,atv->zlv", piece, kernel_k, preferred_element_type=jnp.float32)
+            for piece in (dense[:1], dense[planes - 1 :], dense[1 : planes - 1])
+        ]
+        total = parts if total is None else [t + p for t, p in zip(total, parts)]
+    low, high, middle = total
+    size = lax.axis_size("slab")
+    up = [(i, (i + 1) % size) for i in range(size - 1)]
+    down = [(j, i) for i, j in up]
+    from_below = lax.ppermute(weight[planes - 1 :] * high, "slab", up)
+    from_above = lax.ppermute(weight[:1] * low, "slab", down)
+    total = jnp.concatenate([low, middle, high], axis=0)
+    weighted = weight * total
+    below = jnp.concatenate([from_below, weighted[: planes - 1]], axis=0)
+    above = jnp.concatenate([weighted[1:], from_above], axis=0)
+    smoothed = (1.0 - 2.0 * weight) * total + below + above
     return activity * smoothed / sensitivity
 
 

time: 148 us -> 149 us (level)
  matrix products: 28.3 us -> 35.7 us
  local copies, waits for them, and re-layouts: 20.3 us -> 13.4 us
    ppermute x0 -> x2, starting transfers between devices: none -> 10.5 us  [the longest x1 5.37 us: on_device(): from_below = lax.ppermute(weight[planes - 1:] * high, 'slab', up)]
    ppermute x2 -> x1, starting transfers between devices: 12.6 us -> 4.02 us  [with_halo(): before = lax.ppermute(last, axis, up)]
    dot_general x6 -> x15, matrix products: 25.1 us -> 32.5 us  [the longest x12 20 us: on_device(): jnp.einsum('zlat,atv->zlv', piece, kernel_k, preferred_element_type=jnp.f...]
    ppermute x2 -> x1, waiting for transfers between devices: 6.46 us -> 0.01 us  [with_halo(): after = lax.ppermute(leading, axis, down)]
    all_to_all x1, waiting for transfers between devices: 9.35 us -> 14.5 us  [on_device(): lax.all_to_all(send.reshape(slab_count, capacity, row + extra), 'slab', 0...]
    reshape x1 -> x0, local copies, waits for them, and re-layouts: 4.44 us -> none  [on_device(): projected = projected.reshape(planes, pairs, bins)]
    gather x1 -> x0, local copies, waits for them, and re-layouts: 4.22 us -> none  [on_device(): estimate = projected[:, index, :]]
    dot_general x1 -> x0, local copies, waits for them, and re-layouts: 3.79 us -> none  [on_device(): jnp.einsum('zlv,atv->zlat', blurred, tof_kernel, preferred_element_type=j...]
  transfers between devices with their start and end apart: 5 -> 5, of which waited for: 2 -> 1; matrix products, arithmetic and copies ran while one was open for 17% -> 19% of each run, Pallas kernels for 0% -> 0%
where the time goes in v4:
time: 149 us; the launch traced here: 147 us
  Pallas kernels  36.6 us (25%)
  matrix products  35.7 us (24%)
  starting transfers between devices  29.2 us (20%)
  other arithmetic  17.6 us (12%)
  waiting for transfers between devices  14.5 us (10%)
  local copies, waits for them, and re-layouts  13.4 us (9%)
    pallas_call x1, Pallas kernels, ring_gather(): pl.pallas_call(ring_gather_kernel, out_shape=jax.ShapeDtypeStruct((3,) +...  36.6 us
    dot_general x12, matrix products, on_device(): jnp.einsum('zlat,atv->zlv', piece, kernel_k, preferred_element_type=jnp.f...  20 us
    all_to_all x1, waiting for transfers between devices, on_device(): lax.all_to_all(send.reshape(slab_count, capacity, row + extra), 'slab', 0...  14.5 us
    all_to_all x1, starting transfers between devices, on_device(): lax.all_to_all(send.reshape(slab_count, capacity, row + extra), 'slab', 0...  12.8 us
    dot_general x1, matrix products, on_device(): jnp.einsum('zlv,atv->zalt', blurred, tof_kernel, preferred_element_type=j...  7.22 us
    div x1, other arithmetic, on_device(): return activity * smoothed / sensitivity  5.78 us
    ppermute x1, starting transfers between devices, on_device(): from_below = lax.ppermute(weight[planes - 1:] * high, 'slab', up)  5.37 us
    ppermute x1, starting transfers between devices, on_device(): from_above = lax.ppermute(weight[:1] * low, 'slab', down)  5.11 us
  transfers between devices with their start and end apart: 5, of which 1 were waited for; matrix products, arithmetic and copies ran while one was open for 19% of the time, Pallas kernels for 0%

profile of v4, /device:TPU:31, one launch (start us, length us, event | category | flops | bytes accessed | tf_op | source)
XLA Modules:
  0.0 147.4 jit_solution(5011311373614889452)
XLA Ops:
  0.0 1.0 fusion.190
  1.0 4.0 %collective-permute-start = (f32[1,32,1024]{2,1,0:T(8,128)S(1)}, f32[1,32,1024]{2,1,0:T(8,128)S(1)}, u32[]{:S(2)}, u32[]{:S(2)}) collective-permute-start(f32[1,32,1024]{2,1,0:T(8,128)S(1)} %get-tuple-element.51), channel_id=1, source_target_pairs={{0,4},{4,8},{8,12},{12,16},{16,20},{20,24},{24,28},{28,32},{32,36}... | collective-permute-start | bytes 393224 | tf_op jit(solution)/shard_map/ppermute | solution.py:25
  5.0 1.9 %collective-permute-start.1 = (f32[1,32,1024]{2,1,0:T(8,128)S(1)}, f32[1,32,1024]{2,1,0:T(8,128)S(1)}, u32[]{:S(2)}, u32[]{:S(2)}) collective-permute-start(f32[1,32,1024]{2,1,0:T(8,128)S(1)} %get-tuple-element.52), channel_id=1, source_target_pairs={{4,0},{8,4},{12,8},{16,12},{20,16},{24,20},{28,24},{32,28},{36,32}... | collective-permute-start | bytes 393224 | tf_op jit(solution)/shard_map/ppermute | solution.py:26
  7.0 0.7 fusion.152
  7.8 0.8 select_reduce_fusion
  8.6 0.7 multiply_add_fusion.5
  9.3 1.3 copy.76
  10.6 0.7 convert_bitcast_fusion.2
  11.3 0.4 convolution_convert_fusion
  11.8 1.2 reshape.705
  13.0 12.8 %all-to-all-start = ((bf16[64,2,4224]{2,1,0:T(2,128)(2,1)}), bf16[64,2,4224]{2,1,0:T(2,128)(2,1)S(1)}, u32[]{:S(2)}, u32[]{:S(2)}) async-start(bf16[64,2,4224]{2,1,0:T(2,128)(2,1)} %reshape.705), calls=%async_computation | async-start | bytes 2162688 | tf_op jit(solution)/shard_map/all_to_all | solution.py:140
  25.8 0.6 compare_reduce_fusion.1
  26.5 0.7 fusion.157
  27.3 0.7 compare_reduce_fusion.2
  27.9 0.7 compare_reduce_fusion
  28.6 0.6 fusion.191
  29.2 7.2 %convolution_bitcast_fusion = f32[32,8,32,128]{3,2,0,1:T(8,128)S(1)} fusion(f32[8,128]{1,0:T(8,128)S(1)} %multiply_add_fusion.4, f32[1024]{0:T(1024)S(1)} %iota_add_fusion, f32[1,32,1024]{2,1,0:T(8,128)S(1)} %collective-permute-done.1, f32[32,32,1024]{2,1,0:T(8,128)} %param.14, f32[1,32,1024]{2,1,0:T(8,128)S(1)} %collective-permute-done, ...), kind=kOutput, calls=%fused_computation.41 | convolution fusion | flops 2161115136 | bytes 8659200 | tf_op jit(solution)/shard_map/zlv,atv->zalt/dot_general | solution.py:119
  36.4 2.5 %copy.23 = f32[32,8,32,128]{3,2,1,0:T(8,128)} copy(f32[32,8,32,128]{3,2,0,1:T(8,128)S(1)} %convolution_bitcast_fusion) | data formatting | bytes 8388608 | tf_op jit(solution)/shard_map/zlv,atv->zalt/transpose | solution.py:119
  38.9 14.5 %all-to-all-done = bf16[64,2,4224]{2,1,0:T(2,128)(2,1)S(1)} async-done(((bf16[64,2,4224]{2,1,0:T(2,128)(2,1)}), bf16[64,2,4224]{2,1,0:T(2,128)(2,1)S(1)}, u32[]{:S(2)}, u32[]{:S(2)}) %all-to-all-start) | async-done | bytes 1081376 | tf_op jit(solution)/shard_map/all_to_all | solution.py:140
  53.4 0.4 reshape.706
  54.1 0.2 fusion.149
  54.4 0.6 fusion.140
  55.0 4.2 %fusion.68 = f32[32,128,128]{2,1,0:T(8,128)S(1)} fusion(f32[32,256,128]{2,1,0:T(8,128)} %bitcast.172, f32[128,256]{1,0:T(8,128)S(1)} %fusion.139), kind=kOutput, calls=%fused_computation.70 | convolution fusion | flops 805306368 | bytes 6422528 | tf_op jit(solution)/shard_map/zjp,zpt->zjt/dot_general | solution.py:147
  59.2 1.1 fusion.75
  60.4 0.4 scatter.11
  60.8 0.7 slice_select_fusion
  61.5 0.6 scatter.14
  62.1 1.1 pad_maximum_fusion.3.payload
  63.2 36.6 %shard_map.82 = bf16[3,33,128,128]{3,2,1,0:T(8,128)(2,1)} custom-call(bf16[33,128,128]{2,1,0:T(8,128)(2,1)} %pad_maximum_fusion.3.payload), custom_call_target="tpu_custom_call" | custom-call | tf_op jit(solution)/shard_map/pallas_call | solution.py:95
  99.8 2.4 %slice_bitcast_fusion.4 = (bf16[33,128,128]{2,1,0:T(8,128)(2,1)S(1)}, bf16[33,128,128]{2,1,0:T(8,128)(2,1)S(1)}, bf16[33,128,128]{2,1,0:T(8,128)(2,1)S(1)}) fusion(bf16[3,33,128,128]{3,2,1,0:T(8,128)(2,1)} %shard_map.82), kind=kLoop, calls=%fused_computation.100 | loop fusion | bytes 6488064 | tf_op jit(solution)/shard_map/squeeze | solution.py:171
  102.2 0.1 convert_reduce_fusion.1
  102.3 0.1 convert_reduce_fusion.3
  102.5 0.1 compare_convert_fusion
  102.6 0.7 convolution_convert_fusion.3
  103.4 0.2 slice_bitcast_fusion.2
  103.6 0.7 convolution_convert_fusion.2
  104.3 0.1 slice_bitcast_fusion.1
  104.4 0.7 convolution_convert_fusion.1
  105.2 0.2 slice_bitcast_fusion
  105.4 0.7 convolution_convert_fusion.4
  106.1 0.1 slice_bitcast_fusion.3
  106.2 0.1 multiply_bitcast_fusion.2
  106.4 0.1 multiply_bitcast_fusion.3
  106.6 0.1 multiply_bitcast_fusion.4
  106.9 1.2 fusion.82
  108.1 1.2 fusion.85
  109.4 2.4 %fusion.38 = f32[30,32,1024,1]{2,1,3,0:T(8,128)S(1)} fusion(f32[8,128]{1,0:T(8,128)S(1)} %get-tuple-element.72, f32[1024]{0:T(1024)S(1)} %iota_add_fusion, bf16[30,32,8,128]{3,2,1,0:T(8,128)(2,1)S(1)} %slice_bitcast_fusion.2), kind=kOutput, calls=%fused_computation.51 | convolution fusion | flops 2019557376 | bytes 5906432 | tf_op jit(solution)/shard_map/zlat,atv->zlv/dot_general | solution.py:185
  111.8 1.2 fusion.121
  113.0 2.4 %fusion.36 = f32[30,32,1024,1]{2,1,3,0:T(8,128)S(1)} fusion(f32[8,128]{1,0:T(8,128)S(1)} %get-tuple-element.73, f32[1024]{0:T(1024)S(1)} %iota_add_fusion, bf16[30,32,8,128]{3,2,1,0:T(8,128)(2,1)S(1)} %slice_bitcast_fusion.1), kind=kOutput, calls=%fused_computation.49 | convolution fusion | flops 2019557376 | bytes 5906432 | tf_op jit(solution)/shard_map/zlat,atv->zlv/dot_general | solution.py:185
  115.4 1.5 fusion.115
  116.9 2.4 %fusion.34 = f32[30,32,1024,1]{2,1,3,0:T(8,128)S(1)} fusion(f32[8,128]{1,0:T(8,128)S(1)} %get-tuple-element.70, f32[1024]{0:T(1024)S(1)} %iota_add_fusion, bf16[30,32,8,128]{3,2,1,0:T(8,128)(2,1)S(1)} %slice_bitcast_fusion), kind=kOutput, calls=%fused_computation.47 | convolution fusion | flops 2019557376 | bytes 5906432 | tf_op jit(solution)/shard_map/zlat,atv->zlv/dot_general | solution.py:185
  119.3 1.2 fusion.109
  120.6 0.7 multiply_bitcast_fusion
  121.3 5.1 %collective-permute-start.3 = (f32[1,32,1024]{2,1,0:T(8,128)S(1)}, f32[1,32,1024]{2,1,0:T(8,128)S(1)}, u32[]{:S(2)}, u32[]{:S(2)}) collective-permute-start(f32[1,32,1024]{2,1,0:T(8,128)S(1)} %multiply_bitcast_fusion), channel_id=1, source_target_pairs={{4,0},{8,4},{12,8},{16,12},{20,16},{24,20},{28,24},{32,28},{36,32}... | collective-permute-start | bytes 393224 | tf_op jit(solution)/shard_map/ppermute | solution.py:194
  126.4 1.2 fusion.118
  127.6 1.3 fusion.112
  128.9 1.3 fusion.106
  130.1 0.6 multiply_bitcast_fusion.1
  130.7 5.4 %collective-permute-start.2 = (f32[1,32,1024]{2,1,0:T(8,128)S(1)}, f32[1,32,1024]{2,1,0:T(8,128)S(1)}, u32[]{:S(2)}, u32[]{:S(2)}) collective-permute-start(f32[1,32,1024]{2,1,0:T(8,128)S(1)} %multiply_bitcast_fusion.1), channel_id=1, source_target_pairs={{0,4},{4,8},{8,12},{12,16},{16,20},{20,24},{24,28},{28,32},{32,36}... | collective-permute-start | bytes 393224 | tf_op jit(solution)/shard_map/ppermute | solution.py:193
  136.1 2.5 %bitcast_add_fusion = f32[30,32,1024]{2,1,0:T(8,128)S(1)} fusion(f32[30,32,1024,1]{2,1,3,0:T(8,128)S(1)} %fusion.34, f32[30,32,1024,1]{2,1,3,0:T(8,128)S(1)} %fusion.36, f32[30,32,1024,1]{2,1,3,0:T(8,128)S(1)} %fusion.38, f32[8,128]{1,0:T(8,128)S(1)} %get-tuple-element.71, f32[1024]{0:T(1024)S(1)} %iota_add_fusion, ...), kind=kOutput, calls=%fused_computation.37 | convolution fusion | flops 2022506496 | bytes 17702912 | tf_op jit(solution)/shard_map/zlat,atv->zlv/dot_general | solution.py:185
  138.6 0.8 fusion.27
  139.5 1.3 fusion.189
  140.8 0.8 copy-done.1
  141.7 5.8 %fusion.26 = f32[32,32,1024]{2,1,0:T(8,128)} fusion(f32[32,32,1024]{2,1,0:T(8,128)} %param.15, f32[32,32,1024]{2,1,0:T(8,128)S(1)} %copy-done.1, f32[31,32,1024]{2,1,0:T(8,128)S(1)} %get-tuple-element.50, f32[1,32,1024]{2,1,0:T(8,128)S(1)} %collective-permute-done.2, f32[1,32,1024]{2,1,0:T(8,128)S(1)} %collective-permute-done.3, ...), kind=kLoop, calls=%fused_computation.36 | loop fusion | flops 9437184 | bytes 25165952 | tf_op jit(solution)/shard_map/div | solution.py:200
  (38 shorter events, 1.0 us)
Async XLA Ops:
  0.0 26.4 %copy-start.2 = (f32[32]{0:T(128)S(1)}, f32[32]{0:T(128)}, u32[]{:S(2)}) copy-start(f32[32]{0:T(128)} %param.16) | copy-start | bytes 388
  0.0 26.4 %copy-start.3 = (s32[1,8]{1,0:T(1,128)S(1)}, s32[1,8]{1,0:T(1,128)}, u32[]{:S(2)}) copy-start(s32[1,8]{1,0:T(1,128)} %param.21) | copy-start | bytes 100
  1.0 28.2 %collective-permute-start = (f32[1,32,1024]{2,1,0:T(8,128)S(1)}, f32[1,32,1024]{2,1,0:T(8,128)S(1)}, u32[]{:S(2)}, u32[]{:S(2)}) collective-permute-start(f32[1,32,1024]{2,1,0:T(8,128)S(1)} %get-tuple-element.51), channel_id=1, source_target_pairs={{0,4},{4,8},{8,12},{12,16},{16,20},{20,24},{24,28},{28,32},{32,36}... | collective-permute-start | bytes 393224 | tf_op jit(solution)/shard_map/ppermute | solution.py:25
  5.0 24.2 %collective-permute-start.1 = (f32[1,32,1024]{2,1,0:T(8,128)S(1)}, f32[1,32,1024]{2,1,0:T(8,128)S(1)}, u32[]{:S(2)}, u32[]{:S(2)}) collective-permute-start(f32[1,32,1024]{2,1,0:T(8,128)S(1)} %get-tuple-element.52), channel_id=1, source_target_pairs={{4,0},{8,4},{12,8},{16,12},{20,16},{24,20},{28,24},{32,28},{36,32}... | collective-permute-start | bytes 393224 | tf_op jit(solution)/shard_map/ppermute | solution.py:26
  13.0 40.4 %all-to-all-start = ((bf16[64,2,4224]{2,1,0:T(2,128)(2,1)}), bf16[64,2,4224]{2,1,0:T(2,128)(2,1)S(1)}, u32[]{:S(2)}, u32[]{:S(2)}) async-start(bf16[64,2,4224]{2,1,0:T(2,128)(2,1)} %reshape.705), calls=%async_computation | async-start | bytes 2162688 | tf_op jit(solution)/shard_map/all_to_all | solution.py:140
  99.8 2.9 %copy-start = (bf16[3,33,128,128]{3,2,1,0:T(8,128)(2,1)S(1)}, bf16[3,33,128,128]{3,2,1,0:T(8,128)(2,1)}, u32[]{:S(2)}) copy-start(bf16[3,33,128,128]{3,2,1,0:T(8,128)(2,1)} %shard_map.82) | copy-start | bytes 9732100
  121.3 19.5 %collective-permute-start.3 = (f32[1,32,1024]{2,1,0:T(8,128)S(1)}, f32[1,32,1024]{2,1,0:T(8,128)S(1)}, u32[]{:S(2)}, u32[]{:S(2)}) collective-permute-start(f32[1,32,1024]{2,1,0:T(8,128)S(1)} %multiply_bitcast_fusion), channel_id=1, source_target_pairs={{4,0},{8,4},{12,8},{16,12},{20,16},{24,20},{28,24},{32,28},{36,32}... | collective-permute-start | bytes 393224 | tf_op jit(solution)/shard_map/ppermute | solution.py:194
  130.7 10.1 %collective-permute-start.2 = (f32[1,32,1024]{2,1,0:T(8,128)S(1)}, f32[1,32,1024]{2,1,0:T(8,128)S(1)}, u32[]{:S(2)}, u32[]{:S(2)}) collective-permute-start(f32[1,32,1024]{2,1,0:T(8,128)S(1)} %multiply_bitcast_fusion.1), channel_id=1, source_target_pairs={{0,4},{4,8},{8,12},{12,16},{16,20},{20,24},{24,28},{28,32},{32,36}... | collective-permute-start | bytes 393224 | tf_op jit(solution)/shard_map/ppermute | solution.py:193
  139.5 2.2 %copy-start.1 = (f32[32,32,1024]{2,1,0:T(8,128)S(1)}, f32[32,32,1024]{2,1,0:T(8,128)}, u32[]{:S(2)}) copy-start(f32[32,32,1024]{2,1,0:T(8,128)} %param.14) | copy-start | bytes 12582916

commit v5 on v3

--- a/solution.py
+++ b/solution.py
@@ -102,6 +102,63 @@
     )(payload)
 
 
+def exchange_kernel(send, out, local_sem, send_sems, recv_sems):
+    count = lax.axis_size("slab")
+    me = lax.axis_index("slab")
+    view = lax.axis_index("view")
+
+    barrier = pltpu.get_barrier_semaphore()
+
+    def greet(step, carry):
+        peer = lax.rem(me + step, count)
+        pl.semaphore_signal(barrier, inc=1, device_id=(peer, view), device_id_type=MESH)
+        return carry
+
+    lax.fori_loop(1, count, greet, 0)
+    pl.semaphore_wait(barrier, count - 1)
+
+    local = pltpu.make_async_copy(send.at[me], out.at[me], local_sem)
+    local.start()
+
+    def copy_to(step):
+        peer = lax.rem(me + step, count)
+        return pltpu.make_async_remote_copy(
+            src_ref=send.at[peer], dst_ref=out.at[me],
+            send_sem=send_sems.at[step], recv_sem=recv_sems.at[step],
+            device_id=(peer, view), device_id_type=MESH,
+        )
+
+    def start(step, carry):
+        copy_to(step).start()
+        return carry
+
+    def finish(step, carry):
+        copy = copy_to(step)
+        copy.wait_send()
+        copy.wait_recv()
+        return carry
+
+    lax.fori_loop(1, count, start, 0)
+    lax.fori_loop(1, count, finish, 0)
+    local.wait()
+
+
+def exchange(send):
+    count = send.shape[0]
+    return pl.pallas_call(
+        exchange_kernel,
+        out_shape=jax.ShapeDtypeStruct(send.shape, send.dtype),
+        in_specs=[pl.BlockSpec(memory_space=pl.ANY)],
+        out_specs=pl.BlockSpec(memory_space=pl.ANY),
+        scratch_shapes=[
+            pltpu.SemaphoreType.DMA(()),
+            pltpu.SemaphoreType.DMA((count,)),
+            pltpu.SemaphoreType.DMA((count,)),
+        ],
+        compiler_params=pltpu.CompilerParams(collective_id=1, has_side_effects=True),
+    )(send)
+
+
 def on_device(
     activity, sensitivity, psf_width, measured, block_slab, block_line, block_angle, subset_views
 ):
@@ -116,7 +173,7 @@
     tof_kernel = kernels(subset_views[0], bins, length)
     angle_count = tof_kernel.shape[0]
     pairs = angle_count * lines_here
-    projected = jnp.einsum("zlv,atv->zlat", blurred, tof_kernel, preferred_element_type=jnp.float32)
+    projected = jnp.einsum("zlv,atv->zalt", blurred, tof_kernel, preferred_element_type=jnp.float32)
     projected = projected.reshape(planes, pairs, bins)
 
     slab_count = lax.axis_size("slab")
@@ -132,17 +189,17 @@
     place = (jnp.arange(slots, dtype=jnp.int32)[:, None] == flat_slot[None, :]).astype(
         jnp.bfloat16
     )
-    pair_id = block_line[0] * angle_count + block_angle[0]
+    pair_id = block_angle[0] * lines_here + block_line[0]
     extra = 128
     tag = jnp.broadcast_to(pair_id.astype(jnp.bfloat16)[:, None], (block_total, extra))
     outgoing = jnp.concatenate([measured[0].reshape(block_total, row), tag], axis=1)
     send = jnp.dot(place, outgoing, preferred_element_type=jnp.float32).astype(jnp.bfloat16)
-    recv = lax.all_to_all(
-        send.reshape(slab_count, capacity, row + extra), "slab", 0, 0, tiled=True
-    ).reshape(slots, row + extra)
+    recv = exchange(send.reshape(slab_count, capacity, row + extra)).reshape(slots, row + extra)
     index = recv[:, row].astype(jnp.int32)
     rows = recv[:, :row].reshape(slots, planes, bins).transpose(1, 0, 2)
-    estimate = projected[:, index, :]
+    pick = (index[:, None] == jnp.arange(pairs, dtype=jnp.int32)[None, :]).astype(jnp.float32)
+    pick = jnp.broadcast_to(pick[None], (planes, slots, pairs))
+    estimate = jnp.einsum("zjp,zpt->zjt", pick, projected, precision=lax.Precision.HIGH)
     ratios = rows.astype(jnp.float32) / (estimate + BACKGROUND)
 
     same = index[:, None] == index[None, :]
@@ -150,7 +207,7 @@
     first = ~jnp.any(same & earlier, axis=1)
     merge = jnp.broadcast_to((same & first[:, None]).astype(jnp.float32)[None], (planes, slots, slots))
     merged = jnp.einsum(
-        "zij,zjt->zit", merge, ratios, precision=lax.Precision.HIGHEST
+        "zij,zjt->zit", merge, ratios, precision=lax.Precision.HIGH
     ).astype(jnp.bfloat16)
 
     views = subset_views[0]
@@ -171,9 +228,9 @@
         views_k = tail[1 : 1 + angle_count] * 16 + tail[1 + angle_count : 1 + 2 * angle_count]
         kernel_k = kernels(views_k, bins, length)
         index_k = got[planes, :, 0].astype(jnp.int32)
-        scatter = (jnp.arange(pairs, dtype=jnp.int32)[:, None] == index_k[None, :]).astype(
-            jnp.bfloat16
-        )
+        order = jnp.arange(pairs, dtype=jnp.int32)
+        wanted = (order % angle_count) * lines_here + order // angle_count
+        scatter = (wanted[:, None] == index_k[None, :]).astype(jnp.bfloat16)
         scatter = jnp.broadcast_to(scatter[None], (planes, pairs, slots))
         dense = jnp.einsum(
             "zpi,zit->zpt", scatter, got[:planes], preferred_element_type=jnp.float32

time: 148 us -> 149 us (level)
  Pallas kernels: 36.6 us -> 77.1 us
  starting transfers between devices: 29.2 us -> 11.8 us
  local copies, waits for them, and re-layouts: 20.3 us -> 8.77 us
  waiting for transfers between devices: 15.8 us -> 6.47 us
    pallas_call x0 -> x1, Pallas kernels: none -> 37.9 us  [exchange(): pl.pallas_call(exchange_kernel, out_shape=jax.ShapeDtypeStruct(send.shape...]
    all_to_all x1 -> x0, starting transfers between devices: 12.8 us -> none  [on_device(): lax.all_to_all(send.reshape(slab_count, capacity, row + extra), 'slab', 0...]
    all_to_all x1 -> x0, waiting for transfers between devices: 9.35 us -> none  [on_device(): lax.all_to_all(send.reshape(slab_count, capacity, row + extra), 'slab', 0...]
    ppermute x2, starting transfers between devices: 12.6 us -> 8 us  [with_halo(): before = lax.ppermute(last, axis, up)]
    gather x1 -> x0, local copies, waits for them, and re-layouts: 4.22 us -> none  [on_device(): estimate = projected[:, index, :]]
    dot_general x1 -> x0, local copies, waits for them, and re-layouts: 3.79 us -> none  [on_device(): jnp.einsum('zlv,atv->zlat', blurred, tof_kernel, preferred_element_type=j...]
    reshape x2 -> x1, local copies, waits for them, and re-layouts: 4.87 us -> 1.48 us  [on_device(): exchange(send.reshape(slab_count, capacity, row + extra))]
    pallas_call x1, Pallas kernels: 36.6 us -> 39.2 us  [ring_gather(): pl.pallas_call(ring_gather_kernel, out_shape=jax.ShapeDtypeStruct((3,) +...]
  transfers between devices with their start and end apart: 5 -> 4, of which waited for: 2 -> 1; matrix products, arithmetic and copies ran while one was open for 17% -> 10% of each run, Pallas kernels for 0% -> 26%
where the time goes in v5:
time: 149 us; the launch traced here: 148 us
  Pallas kernels  77.1 us (52%)
  matrix products  28.1 us (19%)
  other arithmetic  15.2 us (10%)
  starting transfers between devices  11.8 us (8%)
  local copies, waits for them, and re-layouts  8.77 us (6%)
  waiting for transfers between devices  6.47 us (4%)
    pallas_call x1, Pallas kernels, ring_gather(): pl.pallas_call(ring_gather_kernel, out_shape=jax.ShapeDtypeStruct((3,) +...  39.2 us
    pallas_call x1, Pallas kernels, exchange(): pl.pallas_call(exchange_kernel, out_shape=jax.ShapeDtypeStruct(send.shape...  37.9 us
    dot_general x4, matrix products, on_device(): jnp.einsum('zlat,atv->zlv', dense, kernel_k, preferred_element_type=jnp.f...  14.6 us
    ppermute x2, starting transfers between devices, with_halo(): before = lax.ppermute(last, axis, up)  8 us
    dot_general x1, matrix products, on_device(): jnp.einsum('zlv,atv->zalt', blurred, tof_kernel, preferred_element_type=j...  7.39 us
    ppermute x2, waiting for transfers between devices, with_halo(): after = lax.ppermute(leading, axis, down)  6.46 us
    div x1, other arithmetic, on_device(): return activity * smoothed / sensitivity  4.26 us
    another operation x6, other arithmetic  3.92 us
  transfers between devices with their start and end apart: 4, of which 1 were waited for; matrix products, arithmetic and copies ran while one was open for 10% of the time, Pallas kernels for 26%

profile of v5, /device:TPU:31, one launch (start us, length us, event | category | flops | bytes accessed | tf_op | source)
XLA Modules:
  0.0 147.9 jit_solution(18339101955225934914)
XLA Ops:
  0.0 1.0 fusion.119
  1.0 4.0 %collective-permute-start = (f32[1,32,1024]{2,1,0:T(8,128)S(1)}, f32[1,32,1024]{2,1,0:T(8,128)S(1)}, u32[]{:S(2)}, u32[]{:S(2)}) collective-permute-start(f32[1,32,1024]{2,1,0:T(8,128)S(1)} %get-tuple-element.51), channel_id=1, source_target_pairs={{0,4},{4,8},{8,12},{12,16},{16,20},{20,24},{24,28},{28,32},{32,36}... | collective-permute-start | bytes 393224 | tf_op jit(solution)/shard_map/ppermute | solution.py:25
  5.0 1.9 %collective-permute-start.1 = (f32[1,32,1024]{2,1,0:T(8,128)S(1)}, f32[1,32,1024]{2,1,0:T(8,128)S(1)}, u32[]{:S(2)}, u32[]{:S(2)}) collective-permute-start(f32[1,32,1024]{2,1,0:T(8,128)S(1)} %get-tuple-element.52), channel_id=1, source_target_pairs={{4,0},{8,4},{12,8},{16,12},{20,16},{24,20},{28,24},{32,28},{36,32}... | collective-permute-start | bytes 393224 | tf_op jit(solution)/shard_map/ppermute | solution.py:26
  6.9 0.7 compare_reduce_fusion.2
  7.6 0.6 compare_reduce_fusion.1
  8.2 0.7 compare_reduce_fusion
  8.9 0.7 fusion.104
  9.6 0.7 multiply_bitcast_fusion.8
  10.3 0.7 fusion.97
  11.0 0.1 reduce_window_sum.11
  11.1 0.8 select_reduce_fusion
  12.0 0.7 multiply_add_fusion.5
  12.6 1.3 copy.44
  13.9 0.0 copy-start.4
  13.9 0.0 copy-start.3
  13.9 0.7 convert_bitcast_fusion.6
  14.6 0.1 broadcast_in_dim.18
  14.7 0.4 convolution_convert_fusion
  15.1 1.2 reshape.645.send
  16.4 37.9 %shard_map.82 = bf16[64,2,4224]{2,1,0:T(2,128)(2,1)} custom-call(bf16[64,2,4224]{2,1,0:T(2,128)(2,1)} %reshape.645.send), custom_call_target="tpu_custom_call" | custom-call | tf_op jit(solution)/shard_map/pallas_call | solution.py:148
  54.3 1.5 %reshape.646 = bf16[128,4224]{1,0:T(8,128)(2,1)S(1)} reshape(bf16[64,2,4224]{2,1,0:T(2,128)(2,1)} %shard_map.82) | data formatting | bytes 2162688 | tf_op jit(solution)/shard_map/reshape | solution.py:197
  55.8 0.1 convert_reduce_fusion
  55.9 0.2 fusion.94
  56.1 0.1 fusion.92
  56.2 0.0 copy-done.4
  56.2 0.6 fusion.102
  56.8 0.0 copy-done.3
  56.8 0.6 fusion.93
  57.5 0.4 scatter.11
  57.9 0.7 slice_select_fusion
  58.6 0.4 scatter.14
  59.0 0.1 fusion.95
  59.1 0.1 multiply_add_fusion.4
  59.2 0.0 collective-permute-done
  59.2 0.0 collective-permute-done.1
  59.2 7.4 %convolution_bitcast_fusion = f32[32,8,32,128]{3,2,0,1:T(8,128)S(1)} fusion(f32[8,128]{1,0:T(8,128)S(1)} %multiply_add_fusion.4, f32[1024]{0:T(1024)S(1)} %iota_add_fusion, f32[1,32,1024]{2,1,0:T(8,128)S(1)} %collective-permute-done.1, f32[32,32,1024]{2,1,0:T(8,128)} %param.14, f32[1,32,1024]{2,1,0:T(8,128)S(1)} %collective-permute-done, ...), kind=kOutput, calls=%fused_computation.41 | convolution fusion | flops 2161115136 | bytes 8659200 | tf_op jit(solution)/shard_map/zlv,atv->zalt/dot_general | solution.py:176
  66.6 0.4 copy.15
  67.1 1.9 %fusion.71 = f32[32,128,128]{2,1,0:T(8,128)S(1)} fusion(f32[32,256,128]{2,1,0:T(8,128)S(1)} %bitcast.120, f32[128,256]{1,0:T(8,128)S(1)} %fusion.92), kind=kOutput, calls=%fused_computation.86 | convolution fusion | flops 805306368 | bytes 6422528 | tf_op jit(solution)/shard_map/zjp,zpt->zjt/dot_general | solution.py:202
  68.9 1.1 fusion.74
  70.1 1.1 pad_maximum_fusion.4.payload
  71.1 39.2 %shard_map.83 = bf16[3,33,128,128]{3,2,1,0:T(8,128)(2,1)} custom-call(bf16[33,128,128]{2,1,0:T(8,128)(2,1)} %pad_maximum_fusion.4.payload), custom_call_target="tpu_custom_call" | custom-call | tf_op jit(solution)/shard_map/pallas_call | solution.py:95
  110.3 0.0 copy-start
  110.3 2.4 %slice_bitcast_fusion = (bf16[33,128,128]{2,1,0:T(8,128)(2,1)S(1)}, bf16[33,128,128]{2,1,0:T(8,128)(2,1)S(1)}, bf16[33,128,128]{2,1,0:T(8,128)(2,1)S(1)}) fusion(bf16[3,33,128,128]{3,2,1,0:T(8,128)(2,1)} %shard_map.83), kind=kLoop, calls=%fused_computation.90 | loop fusion | bytes 6488064 | tf_op jit(solution)/shard_map/squeeze | solution.py:226
  112.7 0.1 convert_reduce_fusion.3
  112.9 0.1 convert_reduce_fusion.1
  113.0 0.1 multiply_bitcast_fusion.2
  113.2 0.1 multiply_bitcast_fusion
  113.4 0.1 multiply_bitcast_fusion.1
  113.6 0.1 compare_convert_fusion
  113.7 0.7 convert_bitcast_fusion.4
  114.4 0.0 copy-done
  114.4 0.7 convert_bitcast_fusion.1
  115.1 0.7 convert_bitcast_fusion.3
  115.8 0.7 convert_bitcast_fusion.2
  116.5 0.1 multiply_add_fusion
  116.6 2.5 %fusion.34 = f32[32,32,1024,1]{2,1,3,0:T(8,128)S(1)} fusion(bf16[32,32,8,128]{3,2,1,0:T(8,128)(2,1)S(1)} %convert_bitcast_fusion.4, f32[8,128]{1,0:T(8,128)S(1)} %get-tuple-element.61, f32[1024]{0:T(1024)S(1)} %iota_add_fusion), kind=kOutput, calls=%fused_computation.47 | convolution fusion | flops 2153775104 | bytes 6299648 | tf_op jit(solution)/shard_map/zlat,atv->zlv/dot_general | solution.py:239
  119.2 2.5 %fusion.38 = f32[32,32,1024,1]{2,1,3,0:T(8,128)S(1)} fusion(bf16[32,32,8,128]{3,2,1,0:T(8,128)(2,1)S(1)} %convert_bitcast_fusion.2, f32[8,128]{1,0:T(8,128)S(1)} %get-tuple-element.63, f32[1024]{0:T(1024)S(1)} %iota_add_fusion), kind=kOutput, calls=%fused_computation.49 | convolution fusion | flops 2153775104 | bytes 6299648 | tf_op jit(solution)/shard_map/zlat,atv->zlv/dot_general | solution.py:239
  121.7 4.4 %fusion.36 = f32[32,32,1024,1]{2,1,3,0:T(8,128)} fusion(bf16[32,32,8,128]{3,2,1,0:T(8,128)(2,1)S(1)} %convert_bitcast_fusion.3, f32[8,128]{1,0:T(8,128)S(1)} %get-tuple-element.62, f32[1024]{0:T(1024)S(1)} %iota_add_fusion), kind=kOutput, calls=%fused_computation.48 | convolution fusion | flops 2153775104 | bytes 6299648 | tf_op jit(solution)/shard_map/zlat,atv->zlv/dot_general | solution.py:239
  126.1 5.1 %broadcast_multiply_fusion = (f32[32,32,1024]{2,1,0:T(8,128)S(1)}, f32[32,32,1024]{2,1,0:T(8,128)S(1)}) fusion(f32[32]{0:T(128)S(1)} %copy-done.3, f32[8,128]{1,0:T(8,128)S(1)} %get-tuple-element.60, f32[1024]{0:T(1024)S(1)} %iota_add_fusion, bf16[32,32,8,128]{3,2,1,0:T(8,128)(2,1)S(1)} %convert_bitcast_fusion.1, f32[32,32,1024,1]{2,1,3,0:T(8,128)S(1)} %fusion.38, ...), kind=kOutput, calls=%fused_computation.69 | convolution fusion | flops 2157969408 | bytes 23076992 | tf_op jit(solution)/shard_map/zlat,atv->zlv/dot_general | solution.py:239
  131.2 4.0 %collective-permute-start.2 = (f32[1,32,1024]{2,1,0:T(8,128)S(1)}, f32[1,32,1024]{2,1,0:T(8,128)S(1)}, u32[]{:S(2)}, u32[]{:S(2)}) collective-permute-start(f32[1,32,1024]{2,1,0:T(8,128)S(1)} %get-tuple-element.49), channel_id=1, source_target_pairs={{0,4},{4,8},{8,12},{12,16},{16,20},{20,24},{24,28},{28,32},{32,36}... | collective-permute-start | bytes 393224 | tf_op jit(solution)/shard_map/ppermute | solution.py:25
  135.2 1.9 %collective-permute-start.3 = (f32[1,32,1024]{2,1,0:T(8,128)S(1)}, f32[1,32,1024]{2,1,0:T(8,128)S(1)}, u32[]{:S(2)}, u32[]{:S(2)}) collective-permute-start(f32[1,32,1024]{2,1,0:T(8,128)S(1)} %get-tuple-element.50), channel_id=1, source_target_pairs={{4,0},{8,4},{12,8},{16,12},{20,16},{24,20},{28,24},{32,28},{36,32}... | collective-permute-start | bytes 393224 | tf_op jit(solution)/shard_map/ppermute | solution.py:26
  137.1 0.0 collective-permute-done.2
  137.2 6.5 %collective-permute-done.3 = f32[1,32,1024]{2,1,0:T(8,128)S(1)} collective-permute-done((f32[1,32,1024]{2,1,0:T(8,128)S(1)}, f32[1,32,1024]{2,1,0:T(8,128)S(1)}, u32[]{:S(2)}, u32[]{:S(2)}) %collective-permute-start.3) | collective-permute-done | bytes 131104 | tf_op jit(solution)/shard_map/ppermute | solution.py:26
  143.6 4.3 %fusion.22 = f32[32,32,1024]{2,1,0:T(8,128)} fusion(f32[32,32,1024]{2,1,0:T(8,128)S(1)} %copy-done.2, f32[32,32,1024]{2,1,0:T(8,128)S(1)} %copy-done.1, f32[1,32,1024]{2,1,0:T(8,128)S(1)} %collective-permute-done.3, f32[32,32,1024]{2,1,0:T(8,128)S(1)} %get-tuple-element.66, f32[1,32,1024]{2,1,0:T(8,128)S(1)} %collective-permute-done.2, ...), kind=kLoop, calls=%fused_computation.29 | loop fusion | flops 7340032 | bytes 21233792 | tf_op jit(solution)/shard_map/div | solution.py:243
  (19 shorter events, 0.3 us)
Async XLA Ops:
  1.0 58.2 %collective-permute-start = (f32[1,32,1024]{2,1,0:T(8,128)S(1)}, f32[1,32,1024]{2,1,0:T(8,128)S(1)}, u32[]{:S(2)}, u32[]{:S(2)}) collective-permute-start(f32[1,32,1024]{2,1,0:T(8,128)S(1)} %get-tuple-element.51), channel_id=1, source_target_pairs={{0,4},{4,8},{8,12},{12,16},{16,20},{20,24},{24,28},{28,32},{32,36}... | collective-permute-start | bytes 393224 | tf_op jit(solution)/shard_map/ppermute | solution.py:25
  5.0 54.2 %collective-permute-start.1 = (f32[1,32,1024]{2,1,0:T(8,128)S(1)}, f32[1,32,1024]{2,1,0:T(8,128)S(1)}, u32[]{:S(2)}, u32[]{:S(2)}) collective-permute-start(f32[1,32,1024]{2,1,0:T(8,128)S(1)} %get-tuple-element.52), channel_id=1, source_target_pairs={{4,0},{8,4},{12,8},{16,12},{20,16},{24,20},{28,24},{32,28},{36,32}... | collective-permute-start | bytes 393224 | tf_op jit(solution)/shard_map/ppermute | solution.py:26
  13.9 42.3 %copy-start.4 = (s32[1,8]{1,0:T(1,128)S(1)}, s32[1,8]{1,0:T(1,128)}, u32[]{:S(2)}) copy-start(s32[1,8]{1,0:T(1,128)} %param.21) | copy-start | bytes 100
  13.9 42.8 %copy-start.3 = (f32[32]{0:T(128)S(1)}, f32[32]{0:T(128)}, u32[]{:S(2)}) copy-start(f32[32]{0:T(128)} %param.16) | copy-start | bytes 388
  110.3 4.1 %copy-start = (bf16[3,33,128,128]{3,2,1,0:T(8,128)(2,1)S(1)}, bf16[3,33,128,128]{3,2,1,0:T(8,128)(2,1)}, u32[]{:S(2)}) copy-start(bf16[3,33,128,128]{3,2,1,0:T(8,128)(2,1)} %shard_map.83) | copy-start | bytes 9732100
  126.1 17.5 %copy-start.1 = (f32[32,32,1024]{2,1,0:T(8,128)S(1)}, f32[32,32,1024]{2,1,0:T(8,128)}, u32[]{:S(2)}) copy-start(f32[32,32,1024]{2,1,0:T(8,128)} %param.14) | copy-start | bytes 12582916
  126.1 17.5 %copy-start.2 = (f32[32,32,1024]{2,1,0:T(8,128)S(1)}, f32[32,32,1024]{2,1,0:T(8,128)}, u32[]{:S(2)}) copy-start(f32[32,32,1024]{2,1,0:T(8,128)} %param.15) | copy-start | bytes 12582916
  131.2 5.9 %collective-permute-start.2 = (f32[1,32,1024]{2,1,0:T(8,128)S(1)}, f32[1,32,1024]{2,1,0:T(8,128)S(1)}, u32[]{:S(2)}, u32[]{:S(2)}) collective-permute-start(f32[1,32,1024]{2,1,0:T(8,128)S(1)} %get-tuple-element.49), channel_id=1, source_target_pairs={{0,4},{4,8},{8,12},{12,16},{16,20},{20,24},{24,28},{28,32},{32,36}... | collective-permute-start | bytes 393224 | tf_op jit(solution)/shard_map/ppermute | solution.py:25
  135.2 8.4 %collective-permute-start.3 = (f32[1,32,1024]{2,1,0:T(8,128)S(1)}, f32[1,32,1024]{2,1,0:T(8,128)S(1)}, u32[]{:S(2)}, u32[]{:S(2)}) collective-permute-start(f32[1,32,1024]{2,1,0:T(8,128)S(1)} %get-tuple-element.50), channel_id=1, source_target_pairs={{4,0},{8,4},{12,8},{16,12},{20,16},{24,20},{28,24},{32,28},{36,32}... | collective-permute-start | bytes 393224 | tf_op jit(solution)/shard_map/ppermute | solution.py:26

commit v6 on v5

--- a/solution.py
+++ b/solution.py
@@ -218,15 +218,7 @@
         (views % 16).astype(jnp.float32)[None, :]
     )
     payload = jnp.concatenate([merged, info.astype(jnp.bfloat16)[None]], axis=0)
-    everything = jnp.concatenate([payload[None], ring_gather(payload)], axis=0)
-    group_count = everything.shape[0]
-
-    total = None
-    for group in range(group_count):
-        got = everything[group]
-        tail = got[planes, 0].astype(jnp.int32)
-        views_k = tail[1 : 1 + angle_count] * 16 + tail[1 + angle_count : 1 + 2 * angle_count]
-        kernel_k = kernels(views_k, bins, length)
+    def back_project(got, kernel_k):
         index_k = got[planes, :, 0].astype(jnp.int32)
         order = jnp.arange(pairs, dtype=jnp.int32)
         wanted = (order % angle_count) * lines_here + order // angle_count
@@ -236,8 +228,27 @@
             "zpi,zit->zpt", scatter, got[:planes], preferred_element_type=jnp.float32
         ).astype(jnp.bfloat16)
         dense = dense.reshape(planes, lines_here, angle_count, bins)
-        part = jnp.einsum("zlat,atv->zlv", dense, kernel_k, preferred_element_type=jnp.float32)
-        total = part if total is None else total + part
+        return jnp.einsum("zlat,atv->zlv", dense, kernel_k, preferred_element_type=jnp.float32)
+
+    def kernel_of(got):
+        tail = got[planes, 0].astype(jnp.int32)
+        views_k = tail[1 : 1 + angle_count] * 16 + tail[1 + angle_count : 1 + 2 * angle_count]
+        return kernels(views_k, bins, length)
+
+    view_count = lax.axis_size("view")
+    rightward = [(i, (i + 1) % view_count) for i in range(view_count)]
+    leftward = [(i, (i + view_count - 1) % view_count) for i in range(view_count)]
+    half = (planes + 1) // 2
+    from_left = lax.ppermute(payload, "view", rightward)
+    from_right = lax.ppermute(payload, "view", leftward)
+    total = back_project(payload, tof_kernel)
+    total, from_left, from_right = lax.optimization_barrier((total, from_left, from_right))
+    far_low = lax.ppermute(from_left[:half], "view", rightward)
+    far_high = lax.ppermute(from_right[half:], "view", leftward)
+    total = total + back_project(from_left, kernel_of(from_left))
+    total = total + back_project(from_right, kernel_of(from_right))
+    far = jnp.concatenate([far_low, far_high], axis=0)
+    total = total + back_project(far, kernel_of(far))
     edges = with_halo(weight * total, (("slab", 0),), 1)
     smoothed = (1.0 - 2.0 * weight) * total + edges[:-2] + edges[2:]
     return activity * smoothed / sensitivity

time: 149 us -> 141 us (0.946)
  Pallas kernels: 77.1 us -> 37.9 us
  waiting for transfers between devices: 6.47 us -> 39 us
  starting transfers between devices: 11.8 us -> 16.4 us
  local copies, waits for them, and re-layouts: 8.77 us -> 6.42 us
  other arithmetic: 15.2 us -> 13.1 us
    pallas_call x1 -> x0, Pallas kernels: 39.2 us -> none  [ring_gather(): pl.pallas_call(ring_gather_kernel, out_shape=jax.ShapeDtypeStruct((3,) +...]
    ppermute x0 -> x4, waiting for transfers between devices: none -> 32.6 us  [the longest x1 20.2 us: on_device(): from_left = lax.ppermute(payload, 'view', rightward)]
    ppermute x0 -> x4, starting transfers between devices: none -> 4.36 us  [the longest x1 2.74 us: on_device(): far_low = lax.ppermute(from_left[:half], 'view', rightward)]
    squeeze x1 -> x0, local copies, waits for them, and re-layouts: 2.44 us -> none  [on_device(): got = everything[group]]
  transfers between devices with their start and end apart: 4 -> 8, of which waited for: 1 -> 4; matrix products, arithmetic and copies ran while one was open for 10% -> 18% of each run, Pallas kernels for 26% -> 27%
where the time goes in v6:
time: 141 us
  waiting for transfers between devices  39 us (28%)
  Pallas kernels  37.9 us (27%)
  matrix products  27.8 us (20%)
  starting transfers between devices  16.4 us (12%)
  other arithmetic  13.1 us (9%)
  local copies, waits for them, and re-layouts  6.42 us (5%)
    pallas_call x1, Pallas kernels, exchange(): pl.pallas_call(exchange_kernel, out_shape=jax.ShapeDtypeStruct(send.shape...  37.9 us
    ppermute x1, waiting for transfers between devices, on_device(): from_left = lax.ppermute(payload, 'view', rightward)  20.2 us
    dot_general x4, matrix products, back_project(): jnp.einsum('zlat,atv->zlv', dense, kernel_k, preferred_element_type=jnp.f...  14.4 us
    ppermute x1, waiting for transfers between devices, on_device(): far_high = lax.ppermute(from_right[half:], 'view', leftward)  10.9 us
    ppermute x2, starting transfers between devices, with_halo(): before = lax.ppermute(last, axis, up)  8.2 us
    dot_general x1, matrix products, on_device(): jnp.einsum('zlv,atv->zalt', blurred, tof_kernel, preferred_element_type=j...  7.22 us
    ppermute x2, waiting for transfers between devices, with_halo(): after = lax.ppermute(leading, axis, down)  6.46 us
    div x1, other arithmetic, on_device(): return activity * smoothed / sensitivity  4.26 us
  transfers between devices with their start and end apart: 8, of which 4 were waited for; matrix products, arithmetic and copies ran while one was open for 18% of the time, Pallas kernels for 27%

profile of v6, /device:TPU:31, one launch (start us, length us, event | category | flops | bytes accessed | tf_op | source)
XLA Modules:
  0.0 141.1 jit_solution(17526858766707050947)
XLA Ops:
  0.0 1.0 fusion.110
  1.0 4.0 %collective-permute-start = (f32[1,32,1024]{2,1,0:T(8,128)S(1)}, f32[1,32,1024]{2,1,0:T(8,128)S(1)}, u32[]{:S(2)}, u32[]{:S(2)}) collective-permute-start(f32[1,32,1024]{2,1,0:T(8,128)S(1)} %get-tuple-element.55), channel_id=1, source_target_pairs={{0,4},{4,8},{8,12},{12,16},{16,20},{20,24},{24,28},{28,32},{32,36}... | collective-permute-start | bytes 393224 | tf_op jit(solution)/shard_map/ppermute | solution.py:25
  5.0 1.9 %collective-permute-start.1 = (f32[1,32,1024]{2,1,0:T(8,128)S(1)}, f32[1,32,1024]{2,1,0:T(8,128)S(1)}, u32[]{:S(2)}, u32[]{:S(2)}) collective-permute-start(f32[1,32,1024]{2,1,0:T(8,128)S(1)} %get-tuple-element.56), channel_id=1, source_target_pairs={{4,0},{8,4},{12,8},{16,12},{20,16},{24,20},{28,24},{32,28},{36,32}... | collective-permute-start | bytes 393224 | tf_op jit(solution)/shard_map/ppermute | solution.py:26
  7.0 0.7 fusion.83
  7.7 0.1 reduce_window_sum.11
  7.8 0.8 select_reduce_fusion
  8.6 0.7 multiply_add_fusion.4
  9.3 1.3 copy.46
  10.5 0.0 copy-start.3
  10.6 0.7 convert_bitcast_fusion.6
  11.3 0.1 broadcast_in_dim.18
  11.3 0.4 convolution_convert_fusion
  11.8 1.2 reshape.591.send
  13.0 37.9 %shard_map.82 = bf16[64,2,4224]{2,1,0:T(2,128)(2,1)} custom-call(bf16[64,2,4224]{2,1,0:T(2,128)(2,1)} %reshape.591.send), custom_call_target="tpu_custom_call" | custom-call | tf_op jit(solution)/shard_map/pallas_call | solution.py:148
  50.9 1.5 %reshape.592 = bf16[128,4224]{1,0:T(8,128)(2,1)S(1)} reshape(bf16[64,2,4224]{2,1,0:T(2,128)(2,1)} %shard_map.82) | data formatting | bytes 2162688 | tf_op jit(solution)/shard_map/reshape | solution.py:197
  52.4 0.1 convert_reduce_fusion
  52.5 0.1 fusion.78
  52.6 0.2 fusion.80
  52.8 0.6 compare_reduce_fusion.2
  53.4 0.7 compare_reduce_fusion.1
  54.2 0.6 compare_reduce_fusion
  54.8 0.1 multiply_bitcast_fusion.6
  54.9 0.1 fusion.81
  55.0 0.7 fusion.79
  55.7 0.7 fusion.88
  56.4 0.1 multiply_add_fusion.3
  56.5 0.4 scatter.11
  56.9 0.6 slice_select_fusion
  57.5 0.4 scatter.14
  58.0 0.1 convert_reduce_fusion.4
  58.1 7.2 %convolution_bitcast_fusion.1 = f32[32,8,32,128]{3,2,0,1:T(8,128)S(1)} fusion(f32[1,32,1024]{2,1,0:T(8,128)S(1)} %collective-permute-done.1, f32[32,32,1024]{2,1,0:T(8,128)} %param.14, f32[1,32,1024]{2,1,0:T(8,128)S(1)} %collective-permute-done, f32[32]{0:T(128)S(1)} %copy-done.2, f32[8,128]{1,0:T(8,128)S(1)} %multiply_add_fusion.3, ...), kind=kOutput, calls=%fused_computation.37 | convolution fusion | flops 2161115136 | bytes 8659200 | tf_op jit(solution)/shard_map/zlv,atv->zalt/dot_general | solution.py:176
  65.3 0.4 copy.15
  65.8 1.9 %fusion.60 = f32[32,128,128]{2,1,0:T(8,128)S(1)} fusion(f32[32,256,128]{2,1,0:T(8,128)S(1)} %bitcast.102, f32[128,256]{1,0:T(8,128)S(1)} %fusion.78), kind=kOutput, calls=%fused_computation.74 | convolution fusion | flops 805306368 | bytes 6422528 | tf_op jit(solution)/shard_map/zjp,zpt->zjt/dot_general | solution.py:202
  67.6 1.1 fusion.63
  68.8 0.1 pad_maximum_fusion.4
  68.9 0.1 collective-permute-start.2
  69.0 1.5 %collective-permute-start.3 = (bf16[33,128,128]{2,1,0:T(8,128)(2,1)S(1)}, bf16[33,128,128]{2,1,0:T(8,128)(2,1)S(1)}, u32[]{:S(2)}, u32[]{:S(2)}) collective-permute-start(bf16[33,128,128]{2,1,0:T(8,128)(2,1)S(1)} %pad_maximum_fusion.4), channel_id=1, source_target_pairs={{0,3},{1,0},{2,1},{3,2},{4,7},{5,4},{6,5},{7,6},{8,11},{9,8},{10,9... | collective-permute-start | bytes 3244040 | tf_op jit(solution)/shard_map/ppermute | solution.py:243
  70.4 0.1 compare_convert_fusion.3
  70.5 0.7 convert_bitcast_fusion.4
  71.2 2.5 %convolution_bitcast_fusion = f32[32,32,1024]{2,1,0:T(8,128)S(1)} fusion(bf16[32,32,8,128]{3,2,1,0:T(8,128)(2,1)S(1)} %convert_bitcast_fusion.4, f32[8,128]{1,0:T(8,128)S(1)} %multiply_add_fusion.3, f32[1024]{0:T(1024)S(1)} %iota_add_fusion), kind=kOutput, calls=%fused_computation.36 | convolution fusion | flops 2153775104 | bytes 6299648 | tf_op jit(solution)/shard_map/zlat,atv->zlv/dot_general | solution.py:231
  73.8 20.2 %collective-permute-done.2 = bf16[33,128,128]{2,1,0:T(8,128)(2,1)S(1)} collective-permute-done((bf16[33,128,128]{2,1,0:T(8,128)(2,1)S(1)}, bf16[33,128,128]{2,1,0:T(8,128)(2,1)S(1)}, u32[]{:S(2)}, u32[]{:S(2)}) %collective-permute-start.2) | collective-permute-done | bytes 1081376 | tf_op jit(solution)/shard_map/ppermute | solution.py:242
  94.0 1.5 %collective-permute-done.3 = bf16[33,128,128]{2,1,0:T(8,128)(2,1)S(1)} collective-permute-done((bf16[33,128,128]{2,1,0:T(8,128)(2,1)S(1)}, bf16[33,128,128]{2,1,0:T(8,128)(2,1)S(1)}, u32[]{:S(2)}, u32[]{:S(2)}) %collective-permute-start.3) | collective-permute-done | bytes 1081376 | tf_op jit(solution)/shard_map/ppermute | solution.py:243
  95.6 0.1 collective-permute-start.4
  95.7 0.1 multiply_bitcast_fusion.1
  95.8 2.7 %collective-permute-start.5 = (bf16[16,128,128]{2,1,0:T(8,128)(2,1)S(1)}, bf16[16,128,128]{2,1,0:T(8,128)(2,1)S(1)}, u32[]{:S(2)}, u32[]{:S(2)}) collective-permute-start(bf16[16,128,128]{2,1,0:T(8,128)(2,1)S(1)} %slice.164), channel_id=1, source_target_pairs={{0,1},{1,2},{2,3},{3,0},{4,5},{5,6},{6,7},{7,4},{8,9},{9,10},{10,1... | collective-permute-start | bytes 1572872 | tf_op jit(solution)/shard_map/ppermute | solution.py:246
  98.6 0.1 convert_reduce_fusion.2
  98.7 0.1 multiply_bitcast_fusion.2
  98.9 10.9 %collective-permute-done.4 = bf16[17,128,128]{2,1,0:T(8,128)(2,1)S(1)} collective-permute-done((bf16[17,128,128]{2,1,0:T(8,128)(2,1)S(1)}, bf16[17,128,128]{2,1,0:T(8,128)(2,1)S(1)}, u32[]{:S(2)}, u32[]{:S(2)}) %collective-permute-start.4) | collective-permute-done | bytes 557088 | tf_op jit(solution)/shard_map/ppermute | solution.py:247
  109.7 0.1 convert_reduce_fusion.1
  109.9 0.1 compare_convert_fusion
  110.0 0.7 convert_bitcast_fusion.3
  110.7 0.1 multiply_bitcast_fusion
  110.9 0.7 convert_bitcast_fusion.2
  111.6 0.1 multiply_add_fusion
  111.6 2.5 %fusion.27 = f32[32,32,1024,1]{2,1,3,0:T(8,128)S(1)} fusion(bf16[32,32,8,128]{3,2,1,0:T(8,128)(2,1)S(1)} %convert_bitcast_fusion.3, f32[8,128]{1,0:T(8,128)S(1)} %get-tuple-element.61, f32[1024]{0:T(1024)S(1)} %iota_add_fusion), kind=kOutput, calls=%fused_computation.41 | convolution fusion | flops 2153775104 | bytes 6299648 | tf_op jit(solution)/shard_map/zlat,atv->zlv/dot_general | solution.py:231
  114.2 4.2 %fusion.29 = f32[32,32,1024,1]{2,1,3,0:T(8,128)} fusion(bf16[32,32,8,128]{3,2,1,0:T(8,128)(2,1)S(1)} %convert_bitcast_fusion.2, f32[8,128]{1,0:T(8,128)S(1)} %get-tuple-element.62, f32[1024]{0:T(1024)S(1)} %iota_add_fusion), kind=kOutput, calls=%fused_computation.42 | convolution fusion | flops 2153775104 | bytes 6299648 | tf_op jit(solution)/shard_map/zlat,atv->zlv/dot_general | solution.py:231
  118.4 0.7 convert_bitcast_fusion.1
  119.1 0.0 copy-start
  119.1 0.0 copy-start.1
  119.1 5.1 %broadcast_multiply_fusion = (f32[32,32,1024]{2,1,0:T(8,128)S(1)}, f32[32,32,1024]{2,1,0:T(8,128)S(1)}) fusion(f32[32]{0:T(128)S(1)} %copy-done.2, f32[8,128]{1,0:T(8,128)S(1)} %get-tuple-element.60, f32[1024]{0:T(1024)S(1)} %iota_add_fusion, bf16[32,32,8,128]{3,2,1,0:T(8,128)(2,1)S(1)} %convert_bitcast_fusion.1, f32[32,32,1024,1]{2,1,3,0:T(8,128)} %fusion.29, ...), kind=kOutput, calls=%fused_computation.64 | convolution fusion | flops 2157969408 | bytes 23076992 | tf_op jit(solution)/shard_map/zlat,atv->zlv/dot_general | solution.py:231
  124.3 4.2 %collective-permute-start.6 = (f32[1,32,1024]{2,1,0:T(8,128)S(1)}, f32[1,32,1024]{2,1,0:T(8,128)S(1)}, u32[]{:S(2)}, u32[]{:S(2)}) collective-permute-start(f32[1,32,1024]{2,1,0:T(8,128)S(1)} %get-tuple-element.53), channel_id=1, source_target_pairs={{0,4},{4,8},{8,12},{12,16},{16,20},{20,24},{24,28},{28,32},{32,36}... | collective-permute-start | bytes 393224 | tf_op jit(solution)/shard_map/ppermute | solution.py:25
  128.5 1.9 %collective-permute-start.7 = (f32[1,32,1024]{2,1,0:T(8,128)S(1)}, f32[1,32,1024]{2,1,0:T(8,128)S(1)}, u32[]{:S(2)}, u32[]{:S(2)}) collective-permute-start(f32[1,32,1024]{2,1,0:T(8,128)S(1)} %get-tuple-element.54), channel_id=1, source_target_pairs={{4,0},{8,4},{12,8},{16,12},{20,16},{24,20},{28,24},{32,28},{36,32}... | collective-permute-start | bytes 393224 | tf_op jit(solution)/shard_map/ppermute | solution.py:26
  130.4 6.5 %collective-permute-done.7 = f32[1,32,1024]{2,1,0:T(8,128)S(1)} collective-permute-done((f32[1,32,1024]{2,1,0:T(8,128)S(1)}, f32[1,32,1024]{2,1,0:T(8,128)S(1)}, u32[]{:S(2)}, u32[]{:S(2)}) %collective-permute-start.7) | collective-permute-done | bytes 131104 | tf_op jit(solution)/shard_map/ppermute | solution.py:26
  136.9 4.3 %fusion.18 = f32[32,32,1024]{2,1,0:T(8,128)} fusion(f32[32,32,1024]{2,1,0:T(8,128)S(1)} %copy-done.1, f32[32,32,1024]{2,1,0:T(8,128)S(1)} %copy-done, f32[1,32,1024]{2,1,0:T(8,128)S(1)} %collective-permute-done.7, f32[32,32,1024]{2,1,0:T(8,128)S(1)} %get-tuple-element.65, f32[1,32,1024]{2,1,0:T(8,128)S(1)} %collective-permute-done.6, ...), kind=kLoop, calls=%fused_computation.24 | loop fusion | flops 7340032 | bytes 21233792 | tf_op jit(solution)/shard_map/div | solution.py:254
  (25 shorter events, 0.3 us)
Async XLA Ops:
  1.0 57.1 %collective-permute-start = (f32[1,32,1024]{2,1,0:T(8,128)S(1)}, f32[1,32,1024]{2,1,0:T(8,128)S(1)}, u32[]{:S(2)}, u32[]{:S(2)}) collective-permute-start(f32[1,32,1024]{2,1,0:T(8,128)S(1)} %get-tuple-element.55), channel_id=1, source_target_pairs={{0,4},{4,8},{8,12},{12,16},{16,20},{20,24},{24,28},{28,32},{32,36}... | collective-permute-start | bytes 393224 | tf_op jit(solution)/shard_map/ppermute | solution.py:25
  5.0 53.1 %collective-permute-start.1 = (f32[1,32,1024]{2,1,0:T(8,128)S(1)}, f32[1,32,1024]{2,1,0:T(8,128)S(1)}, u32[]{:S(2)}, u32[]{:S(2)}) collective-permute-start(f32[1,32,1024]{2,1,0:T(8,128)S(1)} %get-tuple-element.56), channel_id=1, source_target_pairs={{4,0},{8,4},{12,8},{16,12},{20,16},{24,20},{28,24},{32,28},{36,32}... | collective-permute-start | bytes 393224 | tf_op jit(solution)/shard_map/ppermute | solution.py:26
  10.5 44.3 %copy-start.3 = (s32[1,8]{1,0:T(1,128)S(1)}, s32[1,8]{1,0:T(1,128)}, u32[]{:S(2)}) copy-start(s32[1,8]{1,0:T(1,128)} %param.21) | copy-start | bytes 100
  10.6 44.3 %copy-start.2 = (f32[32]{0:T(128)S(1)}, f32[32]{0:T(128)}, u32[]{:S(2)}) copy-start(f32[32]{0:T(128)} %param.16) | copy-start | bytes 388
  68.9 25.1 %collective-permute-start.2 = (bf16[33,128,128]{2,1,0:T(8,128)(2,1)S(1)}, bf16[33,128,128]{2,1,0:T(8,128)(2,1)S(1)}, u32[]{:S(2)}, u32[]{:S(2)}) collective-permute-start(bf16[33,128,128]{2,1,0:T(8,128)(2,1)S(1)} %pad_maximum_fusion.4), channel_id=1, source_target_pairs={{0,1},{1,2},{2,3},{3,0},{4,5},{5,6},{6,7},{7,4},{8,9},{9,10},{10,1... | collective-permute-start | bytes 3244040 | tf_op jit(solution)/shard_map/ppermute | solution.py:242
  69.0 26.5 %collective-permute-start.3 = (bf16[33,128,128]{2,1,0:T(8,128)(2,1)S(1)}, bf16[33,128,128]{2,1,0:T(8,128)(2,1)S(1)}, u32[]{:S(2)}, u32[]{:S(2)}) collective-permute-start(bf16[33,128,128]{2,1,0:T(8,128)(2,1)S(1)} %pad_maximum_fusion.4), channel_id=1, source_target_pairs={{0,3},{1,0},{2,1},{3,2},{4,7},{5,4},{6,5},{7,6},{8,11},{9,8},{10,9... | collective-permute-start | bytes 3244040 | tf_op jit(solution)/shard_map/ppermute | solution.py:243
  95.6 14.2 %collective-permute-start.4 = (bf16[17,128,128]{2,1,0:T(8,128)(2,1)S(1)}, bf16[17,128,128]{2,1,0:T(8,128)(2,1)S(1)}, u32[]{:S(2)}, u32[]{:S(2)}) collective-permute-start(bf16[17,128,128]{2,1,0:T(8,128)(2,1)S(1)} %slice.162), channel_id=1, source_target_pairs={{0,3},{1,0},{2,1},{3,2},{4,7},{5,4},{6,5},{7,6},{8,11},{9,8},{10,9... | collective-permute-start | bytes 1671176 | tf_op jit(solution)/shard_map/ppermute | solution.py:247
  95.8 22.6 %collective-permute-start.5 = (bf16[16,128,128]{2,1,0:T(8,128)(2,1)S(1)}, bf16[16,128,128]{2,1,0:T(8,128)(2,1)S(1)}, u32[]{:S(2)}, u32[]{:S(2)}) collective-permute-start(bf16[16,128,128]{2,1,0:T(8,128)(2,1)S(1)} %slice.164), channel_id=1, source_target_pairs={{0,1},{1,2},{2,3},{3,0},{4,5},{5,6},{6,7},{7,4},{8,9},{9,10},{10,1... | collective-permute-start | bytes 1572872 | tf_op jit(solution)/shard_map/ppermute | solution.py:246
  119.1 17.8 %copy-start = (f32[32,32,1024]{2,1,0:T(8,128)S(1)}, f32[32,32,1024]{2,1,0:T(8,128)}, u32[]{:S(2)}) copy-start(f32[32,32,1024]{2,1,0:T(8,128)} %param.14) | copy-start | bytes 12582916
  119.1 17.8 %copy-start.1 = (f32[32,32,1024]{2,1,0:T(8,128)S(1)}, f32[32,32,1024]{2,1,0:T(8,128)}, u32[]{:S(2)}) copy-start(f32[32,32,1024]{2,1,0:T(8,128)} %param.15) | copy-start | bytes 12582916
  124.3 6.1 %collective-permute-start.6 = (f32[1,32,1024]{2,1,0:T(8,128)S(1)}, f32[1,32,1024]{2,1,0:T(8,128)S(1)}, u32[]{:S(2)}, u32[]{:S(2)}) collective-permute-start(f32[1,32,1024]{2,1,0:T(8,128)S(1)} %get-tuple-element.53), channel_id=1, source_target_pairs={{0,4},{4,8},{8,12},{12,16},{16,20},{20,24},{24,28},{28,32},{32,36}... | collective-permute-start | bytes 393224 | tf_op jit(solution)/shard_map/ppermute | solution.py:25
  128.5 8.4 %collective-permute-start.7 = (f32[1,32,1024]{2,1,0:T(8,128)S(1)}, f32[1,32,1024]{2,1,0:T(8,128)S(1)}, u32[]{:S(2)}, u32[]{:S(2)}) collective-permute-start(f32[1,32,1024]{2,1,0:T(8,128)S(1)} %get-tuple-element.54), channel_id=1, source_target_pairs={{4,0},{8,4},{12,8},{16,12},{20,16},{24,20},{28,24},{32,28},{36,32}... | collective-permute-start | bytes 393224 | tf_op jit(solution)/shard_map/ppermute | solution.py:26

commit v7 on v6

--- a/solution.py
+++ b/solution.py
@@ -163,6 +163,7 @@
     activity, sensitivity, psf_width, measured, block_slab, block_line, block_angle, subset_views
 ):
     weight = psf_width[:, None, None]
+    view_table = lax.all_gather(subset_views[0], "view")
     padded = with_halo(activity, (("slab", 0),), 1)
     blurred = ((1.0 - 2.0 * weight) * activity + weight * (padded[:-2] + padded[2:])).astype(
         jnp.bfloat16
@@ -241,14 +242,22 @@
     half = (planes + 1) // 2
     from_left = lax.ppermute(payload, "view", rightward)
     from_right = lax.ppermute(payload, "view", leftward)
+    me = lax.axis_index("view")
+    payload, view_table = lax.optimization_barrier((payload, view_table))
+    kernel_left = kernels(view_table[lax.rem(me + view_count - 1, view_count)], bins, length)
+    kernel_right = kernels(view_table[lax.rem(me + 1, view_count)], bins, length)
+    kernel_far = kernels(view_table[lax.rem(me + 2, view_count)], bins, length)
     total = back_project(payload, tof_kernel)
-    total, from_left, from_right = lax.optimization_barrier((total, from_left, from_right))
+    total, from_left, from_right, kernel_left, kernel_right, kernel_far = lax.optimization_barrier(
+        (total, from_left, from_right, kernel_left, kernel_right, kernel_far)
+    )
     far_low = lax.ppermute(from_left[:half], "view", rightward)
     far_high = lax.ppermute(from_right[half:], "view", leftward)
-    total = total + back_project(from_left, kernel_of(from_left))
-    total = total + back_project(from_right, kernel_of(from_right))
+    total = total + back_project(from_left, kernel_left)
+    total = total + back_project(from_right, kernel_right)
+    total, far_low, far_high = lax.optimization_barrier((total, far_low, far_high))
     far = jnp.concatenate([far_low, far_high], axis=0)
-    total = total + back_project(far, kernel_of(far))
+    total = total + back_project(far, kernel_far)
     edges = with_halo(weight * total, (("slab", 0),), 1)
     smoothed = (1.0 - 2.0 * weight) * total + edges[:-2] + edges[2:]
     return activity * smoothed / sensitivity

time: 141 us -> 143 us (1.014); the launches traced: 141 us -> 140 us
  waiting for transfers between devices: 39 us -> 24.5 us
  other arithmetic: 13.1 us -> 18.5 us
  blocking collectives: 0 us -> 4.96 us
  matrix products: 27.8 us -> 23 us
  starting transfers between devices: 16.4 us -> 20.8 us
  local copies, waits for them, and re-layouts: 6.42 us -> 10.8 us
    ppermute x1, waiting for transfers between devices: 10.9 us -> 2.22 us  [on_device(): far_high = lax.ppermute(from_right[half:], 'view', leftward)]
    ppermute x1, waiting for transfers between devices: 20.2 us -> 13.7 us  [on_device(): from_left = lax.ppermute(payload, 'view', rightward)]
    ppermute x2, waiting for transfers between devices: 6.46 us -> 0.01 us  [with_halo(): after = lax.ppermute(leading, axis, down)]
    ppermute x2, starting transfers between devices: 3.84 us -> 9.26 us  [with_halo(): after = lax.ppermute(leading, axis, down)]
    all_gather x0 -> x1, blocking collectives: none -> 4.96 us  [on_device(): view_table = lax.all_gather(subset_views[0], 'view')]
    dot_general x4, matrix products: 14.4 us -> 9.61 us  [back_project(): jnp.einsum('zlat,atv->zlv', dense, kernel_k, preferred_element_type=jnp.f...]
    convert_element_type x0 -> x2, local copies, waits for them, and re-layouts: none -> 3.72 us  [on_device(): ratios = rows.astype(jnp.float32) / (estimate + BACKGROUND)]
    ppermute x1, waiting for transfers between devices: 0.01 us -> 3.51 us  [on_device(): far_low = lax.ppermute(from_left[:half], 'view', rightward)]
  transfers between devices with their start and end apart: 8 -> 8, of which waited for: 4 -> 5; matrix products, arithmetic and copies ran while one was open for 18% -> 21% of each run, Pallas kernels for 27% -> 26%
where the time goes in v7:
time: 143 us; the launch traced here: 140 us
  Pallas kernels  36.8 us (26%)
  waiting for transfers between devices  24.5 us (17%)
  matrix products  23 us (16%)
  starting transfers between devices  20.8 us (15%)
  other arithmetic  18.5 us (13%)
  local copies, waits for them, and re-layouts  10.8 us (8%)
  blocking collectives  4.96 us (3%)
    pallas_call x1, Pallas kernels, exchange(): pl.pallas_call(exchange_kernel, out_shape=jax.ShapeDtypeStruct(send.shape...  36.8 us
    ppermute x1, waiting for transfers between devices, on_device(): from_left = lax.ppermute(payload, 'view', rightward)  13.7 us
    dot_general x4, matrix products, back_project(): jnp.einsum('zlat,atv->zlv', dense, kernel_k, preferred_element_type=jnp.f...  9.61 us
    ppermute x2, starting transfers between devices, with_halo(): after = lax.ppermute(leading, axis, down)  9.26 us
    dot_general x1, matrix products, on_device(): jnp.einsum('zlv,atv->zalt', blurred, tof_kernel, preferred_element_type=j...  7.33 us
    ppermute x2, starting transfers between devices, with_halo(): before = lax.ppermute(last, axis, up)  7.01 us
    div x1, other arithmetic, on_device(): return activity * smoothed / sensitivity  5.14 us
    all_gather x1, blocking collectives, on_device(): view_table = lax.all_gather(subset_views[0], 'view')  4.96 us
  transfers between devices with their start and end apart: 8, of which 5 were waited for; matrix products, arithmetic and copies ran while one was open for 21% of the time, Pallas kernels for 26%

profile of v7, /device:TPU:31, one launch (start us, length us, event | category | flops | bytes accessed | tf_op | source)
XLA Modules:
  0.0 139.8 jit_solution(10729365002469517606)
XLA Ops:
  0.0 1.6 %fusion.83 = (f32[1,32,1024]{2,1,0:T(8,128)S(1)}, f32[1,32,1024]{2,1,0:T(8,128)}) fusion(f32[32,32,1024]{2,1,0:T(8,128)} %param.14), kind=kLoop, calls=%fused_computation.158 | loop fusion | bytes 524288 | tf_op jit(solution)/shard_map/slice | solution.py:23
  1.6 2.6 %collective-permute-start.1 = (f32[1,32,1024]{2,1,0:T(8,128)}, f32[1,32,1024]{2,1,0:T(8,128)}, u32[]{:S(2)}, u32[]{:S(2)}) collective-permute-start(f32[1,32,1024]{2,1,0:T(8,128)} %get-tuple-element.66), channel_id=1, source_target_pairs={{4,0},{8,4},{12,8},{16,12},{20,16},{24,20},{28,24},{32,28},{36,32}... | collective-permute-start | bytes 393224 | tf_op jit(solution)/shard_map/ppermute | solution.py:26
  4.2 5.1 %collective-permute-start = (f32[1,32,1024]{2,1,0:T(8,128)S(1)}, f32[1,32,1024]{2,1,0:T(8,128)}, u32[]{:S(2)}, u32[]{:S(2)}) collective-permute-start(f32[1,32,1024]{2,1,0:T(8,128)S(1)} %get-tuple-element.65), channel_id=1, source_target_pairs={{0,4},{4,8},{8,12},{12,16},{16,20},{20,24},{24,28},{28,32},{32,36}... | collective-permute-start | bytes 393224 | tf_op jit(solution)/shard_map/ppermute | solution.py:25
  9.3 0.7 compare_reduce_fusion.2
  10.0 0.7 compare_reduce_fusion.1
  10.7 0.7 compare_reduce_fusion
  11.4 0.7 fusion.73
  12.0 0.7 multiply_bitcast_fusion.3
  12.8 1.3 copy.49
  14.0 0.7 fusion.63
  14.7 0.1 reduce_window_sum.11
  14.8 0.8 select_reduce_fusion
  15.7 0.7 multiply_add_fusion.4
  16.3 0.7 convert_bitcast_fusion.5
  17.1 0.4 convolution_convert_fusion
  17.5 1.2 reshape.645.send
  18.8 36.8 %shard_map.82 = bf16[64,2,4224]{2,1,0:T(2,128)(2,1)} custom-call(bf16[64,2,4224]{2,1,0:T(2,128)(2,1)} %reshape.645.send), custom_call_target="tpu_custom_call" | custom-call | tf_op jit(solution)/shard_map/pallas_call | solution.py:148
  55.6 1.5 %reshape.646 = bf16[128,4224]{1,0:T(8,128)(2,1)S(1)} reshape(bf16[64,2,4224]{2,1,0:T(2,128)(2,1)} %shard_map.82) | data formatting | bytes 2162688 | tf_op jit(solution)/shard_map/reshape | solution.py:198
  57.0 0.2 slice_convert_fusion
  57.3 0.1 convert_reduce_fusion
  57.4 0.1 fusion.58
  57.5 0.2 fusion.60
  57.6 0.6 fusion.59
  58.3 0.6 fusion.71
  59.0 0.1 fusion.61
  59.1 0.4 scatter.11
  59.5 0.7 slice_select_fusion
  60.3 5.0 %all-gather = s32[4,1,8]{2,1,0:T(1,128)S(1)} all-gather(s32[1,1,8]{2,1,0:T(1,128)S(1)} %bitcast.99), channel_id=1, replica_groups=mesh['slab'=64,'view'=4] {'view'}, dimensions={0}, use_global_device_ids=true | all-gather | bytes 160 | tf_op jit(solution)/shard_map/all_gather | solution.py:166
  65.3 1.8 %copy.25 = f32[128,4096]{0,1:T(8,128)} copy(f32[128,4096]{1,0:T(8,128)S(1)} %slice_convert_fusion) | data formatting | bytes 4194304 | tf_op jit(solution)/shard_map/convert_element_type | solution.py:204
  67.1 1.9 %copy.26 = f32[128,32,128]{2,0,1:T(8,128)S(1)} copy(f32[128,32,128]{0,2,1:T(8,128)} %bitcast.92) | data formatting | bytes 4194304 | tf_op jit(solution)/shard_map/convert_element_type | solution.py:204
  69.0 0.4 scatter.14
  69.4 7.3 %convolution_bitcast_fusion.1 = f32[32,8,32,128]{3,2,0,1:T(8,128)S(1)} fusion(f32[1,32,1024]{2,1,0:T(8,128)} %collective-permute-done.1, f32[32,32,1024]{2,1,0:T(8,128)} %param.14, f32[1,32,1024]{2,1,0:T(8,128)} %collective-permute-done, f32[32]{0:T(128)S(1)} %copy-done.2, f32[8,128]{1,0:T(8,128)S(1)} %multiply_add_fusion.3, f32[1024]{0:T(1024)S(1)} %iota_add_fusion, ...), kind=kOutput, calls=%fused_computation.37 | convolution fusion | flops 2161115136 | bytes 8659200 | tf_op jit(solution)/shard_map/zlv,atv->zalt/dot_general | solution.py:177
  76.8 0.4 copy.27
  77.2 1.9 %fusion.41 = f32[32,128,128]{2,1,0:T(8,128)S(1)} fusion(f32[32,256,128]{2,1,0:T(8,128)S(1)} %bitcast.91, f32[128,256]{1,0:T(8,128)S(1)} %fusion.58), kind=kOutput, calls=%fused_computation.58 | convolution fusion | flops 805306368 | bytes 6422528 | tf_op jit(solution)/shard_map/zjp,zpt->zjt/dot_general | solution.py:203
  79.1 1.0 fusion.44
  80.2 0.1 pad_maximum_fusion.4
  80.3 3.0 %collective-permute-start.2 = (bf16[33,128,128]{2,1,0:T(8,128)(2,1)S(1)}, bf16[33,128,128]{2,1,0:T(8,128)(2,1)S(1)}, u32[]{:S(2)}, u32[]{:S(2)}) collective-permute-start(bf16[33,128,128]{2,1,0:T(8,128)(2,1)S(1)} %pad_maximum_fusion.4), channel_id=1, source_target_pairs={{0,1},{1,2},{2,3},{3,0},{4,5},{5,6},{6,7},{7,4},{8,9},{9,10},{10,1... | collective-permute-start | bytes 3244040 | tf_op jit(solution)/shard_map/ppermute | solution.py:243
  83.2 0.1 convert_reduce_fusion.4
  83.3 0.1 compare_convert_fusion.3
  83.4 0.7 convert_bitcast_fusion.3
  84.1 0.1 multiply_bitcast_fusion
  84.3 0.1 multiply_add_fusion
  84.3 2.5 %convolution_bitcast_fusion = f32[32,32,1024]{2,1,0:T(8,128)S(1)} fusion(bf16[32,32,8,128]{3,2,1,0:T(8,128)(2,1)S(1)} %convert_bitcast_fusion.3, f32[8,128]{1,0:T(8,128)S(1)} %multiply_add_fusion.3, f32[1024]{0:T(1024)S(1)} %iota_add_fusion), kind=kOutput, calls=%fused_computation.36 | convolution fusion | flops 2153775104 | bytes 6299648 | tf_op jit(solution)/shard_map/zlat,atv->zlv/dot_general | solution.py:232
  86.9 3.2 %fusion.15 = (bf16[8,128,1024]{2,1,0:T(8,128)(2,1)S(1)}, bf16[8,128,1024]{2,1,0:T(8,128)(2,1)S(1)}, bf16[8,128,1024]{2,1,0:T(8,128)(2,1)S(1)}) fusion(f32[8,128]{1,0:T(8,128)S(1)} %get-tuple-element.78, f32[1024]{0:T(1024)S(1)} %iota_add_fusion, f32[8,128]{1,0:T(8,128)S(1)} %get-tuple-element.79, f32[8,128]{1,0:T(8,128)S(1)} %get-tuple-element.80), kind=kLoop, calls=%fused_computation.20 | loop fusion | flops 18874368 | bytes 6307840 | tf_op jit(solution)/shard_map/convert_element_type | solution.py:45
  90.1 13.7 %collective-permute-done.2 = bf16[33,128,128]{2,1,0:T(8,128)(2,1)S(1)} collective-permute-done((bf16[33,128,128]{2,1,0:T(8,128)(2,1)S(1)}, bf16[33,128,128]{2,1,0:T(8,128)(2,1)S(1)}, u32[]{:S(2)}, u32[]{:S(2)}) %collective-permute-start.2) | collective-permute-done | bytes 1081376 | tf_op jit(solution)/shard_map/ppermute | solution.py:243
  103.8 3.1 %collective-permute-done.3 = bf16[33,128,128]{2,1,0:T(8,128)(2,1)S(1)} collective-permute-done((bf16[33,128,128]{2,1,0:T(8,128)(2,1)S(1)}, bf16[33,128,128]{2,1,0:T(8,128)(2,1)S(1)}, u32[]{:S(2)}, u32[]{:S(2)}) %collective-permute-start.3) | collective-permute-done | bytes 1081376 | tf_op jit(solution)/shard_map/ppermute | solution.py:244
  107.0 0.1 convert_reduce_fusion.2
  107.2 0.1 compare_convert_fusion.1
  107.3 0.7 convert_bitcast_fusion.2
  108.0 0.7 convert_bitcast_fusion.1
  108.7 0.4 collective-permute-start.4
  109.1 1.2 collective-permute-start.5
  110.2 2.3 %fusion.28 = f32[32,32,1024,1]{2,1,3,0:T(8,128)S(1)} fusion(bf16[8,128,1024]{2,1,0:T(8,128)(2,1)S(1)} %get-tuple-element.56, bf16[32,32,8,128]{3,2,1,0:T(8,128)(2,1)S(1)} %convert_bitcast_fusion.2), kind=kOutput, calls=%fused_computation.42 | convolution fusion | flops 2147483648 | bytes 8388608 | tf_op jit(solution)/shard_map/zlat,atv->zlv/dot_general | solution.py:232
  112.6 2.4 %bitcast_add_fusion.1 = f32[32,32,1024]{2,1,0:T(8,128)S(1)} fusion(f32[32,32,1024]{2,1,0:T(8,128)S(1)} %convolution_bitcast_fusion, f32[32,32,1024,1]{2,1,3,0:T(8,128)S(1)} %fusion.28, bf16[8,128,1024]{2,1,0:T(8,128)(2,1)S(1)} %get-tuple-element.58, bf16[32,32,8,128]{3,2,1,0:T(8,128)(2,1)S(1)} %convert_bitcast_fusion.1), kind=kOutput, calls=%fused_computation.34 | convolution fusion | flops 2149580800 | bytes 16777216 | tf_op jit(solution)/shard_map/zlat,atv->zlv/dot_general | solution.py:232
  115.0 3.5 %collective-permute-done.4 = bf16[16,128,128]{2,1,0:T(8,128)(2,1)S(1)} collective-permute-done((bf16[16,128,128]{2,1,0:T(8,128)(2,1)S(1)}, bf16[16,128,128]{2,1,0:T(8,128)(2,1)S(1)}, u32[]{:S(2)}, u32[]{:S(2)}) %collective-permute-start.4) | collective-permute-done | bytes 524320 | tf_op jit(solution)/shard_map/ppermute | solution.py:254
  118.5 2.2 %collective-permute-done.5 = bf16[17,128,128]{2,1,0:T(8,128)(2,1)S(1)} collective-permute-done((bf16[17,128,128]{2,1,0:T(8,128)(2,1)S(1)}, bf16[17,128,128]{2,1,0:T(8,128)(2,1)S(1)}, u32[]{:S(2)}, u32[]{:S(2)}) %collective-permute-start.5) | collective-permute-done | bytes 557088 | tf_op jit(solution)/shard_map/ppermute | solution.py:255
  120.7 0.1 convert_reduce_fusion.1
  120.8 0.1 compare_convert_fusion
  120.9 0.7 convert_bitcast_fusion
  121.7 2.4 %broadcast_multiply_fusion = (f32[32,32,1024]{2,1,0:T(8,128)S(1)}, f32[32,32,1024,1]{2,1,3,0:T(8,128)S(1)}) fusion(f32[32]{0:T(128)S(1)} %copy-done.2, f32[32,32,1024]{2,1,0:T(8,128)S(1)} %bitcast_add_fusion.1, bf16[8,128,1024]{2,1,0:T(8,128)(2,1)S(1)} %get-tuple-element.62, bf16[32,32,8,128]{3,2,1,0:T(8,128)(2,1)S(1)} %convert_bitcast_fusion), kind=kOutput, calls=%fused_computation.57 | convolution fusion | flops 2149580800 | bytes 16777344 | tf_op jit(solution)/shard_map/zlat,atv->zlv/dot_general | solution.py:232
  124.1 6.7 %collective-permute-start.7 = (f32[1,32,1024]{2,1,0:T(8,128)S(1)}, f32[1,32,1024]{2,1,0:T(8,128)S(1)}, u32[]{:S(2)}, u32[]{:S(2)}) collective-permute-start(f32[1,32,1024]{2,1,0:T(8,128)S(1)} %get-tuple-element.64), channel_id=1, source_target_pairs={{4,0},{8,4},{12,8},{16,12},{20,16},{24,20},{28,24},{32,28},{36,32}... | collective-permute-start | bytes 393224 | tf_op jit(solution)/shard_map/ppermute | solution.py:26
  130.8 1.9 %collective-permute-start.6 = (f32[1,32,1024]{2,1,0:T(8,128)S(1)}, f32[1,32,1024]{2,1,0:T(8,128)S(1)}, u32[]{:S(2)}, u32[]{:S(2)}) collective-permute-start(f32[1,32,1024]{2,1,0:T(8,128)S(1)} %get-tuple-element.63), channel_id=1, source_target_pairs={{0,4},{4,8},{8,12},{12,16},{16,20},{20,24},{24,28},{28,32},{32,36}... | collective-permute-start | bytes 393224 | tf_op jit(solution)/shard_map/ppermute | solution.py:25
  132.7 1.9 %collective-permute-done.6 = f32[1,32,1024]{2,1,0:T(8,128)S(1)} collective-permute-done((f32[1,32,1024]{2,1,0:T(8,128)S(1)}, f32[1,32,1024]{2,1,0:T(8,128)S(1)}, u32[]{:S(2)}, u32[]{:S(2)}) %collective-permute-start.6) | collective-permute-done | bytes 131104 | tf_op jit(solution)/shard_map/ppermute | solution.py:25
  134.6 5.1 %fusion.18 = f32[32,32,1024]{2,1,0:T(8,128)} fusion(f32[32,32,1024]{2,1,0:T(8,128)S(1)} %copy-done.1, f32[32,32,1024]{2,1,0:T(8,128)S(1)} %copy-done, f32[1,32,1024]{2,1,0:T(8,128)S(1)} %collective-permute-done.7, f32[32,32,1024]{2,1,0:T(8,128)S(1)} %get-tuple-element.83, f32[1,32,1024]{2,1,0:T(8,128)S(1)} %collective-permute-done.6, ...), kind=kLoop, calls=%fused_computation.24 | loop fusion | flops 8388608 | bytes 25428096 | tf_op jit(solution)/shard_map/div | solution.py:263
  (24 shorter events, 0.3 us)
Async XLA Ops:
  1.6 67.8 %collective-permute-start.1 = (f32[1,32,1024]{2,1,0:T(8,128)}, f32[1,32,1024]{2,1,0:T(8,128)}, u32[]{:S(2)}, u32[]{:S(2)}) collective-permute-start(f32[1,32,1024]{2,1,0:T(8,128)} %get-tuple-element.66), channel_id=1, source_target_pairs={{4,0},{8,4},{12,8},{16,12},{20,16},{24,20},{28,24},{32,28},{36,32}... | collective-permute-start | bytes 393224 | tf_op jit(solution)/shard_map/ppermute | solution.py:26
  4.2 65.2 %collective-permute-start = (f32[1,32,1024]{2,1,0:T(8,128)S(1)}, f32[1,32,1024]{2,1,0:T(8,128)}, u32[]{:S(2)}, u32[]{:S(2)}) collective-permute-start(f32[1,32,1024]{2,1,0:T(8,128)S(1)} %get-tuple-element.65), channel_id=1, source_target_pairs={{0,4},{4,8},{8,12},{12,16},{16,20},{20,24},{24,28},{28,32},{32,36}... | collective-permute-start | bytes 393224 | tf_op jit(solution)/shard_map/ppermute | solution.py:25
  18.8 39.5 %copy-start.3 = (s32[1,8]{1,0:T(1,128)S(1)}, s32[1,8]{1,0:T(1,128)}, u32[]{:S(2)}) copy-start(s32[1,8]{1,0:T(1,128)} %param.21) | copy-start | bytes 100
  18.8 40.2 %copy-start.2 = (f32[32]{0:T(128)S(1)}, f32[32]{0:T(128)}, u32[]{:S(2)}) copy-start(f32[32]{0:T(128)} %param.16) | copy-start | bytes 388
  80.3 23.6 %collective-permute-start.2 = (bf16[33,128,128]{2,1,0:T(8,128)(2,1)S(1)}, bf16[33,128,128]{2,1,0:T(8,128)(2,1)S(1)}, u32[]{:S(2)}, u32[]{:S(2)}) collective-permute-start(bf16[33,128,128]{2,1,0:T(8,128)(2,1)S(1)} %pad_maximum_fusion.4), channel_id=1, source_target_pairs={{0,1},{1,2},{2,3},{3,0},{4,5},{5,6},{6,7},{7,4},{8,9},{9,10},{10,1... | collective-permute-start | bytes 3244040 | tf_op jit(solution)/shard_map/ppermute | solution.py:243
  83.2 23.8 %collective-permute-start.3 = (bf16[33,128,128]{2,1,0:T(8,128)(2,1)S(1)}, bf16[33,128,128]{2,1,0:T(8,128)(2,1)S(1)}, u32[]{:S(2)}, u32[]{:S(2)}) collective-permute-start(bf16[33,128,128]{2,1,0:T(8,128)(2,1)S(1)} %pad_maximum_fusion.4), channel_id=1, source_target_pairs={{0,3},{1,0},{2,1},{3,2},{4,7},{5,4},{6,5},{7,6},{8,11},{9,8},{10,9... | collective-permute-start | bytes 3244040 | tf_op jit(solution)/shard_map/ppermute | solution.py:244
  108.7 9.8 %collective-permute-start.4 = (bf16[16,128,128]{2,1,0:T(8,128)(2,1)S(1)}, bf16[16,128,128]{2,1,0:T(8,128)(2,1)S(1)}, u32[]{:S(2)}, u32[]{:S(2)}) collective-permute-start(bf16[16,128,128]{2,1,0:T(8,128)(2,1)S(1)} %slice.127), channel_id=1, source_target_pairs={{0,1},{1,2},{2,3},{3,0},{4,5},{5,6},{6,7},{7,4},{8,9},{9,10},{10,1... | collective-permute-start | bytes 1572872 | tf_op jit(solution)/shard_map/ppermute | solution.py:254
  109.1 11.6 %collective-permute-start.5 = (bf16[17,128,128]{2,1,0:T(8,128)(2,1)S(1)}, bf16[17,128,128]{2,1,0:T(8,128)(2,1)S(1)}, u32[]{:S(2)}, u32[]{:S(2)}) collective-permute-start(bf16[17,128,128]{2,1,0:T(8,128)(2,1)S(1)} %slice.128), channel_id=1, source_target_pairs={{0,3},{1,0},{2,1},{3,2},{4,7},{5,4},{6,5},{7,6},{8,11},{9,8},{10,9... | collective-permute-start | bytes 1671176 | tf_op jit(solution)/shard_map/ppermute | solution.py:255
  121.6 13.0 %copy-start = (f32[32,32,1024]{2,1,0:T(8,128)S(1)}, f32[32,32,1024]{2,1,0:T(8,128)}, u32[]{:S(2)}) copy-start(f32[32,32,1024]{2,1,0:T(8,128)} %param.14) | copy-start | bytes 12582916
  121.6 13.0 %copy-start.1 = (f32[32,32,1024]{2,1,0:T(8,128)S(1)}, f32[32,32,1024]{2,1,0:T(8,128)}, u32[]{:S(2)}) copy-start(f32[32,32,1024]{2,1,0:T(8,128)} %param.15) | copy-start | bytes 12582916
  124.1 8.6 %collective-permute-start.7 = (f32[1,32,1024]{2,1,0:T(8,128)S(1)}, f32[1,32,1024]{2,1,0:T(8,128)S(1)}, u32[]{:S(2)}, u32[]{:S(2)}) collective-permute-start(f32[1,32,1024]{2,1,0:T(8,128)S(1)} %get-tuple-element.64), channel_id=1, source_target_pairs={{4,0},{8,4},{12,8},{16,12},{20,16},{24,20},{28,24},{32,28},{36,32}... | collective-permute-start | bytes 393224 | tf_op jit(solution)/shard_map/ppermute | solution.py:26
  130.8 3.9 %collective-permute-start.6 = (f32[1,32,1024]{2,1,0:T(8,128)S(1)}, f32[1,32,1024]{2,1,0:T(8,128)S(1)}, u32[]{:S(2)}, u32[]{:S(2)}) collective-permute-start(f32[1,32,1024]{2,1,0:T(8,128)S(1)} %get-tuple-element.63), channel_id=1, source_target_pairs={{0,4},{4,8},{8,12},{12,16},{16,20},{20,24},{24,28},{28,32},{32,36}... | collective-permute-start | bytes 393224 | tf_op jit(solution)/shard_map/ppermute | solution.py:25

commit v8 on v6

--- a/solution.py
+++ b/solution.py
@@ -247,6 +247,7 @@
     far_high = lax.ppermute(from_right[half:], "view", leftward)
     total = total + back_project(from_left, kernel_of(from_left))
     total = total + back_project(from_right, kernel_of(from_right))
+    total, far_low, far_high = lax.optimization_barrier((total, far_low, far_high))
     far = jnp.concatenate([far_low, far_high], axis=0)
     total = total + back_project(far, kernel_of(far))
     edges = with_halo(weight * total, (("slab", 0),), 1)

time: 141 us -> 135 us (0.957)
  waiting for transfers between devices: 39 us -> 31.5 us
  matrix products: 27.8 us -> 23.6 us
  other arithmetic: 13.1 us -> 17 us
  starting transfers between devices: 16.4 us -> 17.9 us
    ppermute x1, waiting for transfers between devices: 20.2 us -> 0.01 us  [on_device(): from_left = lax.ppermute(payload, 'view', rightward)]
    ppermute x1, waiting for transfers between devices: 1.48 us -> 20.2 us  [on_device(): from_right = lax.ppermute(payload, 'view', leftward)]
    ppermute x1, waiting for transfers between devices: 10.9 us -> 3.67 us  [on_device(): far_high = lax.ppermute(from_right[half:], 'view', leftward)]
    dot_general x4, matrix products: 14.4 us -> 10.2 us  [back_project(): jnp.einsum('zlat,atv->zlv', dense, kernel_k, preferred_element_type=jnp.f...]
    ppermute x1, starting transfers between devices: 0.08 us -> 2.21 us  [on_device(): from_left = lax.ppermute(payload, 'view', rightward)]
    add x0 -> x1, other arithmetic: none -> 1.95 us  [on_device(): total = total + back_project(from_right, kernel_of(from_right))]
  transfers between devices with their start and end apart: 8 -> 8, of which waited for: 4 -> 4; matrix products, arithmetic and copies ran while one was open for 18% -> 19% of each run, Pallas kernels for 27% -> 28%
where the time goes in v8:
time: 135 us
  Pallas kernels  37.9 us (28%)
  waiting for transfers between devices  31.5 us (23%)
  matrix products  23.6 us (17%)
  starting transfers between devices  17.9 us (13%)
  other arithmetic  17 us (13%)
  local copies, waits for them, and re-layouts  6.41 us (5%)
    pallas_call x1, Pallas kernels, exchange(): pl.pallas_call(exchange_kernel, out_shape=jax.ShapeDtypeStruct(send.shape...  37.9 us
    ppermute x1, waiting for transfers between devices, on_device(): from_right = lax.ppermute(payload, 'view', leftward)  20.2 us
    dot_general x4, matrix products, back_project(): jnp.einsum('zlat,atv->zlv', dense, kernel_k, preferred_element_type=jnp.f...  10.2 us
    ppermute x2, starting transfers between devices, with_halo(): before = lax.ppermute(last, axis, up)  8.83 us
    dot_general x1, matrix products, on_device(): jnp.einsum('zlv,atv->zalt', blurred, tof_kernel, preferred_element_type=j...  7.21 us
    ppermute x2, waiting for transfers between devices, with_halo(): after = lax.ppermute(leading, axis, down)  6.46 us
    div x1, other arithmetic, on_device(): return activity * smoothed / sensitivity  4.79 us
    another operation x6, other arithmetic  3.92 us
  transfers between devices with their start and end apart: 8, of which 4 were waited for; matrix products, arithmetic and copies ran while one was open for 19% of the time, Pallas kernels for 28%

profile of v8, /device:TPU:31, one launch (start us, length us, event | category | flops | bytes accessed | tf_op | source)
XLA Modules:
  0.0 134.7 jit_solution(8382278750621241186)
XLA Ops:
  0.0 1.0 fusion.106
  1.0 4.0 %collective-permute-start = (f32[1,32,1024]{2,1,0:T(8,128)S(1)}, f32[1,32,1024]{2,1,0:T(8,128)S(1)}, u32[]{:S(2)}, u32[]{:S(2)}) collective-permute-start(f32[1,32,1024]{2,1,0:T(8,128)S(1)} %get-tuple-element.61), channel_id=1, source_target_pairs={{0,4},{4,8},{8,12},{12,16},{16,20},{20,24},{24,28},{28,32},{32,36}... | collective-permute-start | bytes 393224 | tf_op jit(solution)/shard_map/ppermute | solution.py:25
  5.0 1.9 %collective-permute-start.1 = (f32[1,32,1024]{2,1,0:T(8,128)S(1)}, f32[1,32,1024]{2,1,0:T(8,128)S(1)}, u32[]{:S(2)}, u32[]{:S(2)}) collective-permute-start(f32[1,32,1024]{2,1,0:T(8,128)S(1)} %get-tuple-element.62), channel_id=1, source_target_pairs={{4,0},{8,4},{12,8},{16,12},{20,16},{24,20},{28,24},{32,28},{36,32}... | collective-permute-start | bytes 393224 | tf_op jit(solution)/shard_map/ppermute | solution.py:26
  6.9 0.7 compare_reduce_fusion.2
  7.6 0.6 compare_reduce_fusion.1
  8.2 0.7 compare_reduce_fusion
  8.9 0.7 fusion.90
  9.6 0.7 multiply_bitcast_fusion.6
  10.3 0.7 fusion.83
  11.0 0.1 reduce_window_sum.11
  11.1 0.8 select_reduce_fusion
  12.0 0.7 multiply_add_fusion.4
  12.6 1.3 copy.44
  13.9 0.7 convert_bitcast_fusion.6
  14.6 0.1 broadcast_in_dim.18
  14.7 0.4 convolution_convert_fusion
  15.1 1.2 reshape.591.send
  16.4 37.9 %shard_map.82 = bf16[64,2,4224]{2,1,0:T(2,128)(2,1)} custom-call(bf16[64,2,4224]{2,1,0:T(2,128)(2,1)} %reshape.591.send), custom_call_target="tpu_custom_call" | custom-call | tf_op jit(solution)/shard_map/pallas_call | solution.py:148
  54.3 1.5 %reshape.592 = bf16[128,4224]{1,0:T(8,128)(2,1)S(1)} reshape(bf16[64,2,4224]{2,1,0:T(2,128)(2,1)} %shard_map.82) | data formatting | bytes 2162688 | tf_op jit(solution)/shard_map/reshape | solution.py:197
  55.8 0.1 convert_reduce_fusion
  55.9 0.2 fusion.80
  56.1 0.1 fusion.78
  56.2 0.6 fusion.88
  56.8 0.6 fusion.79
  57.4 0.1 fusion.81
  57.6 0.1 multiply_add_fusion.3
  57.6 0.4 scatter.11
  58.1 0.7 slice_select_fusion
  58.8 0.4 scatter.14
  59.2 0.1 convert_reduce_fusion.4
  59.3 7.2 %convolution_bitcast_fusion.1 = f32[32,8,32,128]{3,2,0,1:T(8,128)S(1)} fusion(f32[1,32,1024]{2,1,0:T(8,128)S(1)} %collective-permute-done.1, f32[32,32,1024]{2,1,0:T(8,128)} %param.14, f32[1,32,1024]{2,1,0:T(8,128)S(1)} %collective-permute-done, f32[32]{0:T(128)S(1)} %copy-done.3, f32[8,128]{1,0:T(8,128)S(1)} %multiply_add_fusion.3, ...), kind=kOutput, calls=%fused_computation.37 | convolution fusion | flops 2161115136 | bytes 8659200 | tf_op jit(solution)/shard_map/zlv,atv->zalt/dot_general | solution.py:176
  66.5 0.4 copy.15
  67.0 1.9 %fusion.60 = f32[32,128,128]{2,1,0:T(8,128)S(1)} fusion(f32[32,256,128]{2,1,0:T(8,128)S(1)} %bitcast.102, f32[128,256]{1,0:T(8,128)S(1)} %fusion.78), kind=kOutput, calls=%fused_computation.74 | convolution fusion | flops 805306368 | bytes 6422528 | tf_op jit(solution)/shard_map/zjp,zpt->zjt/dot_general | solution.py:202
  68.9 1.1 fusion.63
  70.0 0.1 pad_maximum_fusion.4
  70.1 0.5 collective-permute-start.3
  70.6 2.2 %collective-permute-start.2 = (bf16[33,128,128]{2,1,0:T(8,128)(2,1)S(1)}, bf16[33,128,128]{2,1,0:T(8,128)(2,1)S(1)}, u32[]{:S(2)}, u32[]{:S(2)}) collective-permute-start(bf16[33,128,128]{2,1,0:T(8,128)(2,1)S(1)} %pad_maximum_fusion.4), channel_id=1, source_target_pairs={{0,1},{1,2},{2,3},{3,0},{4,5},{5,6},{6,7},{7,4},{8,9},{9,10},{10,1... | collective-permute-start | bytes 3244040 | tf_op jit(solution)/shard_map/ppermute | solution.py:242
  72.8 0.1 compare_convert_fusion.3
  73.0 0.7 convert_bitcast_fusion.4
  73.7 2.5 %convolution_bitcast_fusion = f32[32,32,1024]{2,1,0:T(8,128)S(1)} fusion(bf16[32,32,8,128]{3,2,1,0:T(8,128)(2,1)S(1)} %convert_bitcast_fusion.4, f32[8,128]{1,0:T(8,128)S(1)} %multiply_add_fusion.3, f32[1024]{0:T(1024)S(1)} %iota_add_fusion), kind=kOutput, calls=%fused_computation.36 | convolution fusion | flops 2153775104 | bytes 6299648 | tf_op jit(solution)/shard_map/zlat,atv->zlv/dot_general | solution.py:231
  76.2 20.2 %collective-permute-done.3 = bf16[33,128,128]{2,1,0:T(8,128)(2,1)S(1)} collective-permute-done((bf16[33,128,128]{2,1,0:T(8,128)(2,1)S(1)}, bf16[33,128,128]{2,1,0:T(8,128)(2,1)S(1)}, u32[]{:S(2)}, u32[]{:S(2)}) %collective-permute-start.3) | collective-permute-done | bytes 1081376 | tf_op jit(solution)/shard_map/ppermute | solution.py:243
  96.4 0.1 convert_reduce_fusion.2
  96.6 0.1 multiply_bitcast_fusion.1
  96.8 0.1 multiply_bitcast_fusion.2
  97.0 2.4 %collective-permute-start.4 = (bf16[16,128,128]{2,1,0:T(8,128)(2,1)S(1)}, bf16[16,128,128]{2,1,0:T(8,128)(2,1)S(1)}, u32[]{:S(2)}, u32[]{:S(2)}) collective-permute-start(bf16[16,128,128]{2,1,0:T(8,128)(2,1)S(1)} %slice.162), channel_id=1, source_target_pairs={{0,1},{1,2},{2,3},{3,0},{4,5},{5,6},{6,7},{7,4},{8,9},{9,10},{10,1... | collective-permute-start | bytes 1572872 | tf_op jit(solution)/shard_map/ppermute | solution.py:246
  99.4 0.1 compare_convert_fusion.2
  99.5 0.7 convert_bitcast_fusion.2
  100.2 0.7 convert_bitcast_fusion.3
  100.9 0.1 multiply_add_fusion.2
  101.0 2.5 %fusion.27 = f32[32,32,1024,1]{2,1,3,0:T(8,128)S(1)} fusion(bf16[32,32,8,128]{3,2,1,0:T(8,128)(2,1)S(1)} %convert_bitcast_fusion.3, f32[8,128]{1,0:T(8,128)S(1)} %get-tuple-element.65, f32[1024]{0:T(1024)S(1)} %iota_add_fusion), kind=kOutput, calls=%fused_computation.41 | convolution fusion | flops 2153775104 | bytes 6299648 | tf_op jit(solution)/shard_map/zlat,atv->zlv/dot_general | solution.py:231
  103.5 2.5 %fusion.29 = f32[32,32,1024,1]{2,1,3,0:T(8,128)S(1)} fusion(bf16[32,32,8,128]{3,2,1,0:T(8,128)(2,1)S(1)} %convert_bitcast_fusion.2, f32[8,128]{1,0:T(8,128)S(1)} %get-tuple-element.66, f32[1024]{0:T(1024)S(1)} %iota_add_fusion), kind=kOutput, calls=%fused_computation.42 | convolution fusion | flops 2153775104 | bytes 6299648 | tf_op jit(solution)/shard_map/zlat,atv->zlv/dot_general | solution.py:231
  106.1 1.9 %bitcast_add_fusion.1 = f32[32,32,1024]{2,1,0:T(8,128)S(1)} fusion(f32[32,32,1024,1]{2,1,3,0:T(8,128)S(1)} %fusion.29, f32[32,32,1024]{2,1,0:T(8,128)S(1)} %convolution_bitcast_fusion, f32[32,32,1024,1]{2,1,3,0:T(8,128)S(1)} %fusion.27), kind=kLoop, calls=%fused_computation.34 | loop fusion | flops 2097152 | bytes 16777216 | tf_op jit(solution)/shard_map/add | solution.py:249
  108.0 1.2 collective-permute-done.4
  109.2 3.7 %collective-permute-done.5 = bf16[17,128,128]{2,1,0:T(8,128)(2,1)S(1)} collective-permute-done((bf16[17,128,128]{2,1,0:T(8,128)(2,1)S(1)}, bf16[17,128,128]{2,1,0:T(8,128)(2,1)S(1)}, u32[]{:S(2)}, u32[]{:S(2)}) %collective-permute-start.5) | collective-permute-done | bytes 557088 | tf_op jit(solution)/shard_map/ppermute | solution.py:247
  112.9 0.1 convert_reduce_fusion.1
  113.0 0.1 multiply_bitcast_fusion
  113.2 0.1 compare_convert_fusion
  113.3 0.1 multiply_add_fusion
  113.4 0.7 convert_bitcast_fusion.1
  114.1 2.6 %broadcast_multiply_fusion = (f32[32,32,1024]{2,1,0:T(8,128)S(1)}, f32[32,32,1024,1]{2,1,3,0:T(8,128)S(1)}) fusion(f32[32]{0:T(128)S(1)} %copy-done.3, f32[32,32,1024]{2,1,0:T(8,128)S(1)} %bitcast_add_fusion.1, f32[8,128]{1,0:T(8,128)S(1)} %multiply_add_fusion, f32[1024]{0:T(1024)S(1)} %iota_add_fusion, bf16[32,32,8,128]{3,2,1,0:T(8,128)(2,1)S(1)} %convert_bitcast_fusion.1), kind=kOutput, calls=%fused_computation.64 | convolution fusion | flops 2155872256 | bytes 14688384 | tf_op jit(solution)/shard_map/zlat,atv->zlv/dot_general | solution.py:231
  116.7 4.8 %collective-permute-start.6 = (f32[1,32,1024]{2,1,0:T(8,128)S(1)}, f32[1,32,1024]{2,1,0:T(8,128)S(1)}, u32[]{:S(2)}, u32[]{:S(2)}) collective-permute-start(f32[1,32,1024]{2,1,0:T(8,128)S(1)} %get-tuple-element.59), channel_id=1, source_target_pairs={{0,4},{4,8},{8,12},{12,16},{16,20},{20,24},{24,28},{28,32},{32,36}... | collective-permute-start | bytes 393224 | tf_op jit(solution)/shard_map/ppermute | solution.py:25
  121.5 1.9 %collective-permute-start.7 = (f32[1,32,1024]{2,1,0:T(8,128)S(1)}, f32[1,32,1024]{2,1,0:T(8,128)S(1)}, u32[]{:S(2)}, u32[]{:S(2)}) collective-permute-start(f32[1,32,1024]{2,1,0:T(8,128)S(1)} %get-tuple-element.60), channel_id=1, source_target_pairs={{4,0},{8,4},{12,8},{16,12},{20,16},{24,20},{28,24},{32,28},{36,32}... | collective-permute-start | bytes 393224 | tf_op jit(solution)/shard_map/ppermute | solution.py:26
  123.5 6.5 %collective-permute-done.7 = f32[1,32,1024]{2,1,0:T(8,128)S(1)} collective-permute-done((f32[1,32,1024]{2,1,0:T(8,128)S(1)}, f32[1,32,1024]{2,1,0:T(8,128)S(1)}, u32[]{:S(2)}, u32[]{:S(2)}) %collective-permute-start.7) | collective-permute-done | bytes 131104 | tf_op jit(solution)/shard_map/ppermute | solution.py:26
  129.9 4.8 %fusion.18 = f32[32,32,1024]{2,1,0:T(8,128)} fusion(f32[32,32,1024]{2,1,0:T(8,128)S(1)} %copy-done.1, f32[32,32,1024]{2,1,0:T(8,128)S(1)} %copy-done, f32[1,32,1024]{2,1,0:T(8,128)S(1)} %collective-permute-done.7, f32[32,32,1024]{2,1,0:T(8,128)S(1)} %get-tuple-element.69, f32[1,32,1024]{2,1,0:T(8,128)S(1)} %collective-permute-done.6, ...), kind=kLoop, calls=%fused_computation.24 | loop fusion | flops 8388608 | bytes 25428096 | tf_op jit(solution)/shard_map/div | solution.py:255
  (28 shorter events, 0.3 us)
Async XLA Ops:
  1.0 58.3 %collective-permute-start = (f32[1,32,1024]{2,1,0:T(8,128)S(1)}, f32[1,32,1024]{2,1,0:T(8,128)S(1)}, u32[]{:S(2)}, u32[]{:S(2)}) collective-permute-start(f32[1,32,1024]{2,1,0:T(8,128)S(1)} %get-tuple-element.61), channel_id=1, source_target_pairs={{0,4},{4,8},{8,12},{12,16},{16,20},{20,24},{24,28},{28,32},{32,36}... | collective-permute-start | bytes 393224 | tf_op jit(solution)/shard_map/ppermute | solution.py:25
  5.0 54.3 %collective-permute-start.1 = (f32[1,32,1024]{2,1,0:T(8,128)S(1)}, f32[1,32,1024]{2,1,0:T(8,128)S(1)}, u32[]{:S(2)}, u32[]{:S(2)}) collective-permute-start(f32[1,32,1024]{2,1,0:T(8,128)S(1)} %get-tuple-element.62), channel_id=1, source_target_pairs={{4,0},{8,4},{12,8},{16,12},{20,16},{24,20},{28,24},{32,28},{36,32}... | collective-permute-start | bytes 393224 | tf_op jit(solution)/shard_map/ppermute | solution.py:26
  13.9 42.3 %copy-start.2 = (s32[1,8]{1,0:T(1,128)S(1)}, s32[1,8]{1,0:T(1,128)}, u32[]{:S(2)}) copy-start(s32[1,8]{1,0:T(1,128)} %param.21) | copy-start | bytes 100
  13.9 42.8 %copy-start.3 = (f32[32]{0:T(128)S(1)}, f32[32]{0:T(128)}, u32[]{:S(2)}) copy-start(f32[32]{0:T(128)} %param.16) | copy-start | bytes 388
  70.1 26.3 %collective-permute-start.3 = (bf16[33,128,128]{2,1,0:T(8,128)(2,1)S(1)}, bf16[33,128,128]{2,1,0:T(8,128)(2,1)S(1)}, u32[]{:S(2)}, u32[]{:S(2)}) collective-permute-start(bf16[33,128,128]{2,1,0:T(8,128)(2,1)S(1)} %pad_maximum_fusion.4), channel_id=1, source_target_pairs={{0,3},{1,0},{2,1},{3,2},{4,7},{5,4},{6,5},{7,6},{8,11},{9,8},{10,9... | collective-permute-start | bytes 3244040 | tf_op jit(solution)/shard_map/ppermute | solution.py:243
  70.6 25.8 %collective-permute-start.2 = (bf16[33,128,128]{2,1,0:T(8,128)(2,1)S(1)}, bf16[33,128,128]{2,1,0:T(8,128)(2,1)S(1)}, u32[]{:S(2)}, u32[]{:S(2)}) collective-permute-start(bf16[33,128,128]{2,1,0:T(8,128)(2,1)S(1)} %pad_maximum_fusion.4), channel_id=1, source_target_pairs={{0,1},{1,2},{2,3},{3,0},{4,5},{5,6},{6,7},{7,4},{8,9},{9,10},{10,1... | collective-permute-start | bytes 3244040 | tf_op jit(solution)/shard_map/ppermute | solution.py:242
  97.0 12.3 %collective-permute-start.4 = (bf16[16,128,128]{2,1,0:T(8,128)(2,1)S(1)}, bf16[16,128,128]{2,1,0:T(8,128)(2,1)S(1)}, u32[]{:S(2)}, u32[]{:S(2)}) collective-permute-start(bf16[16,128,128]{2,1,0:T(8,128)(2,1)S(1)} %slice.162), channel_id=1, source_target_pairs={{0,1},{1,2},{2,3},{3,0},{4,5},{5,6},{6,7},{7,4},{8,9},{9,10},{10,1... | collective-permute-start | bytes 1572872 | tf_op jit(solution)/shard_map/ppermute | solution.py:246
  99.4 13.5 %collective-permute-start.5 = (bf16[17,128,128]{2,1,0:T(8,128)(2,1)S(1)}, bf16[17,128,128]{2,1,0:T(8,128)(2,1)S(1)}, u32[]{:S(2)}, u32[]{:S(2)}) collective-permute-start(bf16[17,128,128]{2,1,0:T(8,128)(2,1)S(1)} %slice.163), channel_id=1, source_target_pairs={{0,3},{1,0},{2,1},{3,2},{4,7},{5,4},{6,5},{7,6},{8,11},{9,8},{10,9... | collective-permute-start | bytes 1671176 | tf_op jit(solution)/shard_map/ppermute | solution.py:247
  114.1 15.9 %copy-start = (f32[32,32,1024]{2,1,0:T(8,128)S(1)}, f32[32,32,1024]{2,1,0:T(8,128)}, u32[]{:S(2)}) copy-start(f32[32,32,1024]{2,1,0:T(8,128)} %param.14) | copy-start | bytes 12582916
  114.1 15.9 %copy-start.1 = (f32[32,32,1024]{2,1,0:T(8,128)S(1)}, f32[32,32,1024]{2,1,0:T(8,128)}, u32[]{:S(2)}) copy-start(f32[32,32,1024]{2,1,0:T(8,128)} %param.15) | copy-start | bytes 12582916
  116.7 6.8 %collective-permute-start.6 = (f32[1,32,1024]{2,1,0:T(8,128)S(1)}, f32[1,32,1024]{2,1,0:T(8,128)S(1)}, u32[]{:S(2)}, u32[]{:S(2)}) collective-permute-start(f32[1,32,1024]{2,1,0:T(8,128)S(1)} %get-tuple-element.59), channel_id=1, source_target_pairs={{0,4},{4,8},{8,12},{12,16},{16,20},{20,24},{24,28},{28,32},{32,36}... | collective-permute-start | bytes 393224 | tf_op jit(solution)/shard_map/ppermute | solution.py:25
  121.5 8.4 %collective-permute-start.7 = (f32[1,32,1024]{2,1,0:T(8,128)S(1)}, f32[1,32,1024]{2,1,0:T(8,128)S(1)}, u32[]{:S(2)}, u32[]{:S(2)}) collective-permute-start(f32[1,32,1024]{2,1,0:T(8,128)S(1)} %get-tuple-element.60), channel_id=1, source_target_pairs={{4,0},{8,4},{12,8},{16,12},{20,16},{24,20},{28,24},{32,28},{36,32}... | collective-permute-start | bytes 393224 | tf_op jit(solution)/shard_map/ppermute | solution.py:26

commit v9 on v8

--- a/solution.py
+++ b/solution.py
@@ -102,7 +102,7 @@
     )(payload)
 
 
-def exchange_kernel(send, out, local_sem, send_sems, recv_sems):
+def exchange_kernel(send, image, spread, out, projected, local_sem, send_sems, recv_sems):
     count = lax.axis_size("slab")
     me = lax.axis_index("slab")
     view = lax.axis_index("view")
@@ -139,24 +139,39 @@
         return carry
 
     lax.fori_loop(1, count, start, 0)
+
+    tile = 128
+
+    @pl.loop(0, image.shape[0] // tile)
+    def _(step):
+        rows = pl.ds(pl.multiple_of(step * tile, tile), tile)
+        projected[rows, :] = lax.dot_general(
+            image[rows, :], spread[...], (((1,), (1,)), ((), ())),
+            preferred_element_type=jnp.float32,
+        )
+
     lax.fori_loop(1, count, finish, 0)
     local.wait()
 
 
-def exchange(send):
+def exchange(send, image, spread):
     count = send.shape[0]
+    vmem = pl.BlockSpec(memory_space=pltpu.VMEM)
     return pl.pallas_call(
         exchange_kernel,
-        out_shape=jax.ShapeDtypeStruct(send.shape, send.dtype),
-        in_specs=[pl.BlockSpec(memory_space=pl.ANY)],
-        out_specs=pl.BlockSpec(memory_space=pl.ANY),
+        out_shape=(
+            jax.ShapeDtypeStruct(send.shape, send.dtype),
+            jax.ShapeDtypeStruct((image.shape[0], spread.shape[0]), jnp.float32),
+        ),
+        in_specs=[pl.BlockSpec(memory_space=pl.ANY), vmem, vmem],
+        out_specs=(pl.BlockSpec(memory_space=pl.ANY), vmem),
         scratch_shapes=[
             pltpu.SemaphoreType.DMA(()),
             pltpu.SemaphoreType.DMA((count,)),
             pltpu.SemaphoreType.DMA((count,)),
         ],
         compiler_params=pltpu.CompilerParams(collective_id=1, has_side_effects=True),
-    )(send)
+    )(send, image, spread)
 
 
 def on_device(
@@ -173,8 +188,6 @@
     tof_kernel = kernels(subset_views[0], bins, length)
     angle_count = tof_kernel.shape[0]
     pairs = angle_count * lines_here
-    projected = jnp.einsum("zlv,atv->zalt", blurred, tof_kernel, preferred_element_type=jnp.float32)
-    projected = projected.reshape(planes, pairs, bins)
 
     slab_count = lax.axis_size("slab")
     block_total = measured.shape[1]
@@ -189,12 +202,18 @@
     place = (jnp.arange(slots, dtype=jnp.int32)[:, None] == flat_slot[None, :]).astype(
         jnp.bfloat16
     )
-    pair_id = block_angle[0] * lines_here + block_line[0]
+    pair_id = block_line[0] * angle_count + block_angle[0]
     extra = 128
     tag = jnp.broadcast_to(pair_id.astype(jnp.bfloat16)[:, None], (block_total, extra))
     outgoing = jnp.concatenate([measured[0].reshape(block_total, row), tag], axis=1)
     send = jnp.dot(place, outgoing, preferred_element_type=jnp.float32).astype(jnp.bfloat16)
-    recv = exchange(send.reshape(slab_count, capacity, row + extra)).reshape(slots, row + extra)
+    recv, projected = exchange(
+        send.reshape(slab_count, capacity, row + extra),
+        blurred.reshape(planes * lines_here, length),
+        tof_kernel.reshape(pairs // lines_here * bins, length),
+    )
+    recv = recv.reshape(slots, row + extra)
+    projected = projected.reshape(planes, pairs, bins)
     index = recv[:, row].astype(jnp.int32)
     rows = recv[:, :row].reshape(slots, planes, bins).transpose(1, 0, 2)
     pick = (index[:, None] == jnp.arange(pairs, dtype=jnp.int32)[None, :]).astype(jnp.float32)
@@ -221,8 +240,7 @@
     def back_project(got, kernel_k):
         index_k = got[planes, :, 0].astype(jnp.int32)
         order = jnp.arange(pairs, dtype=jnp.int32)
-        wanted = (order % angle_count) * lines_here + order // angle_count
-        scatter = (wanted[:, None] == index_k[None, :]).astype(jnp.bfloat16)
+        scatter = (order[:, None] == index_k[None, :]).astype(jnp.bfloat16)
         scatter = jnp.broadcast_to(scatter[None], (planes, pairs, slots))
         dense = jnp.einsum(
             "zpi,zit->zpt", scatter, got[:planes], preferred_element_type=jnp.float32

time: 135 us -> 149 us (1.10)
  other arithmetic: 17 us -> 26.9 us
  matrix products: 23.6 us -> 18.7 us
  local copies, waits for them, and re-layouts: 6.41 us -> 10.9 us
  Pallas kernels: 37.9 us -> 42 us
    convert_element_type x3 -> x6, other arithmetic: 0.3 us -> 9.39 us  [the longest x1 6.88 us: on_device(): ((1.0 - 2.0 * weight) * activity + weight * (padded[:-2] + padded[2:])).a...]
    dot_general x1 -> x0, matrix products: 7.21 us -> none  [on_device(): jnp.einsum('zlv,atv->zalt', blurred, tof_kernel, preferred_element_type=j...]
    reshape x1 -> x2, local copies, waits for them, and re-layouts: 1.48 us -> 6.37 us  [the longest x1 4.89 us: on_device(): projected = projected.reshape(planes, pairs, bins)]
    pallas_call x1, Pallas kernels: 37.9 us -> 42 us  [exchange(): pl.pallas_call(exchange_kernel, out_shape=(jax.ShapeDtypeStruct(send.shap...]
    dot_general x1, matrix products: 1.86 us -> 4.15 us  [on_device(): jnp.einsum('zjp,zpt->zjt', pick, projected, precision=lax.Precision.HIGH)]
  transfers between devices with their start and end apart: 8 -> 8, of which waited for: 4 -> 4; matrix products, arithmetic and copies ran while one was open for 19% -> 17% of each run, Pallas kernels for 28% -> 0%
where the time goes in v9:
time: 149 us; the launch traced here: 148 us
  Pallas kernels  42 us (28%)
  waiting for transfers between devices  31.6 us (21%)
  other arithmetic  26.9 us (18%)
  matrix products  18.7 us (13%)
  starting transfers between devices  17.8 us (12%)
  local copies, waits for them, and re-layouts  10.9 us (7%)
    pallas_call x1, Pallas kernels, exchange(): pl.pallas_call(exchange_kernel, out_shape=(jax.ShapeDtypeStruct(send.shap...  42 us
    ppermute x1, waiting for transfers between devices, on_device(): from_right = lax.ppermute(payload, 'view', leftward)  20.2 us
    dot_general x4, matrix products, back_project(): jnp.einsum('zlat,atv->zlv', dense, kernel_k, preferred_element_type=jnp.f...  10.2 us
    ppermute x2, starting transfers between devices, with_halo(): before = lax.ppermute(last, axis, up)  8.8 us
    convert_element_type x1, other arithmetic, on_device(): ((1.0 - 2.0 * weight) * activity + weight * (padded[:-2] + padded[2:])).a...  6.88 us
    ppermute x2, waiting for transfers between devices, with_halo(): after = lax.ppermute(leading, axis, down)  6.46 us
    reshape x1, local copies, waits for them, and re-layouts, on_device(): projected = projected.reshape(planes, pairs, bins)  4.89 us
    div x1, other arithmetic, on_device(): return activity * smoothed / sensitivity  4.79 us
  transfers between devices with their start and end apart: 8, of which 4 were waited for; matrix products, arithmetic and copies ran while one was open for 17% of the time, Pallas kernels for 0%

profile of v9, /device:TPU:31, one launch (start us, length us, event | category | flops | bytes accessed | tf_op | source)
XLA Modules:
  0.0 148.3 jit_solution(14717682979207219001)
XLA Ops:
  0.0 1.0 fusion.106
  1.0 4.0 %collective-permute-start = (f32[1,32,1024]{2,1,0:T(8,128)S(1)}, f32[1,32,1024]{2,1,0:T(8,128)S(1)}, u32[]{:S(2)}, u32[]{:S(2)}) collective-permute-start(f32[1,32,1024]{2,1,0:T(8,128)S(1)} %get-tuple-element.65), channel_id=1, source_target_pairs={{0,4},{4,8},{8,12},{12,16},{16,20},{20,24},{24,28},{28,32},{32,36}... | collective-permute-start | bytes 393224 | tf_op jit(solution)/shard_map/ppermute | solution.py:25
  5.0 1.9 %collective-permute-start.1 = (f32[1,32,1024]{2,1,0:T(8,128)S(1)}, f32[1,32,1024]{2,1,0:T(8,128)S(1)}, u32[]{:S(2)}, u32[]{:S(2)}) collective-permute-start(f32[1,32,1024]{2,1,0:T(8,128)S(1)} %get-tuple-element.66), channel_id=1, source_target_pairs={{4,0},{8,4},{12,8},{16,12},{20,16},{24,20},{28,24},{32,28},{36,32}... | collective-permute-start | bytes 393224 | tf_op jit(solution)/shard_map/ppermute | solution.py:26
  7.0 0.7 compare_reduce_fusion.2
  7.7 0.6 compare_reduce_fusion.1
  8.3 0.6 compare_reduce_fusion
  8.9 0.7 fusion.93
  9.6 0.7 multiply_bitcast_fusion.6
  10.3 1.3 fusion.91
  11.6 0.1 multiply_add_fusion.3
  11.7 0.1 bitcast_add_fusion.3
  11.8 0.7 fusion.90
  12.5 0.1 reduce_window_sum.11
  12.6 0.8 select_reduce_fusion
  13.4 0.7 multiply_add_fusion.4
  14.1 1.3 copy.42
  15.3 0.7 convert_bitcast_fusion.6
  16.0 0.1 broadcast_in_dim.18
  16.1 0.4 convolution_convert_fusion
  16.5 1.3 reshape.549.send
  17.8 2.4 %fusion.3.spread = bf16[1024,1024]{1,0:T(8,128)(2,1)} fusion(f32[1024]{0:T(1024)S(1)} %get-tuple-element.73, f32[1024]{0:T(1024)S(1)} %get-tuple-element.74), kind=kLoop, calls=%fused_computation.9 | loop fusion | flops 6291456 | bytes 2105344 | tf_op jit(solution)/shard_map/convert_element_type | solution.py:45
  20.2 6.9 %fusion.27 = bf16[32,32,1024]{2,1,0:T(8,128)(2,1)} fusion(f32[1,32,1024]{2,1,0:T(8,128)S(1)} %collective-permute-done.1, f32[32,32,1024]{2,1,0:T(8,128)} %param.14, f32[1,32,1024]{2,1,0:T(8,128)S(1)} %collective-permute-done, f32[32]{0:T(128)S(1)} %copy-done.2, f32[32]{0:T(128)S(1)} %multiply_subtract_fusion), kind=kLoop, calls=%fused_computation.36 | loop fusion | flops 7340032 | bytes 6553856 | tf_op jit(solution)/shard_map/convert_element_type | solution.py:182
  27.1 42.0 %shard_map.82 = (bf16[64,2,4224]{2,1,0:T(2,128)(2,1)}, f32[1024,1024]{1,0:T(8,128)}) custom-call(bf16[64,2,4224]{2,1,0:T(2,128)(2,1)} %reshape.549.send, bf16[1024,1024]{1,0:T(8,128)(2,1)} %bitcast.100, bf16[1024,1024]{1,0:T(8,128)(2,1)} %fusion.3.spread), custom_call_target="tpu_custom_call" | custom-call | tf_op jit(solution)/shard_map/pallas_call | solution.py:160
  69.1 1.5 %reshape.551 = bf16[128,4224]{1,0:T(8,128)(2,1)S(1)} reshape(bf16[64,2,4224]{2,1,0:T(2,128)(2,1)} %get-tuple-element.49) | data formatting | bytes 2162688 | tf_op jit(solution)/shard_map/reshape | solution.py:215
  70.6 0.1 convert_reduce_fusion
  70.7 0.2 fusion.87
  70.9 0.1 fusion.82
  71.0 0.7 fusion.86
  71.7 0.1 fusion.88
  71.8 4.9 %reshape.553 = f32[32,256,128]{2,1,0:T(8,128)} reshape(f32[1024,1024]{1,0:T(8,128)} %get-tuple-element.50) | data formatting | bytes 8388608 | tf_op jit(solution)/shard_map/reshape | solution.py:216
  76.7 0.4 scatter.11
  77.1 0.6 slice_select_fusion
  77.8 0.4 scatter.14
  78.2 4.2 %fusion.64 = f32[32,128,128]{2,1,0:T(8,128)S(1)} fusion(f32[32,256,128]{2,1,0:T(8,128)} %reshape.553, f32[128,256]{1,0:T(8,128)S(1)} %fusion.82), kind=kOutput, calls=%fused_computation.79 | convolution fusion | flops 805306368 | bytes 6422528 | tf_op jit(solution)/shard_map/zjp,zpt->zjt/dot_general | solution.py:221
  82.3 1.1 fusion.66
  83.5 0.1 pad_maximum_fusion.4
  83.6 0.5 collective-permute-start.3
  84.1 2.2 %collective-permute-start.2 = (bf16[33,128,128]{2,1,0:T(8,128)(2,1)S(1)}, bf16[33,128,128]{2,1,0:T(8,128)(2,1)S(1)}, u32[]{:S(2)}, u32[]{:S(2)}) collective-permute-start(bf16[33,128,128]{2,1,0:T(8,128)(2,1)S(1)} %pad_maximum_fusion.4), channel_id=1, source_target_pairs={{0,1},{1,2},{2,3},{3,0},{4,5},{5,6},{6,7},{7,4},{8,9},{9,10},{10,1... | collective-permute-start | bytes 3244040 | tf_op jit(solution)/shard_map/ppermute | solution.py:260
  86.3 0.1 convert_reduce_fusion.4
  86.5 0.7 convert_bitcast_fusion.4
  87.2 2.5 %convolution_bitcast_fusion = f32[32,32,1024]{2,1,0:T(8,128)S(1)} fusion(bf16[32,32,8,128]{3,2,1,0:T(8,128)(2,1)S(1)} %convert_bitcast_fusion.4, f32[8,128]{1,0:T(8,128)S(1)} %multiply_add_fusion.3, f32[1024]{0:T(1024)S(1)} %get-tuple-element.74), kind=kOutput, calls=%fused_computation.41 | convolution fusion | flops 2153775104 | bytes 6299648 | tf_op jit(solution)/shard_map/zlat,atv->zlv/dot_general | solution.py:249
  89.7 20.2 %collective-permute-done.3 = bf16[33,128,128]{2,1,0:T(8,128)(2,1)S(1)} collective-permute-done((bf16[33,128,128]{2,1,0:T(8,128)(2,1)S(1)}, bf16[33,128,128]{2,1,0:T(8,128)(2,1)S(1)}, u32[]{:S(2)}, u32[]{:S(2)}) %collective-permute-start.3) | collective-permute-done | bytes 1081376 | tf_op jit(solution)/shard_map/ppermute | solution.py:261
  109.9 0.1 convert_reduce_fusion.3
  110.0 0.1 convert_reduce_fusion.2
  110.2 0.1 multiply_bitcast_fusion.1
  110.4 0.1 multiply_bitcast_fusion.2
  110.6 2.4 %collective-permute-start.4 = (bf16[16,128,128]{2,1,0:T(8,128)(2,1)S(1)}, bf16[16,128,128]{2,1,0:T(8,128)(2,1)S(1)}, u32[]{:S(2)}, u32[]{:S(2)}) collective-permute-start(bf16[16,128,128]{2,1,0:T(8,128)(2,1)S(1)} %slice.162), channel_id=1, source_target_pairs={{0,1},{1,2},{2,3},{3,0},{4,5},{5,6},{6,7},{7,4},{8,9},{9,10},{10,1... | collective-permute-start | bytes 1572872 | tf_op jit(solution)/shard_map/ppermute | solution.py:264
  113.1 0.7 convert_bitcast_fusion.2
  113.8 0.7 convert_bitcast_fusion.3
  114.5 0.1 multiply_add_fusion.2
  114.5 2.5 %fusion.33 = f32[32,32,1024,1]{2,1,3,0:T(8,128)S(1)} fusion(bf16[32,32,8,128]{3,2,1,0:T(8,128)(2,1)S(1)} %convert_bitcast_fusion.3, f32[8,128]{1,0:T(8,128)S(1)} %get-tuple-element.67, f32[1024]{0:T(1024)S(1)} %get-tuple-element.74), kind=kOutput, calls=%fused_computation.46 | convolution fusion | flops 2153775104 | bytes 6299648 | tf_op jit(solution)/shard_map/zlat,atv->zlv/dot_general | solution.py:249
  117.1 2.5 %fusion.35 = f32[32,32,1024,1]{2,1,3,0:T(8,128)S(1)} fusion(bf16[32,32,8,128]{3,2,1,0:T(8,128)(2,1)S(1)} %convert_bitcast_fusion.2, f32[8,128]{1,0:T(8,128)S(1)} %get-tuple-element.68, f32[1024]{0:T(1024)S(1)} %get-tuple-element.74), kind=kOutput, calls=%fused_computation.47 | convolution fusion | flops 2153775104 | bytes 6299648 | tf_op jit(solution)/shard_map/zlat,atv->zlv/dot_general | solution.py:249
  119.6 1.9 %bitcast_add_fusion.1 = f32[32,32,1024]{2,1,0:T(8,128)S(1)} fusion(f32[32,32,1024,1]{2,1,3,0:T(8,128)S(1)} %fusion.35, f32[32,32,1024]{2,1,0:T(8,128)S(1)} %convolution_bitcast_fusion, f32[32,32,1024,1]{2,1,3,0:T(8,128)S(1)} %fusion.33), kind=kLoop, calls=%fused_computation.39 | loop fusion | flops 2097152 | bytes 16777216 | tf_op jit(solution)/shard_map/add | solution.py:267
  121.6 1.3 collective-permute-done.4
  122.9 3.7 %collective-permute-done.5 = bf16[17,128,128]{2,1,0:T(8,128)(2,1)S(1)} collective-permute-done((bf16[17,128,128]{2,1,0:T(8,128)(2,1)S(1)}, bf16[17,128,128]{2,1,0:T(8,128)(2,1)S(1)}, u32[]{:S(2)}, u32[]{:S(2)}) %collective-permute-start.5) | collective-permute-done | bytes 557088 | tf_op jit(solution)/shard_map/ppermute | solution.py:265
  126.6 0.1 convert_reduce_fusion.1
  126.7 0.1 multiply_bitcast_fusion
  126.9 0.1 multiply_add_fusion
  126.9 0.7 convert_bitcast_fusion.1
  127.7 2.6 %broadcast_multiply_fusion = (f32[32,32,1024]{2,1,0:T(8,128)S(1)}, f32[32,32,1024,1]{2,1,3,0:T(8,128)S(1)}) fusion(f32[32]{0:T(128)S(1)} %copy-done.2, f32[32,32,1024]{2,1,0:T(8,128)S(1)} %bitcast_add_fusion.1, f32[8,128]{1,0:T(8,128)S(1)} %multiply_add_fusion, f32[1024]{0:T(1024)S(1)} %get-tuple-element.74, ...), kind=kOutput, calls=%fused_computation.81 | convolution fusion | flops 2155872256 | bytes 14688384 | tf_op jit(solution)/shard_map/zlat,atv->zlv/dot_general | solution.py:249
  130.3 4.8 %collective-permute-start.6 = (f32[1,32,1024]{2,1,0:T(8,128)S(1)}, f32[1,32,1024]{2,1,0:T(8,128)S(1)}, u32[]{:S(2)}, u32[]{:S(2)}) collective-permute-start(f32[1,32,1024]{2,1,0:T(8,128)S(1)} %get-tuple-element.63), channel_id=1, source_target_pairs={{0,4},{4,8},{8,12},{12,16},{16,20},{20,24},{24,28},{28,32},{32,36}... | collective-permute-start | bytes 393224 | tf_op jit(solution)/shard_map/ppermute | solution.py:25
  135.1 1.9 %collective-permute-start.7 = (f32[1,32,1024]{2,1,0:T(8,128)S(1)}, f32[1,32,1024]{2,1,0:T(8,128)S(1)}, u32[]{:S(2)}, u32[]{:S(2)}) collective-permute-start(f32[1,32,1024]{2,1,0:T(8,128)S(1)} %get-tuple-element.64), channel_id=1, source_target_pairs={{4,0},{8,4},{12,8},{16,12},{20,16},{24,20},{28,24},{32,28},{36,32}... | collective-permute-start | bytes 393224 | tf_op jit(solution)/shard_map/ppermute | solution.py:26
  137.0 6.5 %collective-permute-done.7 = f32[1,32,1024]{2,1,0:T(8,128)S(1)} collective-permute-done((f32[1,32,1024]{2,1,0:T(8,128)S(1)}, f32[1,32,1024]{2,1,0:T(8,128)S(1)}, u32[]{:S(2)}, u32[]{:S(2)}) %collective-permute-start.7) | collective-permute-done | bytes 131104 | tf_op jit(solution)/shard_map/ppermute | solution.py:26
  143.5 4.8 %fusion.22 = f32[32,32,1024]{2,1,0:T(8,128)} fusion(f32[32,32,1024]{2,1,0:T(8,128)S(1)} %copy-done.1, f32[32,32,1024]{2,1,0:T(8,128)S(1)} %copy-done, f32[1,32,1024]{2,1,0:T(8,128)S(1)} %collective-permute-done.7, f32[32,32,1024]{2,1,0:T(8,128)S(1)} %get-tuple-element.71, f32[1,32,1024]{2,1,0:T(8,128)S(1)} %collective-permute-done.6, ...), kind=kLoop, calls=%fused_computation.29 | loop fusion | flops 8388608 | bytes 25428096 | tf_op jit(solution)/shard_map/div | solution.py:273
  (30 shorter events, 0.4 us)
Async XLA Ops:
  0.0 20.2 %copy-start.2 = (f32[32]{0:T(128)S(1)}, f32[32]{0:T(128)}, u32[]{:S(2)}) copy-start(f32[32]{0:T(128)} %param.16) | copy-start | bytes 388
  1.0 19.2 %collective-permute-start = (f32[1,32,1024]{2,1,0:T(8,128)S(1)}, f32[1,32,1024]{2,1,0:T(8,128)S(1)}, u32[]{:S(2)}, u32[]{:S(2)}) collective-permute-start(f32[1,32,1024]{2,1,0:T(8,128)S(1)} %get-tuple-element.65), channel_id=1, source_target_pairs={{0,4},{4,8},{8,12},{12,16},{16,20},{20,24},{24,28},{28,32},{32,36}... | collective-permute-start | bytes 393224 | tf_op jit(solution)/shard_map/ppermute | solution.py:25
  5.0 15.2 %collective-permute-start.1 = (f32[1,32,1024]{2,1,0:T(8,128)S(1)}, f32[1,32,1024]{2,1,0:T(8,128)S(1)}, u32[]{:S(2)}, u32[]{:S(2)}) collective-permute-start(f32[1,32,1024]{2,1,0:T(8,128)S(1)} %get-tuple-element.66), channel_id=1, source_target_pairs={{4,0},{8,4},{12,8},{16,12},{20,16},{24,20},{28,24},{32,28},{36,32}... | collective-permute-start | bytes 393224 | tf_op jit(solution)/shard_map/ppermute | solution.py:26
  83.6 26.3 %collective-permute-start.3 = (bf16[33,128,128]{2,1,0:T(8,128)(2,1)S(1)}, bf16[33,128,128]{2,1,0:T(8,128)(2,1)S(1)}, u32[]{:S(2)}, u32[]{:S(2)}) collective-permute-start(bf16[33,128,128]{2,1,0:T(8,128)(2,1)S(1)} %pad_maximum_fusion.4), channel_id=1, source_target_pairs={{0,3},{1,0},{2,1},{3,2},{4,7},{5,4},{6,5},{7,6},{8,11},{9,8},{10,9... | collective-permute-start | bytes 3244040 | tf_op jit(solution)/shard_map/ppermute | solution.py:261
  84.1 25.8 %collective-permute-start.2 = (bf16[33,128,128]{2,1,0:T(8,128)(2,1)S(1)}, bf16[33,128,128]{2,1,0:T(8,128)(2,1)S(1)}, u32[]{:S(2)}, u32[]{:S(2)}) collective-permute-start(bf16[33,128,128]{2,1,0:T(8,128)(2,1)S(1)} %pad_maximum_fusion.4), channel_id=1, source_target_pairs={{0,1},{1,2},{2,3},{3,0},{4,5},{5,6},{6,7},{7,4},{8,9},{9,10},{10,1... | collective-permute-start | bytes 3244040 | tf_op jit(solution)/shard_map/ppermute | solution.py:260
  110.6 12.2 %collective-permute-start.4 = (bf16[16,128,128]{2,1,0:T(8,128)(2,1)S(1)}, bf16[16,128,128]{2,1,0:T(8,128)(2,1)S(1)}, u32[]{:S(2)}, u32[]{:S(2)}) collective-permute-start(bf16[16,128,128]{2,1,0:T(8,128)(2,1)S(1)} %slice.162), channel_id=1, source_target_pairs={{0,1},{1,2},{2,3},{3,0},{4,5},{5,6},{6,7},{7,4},{8,9},{9,10},{10,1... | collective-permute-start | bytes 1572872 | tf_op jit(solution)/shard_map/ppermute | solution.py:264
  113.1 13.5 %collective-permute-start.5 = (bf16[17,128,128]{2,1,0:T(8,128)(2,1)S(1)}, bf16[17,128,128]{2,1,0:T(8,128)(2,1)S(1)}, u32[]{:S(2)}, u32[]{:S(2)}) collective-permute-start(bf16[17,128,128]{2,1,0:T(8,128)(2,1)S(1)} %slice.163), channel_id=1, source_target_pairs={{0,3},{1,0},{2,1},{3,2},{4,7},{5,4},{6,5},{7,6},{8,11},{9,8},{10,9... | collective-permute-start | bytes 1671176 | tf_op jit(solution)/shard_map/ppermute | solution.py:265
  127.6 15.8 %copy-start = (f32[32,32,1024]{2,1,0:T(8,128)S(1)}, f32[32,32,1024]{2,1,0:T(8,128)}, u32[]{:S(2)}) copy-start(f32[32,32,1024]{2,1,0:T(8,128)} %param.14) | copy-start | bytes 12582916
  127.7 15.8 %copy-start.1 = (f32[32,32,1024]{2,1,0:T(8,128)S(1)}, f32[32,32,1024]{2,1,0:T(8,128)}, u32[]{:S(2)}) copy-start(f32[32,32,1024]{2,1,0:T(8,128)} %param.15) | copy-start | bytes 12582916
  130.3 6.7 %collective-permute-start.6 = (f32[1,32,1024]{2,1,0:T(8,128)S(1)}, f32[1,32,1024]{2,1,0:T(8,128)S(1)}, u32[]{:S(2)}, u32[]{:S(2)}) collective-permute-start(f32[1,32,1024]{2,1,0:T(8,128)S(1)} %get-tuple-element.63), channel_id=1, source_target_pairs={{0,4},{4,8},{8,12},{12,16},{16,20},{20,24},{24,28},{28,32},{32,36}... | collective-permute-start | bytes 393224 | tf_op jit(solution)/shard_map/ppermute | solution.py:25
  135.1 8.4 %collective-permute-start.7 = (f32[1,32,1024]{2,1,0:T(8,128)S(1)}, f32[1,32,1024]{2,1,0:T(8,128)S(1)}, u32[]{:S(2)}, u32[]{:S(2)}) collective-permute-start(f32[1,32,1024]{2,1,0:T(8,128)S(1)} %get-tuple-element.64), channel_id=1, source_target_pairs={{4,0},{8,4},{12,8},{16,12},{20,16},{24,20},{28,24},{32,28},{36,32}... | collective-permute-start | bytes 393224 | tf_op jit(solution)/shard_map/ppermute | solution.py:26

commit v10 on v8

--- a/solution.py
+++ b/solution.py
@@ -194,7 +194,9 @@
     tag = jnp.broadcast_to(pair_id.astype(jnp.bfloat16)[:, None], (block_total, extra))
     outgoing = jnp.concatenate([measured[0].reshape(block_total, row), tag], axis=1)
     send = jnp.dot(place, outgoing, preferred_element_type=jnp.float32).astype(jnp.bfloat16)
-    recv = exchange(send.reshape(slab_count, capacity, row + extra)).reshape(slots, row + extra)
+    recv = lax.all_to_all(
+        send.reshape(slab_count, capacity, row + extra), "slab", 0, 0, tiled=True
+    ).reshape(slots, row + extra)
     index = recv[:, row].astype(jnp.int32)
     rows = recv[:, :row].reshape(slots, planes, bins).transpose(1, 0, 2)
     pick = (index[:, None] == jnp.arange(pairs, dtype=jnp.int32)[None, :]).astype(jnp.float32)

time: 135 us -> 129 us (0.956)
  Pallas kernels: 37.9 us -> 0 us
  starting transfers between devices: 17.9 us -> 36.5 us
  waiting for transfers between devices: 31.5 us -> 42.7 us
  matrix products: 23.6 us -> 25.9 us
    pallas_call x1 -> x0, Pallas kernels: 37.9 us -> none  [exchange(): pl.pallas_call(exchange_kernel, out_shape=jax.ShapeDtypeStruct(send.shape...]
    all_to_all x0 -> x1, waiting for transfers between devices: none -> 15.1 us  [on_device(): lax.all_to_all(send.reshape(slab_count, capacity, row + extra), 'slab', 0...]
    all_to_all x0 -> x1, starting transfers between devices: none -> 12.8 us  [on_device(): lax.all_to_all(send.reshape(slab_count, capacity, row + extra), 'slab', 0...]
    ppermute x2, starting transfers between devices: 8.83 us -> 14.7 us  [with_halo(): before = lax.ppermute(last, axis, up)]
    dot_general x1, matrix products: 1.86 us -> 4.15 us  [on_device(): jnp.einsum('zjp,zpt->zjt', pick, projected, precision=lax.Precision.HIGH)]
    ppermute x1, waiting for transfers between devices: 20.2 us -> 18.2 us  [on_device(): from_right = lax.ppermute(payload, 'view', leftward)]
    transpose x1, local copies, waits for them, and re-layouts: 0.44 us -> 2.45 us  [on_device(): jnp.einsum('zlv,atv->zalt', blurred, tof_kernel, preferred_element_type=j...]
  transfers between devices with their start and end apart: 8 -> 9, of which waited for: 4 -> 4; matrix products, arithmetic and copies ran while one was open for 19% -> 24% of each run, Pallas kernels for 28% -> 0%
where the time goes in v10:
time: 129 us
  waiting for transfers between devices  42.7 us (33%)
  starting transfers between devices  36.5 us (28%)
  matrix products  25.9 us (20%)
  other arithmetic  15.8 us (12%)
  local copies, waits for them, and re-layouts  7.4 us (6%)
    ppermute x1, waiting for transfers between devices, on_device(): from_right = lax.ppermute(payload, 'view', leftward)  18.2 us
    all_to_all x1, waiting for transfers between devices, on_device(): lax.all_to_all(send.reshape(slab_count, capacity, row + extra), 'slab', 0...  15.1 us
    ppermute x2, starting transfers between devices, with_halo(): before = lax.ppermute(last, axis, up)  14.7 us
    all_to_all x1, starting transfers between devices, on_device(): lax.all_to_all(send.reshape(slab_count, capacity, row + extra), 'slab', 0...  12.8 us
    dot_general x4, matrix products, back_project(): jnp.einsum('zlat,atv->zlv', dense, kernel_k, preferred_element_type=jnp.f...  10.2 us
    dot_general x1, matrix products, on_device(): jnp.einsum('zlv,atv->zalt', blurred, tof_kernel, preferred_element_type=j...  7.23 us
    ppermute x2, waiting for transfers between devices, with_halo(): after = lax.ppermute(leading, axis, down)  6.46 us
    div x1, other arithmetic, on_device(): return activity * smoothed / sensitivity  4.79 us
  transfers between devices with their start and end apart: 9, of which 4 were waited for; matrix products, arithmetic and copies ran while one was open for 24% of the time, Pallas kernels for 0%

profile of v10, /device:TPU:31, one launch (start us, length us, event | category | flops | bytes accessed | tf_op | source)
XLA Modules:
  0.0 128.7 jit_solution(15385124016542816814)
XLA Ops:
  0.0 1.0 fusion.106
  1.0 4.0 %collective-permute-start = (f32[1,32,1024]{2,1,0:T(8,128)S(1)}, f32[1,32,1024]{2,1,0:T(8,128)S(1)}, u32[]{:S(2)}, u32[]{:S(2)}) collective-permute-start(f32[1,32,1024]{2,1,0:T(8,128)S(1)} %get-tuple-element.61), channel_id=1, source_target_pairs={{0,4},{4,8},{8,12},{12,16},{16,20},{20,24},{24,28},{28,32},{32,36}... | collective-permute-start | bytes 393224 | tf_op jit(solution)/shard_map/ppermute | solution.py:25
  5.0 1.9 %collective-permute-start.1 = (f32[1,32,1024]{2,1,0:T(8,128)S(1)}, f32[1,32,1024]{2,1,0:T(8,128)S(1)}, u32[]{:S(2)}, u32[]{:S(2)}) collective-permute-start(f32[1,32,1024]{2,1,0:T(8,128)S(1)} %get-tuple-element.62), channel_id=1, source_target_pairs={{4,0},{8,4},{12,8},{16,12},{20,16},{24,20},{28,24},{32,28},{36,32}... | collective-permute-start | bytes 393224 | tf_op jit(solution)/shard_map/ppermute | solution.py:26
  7.0 0.7 fusion.83
  7.7 0.1 reduce_window_sum.11
  7.8 0.8 select_reduce_fusion
  8.6 0.7 multiply_add_fusion.4
  9.3 1.3 copy.44
  10.6 0.7 convert_bitcast_fusion.6
  11.2 0.1 broadcast_in_dim.18
  11.3 0.4 convolution_convert_fusion
  11.8 1.2 reshape.591
  13.0 12.8 %all-to-all-start = ((bf16[64,2,4224]{2,1,0:T(2,128)(2,1)}), bf16[64,2,4224]{2,1,0:T(2,128)(2,1)S(1)}, u32[]{:S(2)}, u32[]{:S(2)}) async-start(bf16[64,2,4224]{2,1,0:T(2,128)(2,1)} %reshape.591), calls=%async_computation | async-start | bytes 2162688 | tf_op jit(solution)/shard_map/all_to_all | solution.py:197
  25.8 0.6 compare_reduce_fusion.1
  26.4 0.7 fusion.88
  27.1 0.1 multiply_bitcast_fusion.6
  27.2 0.1 multiply_add_fusion.3
  27.2 0.7 compare_reduce_fusion.2
  27.9 0.7 compare_reduce_fusion
  28.6 7.2 %convolution_bitcast_fusion.1 = f32[32,8,32,128]{3,2,0,1:T(8,128)S(1)} fusion(f32[1,32,1024]{2,1,0:T(8,128)S(1)} %collective-permute-done.1, f32[32,32,1024]{2,1,0:T(8,128)} %param.14, f32[1,32,1024]{2,1,0:T(8,128)S(1)} %collective-permute-done, f32[32]{0:T(128)S(1)} %copy-done.3, f32[8,128]{1,0:T(8,128)S(1)} %multiply_add_fusion.3, ...), kind=kOutput, calls=%fused_computation.37 | convolution fusion | flops 2161115136 | bytes 8659200 | tf_op jit(solution)/shard_map/zlv,atv->zalt/dot_general | solution.py:176
  35.9 2.5 %copy.15 = f32[32,8,32,128]{3,2,1,0:T(8,128)} copy(f32[32,8,32,128]{3,2,0,1:T(8,128)S(1)} %convolution_bitcast_fusion.1) | data formatting | bytes 8388608 | tf_op jit(solution)/shard_map/zlv,atv->zalt/transpose | solution.py:176
  38.3 15.1 %all-to-all-done = bf16[64,2,4224]{2,1,0:T(2,128)(2,1)S(1)} async-done(((bf16[64,2,4224]{2,1,0:T(2,128)(2,1)}), bf16[64,2,4224]{2,1,0:T(2,128)(2,1)S(1)}, u32[]{:S(2)}, u32[]{:S(2)}) %all-to-all-start) | async-done | bytes 1081376 | tf_op jit(solution)/shard_map/all_to_all | solution.py:197
  53.4 0.4 reshape.592
  53.9 0.1 convert_reduce_fusion
  54.0 0.2 fusion.80
  54.2 0.1 fusion.78
  54.3 0.6 fusion.79
  54.9 0.1 fusion.81
  55.1 0.4 scatter.11
  55.5 0.7 slice_select_fusion
  56.2 0.4 scatter.14
  56.6 4.2 %fusion.60 = f32[32,128,128]{2,1,0:T(8,128)S(1)} fusion(f32[32,256,128]{2,1,0:T(8,128)} %bitcast.102, f32[128,256]{1,0:T(8,128)S(1)} %fusion.78), kind=kOutput, calls=%fused_computation.74 | convolution fusion | flops 805306368 | bytes 6422528 | tf_op jit(solution)/shard_map/zjp,zpt->zjt/dot_general | solution.py:204
  60.8 1.1 fusion.63
  61.9 0.1 pad_maximum_fusion.4
  62.0 0.5 collective-permute-start.3
  62.5 2.2 %collective-permute-start.2 = (bf16[33,128,128]{2,1,0:T(8,128)(2,1)S(1)}, bf16[33,128,128]{2,1,0:T(8,128)(2,1)S(1)}, u32[]{:S(2)}, u32[]{:S(2)}) collective-permute-start(bf16[33,128,128]{2,1,0:T(8,128)(2,1)S(1)} %pad_maximum_fusion.4), channel_id=1, source_target_pairs={{0,1},{1,2},{2,3},{3,0},{4,5},{5,6},{6,7},{7,4},{8,9},{9,10},{10,1... | collective-permute-start | bytes 3244040 | tf_op jit(solution)/shard_map/ppermute | solution.py:244
  64.8 0.1 convert_reduce_fusion.4
  64.9 0.1 compare_convert_fusion.3
  65.0 0.7 convert_bitcast_fusion.4
  65.7 2.5 %convolution_bitcast_fusion = f32[32,32,1024]{2,1,0:T(8,128)S(1)} fusion(bf16[32,32,8,128]{3,2,1,0:T(8,128)(2,1)S(1)} %convert_bitcast_fusion.4, f32[8,128]{1,0:T(8,128)S(1)} %multiply_add_fusion.3, f32[1024]{0:T(1024)S(1)} %iota_add_fusion), kind=kOutput, calls=%fused_computation.36 | convolution fusion | flops 2153775104 | bytes 6299648 | tf_op jit(solution)/shard_map/zlat,atv->zlv/dot_general | solution.py:233
  68.2 18.2 %collective-permute-done.3 = bf16[33,128,128]{2,1,0:T(8,128)(2,1)S(1)} collective-permute-done((bf16[33,128,128]{2,1,0:T(8,128)(2,1)S(1)}, bf16[33,128,128]{2,1,0:T(8,128)(2,1)S(1)}, u32[]{:S(2)}, u32[]{:S(2)}) %collective-permute-start.3) | collective-permute-done | bytes 1081376 | tf_op jit(solution)/shard_map/ppermute | solution.py:245
  86.4 0.1 convert_reduce_fusion.2
  86.6 0.1 multiply_bitcast_fusion.1
  86.8 0.1 multiply_bitcast_fusion.2
  87.0 2.5 %collective-permute-start.4 = (bf16[16,128,128]{2,1,0:T(8,128)(2,1)S(1)}, bf16[16,128,128]{2,1,0:T(8,128)(2,1)S(1)}, u32[]{:S(2)}, u32[]{:S(2)}) collective-permute-start(bf16[16,128,128]{2,1,0:T(8,128)(2,1)S(1)} %slice.162), channel_id=1, source_target_pairs={{0,1},{1,2},{2,3},{3,0},{4,5},{5,6},{6,7},{7,4},{8,9},{9,10},{10,1... | collective-permute-start | bytes 1572872 | tf_op jit(solution)/shard_map/ppermute | solution.py:248
  89.5 0.1 compare_convert_fusion.2
  89.6 0.7 convert_bitcast_fusion.2
  90.3 0.7 convert_bitcast_fusion.3
  91.0 0.1 multiply_add_fusion.2
  91.0 2.5 %fusion.27 = f32[32,32,1024,1]{2,1,3,0:T(8,128)S(1)} fusion(bf16[32,32,8,128]{3,2,1,0:T(8,128)(2,1)S(1)} %convert_bitcast_fusion.3, f32[8,128]{1,0:T(8,128)S(1)} %get-tuple-element.65, f32[1024]{0:T(1024)S(1)} %iota_add_fusion), kind=kOutput, calls=%fused_computation.41 | convolution fusion | flops 2153775104 | bytes 6299648 | tf_op jit(solution)/shard_map/zlat,atv->zlv/dot_general | solution.py:233
  93.6 2.5 %fusion.29 = f32[32,32,1024,1]{2,1,3,0:T(8,128)S(1)} fusion(bf16[32,32,8,128]{3,2,1,0:T(8,128)(2,1)S(1)} %convert_bitcast_fusion.2, f32[8,128]{1,0:T(8,128)S(1)} %get-tuple-element.66, f32[1024]{0:T(1024)S(1)} %iota_add_fusion), kind=kOutput, calls=%fused_computation.42 | convolution fusion | flops 2153775104 | bytes 6299648 | tf_op jit(solution)/shard_map/zlat,atv->zlv/dot_general | solution.py:233
  96.1 1.9 %bitcast_add_fusion.1 = f32[32,32,1024]{2,1,0:T(8,128)S(1)} fusion(f32[32,32,1024,1]{2,1,3,0:T(8,128)S(1)} %fusion.29, f32[32,32,1024]{2,1,0:T(8,128)S(1)} %convolution_bitcast_fusion, f32[32,32,1024,1]{2,1,3,0:T(8,128)S(1)} %fusion.27), kind=kLoop, calls=%fused_computation.34 | loop fusion | flops 2097152 | bytes 16777216 | tf_op jit(solution)/shard_map/add | solution.py:251
  98.1 3.0 %collective-permute-done.5 = bf16[17,128,128]{2,1,0:T(8,128)(2,1)S(1)} collective-permute-done((bf16[17,128,128]{2,1,0:T(8,128)(2,1)S(1)}, bf16[17,128,128]{2,1,0:T(8,128)(2,1)S(1)}, u32[]{:S(2)}, u32[]{:S(2)}) %collective-permute-start.5) | collective-permute-done | bytes 557088 | tf_op jit(solution)/shard_map/ppermute | solution.py:249
  101.1 0.1 convert_reduce_fusion.1
  101.2 0.1 multiply_bitcast_fusion
  101.4 0.1 compare_convert_fusion
  101.5 0.1 multiply_add_fusion
  101.5 0.7 convert_bitcast_fusion.1
  102.2 0.0 copy-start
  102.3 2.6 %broadcast_multiply_fusion = (f32[32,32,1024]{2,1,0:T(8,128)S(1)}, f32[32,32,1024,1]{2,1,3,0:T(8,128)S(1)}) fusion(f32[32]{0:T(128)S(1)} %copy-done.3, f32[32,32,1024]{2,1,0:T(8,128)S(1)} %bitcast_add_fusion.1, f32[8,128]{1,0:T(8,128)S(1)} %multiply_add_fusion, f32[1024]{0:T(1024)S(1)} %iota_add_fusion, bf16[32,32,8,128]{3,2,1,0:T(8,128)(2,1)S(1)} %convert_bitcast_fusion.1), kind=kOutput, calls=%fused_computation.64 | convolution fusion | flops 2155872256 | bytes 14688384 | tf_op jit(solution)/shard_map/zlat,atv->zlv/dot_general | solution.py:233
  104.9 10.6 %collective-permute-start.6 = (f32[1,32,1024]{2,1,0:T(8,128)S(1)}, f32[1,32,1024]{2,1,0:T(8,128)S(1)}, u32[]{:S(2)}, u32[]{:S(2)}) collective-permute-start(f32[1,32,1024]{2,1,0:T(8,128)S(1)} %get-tuple-element.59), channel_id=1, source_target_pairs={{0,4},{4,8},{8,12},{12,16},{16,20},{20,24},{24,28},{28,32},{32,36}... | collective-permute-start | bytes 393224 | tf_op jit(solution)/shard_map/ppermute | solution.py:25
  115.5 1.9 %collective-permute-start.7 = (f32[1,32,1024]{2,1,0:T(8,128)S(1)}, f32[1,32,1024]{2,1,0:T(8,128)S(1)}, u32[]{:S(2)}, u32[]{:S(2)}) collective-permute-start(f32[1,32,1024]{2,1,0:T(8,128)S(1)} %get-tuple-element.60), channel_id=1, source_target_pairs={{4,0},{8,4},{12,8},{16,12},{20,16},{24,20},{28,24},{32,28},{36,32}... | collective-permute-start | bytes 393224 | tf_op jit(solution)/shard_map/ppermute | solution.py:26
  117.5 6.5 %collective-permute-done.7 = f32[1,32,1024]{2,1,0:T(8,128)S(1)} collective-permute-done((f32[1,32,1024]{2,1,0:T(8,128)S(1)}, f32[1,32,1024]{2,1,0:T(8,128)S(1)}, u32[]{:S(2)}, u32[]{:S(2)}) %collective-permute-start.7) | collective-permute-done | bytes 131104 | tf_op jit(solution)/shard_map/ppermute | solution.py:26
  123.9 4.8 %fusion.18 = f32[32,32,1024]{2,1,0:T(8,128)} fusion(f32[32,32,1024]{2,1,0:T(8,128)S(1)} %copy-done.1, f32[32,32,1024]{2,1,0:T(8,128)S(1)} %copy-done, f32[1,32,1024]{2,1,0:T(8,128)S(1)} %collective-permute-done.7, f32[32,32,1024]{2,1,0:T(8,128)S(1)} %get-tuple-element.69, f32[1,32,1024]{2,1,0:T(8,128)S(1)} %collective-permute-done.6, ...), kind=kLoop, calls=%fused_computation.24 | loop fusion | flops 8388608 | bytes 25428096 | tf_op jit(solution)/shard_map/div | solution.py:257
  (29 shorter events, 0.3 us)
Async XLA Ops:
  0.0 26.4 %copy-start.2 = (s32[1,8]{1,0:T(1,128)S(1)}, s32[1,8]{1,0:T(1,128)}, u32[]{:S(2)}) copy-start(s32[1,8]{1,0:T(1,128)} %param.21) | copy-start | bytes 100
  0.0 27.1 %copy-start.3 = (f32[32]{0:T(128)S(1)}, f32[32]{0:T(128)}, u32[]{:S(2)}) copy-start(f32[32]{0:T(128)} %param.16) | copy-start | bytes 388
  1.0 27.6 %collective-permute-start = (f32[1,32,1024]{2,1,0:T(8,128)S(1)}, f32[1,32,1024]{2,1,0:T(8,128)S(1)}, u32[]{:S(2)}, u32[]{:S(2)}) collective-permute-start(f32[1,32,1024]{2,1,0:T(8,128)S(1)} %get-tuple-element.61), channel_id=1, source_target_pairs={{0,4},{4,8},{8,12},{12,16},{16,20},{20,24},{24,28},{28,32},{32,36}... | collective-permute-start | bytes 393224 | tf_op jit(solution)/shard_map/ppermute | solution.py:25
  5.0 23.6 %collective-permute-start.1 = (f32[1,32,1024]{2,1,0:T(8,128)S(1)}, f32[1,32,1024]{2,1,0:T(8,128)S(1)}, u32[]{:S(2)}, u32[]{:S(2)}) collective-permute-start(f32[1,32,1024]{2,1,0:T(8,128)S(1)} %get-tuple-element.62), channel_id=1, source_target_pairs={{4,0},{8,4},{12,8},{16,12},{20,16},{24,20},{28,24},{32,28},{36,32}... | collective-permute-start | bytes 393224 | tf_op jit(solution)/shard_map/ppermute | solution.py:26
  13.0 40.4 %all-to-all-start = ((bf16[64,2,4224]{2,1,0:T(2,128)(2,1)}), bf16[64,2,4224]{2,1,0:T(2,128)(2,1)S(1)}, u32[]{:S(2)}, u32[]{:S(2)}) async-start(bf16[64,2,4224]{2,1,0:T(2,128)(2,1)} %reshape.591), calls=%async_computation | async-start | bytes 2162688 | tf_op jit(solution)/shard_map/all_to_all | solution.py:197
  62.0 24.4 %collective-permute-start.3 = (bf16[33,128,128]{2,1,0:T(8,128)(2,1)S(1)}, bf16[33,128,128]{2,1,0:T(8,128)(2,1)S(1)}, u32[]{:S(2)}, u32[]{:S(2)}) collective-permute-start(bf16[33,128,128]{2,1,0:T(8,128)(2,1)S(1)} %pad_maximum_fusion.4), channel_id=1, source_target_pairs={{0,3},{1,0},{2,1},{3,2},{4,7},{5,4},{6,5},{7,6},{8,11},{9,8},{10,9... | collective-permute-start | bytes 3244040 | tf_op jit(solution)/shard_map/ppermute | solution.py:245
  62.5 23.9 %collective-permute-start.2 = (bf16[33,128,128]{2,1,0:T(8,128)(2,1)S(1)}, bf16[33,128,128]{2,1,0:T(8,128)(2,1)S(1)}, u32[]{:S(2)}, u32[]{:S(2)}) collective-permute-start(bf16[33,128,128]{2,1,0:T(8,128)(2,1)S(1)} %pad_maximum_fusion.4), channel_id=1, source_target_pairs={{0,1},{1,2},{2,3},{3,0},{4,5},{5,6},{6,7},{7,4},{8,9},{9,10},{10,1... | collective-permute-start | bytes 3244040 | tf_op jit(solution)/shard_map/ppermute | solution.py:244
  87.0 11.1 %collective-permute-start.4 = (bf16[16,128,128]{2,1,0:T(8,128)(2,1)S(1)}, bf16[16,128,128]{2,1,0:T(8,128)(2,1)S(1)}, u32[]{:S(2)}, u32[]{:S(2)}) collective-permute-start(bf16[16,128,128]{2,1,0:T(8,128)(2,1)S(1)} %slice.162), channel_id=1, source_target_pairs={{0,1},{1,2},{2,3},{3,0},{4,5},{5,6},{6,7},{7,4},{8,9},{9,10},{10,1... | collective-permute-start | bytes 1572872 | tf_op jit(solution)/shard_map/ppermute | solution.py:248
  89.4 11.6 %collective-permute-start.5 = (bf16[17,128,128]{2,1,0:T(8,128)(2,1)S(1)}, bf16[17,128,128]{2,1,0:T(8,128)(2,1)S(1)}, u32[]{:S(2)}, u32[]{:S(2)}) collective-permute-start(bf16[17,128,128]{2,1,0:T(8,128)(2,1)S(1)} %slice.163), channel_id=1, source_target_pairs={{0,3},{1,0},{2,1},{3,2},{4,7},{5,4},{6,5},{7,6},{8,11},{9,8},{10,9... | collective-permute-start | bytes 1671176 | tf_op jit(solution)/shard_map/ppermute | solution.py:249
  102.2 21.7 %copy-start = (f32[32,32,1024]{2,1,0:T(8,128)S(1)}, f32[32,32,1024]{2,1,0:T(8,128)}, u32[]{:S(2)}) copy-start(f32[32,32,1024]{2,1,0:T(8,128)} %param.14) | copy-start | bytes 12582916
  102.3 21.7 %copy-start.1 = (f32[32,32,1024]{2,1,0:T(8,128)S(1)}, f32[32,32,1024]{2,1,0:T(8,128)}, u32[]{:S(2)}) copy-start(f32[32,32,1024]{2,1,0:T(8,128)} %param.15) | copy-start | bytes 12582916
  104.9 12.6 %collective-permute-start.6 = (f32[1,32,1024]{2,1,0:T(8,128)S(1)}, f32[1,32,1024]{2,1,0:T(8,128)S(1)}, u32[]{:S(2)}, u32[]{:S(2)}) collective-permute-start(f32[1,32,1024]{2,1,0:T(8,128)S(1)} %get-tuple-element.59), channel_id=1, source_target_pairs={{0,4},{4,8},{8,12},{12,16},{16,20},{20,24},{24,28},{28,32},{32,36}... | collective-permute-start | bytes 393224 | tf_op jit(solution)/shard_map/ppermute | solution.py:25
  115.5 8.4 %collective-permute-start.7 = (f32[1,32,1024]{2,1,0:T(8,128)S(1)}, f32[1,32,1024]{2,1,0:T(8,128)S(1)}, u32[]{:S(2)}, u32[]{:S(2)}) collective-permute-start(f32[1,32,1024]{2,1,0:T(8,128)S(1)} %get-tuple-element.60), channel_id=1, source_target_pairs={{4,0},{8,4},{12,8},{16,12},{20,16},{24,20},{28,24},{32,28},{36,32}... | collective-permute-start | bytes 393224 | tf_op jit(solution)/shard_map/ppermute | solution.py:26

commit v11 on v10

--- a/solution.py
+++ b/solution.py
@@ -220,7 +220,7 @@
         (views % 16).astype(jnp.float32)[None, :]
     )
     payload = jnp.concatenate([merged, info.astype(jnp.bfloat16)[None]], axis=0)
-    def back_project(got, kernel_k):
+    def spread_out(got):
         index_k = got[planes, :, 0].astype(jnp.int32)
         order = jnp.arange(pairs, dtype=jnp.int32)
         wanted = (order % angle_count) * lines_here + order // angle_count
@@ -229,8 +229,12 @@
         dense = jnp.einsum(
             "zpi,zit->zpt", scatter, got[:planes], preferred_element_type=jnp.float32
         ).astype(jnp.bfloat16)
-        dense = dense.reshape(planes, lines_here, angle_count, bins)
-        return jnp.einsum("zlat,atv->zlv", dense, kernel_k, preferred_element_type=jnp.float32)
+        return dense.reshape(planes, lines_here, angle_count, bins)
+
+    def back_project(got, kernel_k):
+        return jnp.einsum(
+            "zlat,atv->zlv", spread_out(got), kernel_k, preferred_element_type=jnp.float32
+        )
 
     def kernel_of(got):
         tail = got[planes, 0].astype(jnp.int32)
@@ -251,9 +255,25 @@
     total = total + back_project(from_right, kernel_of(from_right))
     total, far_low, far_high = lax.optimization_barrier((total, far_low, far_high))
     far = jnp.concatenate([far_low, far_high], axis=0)
-    total = total + back_project(far, kernel_of(far))
-    edges = with_halo(weight * total, (("slab", 0),), 1)
-    smoothed = (1.0 - 2.0 * weight) * total + edges[:-2] + edges[2:]
+    kernel_far = kernel_of(far)
+    dense_far = spread_out(far)
+    low, high = (
+        total[plane] + jnp.einsum("lat,atv->lv", dense_far[plane], kernel_far,
+                                  preferred_element_type=jnp.float32)
+        for plane in (0, planes - 1)
+    )
+    size = lax.axis_size("slab")
+    up = [(i, (i + 1) % size) for i in range(size - 1)]
+    down = [(j, i) for i, j in up]
+    from_below = lax.ppermute((weight[planes - 1] * high)[None], "slab", up)
+    from_above = lax.ppermute((weight[0] * low)[None], "slab", down)
+    total = total + jnp.einsum(
+        "zlat,atv->zlv", dense_far, kernel_far, preferred_element_type=jnp.float32
+    )
+    weighted = weight * total
+    below = jnp.concatenate([from_below, weighted[: planes - 1]], axis=0)
+    above = jnp.concatenate([weighted[1:], from_above], axis=0)
+    smoothed = (1.0 - 2.0 * weight) * total + below + above
     return activity * smoothed / sensitivity
 
 

time: 129 us -> 134 us (1.039); the launches traced: 129 us -> 132 us
  waiting for transfers between devices: 42.7 us -> 36.3 us
  matrix products: 25.9 us -> 31.3 us
  local copies, waits for them, and re-layouts: 7.4 us -> 10.8 us
    ppermute x0 -> x2, starting transfers between devices: none -> 12.8 us  [the longest x1 10.6 us: on_device(): from_below = lax.ppermute((weight[planes - 1] * high)[None], 'slab', up)]
    ppermute x2 -> x1, starting transfers between devices: 14.7 us -> 4.02 us  [with_halo(): before = lax.ppermute(last, axis, up)]
    ppermute x2 -> x1, waiting for transfers between devices: 6.46 us -> 0.01 us  [with_halo(): after = lax.ppermute(leading, axis, down)]
    dot_general x8 -> x10, matrix products: 13 us -> 18.4 us  [the longest x3 7.62 us: back_project(): jnp.einsum('zlat,atv->zlv', spread_out(got), kernel_k, preferred_element_...]
    slice x0 -> x2, local copies, waits for them, and re-layouts: none -> 1.95 us  [the longest x1 1.3 us: on_device(): above = jnp.concatenate([weighted[1:], from_above], axis=0)]
    ppermute x2 -> x1, starting transfers between devices: 3.84 us -> 1.92 us  [with_halo(): after = lax.ppermute(leading, axis, down)]
    unnamed x9, local copies, waits for them, and re-layouts: 1.27 us -> 2.71 us
  transfers between devices with their start and end apart: 9 -> 9, of which waited for: 4 -> 4; matrix products, arithmetic and copies ran while one was open for 24% -> 29% of each run, Pallas kernels for 0% -> 0%
where the time goes in v11:
time: 134 us; the launch traced here: 132 us
  starting transfers between devices  36.7 us (27%)
  waiting for transfers between devices  36.3 us (27%)
  matrix products  31.3 us (23%)
  other arithmetic  16.7 us (12%)
  local copies, waits for them, and re-layouts  10.8 us (8%)
    ppermute x1, waiting for transfers between devices, on_device(): from_right = lax.ppermute(payload, 'view', leftward)  18.2 us
    all_to_all x1, waiting for transfers between devices, on_device(): lax.all_to_all(send.reshape(slab_count, capacity, row + extra), 'slab', 0...  14.5 us
    all_to_all x1, starting transfers between devices, on_device(): lax.all_to_all(send.reshape(slab_count, capacity, row + extra), 'slab', 0...  12.8 us
    ppermute x1, starting transfers between devices, on_device(): from_below = lax.ppermute((weight[planes - 1] * high)[None], 'slab', up)  10.6 us
    dot_general x3, matrix products, back_project(): jnp.einsum('zlat,atv->zlv', spread_out(got), kernel_k, preferred_element_...  7.62 us
    dot_general x1, matrix products, on_device(): jnp.einsum('zlv,atv->zalt', blurred, tof_kernel, preferred_element_type=j...  7.21 us
    div x1, other arithmetic, on_device(): return activity * smoothed / sensitivity  5.71 us
    dot_general x1, matrix products, on_device(): jnp.einsum('zlat,atv->zlv', dense_far, kernel_far, preferred_element_type...  4.23 us
  transfers between devices with their start and end apart: 9, of which 4 were waited for; matrix products, arithmetic and copies ran while one was open for 29% of the time, Pallas kernels for 0%

profile of v11, /device:TPU:31, one launch (start us, length us, event | category | flops | bytes accessed | tf_op | source)
XLA Modules:
  0.0 132.2 jit_solution(500385420416602693)
XLA Ops:
  0.0 1.0 fusion.128
  1.0 4.0 %collective-permute-start = (f32[1,32,1024]{2,1,0:T(8,128)S(1)}, f32[1,32,1024]{2,1,0:T(8,128)S(1)}, u32[]{:S(2)}, u32[]{:S(2)}) collective-permute-start(f32[1,32,1024]{2,1,0:T(8,128)S(1)} %get-tuple-element.61), channel_id=1, source_target_pairs={{0,4},{4,8},{8,12},{12,16},{16,20},{20,24},{24,28},{28,32},{32,36}... | collective-permute-start | bytes 393224 | tf_op jit(solution)/shard_map/ppermute | solution.py:25
  5.0 1.9 %collective-permute-start.1 = (f32[1,32,1024]{2,1,0:T(8,128)S(1)}, f32[1,32,1024]{2,1,0:T(8,128)S(1)}, u32[]{:S(2)}, u32[]{:S(2)}) collective-permute-start(f32[1,32,1024]{2,1,0:T(8,128)S(1)} %get-tuple-element.62), channel_id=1, source_target_pairs={{4,0},{8,4},{12,8},{16,12},{20,16},{24,20},{28,24},{32,28},{36,32}... | collective-permute-start | bytes 393224 | tf_op jit(solution)/shard_map/ppermute | solution.py:26
  7.0 0.7 fusion.101
  7.7 0.1 reduce_window_sum.11
  7.8 0.8 select_reduce_fusion
  8.6 0.7 multiply_add_fusion.4
  9.3 1.3 copy.56
  10.6 0.7 convert_bitcast_fusion.5
  11.3 0.4 convolution_convert_fusion
  11.8 1.2 reshape.601
  13.0 12.8 %all-to-all-start = ((bf16[64,2,4224]{2,1,0:T(2,128)(2,1)}), bf16[64,2,4224]{2,1,0:T(2,128)(2,1)S(1)}, u32[]{:S(2)}, u32[]{:S(2)}) async-start(bf16[64,2,4224]{2,1,0:T(2,128)(2,1)} %reshape.601), calls=%async_computation | async-start | bytes 2162688 | tf_op jit(solution)/shard_map/all_to_all | solution.py:197
  25.8 0.6 compare_reduce_fusion.1
  26.4 0.7 fusion.106
  27.3 0.7 compare_reduce_fusion.2
  27.9 0.7 compare_reduce_fusion
  28.6 0.6 fusion.129
  29.3 7.2 %convolution_bitcast_fusion.1 = f32[32,8,32,128]{3,2,0,1:T(8,128)S(1)} fusion(f32[1,32,1024]{2,1,0:T(8,128)S(1)} %collective-permute-done.1, f32[32,32,1024]{2,1,0:T(8,128)} %param.14, f32[1,32,1024]{2,1,0:T(8,128)S(1)} %collective-permute-done, f32[32]{0:T(128)S(1)} %copy-done.2, f32[8,128]{1,0:T(8,128)S(1)} %multiply_add_fusion.3, ...), kind=kOutput, calls=%fused_computation.35 | convolution fusion | flops 2161115136 | bytes 8659200 | tf_op jit(solution)/shard_map/zlv,atv->zalt/dot_general | solution.py:176
  36.5 2.5 %copy.17 = f32[32,8,32,128]{3,2,1,0:T(8,128)} copy(f32[32,8,32,128]{3,2,0,1:T(8,128)S(1)} %convolution_bitcast_fusion.1) | data formatting | bytes 8388608 | tf_op jit(solution)/shard_map/zlv,atv->zalt/transpose | solution.py:176
  39.0 14.5 %all-to-all-done = bf16[64,2,4224]{2,1,0:T(2,128)(2,1)S(1)} async-done(((bf16[64,2,4224]{2,1,0:T(2,128)(2,1)}), bf16[64,2,4224]{2,1,0:T(2,128)(2,1)S(1)}, u32[]{:S(2)}, u32[]{:S(2)}) %all-to-all-start) | async-done | bytes 1081376 | tf_op jit(solution)/shard_map/all_to_all | solution.py:197
  53.4 0.4 reshape.602
  53.9 0.1 convert_reduce_fusion
  54.0 0.2 fusion.98
  54.2 0.1 fusion.86
  54.3 0.6 fusion.87
  54.9 0.1 fusion.99
  55.1 0.4 scatter.11
  55.5 0.7 slice_select_fusion
  56.2 0.4 scatter.14
  56.6 4.2 %fusion.58 = f32[32,128,128]{2,1,0:T(8,128)S(1)} fusion(f32[32,256,128]{2,1,0:T(8,128)} %bitcast.127, f32[128,256]{1,0:T(8,128)S(1)} %fusion.86), kind=kOutput, calls=%fused_computation.68 | convolution fusion | flops 805306368 | bytes 6422528 | tf_op jit(solution)/shard_map/zjp,zpt->zjt/dot_general | solution.py:204
  60.8 1.1 fusion.61
  61.9 0.1 pad_maximum_fusion.2
  62.0 0.5 collective-permute-start.3
  62.5 2.2 %collective-permute-start.2 = (bf16[33,128,128]{2,1,0:T(8,128)(2,1)S(1)}, bf16[33,128,128]{2,1,0:T(8,128)(2,1)S(1)}, u32[]{:S(2)}, u32[]{:S(2)}) collective-permute-start(bf16[33,128,128]{2,1,0:T(8,128)(2,1)S(1)} %pad_maximum_fusion.2), channel_id=1, source_target_pairs={{0,1},{1,2},{2,3},{3,0},{4,5},{5,6},{6,7},{7,4},{8,9},{9,10},{10,1... | collective-permute-start | bytes 3244040 | tf_op jit(solution)/shard_map/ppermute | solution.py:248
  64.8 0.1 convert_reduce_fusion.4
  64.9 0.1 compare_convert_fusion.3
  65.0 0.7 convert_bitcast_fusion.3
  65.7 2.5 %convolution_bitcast_fusion = f32[32,32,1024]{2,1,0:T(8,128)S(1)} fusion(bf16[32,32,8,128]{3,2,1,0:T(8,128)(2,1)S(1)} %convert_bitcast_fusion.3, f32[8,128]{1,0:T(8,128)S(1)} %multiply_add_fusion.3, f32[1024]{0:T(1024)S(1)} %iota_add_fusion), kind=kOutput, calls=%fused_computation.34 | convolution fusion | flops 2153775104 | bytes 6299648 | tf_op jit(solution)/shard_map/zlat,atv->zlv/dot_general | solution.py:235
  68.2 18.2 %collective-permute-done.3 = bf16[33,128,128]{2,1,0:T(8,128)(2,1)S(1)} collective-permute-done((bf16[33,128,128]{2,1,0:T(8,128)(2,1)S(1)}, bf16[33,128,128]{2,1,0:T(8,128)(2,1)S(1)}, u32[]{:S(2)}, u32[]{:S(2)}) %collective-permute-start.3) | collective-permute-done | bytes 1081376 | tf_op jit(solution)/shard_map/ppermute | solution.py:249
  86.4 0.1 convert_reduce_fusion.2
  86.6 0.1 multiply_bitcast_fusion.1
  86.8 0.1 multiply_bitcast_fusion.2
  87.0 2.5 %collective-permute-start.4 = (bf16[16,128,128]{2,1,0:T(8,128)(2,1)S(1)}, bf16[16,128,128]{2,1,0:T(8,128)(2,1)S(1)}, u32[]{:S(2)}, u32[]{:S(2)}) collective-permute-start(bf16[16,128,128]{2,1,0:T(8,128)(2,1)S(1)} %slice.176), channel_id=1, source_target_pairs={{0,1},{1,2},{2,3},{3,0},{4,5},{5,6},{6,7},{7,4},{8,9},{9,10},{10,1... | collective-permute-start | bytes 1572872 | tf_op jit(solution)/shard_map/ppermute | solution.py:252
  89.5 0.1 compare_convert_fusion.2
  89.6 0.7 convert_bitcast_fusion.1
  90.3 0.7 convert_bitcast_fusion.2
  91.0 2.5 %fusion.25 = f32[32,32,1024,1]{2,1,3,0:T(8,128)S(1)} fusion(bf16[32,32,8,128]{3,2,1,0:T(8,128)(2,1)S(1)} %convert_bitcast_fusion.2, f32[8,128]{1,0:T(8,128)S(1)} %get-tuple-element.69, f32[1024]{0:T(1024)S(1)} %iota_add_fusion), kind=kOutput, calls=%fused_computation.38 | convolution fusion | flops 2153775104 | bytes 6299648 | tf_op jit(solution)/shard_map/zlat,atv->zlv/dot_general | solution.py:235
  93.6 2.5 %fusion.27 = f32[32,32,1024,1]{2,1,3,0:T(8,128)S(1)} fusion(bf16[32,32,8,128]{3,2,1,0:T(8,128)(2,1)S(1)} %convert_bitcast_fusion.1, f32[8,128]{1,0:T(8,128)S(1)} %get-tuple-element.70, f32[1024]{0:T(1024)S(1)} %iota_add_fusion), kind=kOutput, calls=%fused_computation.39 | convolution fusion | flops 2153775104 | bytes 6299648 | tf_op jit(solution)/shard_map/zlat,atv->zlv/dot_general | solution.py:235
  96.1 1.9 %bitcast_add_fusion.1 = f32[32,32,1024]{2,1,0:T(8,128)S(1)} fusion(f32[32,32,1024,1]{2,1,3,0:T(8,128)S(1)} %fusion.27, f32[32,32,1024]{2,1,0:T(8,128)S(1)} %convolution_bitcast_fusion, f32[32,32,1024,1]{2,1,3,0:T(8,128)S(1)} %fusion.25), kind=kLoop, calls=%fused_computation.32 | loop fusion | flops 2097152 | bytes 16777216 | tf_op jit(solution)/shard_map/add | solution.py:255
  98.1 3.0 %collective-permute-done.5 = bf16[17,128,128]{2,1,0:T(8,128)(2,1)S(1)} collective-permute-done((bf16[17,128,128]{2,1,0:T(8,128)(2,1)S(1)}, bf16[17,128,128]{2,1,0:T(8,128)(2,1)S(1)}, u32[]{:S(2)}, u32[]{:S(2)}) %collective-permute-start.5) | collective-permute-done | bytes 557088 | tf_op jit(solution)/shard_map/ppermute | solution.py:253
  101.1 0.1 convert_reduce_fusion.1
  101.2 0.1 multiply_bitcast_fusion
  101.4 0.1 compare_convert_fusion
  101.5 0.7 convolution_convert_fusion.1
  102.3 1.9 %fusion.85 = f32[1,32,1024]{2,1,0:T(8,128)S(1)} fusion(f32[32,32,1024]{2,1,0:T(8,128)S(1)} %bitcast_add_fusion.1, f32[8,128]{1,0:T(8,128)S(1)} %multiply_add_fusion, f32[1024]{0:T(1024)S(1)} %iota_add_fusion, bf16[32,8,128]{2,1,0:T(8,128)(2,1)S(1)} %get-tuple-element.64, f32[]{:T(128)} %bitcast.34), kind=kOutput, calls=%fused_computation.95 | convolution fusion | flops 73465856 | bytes 335876 | tf_op jit(solution)/shard_map/lat,atv->lv/dot_general | solution.py:261
  104.2 10.6 %collective-permute-start.6 = (f32[1,32,1024]{2,1,0:T(8,128)S(1)}, f32[1,32,1024]{2,1,0:T(8,128)S(1)}, u32[]{:S(2)}, u32[]{:S(2)}) collective-permute-start(f32[1,32,1024]{2,1,0:T(8,128)S(1)} %fusion.85), channel_id=1, source_target_pairs={{0,4},{4,8},{8,12},{12,16},{16,20},{20,24},{24,28},{28,32},{32,36}... | collective-permute-start | bytes 393224 | tf_op jit(solution)/shard_map/ppermute | solution.py:268
  114.8 1.8 %fusion.83 = f32[1,32,1024]{2,1,0:T(8,128)S(1)} fusion(f32[32,32,1024]{2,1,0:T(8,128)S(1)} %bitcast_add_fusion.1, f32[8,128]{1,0:T(8,128)S(1)} %multiply_add_fusion, f32[1024]{0:T(1024)S(1)} %iota_add_fusion, bf16[32,8,128]{2,1,0:T(8,128)(2,1)S(1)} %get-tuple-element.63, f32[]{:T(128)} %bitcast.39), kind=kOutput, calls=%fused_computation.92 | convolution fusion | flops 73465856 | bytes 335876 | tf_op jit(solution)/shard_map/lat,atv->lv/dot_general | solution.py:261
  116.7 2.1 %collective-permute-start.7 = (f32[1,32,1024]{2,1,0:T(8,128)S(1)}, f32[1,32,1024]{2,1,0:T(8,128)S(1)}, u32[]{:S(2)}, u32[]{:S(2)}) collective-permute-start(f32[1,32,1024]{2,1,0:T(8,128)S(1)} %fusion.83), channel_id=1, source_target_pairs={{4,0},{8,4},{12,8},{16,12},{20,16},{24,20},{28,24},{32,28},{36,32}... | collective-permute-start | bytes 393224 | tf_op jit(solution)/shard_map/ppermute | solution.py:269
  118.8 4.2 %broadcast_multiply_fusion = (f32[32,32,1024]{2,1,0:T(8,128)S(1)}, f32[32,32,1024]{2,1,0:T(8,128)}) fusion(f32[32]{0:T(128)S(1)} %copy-done.2, f32[32,32,1024]{2,1,0:T(8,128)S(1)} %bitcast_add_fusion.1, f32[8,128]{1,0:T(8,128)S(1)} %multiply_add_fusion, f32[1024]{0:T(1024)S(1)} %iota_add_fusion, bf16[32,32,8,128]{3,2,1,0:T(8,128)(2,1)S(1)} %bitcast.132), kind=kOutput, calls=%fused_computation.59 | convolution fusion | flops 2155872256 | bytes 14688384 | tf_op jit(solution)/shard_map/zlat,atv->zlv/dot_general | solution.py:270
  123.1 1.3 fusion.127
  124.4 0.7 collective-permute-done.7
  125.1 0.2 copy-done
  125.2 1.3 copy-done.1
  126.5 5.7 %fusion.22 = f32[32,32,1024]{2,1,0:T(8,128)} fusion(f32[32,32,1024]{2,1,0:T(8,128)S(1)} %copy-done.1, f32[32,32,1024]{2,1,0:T(8,128)S(1)} %copy-done, f32[31,32,1024]{2,1,0:T(8,128)S(1)} %get-tuple-element.60, f32[1,32,1024]{2,1,0:T(8,128)S(1)} %collective-permute-done.6, f32[1,32,1024]{2,1,0:T(8,128)S(1)} %collective-permute-done.7, ...), kind=kLoop, calls=%fused_computation.30 | loop fusion | flops 7340032 | bytes 25165952 | tf_op jit(solution)/shard_map/div | solution.py:277
  (33 shorter events, 0.7 us)
Async XLA Ops:
  0.0 26.4 %copy-start.3 = (s32[1,8]{1,0:T(1,128)S(1)}, s32[1,8]{1,0:T(1,128)}, u32[]{:S(2)}) copy-start(s32[1,8]{1,0:T(1,128)} %param.21) | copy-start | bytes 100
  0.0 27.1 %copy-start.2 = (f32[32]{0:T(128)S(1)}, f32[32]{0:T(128)}, u32[]{:S(2)}) copy-start(f32[32]{0:T(128)} %param.16) | copy-start | bytes 388
  1.0 28.3 %collective-permute-start = (f32[1,32,1024]{2,1,0:T(8,128)S(1)}, f32[1,32,1024]{2,1,0:T(8,128)S(1)}, u32[]{:S(2)}, u32[]{:S(2)}) collective-permute-start(f32[1,32,1024]{2,1,0:T(8,128)S(1)} %get-tuple-element.61), channel_id=1, source_target_pairs={{0,4},{4,8},{8,12},{12,16},{16,20},{20,24},{24,28},{28,32},{32,36}... | collective-permute-start | bytes 393224 | tf_op jit(solution)/shard_map/ppermute | solution.py:25
  5.0 24.2 %collective-permute-start.1 = (f32[1,32,1024]{2,1,0:T(8,128)S(1)}, f32[1,32,1024]{2,1,0:T(8,128)S(1)}, u32[]{:S(2)}, u32[]{:S(2)}) collective-permute-start(f32[1,32,1024]{2,1,0:T(8,128)S(1)} %get-tuple-element.62), channel_id=1, source_target_pairs={{4,0},{8,4},{12,8},{16,12},{20,16},{24,20},{28,24},{32,28},{36,32}... | collective-permute-start | bytes 393224 | tf_op jit(solution)/shard_map/ppermute | solution.py:26
  13.0 40.4 %all-to-all-start = ((bf16[64,2,4224]{2,1,0:T(2,128)(2,1)}), bf16[64,2,4224]{2,1,0:T(2,128)(2,1)S(1)}, u32[]{:S(2)}, u32[]{:S(2)}) async-start(bf16[64,2,4224]{2,1,0:T(2,128)(2,1)} %reshape.601), calls=%async_computation | async-start | bytes 2162688 | tf_op jit(solution)/shard_map/all_to_all | solution.py:197
  62.0 24.4 %collective-permute-start.3 = (bf16[33,128,128]{2,1,0:T(8,128)(2,1)S(1)}, bf16[33,128,128]{2,1,0:T(8,128)(2,1)S(1)}, u32[]{:S(2)}, u32[]{:S(2)}) collective-permute-start(bf16[33,128,128]{2,1,0:T(8,128)(2,1)S(1)} %pad_maximum_fusion.2), channel_id=1, source_target_pairs={{0,3},{1,0},{2,1},{3,2},{4,7},{5,4},{6,5},{7,6},{8,11},{9,8},{10,9... | collective-permute-start | bytes 3244040 | tf_op jit(solution)/shard_map/ppermute | solution.py:249
  62.5 23.9 %collective-permute-start.2 = (bf16[33,128,128]{2,1,0:T(8,128)(2,1)S(1)}, bf16[33,128,128]{2,1,0:T(8,128)(2,1)S(1)}, u32[]{:S(2)}, u32[]{:S(2)}) collective-permute-start(bf16[33,128,128]{2,1,0:T(8,128)(2,1)S(1)} %pad_maximum_fusion.2), channel_id=1, source_target_pairs={{0,1},{1,2},{2,3},{3,0},{4,5},{5,6},{6,7},{7,4},{8,9},{9,10},{10,1... | collective-permute-start | bytes 3244040 | tf_op jit(solution)/shard_map/ppermute | solution.py:248
  87.0 11.1 %collective-permute-start.4 = (bf16[16,128,128]{2,1,0:T(8,128)(2,1)S(1)}, bf16[16,128,128]{2,1,0:T(8,128)(2,1)S(1)}, u32[]{:S(2)}, u32[]{:S(2)}) collective-permute-start(bf16[16,128,128]{2,1,0:T(8,128)(2,1)S(1)} %slice.176), channel_id=1, source_target_pairs={{0,1},{1,2},{2,3},{3,0},{4,5},{5,6},{6,7},{7,4},{8,9},{9,10},{10,1... | collective-permute-start | bytes 1572872 | tf_op jit(solution)/shard_map/ppermute | solution.py:252
  89.4 11.6 %collective-permute-start.5 = (bf16[17,128,128]{2,1,0:T(8,128)(2,1)S(1)}, bf16[17,128,128]{2,1,0:T(8,128)(2,1)S(1)}, u32[]{:S(2)}, u32[]{:S(2)}) collective-permute-start(bf16[17,128,128]{2,1,0:T(8,128)(2,1)S(1)} %slice.177), channel_id=1, source_target_pairs={{0,3},{1,0},{2,1},{3,2},{4,7},{5,4},{6,5},{7,6},{8,11},{9,8},{10,9... | collective-permute-start | bytes 1671176 | tf_op jit(solution)/shard_map/ppermute | solution.py:253
  104.2 20.2 %collective-permute-start.6 = (f32[1,32,1024]{2,1,0:T(8,128)S(1)}, f32[1,32,1024]{2,1,0:T(8,128)S(1)}, u32[]{:S(2)}, u32[]{:S(2)}) collective-permute-start(f32[1,32,1024]{2,1,0:T(8,128)S(1)} %fusion.85), channel_id=1, source_target_pairs={{0,4},{4,8},{8,12},{12,16},{16,20},{20,24},{24,28},{28,32},{32,36}... | collective-permute-start | bytes 393224 | tf_op jit(solution)/shard_map/ppermute | solution.py:268
  116.7 8.4 %collective-permute-start.7 = (f32[1,32,1024]{2,1,0:T(8,128)S(1)}, f32[1,32,1024]{2,1,0:T(8,128)S(1)}, u32[]{:S(2)}, u32[]{:S(2)}) collective-permute-start(f32[1,32,1024]{2,1,0:T(8,128)S(1)} %fusion.83), channel_id=1, source_target_pairs={{4,0},{8,4},{12,8},{16,12},{20,16},{24,20},{28,24},{32,28},{36,32}... | collective-permute-start | bytes 393224 | tf_op jit(solution)/shard_map/ppermute | solution.py:269
  123.0 2.2 %copy-start = (f32[32,32,1024]{2,1,0:T(8,128)S(1)}, f32[32,32,1024]{2,1,0:T(8,128)}, u32[]{:S(2)}) copy-start(f32[32,32,1024]{2,1,0:T(8,128)} %param.14) | copy-start | bytes 12582916
  123.0 3.5 %copy-start.1 = (f32[32,32,1024]{2,1,0:T(8,128)S(1)}, f32[32,32,1024]{2,1,0:T(8,128)}, u32[]{:S(2)}) copy-start(f32[32,32,1024]{2,1,0:T(8,128)} %param.15) | copy-start | bytes 12582916

commit v12 on v10

--- a/solution.py
+++ b/solution.py
@@ -159,6 +159,12 @@
     )(send)
 
 
+def split_bf16(value):
+    high = value.astype(jnp.bfloat16)
+    low = (value - high.astype(jnp.float32)).astype(jnp.bfloat16)
+    return high, low
+
+
 def on_device(
     activity, sensitivity, psf_width, measured, block_slab, block_line, block_angle, subset_views
 ):
@@ -199,17 +205,21 @@
     ).reshape(slots, row + extra)
     index = recv[:, row].astype(jnp.int32)
     rows = recv[:, :row].reshape(slots, planes, bins).transpose(1, 0, 2)
-    pick = (index[:, None] == jnp.arange(pairs, dtype=jnp.int32)[None, :]).astype(jnp.float32)
+    pick = (index[:, None] == jnp.arange(pairs, dtype=jnp.int32)[None, :]).astype(jnp.bfloat16)
     pick = jnp.broadcast_to(pick[None], (planes, slots, pairs))
-    estimate = jnp.einsum("zjp,zpt->zjt", pick, projected, precision=lax.Precision.HIGH)
+    estimate = sum(
+        jnp.einsum("zjp,zpt->zjt", pick, piece, preferred_element_type=jnp.float32)
+        for piece in split_bf16(projected)
+    )
     ratios = rows.astype(jnp.float32) / (estimate + BACKGROUND)
 
     same = index[:, None] == index[None, :]
     earlier = jnp.arange(slots)[None, :] < jnp.arange(slots)[:, None]
     first = ~jnp.any(same & earlier, axis=1)
-    merge = jnp.broadcast_to((same & first[:, None]).astype(jnp.float32)[None], (planes, slots, slots))
-    merged = jnp.einsum(
-        "zij,zjt->zit", merge, ratios, precision=lax.Precision.HIGH
+    merge = jnp.broadcast_to((same & first[:, None]).astype(jnp.bfloat16)[None], (planes, slots, slots))
+    merged = sum(
+        jnp.einsum("zij,zjt->zit", merge, piece, preferred_element_type=jnp.float32)
+        for piece in split_bf16(ratios)
     ).astype(jnp.bfloat16)
 
     views = subset_views[0]

time: 129 us -> 133 us (1.031)
  local copies, waits for them, and re-layouts: 7.4 us -> 12 us
  other arithmetic: 15.8 us -> 19 us
  matrix products: 25.9 us -> 22.9 us
    convert_element_type x0 -> x2, local copies, waits for them, and re-layouts: none -> 4.89 us  [on_device(): ratios = rows.astype(jnp.float32) / (estimate + BACKGROUND)]
    convert_element_type x1 -> x3, other arithmetic: 0.1 us -> 3.31 us  [the longest x1 3.01 us: split_bf16(): low = (value - high.astype(jnp.float32)).astype(jnp.bfloat16)]
    dot_general x2 -> x4, matrix products: 5.28 us -> 2.33 us  [the longest x2 1.44 us: on_device(): jnp.einsum('zjp,zpt->zjt', pick, piece, preferred_element_type=jnp.float32)]
    transpose x1, local copies, waits for them, and re-layouts: 2.45 us -> 0.63 us  [on_device(): jnp.einsum('zlv,atv->zalt', blurred, tof_kernel, preferred_element_type=j...]
    unnamed x9 -> x15, local copies, waits for them, and re-layouts: 1.27 us -> 2.79 us
where the time goes in v12:
time: 133 us; the launch traced here: 132 us
  waiting for transfers between devices  41.6 us (31%)
  starting transfers between devices  36.5 us (27%)
  matrix products  22.9 us (17%)
  other arithmetic  19 us (14%)
  local copies, waits for them, and re-layouts  12 us (9%)
    ppermute x1, waiting for transfers between devices, on_device(): from_right = lax.ppermute(payload, 'view', leftward)  18.2 us
    ppermute x2, starting transfers between devices, with_halo(): before = lax.ppermute(last, axis, up)  14.6 us
    all_to_all x1, waiting for transfers between devices, on_device(): lax.all_to_all(send.reshape(slab_count, capacity, row + extra), 'slab', 0...  13.9 us
    all_to_all x1, starting transfers between devices, on_device(): lax.all_to_all(send.reshape(slab_count, capacity, row + extra), 'slab', 0...  12.8 us
    dot_general x4, matrix products, back_project(): jnp.einsum('zlat,atv->zlv', dense, kernel_k, preferred_element_type=jnp.f...  10.2 us
    dot_general x1, matrix products, on_device(): jnp.einsum('zlv,atv->zalt', blurred, tof_kernel, preferred_element_type=j...  7.16 us
    ppermute x2, waiting for transfers between devices, with_halo(): after = lax.ppermute(leading, axis, down)  6.46 us
    convert_element_type x2, local copies, waits for them, and re-layouts, on_device(): ratios = rows.astype(jnp.float32) / (estimate + BACKGROUND)  4.89 us
  transfers between devices with their start and end apart: 9, of which 4 were waited for; matrix products, arithmetic and copies ran while one was open for 24% of the time, Pallas kernels for 0%

profile of v12, /device:TPU:31, one launch (start us, length us, event | category | flops | bytes accessed | tf_op | source)
XLA Modules:
  0.0 132.3 jit_solution(2764094559845933516)
XLA Ops:
  0.0 1.0 fusion.102
  1.0 4.0 %collective-permute-start = (f32[1,32,1024]{2,1,0:T(8,128)S(1)}, f32[1,32,1024]{2,1,0:T(8,128)S(1)}, u32[]{:S(2)}, u32[]{:S(2)}) collective-permute-start(f32[1,32,1024]{2,1,0:T(8,128)S(1)} %get-tuple-element.63), channel_id=1, source_target_pairs={{0,4},{4,8},{8,12},{12,16},{16,20},{20,24},{24,28},{28,32},{32,36}... | collective-permute-start | bytes 393224 | tf_op jit(solution)/shard_map/ppermute | solution.py:25
  5.0 1.9 %collective-permute-start.1 = (f32[1,32,1024]{2,1,0:T(8,128)S(1)}, f32[1,32,1024]{2,1,0:T(8,128)S(1)}, u32[]{:S(2)}, u32[]{:S(2)}) collective-permute-start(f32[1,32,1024]{2,1,0:T(8,128)S(1)} %get-tuple-element.64), channel_id=1, source_target_pairs={{4,0},{8,4},{12,8},{16,12},{20,16},{24,20},{28,24},{32,28},{36,32}... | collective-permute-start | bytes 393224 | tf_op jit(solution)/shard_map/ppermute | solution.py:26
  7.0 0.7 fusion.80
  7.8 0.8 select_reduce_fusion
  8.6 0.7 multiply_add_fusion.4
  9.3 1.3 copy.37
  10.6 0.7 convert_bitcast_fusion.5
  11.3 0.4 convolution_convert_fusion
  11.8 1.2 reshape.591
  13.0 12.8 %all-to-all-start = ((bf16[64,2,4224]{2,1,0:T(2,128)(2,1)}), bf16[64,2,4224]{2,1,0:T(2,128)(2,1)S(1)}, u32[]{:S(2)}, u32[]{:S(2)}) async-start(bf16[64,2,4224]{2,1,0:T(2,128)(2,1)} %reshape.591), calls=%async_computation | async-start | bytes 2162688 | tf_op jit(solution)/shard_map/all_to_all | solution.py:203
  25.8 0.7 compare_reduce_fusion.1
  26.5 0.7 fusion.85
  27.4 0.6 compare_reduce_fusion.2
  28.0 0.6 compare_reduce_fusion
  28.7 7.2 %convolution_bitcast_fusion.1 = f32[32,8,32,128]{3,2,0,1:T(8,128)S(1)} fusion(f32[1,32,1024]{2,1,0:T(8,128)S(1)} %collective-permute-done.1, f32[32,32,1024]{2,1,0:T(8,128)} %param.14, f32[1,32,1024]{2,1,0:T(8,128)S(1)} %collective-permute-done, f32[32]{0:T(128)S(1)} %copy-done.6, f32[8,128]{1,0:T(8,128)S(1)} %multiply_add_fusion.3, ...), kind=kOutput, calls=%fused_computation.40 | convolution fusion | flops 2161115136 | bytes 8659200 | tf_op jit(solution)/shard_map/zlv,atv->zalt/dot_general | solution.py:182
  35.8 0.6 copy.15
  36.5 3.0 %fusion.24 = (bf16[32,256,128]{2,1,0:T(8,128)(2,1)}, bf16[32,256,128]{2,1,0:T(8,128)(2,1)}) fusion(f32[32,8,32,128]{3,2,1,0:T(8,128)S(1)} %copy.15), kind=kLoop, calls=%fused_computation.38 | loop fusion | flops 4194304 | bytes 8388608 | tf_op jit(solution)/shard_map/convert_element_type | solution.py:164
  39.5 13.9 %all-to-all-done = bf16[64,2,4224]{2,1,0:T(2,128)(2,1)S(1)} async-done(((bf16[64,2,4224]{2,1,0:T(2,128)(2,1)}), bf16[64,2,4224]{2,1,0:T(2,128)(2,1)S(1)}, u32[]{:S(2)}, u32[]{:S(2)}) %all-to-all-start) | async-done | bytes 1081376 | tf_op jit(solution)/shard_map/all_to_all | solution.py:203
  53.4 0.4 reshape.592
  53.9 0.1 convert_reduce_fusion
  54.0 0.2 fusion.77
  54.3 0.2 slice_convert_fusion
  54.5 0.1 fusion.78
  54.6 0.6 fusion.76
  55.2 1.8 %copy.13 = f32[128,4096]{0,1:T(8,128)} copy(f32[128,4096]{1,0:T(8,128)S(1)} %slice_convert_fusion) | data formatting | bytes 4194304 | tf_op jit(solution)/shard_map/convert_element_type | solution.py:214
  57.0 3.1 %copy.14 = f32[128,32,128]{2,0,1:T(8,128)} copy(f32[128,32,128]{0,2,1:T(8,128)} %bitcast.93) | data formatting | bytes 4194304 | tf_op jit(solution)/shard_map/convert_element_type | solution.py:214
  60.1 0.7 fusion.64
  60.8 0.9 copy-done.3
  61.7 0.6 copy-done.4
  62.3 0.7 bitcast_divide_fusion
  63.1 0.4 fusion.71
  63.5 0.5 add_convert_fusion
  64.0 0.4 scatter.11
  64.4 0.7 slice_select_fusion
  65.1 0.4 scatter.14
  65.5 0.1 pad_maximum_fusion.4
  65.6 0.5 collective-permute-start.3
  66.1 2.2 %collective-permute-start.2 = (bf16[33,128,128]{2,1,0:T(8,128)(2,1)S(1)}, bf16[33,128,128]{2,1,0:T(8,128)(2,1)S(1)}, u32[]{:S(2)}, u32[]{:S(2)}) collective-permute-start(bf16[33,128,128]{2,1,0:T(8,128)(2,1)S(1)} %pad_maximum_fusion.4), channel_id=1, source_target_pairs={{0,1},{1,2},{2,3},{3,0},{4,5},{5,6},{6,7},{7,4},{8,9},{9,10},{10,1... | collective-permute-start | bytes 3244040 | tf_op jit(solution)/shard_map/ppermute | solution.py:254
  68.4 0.1 convert_reduce_fusion.4
  68.5 0.1 compare_convert_fusion.3
  68.6 0.7 convert_bitcast_fusion.3
  69.3 2.5 %convolution_bitcast_fusion = f32[32,32,1024]{2,1,0:T(8,128)S(1)} fusion(bf16[32,32,8,128]{3,2,1,0:T(8,128)(2,1)S(1)} %convert_bitcast_fusion.3, f32[8,128]{1,0:T(8,128)S(1)} %multiply_add_fusion.3, f32[1024]{0:T(1024)S(1)} %iota_add_fusion), kind=kOutput, calls=%fused_computation.39 | convolution fusion | flops 2153775104 | bytes 6299648 | tf_op jit(solution)/shard_map/zlat,atv->zlv/dot_general | solution.py:243
  71.8 18.2 %collective-permute-done.3 = bf16[33,128,128]{2,1,0:T(8,128)(2,1)S(1)} collective-permute-done((bf16[33,128,128]{2,1,0:T(8,128)(2,1)S(1)}, bf16[33,128,128]{2,1,0:T(8,128)(2,1)S(1)}, u32[]{:S(2)}, u32[]{:S(2)}) %collective-permute-start.3) | collective-permute-done | bytes 1081376 | tf_op jit(solution)/shard_map/ppermute | solution.py:255
  90.0 0.1 convert_reduce_fusion.2
  90.3 0.1 multiply_bitcast_fusion.1
  90.4 0.1 multiply_bitcast_fusion.2
  90.6 2.5 %collective-permute-start.4 = (bf16[16,128,128]{2,1,0:T(8,128)(2,1)S(1)}, bf16[16,128,128]{2,1,0:T(8,128)(2,1)S(1)}, u32[]{:S(2)}, u32[]{:S(2)}) collective-permute-start(bf16[16,128,128]{2,1,0:T(8,128)(2,1)S(1)} %slice.162), channel_id=1, source_target_pairs={{0,1},{1,2},{2,3},{3,0},{4,5},{5,6},{6,7},{7,4},{8,9},{9,10},{10,1... | collective-permute-start | bytes 1572872 | tf_op jit(solution)/shard_map/ppermute | solution.py:258
  93.1 0.1 compare_convert_fusion.2
  93.2 0.7 convert_bitcast_fusion.1
  93.9 0.7 convert_bitcast_fusion.2
  94.6 2.5 %fusion.28 = f32[32,32,1024,1]{2,1,3,0:T(8,128)S(1)} fusion(bf16[32,32,8,128]{3,2,1,0:T(8,128)(2,1)S(1)} %convert_bitcast_fusion.2, f32[8,128]{1,0:T(8,128)S(1)} %get-tuple-element.67, f32[1024]{0:T(1024)S(1)} %iota_add_fusion), kind=kOutput, calls=%fused_computation.44 | convolution fusion | flops 2153775104 | bytes 6299648 | tf_op jit(solution)/shard_map/zlat,atv->zlv/dot_general | solution.py:243
  97.2 2.5 %fusion.30 = f32[32,32,1024,1]{2,1,3,0:T(8,128)S(1)} fusion(bf16[32,32,8,128]{3,2,1,0:T(8,128)(2,1)S(1)} %convert_bitcast_fusion.1, f32[8,128]{1,0:T(8,128)S(1)} %get-tuple-element.68, f32[1024]{0:T(1024)S(1)} %iota_add_fusion), kind=kOutput, calls=%fused_computation.45 | convolution fusion | flops 2153775104 | bytes 6299648 | tf_op jit(solution)/shard_map/zlat,atv->zlv/dot_general | solution.py:243
  99.7 1.9 %bitcast_add_fusion.1 = f32[32,32,1024]{2,1,0:T(8,128)S(1)} fusion(f32[32,32,1024,1]{2,1,3,0:T(8,128)S(1)} %fusion.30, f32[32,32,1024]{2,1,0:T(8,128)S(1)} %convolution_bitcast_fusion, f32[32,32,1024,1]{2,1,3,0:T(8,128)S(1)} %fusion.28), kind=kLoop, calls=%fused_computation.34 | loop fusion | flops 2097152 | bytes 16777216 | tf_op jit(solution)/shard_map/add | solution.py:261
  101.7 3.0 %collective-permute-done.5 = bf16[17,128,128]{2,1,0:T(8,128)(2,1)S(1)} collective-permute-done((bf16[17,128,128]{2,1,0:T(8,128)(2,1)S(1)}, bf16[17,128,128]{2,1,0:T(8,128)(2,1)S(1)}, u32[]{:S(2)}, u32[]{:S(2)}) %collective-permute-start.5) | collective-permute-done | bytes 557088 | tf_op jit(solution)/shard_map/ppermute | solution.py:259
  104.7 0.1 convert_reduce_fusion.1
  104.8 0.1 multiply_bitcast_fusion
  105.0 0.1 compare_convert_fusion
  105.2 0.7 convert_bitcast_fusion
  105.9 2.6 %broadcast_multiply_fusion = (f32[32,32,1024]{2,1,0:T(8,128)S(1)}, f32[32,32,1024,1]{2,1,3,0:T(8,128)S(1)}) fusion(f32[32]{0:T(128)S(1)} %copy-done.6, f32[32,32,1024]{2,1,0:T(8,128)S(1)} %bitcast_add_fusion.1, f32[8,128]{1,0:T(8,128)S(1)} %multiply_add_fusion, f32[1024]{0:T(1024)S(1)} %iota_add_fusion, bf16[32,32,8,128]{3,2,1,0:T(8,128)(2,1)S(1)} %convert_bitcast_fusion), kind=kOutput, calls=%fused_computation.64 | convolution fusion | flops 2155872256 | bytes 14688384 | tf_op jit(solution)/shard_map/zlat,atv->zlv/dot_general | solution.py:243
  108.5 10.6 %collective-permute-start.6 = (f32[1,32,1024]{2,1,0:T(8,128)S(1)}, f32[1,32,1024]{2,1,0:T(8,128)S(1)}, u32[]{:S(2)}, u32[]{:S(2)}) collective-permute-start(f32[1,32,1024]{2,1,0:T(8,128)S(1)} %get-tuple-element.61), channel_id=1, source_target_pairs={{0,4},{4,8},{8,12},{12,16},{16,20},{20,24},{24,28},{28,32},{32,36}... | collective-permute-start | bytes 393224 | tf_op jit(solution)/shard_map/ppermute | solution.py:25
  119.1 1.9 %collective-permute-start.7 = (f32[1,32,1024]{2,1,0:T(8,128)S(1)}, f32[1,32,1024]{2,1,0:T(8,128)S(1)}, u32[]{:S(2)}, u32[]{:S(2)}) collective-permute-start(f32[1,32,1024]{2,1,0:T(8,128)S(1)} %get-tuple-element.62), channel_id=1, source_target_pairs={{4,0},{8,4},{12,8},{16,12},{20,16},{24,20},{28,24},{32,28},{36,32}... | collective-permute-start | bytes 393224 | tf_op jit(solution)/shard_map/ppermute | solution.py:26
  121.1 6.5 %collective-permute-done.7 = f32[1,32,1024]{2,1,0:T(8,128)S(1)} collective-permute-done((f32[1,32,1024]{2,1,0:T(8,128)S(1)}, f32[1,32,1024]{2,1,0:T(8,128)S(1)}, u32[]{:S(2)}, u32[]{:S(2)}) %collective-permute-start.7) | collective-permute-done | bytes 131104 | tf_op jit(solution)/shard_map/ppermute | solution.py:26
  127.5 4.8 %fusion.18 = f32[32,32,1024]{2,1,0:T(8,128)} fusion(f32[32,32,1024]{2,1,0:T(8,128)S(1)} %copy-done.2, f32[32,32,1024]{2,1,0:T(8,128)S(1)} %copy-done.1, f32[1,32,1024]{2,1,0:T(8,128)S(1)} %collective-permute-done.7, f32[32,32,1024]{2,1,0:T(8,128)S(1)} %get-tuple-element.71, f32[1,32,1024]{2,1,0:T(8,128)S(1)} %collective-permute-done.6, ...), kind=kLoop, calls=%fused_computation.24 | loop fusion | flops 8388608 | bytes 25428096 | tf_op jit(solution)/shard_map/div | solution.py:267
  (41 shorter events, 0.9 us)
Async XLA Ops:
  0.0 26.5 %copy-start.5 = (s32[1,8]{1,0:T(1,128)S(1)}, s32[1,8]{1,0:T(1,128)}, u32[]{:S(2)}) copy-start(s32[1,8]{1,0:T(1,128)} %param.21) | copy-start | bytes 100
  0.0 27.2 %copy-start.6 = (f32[32]{0:T(128)S(1)}, f32[32]{0:T(128)}, u32[]{:S(2)}) copy-start(f32[32]{0:T(128)} %param.16) | copy-start | bytes 388
  1.0 27.6 %collective-permute-start = (f32[1,32,1024]{2,1,0:T(8,128)S(1)}, f32[1,32,1024]{2,1,0:T(8,128)S(1)}, u32[]{:S(2)}, u32[]{:S(2)}) collective-permute-start(f32[1,32,1024]{2,1,0:T(8,128)S(1)} %get-tuple-element.63), channel_id=1, source_target_pairs={{0,4},{4,8},{8,12},{12,16},{16,20},{20,24},{24,28},{28,32},{32,36}... | collective-permute-start | bytes 393224 | tf_op jit(solution)/shard_map/ppermute | solution.py:25
  5.0 23.6 %collective-permute-start.1 = (f32[1,32,1024]{2,1,0:T(8,128)S(1)}, f32[1,32,1024]{2,1,0:T(8,128)S(1)}, u32[]{:S(2)}, u32[]{:S(2)}) collective-permute-start(f32[1,32,1024]{2,1,0:T(8,128)S(1)} %get-tuple-element.64), channel_id=1, source_target_pairs={{4,0},{8,4},{12,8},{16,12},{20,16},{24,20},{28,24},{32,28},{36,32}... | collective-permute-start | bytes 393224 | tf_op jit(solution)/shard_map/ppermute | solution.py:26
  13.0 40.4 %all-to-all-start = ((bf16[64,2,4224]{2,1,0:T(2,128)(2,1)}), bf16[64,2,4224]{2,1,0:T(2,128)(2,1)S(1)}, u32[]{:S(2)}, u32[]{:S(2)}) async-start(bf16[64,2,4224]{2,1,0:T(2,128)(2,1)} %reshape.591), calls=%async_computation | async-start | bytes 2162688 | tf_op jit(solution)/shard_map/all_to_all | solution.py:203
  57.0 3.1 %copy-start = (bf16[32,256,128]{2,1,0:T(8,128)(2,1)S(1)}, bf16[32,256,128]{2,1,0:T(8,128)(2,1)}, u32[]{:S(2)}) copy-start(bf16[32,256,128]{2,1,0:T(8,128)(2,1)} %get-tuple-element.60) | copy-start | bytes 6291460
  60.1 1.6 %copy-start.3 = (f32[128,32,128]{2,0,1:T(8,128)S(1)}, f32[128,32,128]{2,0,1:T(8,128)}, u32[]{:S(2)}) copy-start(f32[128,32,128]{2,0,1:T(8,128)} %copy.14) | copy-start | bytes 6291460
  60.1 2.2 %copy-start.4 = (bf16[32,256,128]{2,1,0:T(8,128)(2,1)S(1)}, bf16[32,256,128]{2,1,0:T(8,128)(2,1)}, u32[]{:S(2)}) copy-start(bf16[32,256,128]{2,1,0:T(8,128)(2,1)} %get-tuple-element.59) | copy-start | bytes 6291460
  65.6 24.4 %collective-permute-start.3 = (bf16[33,128,128]{2,1,0:T(8,128)(2,1)S(1)}, bf16[33,128,128]{2,1,0:T(8,128)(2,1)S(1)}, u32[]{:S(2)}, u32[]{:S(2)}) collective-permute-start(bf16[33,128,128]{2,1,0:T(8,128)(2,1)S(1)} %pad_maximum_fusion.4), channel_id=1, source_target_pairs={{0,3},{1,0},{2,1},{3,2},{4,7},{5,4},{6,5},{7,6},{8,11},{9,8},{10,9... | collective-permute-start | bytes 3244040 | tf_op jit(solution)/shard_map/ppermute | solution.py:255
  66.1 23.9 %collective-permute-start.2 = (bf16[33,128,128]{2,1,0:T(8,128)(2,1)S(1)}, bf16[33,128,128]{2,1,0:T(8,128)(2,1)S(1)}, u32[]{:S(2)}, u32[]{:S(2)}) collective-permute-start(bf16[33,128,128]{2,1,0:T(8,128)(2,1)S(1)} %pad_maximum_fusion.4), channel_id=1, source_target_pairs={{0,1},{1,2},{2,3},{3,0},{4,5},{5,6},{6,7},{7,4},{8,9},{9,10},{10,1... | collective-permute-start | bytes 3244040 | tf_op jit(solution)/shard_map/ppermute | solution.py:254
  90.6 11.1 %collective-permute-start.4 = (bf16[16,128,128]{2,1,0:T(8,128)(2,1)S(1)}, bf16[16,128,128]{2,1,0:T(8,128)(2,1)S(1)}, u32[]{:S(2)}, u32[]{:S(2)}) collective-permute-start(bf16[16,128,128]{2,1,0:T(8,128)(2,1)S(1)} %slice.162), channel_id=1, source_target_pairs={{0,1},{1,2},{2,3},{3,0},{4,5},{5,6},{6,7},{7,4},{8,9},{9,10},{10,1... | collective-permute-start | bytes 1572872 | tf_op jit(solution)/shard_map/ppermute | solution.py:258
  93.1 11.6 %collective-permute-start.5 = (bf16[17,128,128]{2,1,0:T(8,128)(2,1)S(1)}, bf16[17,128,128]{2,1,0:T(8,128)(2,1)S(1)}, u32[]{:S(2)}, u32[]{:S(2)}) collective-permute-start(bf16[17,128,128]{2,1,0:T(8,128)(2,1)S(1)} %slice.163), channel_id=1, source_target_pairs={{0,3},{1,0},{2,1},{3,2},{4,7},{5,4},{6,5},{7,6},{8,11},{9,8},{10,9... | collective-permute-start | bytes 1671176 | tf_op jit(solution)/shard_map/ppermute | solution.py:259
  105.9 21.7 %copy-start.1 = (f32[32,32,1024]{2,1,0:T(8,128)S(1)}, f32[32,32,1024]{2,1,0:T(8,128)}, u32[]{:S(2)}) copy-start(f32[32,32,1024]{2,1,0:T(8,128)} %param.14) | copy-start | bytes 12582916
  105.9 21.7 %copy-start.2 = (f32[32,32,1024]{2,1,0:T(8,128)S(1)}, f32[32,32,1024]{2,1,0:T(8,128)}, u32[]{:S(2)}) copy-start(f32[32,32,1024]{2,1,0:T(8,128)} %param.15) | copy-start | bytes 12582916
  108.5 12.6 %collective-permute-start.6 = (f32[1,32,1024]{2,1,0:T(8,128)S(1)}, f32[1,32,1024]{2,1,0:T(8,128)S(1)}, u32[]{:S(2)}, u32[]{:S(2)}) collective-permute-start(f32[1,32,1024]{2,1,0:T(8,128)S(1)} %get-tuple-element.61), channel_id=1, source_target_pairs={{0,4},{4,8},{8,12},{12,16},{16,20},{20,24},{24,28},{28,32},{32,36}... | collective-permute-start | bytes 393224 | tf_op jit(solution)/shard_map/ppermute | solution.py:25
  119.1 8.4 %collective-permute-start.7 = (f32[1,32,1024]{2,1,0:T(8,128)S(1)}, f32[1,32,1024]{2,1,0:T(8,128)S(1)}, u32[]{:S(2)}, u32[]{:S(2)}) collective-permute-start(f32[1,32,1024]{2,1,0:T(8,128)S(1)} %get-tuple-element.62), channel_id=1, source_target_pairs={{4,0},{8,4},{12,8},{16,12},{20,16},{24,20},{28,24},{32,28},{36,32}... | collective-permute-start | bytes 393224 | tf_op jit(solution)/shard_map/ppermute | solution.py:26

commit v13 on v10

--- a/solution.py
+++ b/solution.py
@@ -243,8 +243,12 @@
     half = (planes + 1) // 2
     from_left = lax.ppermute(payload, "view", rightward)
     from_right = lax.ppermute(payload, "view", leftward)
+    payload, activity, sensitivity = lax.optimization_barrier((payload, activity, sensitivity))
+    scale = activity / sensitivity
     total = back_project(payload, tof_kernel)
-    total, from_left, from_right = lax.optimization_barrier((total, from_left, from_right))
+    total, from_left, from_right, scale = lax.optimization_barrier(
+        (total, from_left, from_right, scale)
+    )
     far_low = lax.ppermute(from_left[:half], "view", rightward)
     far_high = lax.ppermute(from_right[half:], "view", leftward)
     total = total + back_project(from_left, kernel_of(from_left))
@@ -254,7 +258,7 @@
     total = total + back_project(far, kernel_of(far))
     edges = with_halo(weight * total, (("slab", 0),), 1)
     smoothed = (1.0 - 2.0 * weight) * total + edges[:-2] + edges[2:]
-    return activity * smoothed / sensitivity
+    return smoothed * scale
 
 
 def solution(mesh):

time: 129 us -> 130 us (level)
    mul x0 -> x1, other arithmetic: none -> 4.22 us  [on_device(): return smoothed * scale]
    div x1, other arithmetic: 4.79 us -> 0.98 us  [on_device(): scale = activity / sensitivity]
where the time goes in v13:
time: 130 us
  waiting for transfers between devices  41.7 us (32%)
  starting transfers between devices  36.5 us (28%)
  matrix products  27 us (21%)
  other arithmetic  16.2 us (12%)
  local copies, waits for them, and re-layouts  8.2 us (6%)
    ppermute x1, waiting for transfers between devices, on_device(): from_right = lax.ppermute(payload, 'view', leftward)  17.2 us
    all_to_all x1, waiting for transfers between devices, on_device(): lax.all_to_all(send.reshape(slab_count, capacity, row + extra), 'slab', 0...  15.1 us
    ppermute x2, starting transfers between devices, with_halo(): before = lax.ppermute(last, axis, up)  14.7 us
    all_to_all x1, starting transfers between devices, on_device(): lax.all_to_all(send.reshape(slab_count, capacity, row + extra), 'slab', 0...  12.8 us
    dot_general x4, matrix products, back_project(): jnp.einsum('zlat,atv->zlv', dense, kernel_k, preferred_element_type=jnp.f...  10.2 us
    dot_general x1, matrix products, on_device(): jnp.einsum('zlv,atv->zalt', blurred, tof_kernel, preferred_element_type=j...  7.23 us
    ppermute x2, waiting for transfers between devices, with_halo(): after = lax.ppermute(leading, axis, down)  6.46 us
    mul x1, other arithmetic, on_device(): return smoothed * scale  4.22 us
  transfers between devices with their start and end apart: 9, of which 4 were waited for; matrix products, arithmetic and copies ran while one was open for 24% of the time, Pallas kernels for 0%

profile of v13, /device:TPU:31, one launch (start us, length us, event | category | flops | bytes accessed | tf_op | source)
XLA Modules:
  0.0 130.0 jit_solution(6400147886185442715)
XLA Ops:
  0.0 1.0 fusion.106
  1.0 4.0 %collective-permute-start = (f32[1,32,1024]{2,1,0:T(8,128)S(1)}, f32[1,32,1024]{2,1,0:T(8,128)S(1)}, u32[]{:S(2)}, u32[]{:S(2)}) collective-permute-start(f32[1,32,1024]{2,1,0:T(8,128)S(1)} %get-tuple-element.69), channel_id=1, source_target_pairs={{0,4},{4,8},{8,12},{12,16},{16,20},{20,24},{24,28},{28,32},{32,36}... | collective-permute-start | bytes 393224 | tf_op jit(solution)/shard_map/ppermute | solution.py:25
  5.0 1.9 %collective-permute-start.1 = (f32[1,32,1024]{2,1,0:T(8,128)S(1)}, f32[1,32,1024]{2,1,0:T(8,128)S(1)}, u32[]{:S(2)}, u32[]{:S(2)}) collective-permute-start(f32[1,32,1024]{2,1,0:T(8,128)S(1)} %get-tuple-element.70), channel_id=1, source_target_pairs={{4,0},{8,4},{12,8},{16,12},{20,16},{24,20},{28,24},{32,28},{36,32}... | collective-permute-start | bytes 393224 | tf_op jit(solution)/shard_map/ppermute | solution.py:26
  7.0 0.7 fusion.83
  7.7 0.1 reduce_window_sum.11
  7.8 0.8 select_reduce_fusion
  8.6 0.7 multiply_add_fusion.4
  9.3 1.3 copy.44
  10.6 0.7 convert_bitcast_fusion.6
  11.2 0.1 broadcast_in_dim.18
  11.3 0.4 convolution_convert_fusion
  11.8 1.2 reshape.591
  13.0 12.8 %all-to-all-start = ((bf16[64,2,4224]{2,1,0:T(2,128)(2,1)}), bf16[64,2,4224]{2,1,0:T(2,128)(2,1)S(1)}, u32[]{:S(2)}, u32[]{:S(2)}) async-start(bf16[64,2,4224]{2,1,0:T(2,128)(2,1)} %reshape.591), calls=%async_computation | async-start | bytes 2162688 | tf_op jit(solution)/shard_map/all_to_all | solution.py:197
  25.8 0.6 compare_reduce_fusion.1
  26.4 0.7 fusion.88
  27.2 0.1 multiply_add_fusion.3
  27.2 0.7 compare_reduce_fusion.2
  27.9 0.7 compare_reduce_fusion
  28.6 7.2 %convolution_bitcast_fusion.1 = f32[32,8,32,128]{3,2,0,1:T(8,128)S(1)} fusion(f32[1,32,1024]{2,1,0:T(8,128)S(1)} %collective-permute-done.1, f32[32,32,1024]{2,1,0:T(8,128)} %param.14, f32[1,32,1024]{2,1,0:T(8,128)S(1)} %collective-permute-done, f32[32]{0:T(128)S(1)} %copy-done.3, f32[8,128]{1,0:T(8,128)S(1)} %multiply_add_fusion.3, ...), kind=kOutput, calls=%fused_computation.36 | convolution fusion | flops 2161115136 | bytes 8659200 | tf_op jit(solution)/shard_map/zlv,atv->zalt/dot_general | solution.py:176
  35.9 2.5 %copy.15 = f32[32,8,32,128]{3,2,1,0:T(8,128)} copy(f32[32,8,32,128]{3,2,0,1:T(8,128)S(1)} %convolution_bitcast_fusion.1) | data formatting | bytes 8388608 | tf_op jit(solution)/shard_map/zlv,atv->zalt/transpose | solution.py:176
  38.3 15.1 %all-to-all-done = bf16[64,2,4224]{2,1,0:T(2,128)(2,1)S(1)} async-done(((bf16[64,2,4224]{2,1,0:T(2,128)(2,1)}), bf16[64,2,4224]{2,1,0:T(2,128)(2,1)S(1)}, u32[]{:S(2)}, u32[]{:S(2)}) %all-to-all-start) | async-done | bytes 1081376 | tf_op jit(solution)/shard_map/all_to_all | solution.py:197
  53.4 0.4 reshape.592
  53.9 0.1 convert_reduce_fusion
  54.0 0.2 fusion.80
  54.2 0.1 fusion.78
  54.3 0.6 fusion.79
  54.9 0.1 fusion.81
  55.1 0.4 scatter.11
  55.5 0.7 slice_select_fusion
  56.2 0.4 scatter.14
  56.6 4.2 %fusion.59 = f32[32,128,128]{2,1,0:T(8,128)S(1)} fusion(f32[32,256,128]{2,1,0:T(8,128)} %bitcast.101, f32[128,256]{1,0:T(8,128)S(1)} %fusion.78), kind=kOutput, calls=%fused_computation.73 | convolution fusion | flops 805306368 | bytes 6422528 | tf_op jit(solution)/shard_map/zjp,zpt->zjt/dot_general | solution.py:204
  60.8 1.1 fusion.62
  61.9 0.1 pad_maximum_fusion.4
  62.0 0.5 collective-permute-start.3
  62.6 2.2 %collective-permute-start.2 = (bf16[33,128,128]{2,1,0:T(8,128)(2,1)S(1)}, bf16[33,128,128]{2,1,0:T(8,128)(2,1)S(1)}, u32[]{:S(2)}, u32[]{:S(2)}) collective-permute-start(bf16[33,128,128]{2,1,0:T(8,128)(2,1)S(1)} %pad_maximum_fusion.4), channel_id=1, source_target_pairs={{0,1},{1,2},{2,3},{3,0},{4,5},{5,6},{6,7},{7,4},{8,9},{9,10},{10,1... | collective-permute-start | bytes 3244040 | tf_op jit(solution)/shard_map/ppermute | solution.py:244
  64.8 1.0 div.89
  65.8 0.1 convert_reduce_fusion.4
  65.9 0.1 compare_convert_fusion.3
  66.0 0.7 convert_bitcast_fusion.4
  66.7 2.5 %convolution_bitcast_fusion = f32[32,32,1024]{2,1,0:T(8,128)S(1)} fusion(bf16[32,32,8,128]{3,2,1,0:T(8,128)(2,1)S(1)} %convert_bitcast_fusion.4, f32[8,128]{1,0:T(8,128)S(1)} %multiply_add_fusion.3, f32[1024]{0:T(1024)S(1)} %iota_add_fusion), kind=kOutput, calls=%fused_computation.35 | convolution fusion | flops 2153775104 | bytes 6299648 | tf_op jit(solution)/shard_map/zlat,atv->zlv/dot_general | solution.py:233
  69.2 17.2 %collective-permute-done.3 = bf16[33,128,128]{2,1,0:T(8,128)(2,1)S(1)} collective-permute-done((bf16[33,128,128]{2,1,0:T(8,128)(2,1)S(1)}, bf16[33,128,128]{2,1,0:T(8,128)(2,1)S(1)}, u32[]{:S(2)}, u32[]{:S(2)}) %collective-permute-start.3) | collective-permute-done | bytes 1081376 | tf_op jit(solution)/shard_map/ppermute | solution.py:245
  86.4 0.1 convert_reduce_fusion.2
  86.6 0.8 slice.166
  87.4 0.1 multiply_bitcast_fusion.1
  87.6 0.1 multiply_bitcast_fusion.2
  87.8 2.5 %collective-permute-start.4 = (bf16[16,128,128]{2,1,0:T(8,128)(2,1)}, bf16[16,128,128]{2,1,0:T(8,128)(2,1)}, u32[]{:S(2)}, u32[]{:S(2)}) collective-permute-start(bf16[16,128,128]{2,1,0:T(8,128)(2,1)} %slice.166), channel_id=1, source_target_pairs={{0,1},{1,2},{2,3},{3,0},{4,5},{5,6},{6,7},{7,4},{8,9},{9,10},{10,1... | collective-permute-start | bytes 1572872 | tf_op jit(solution)/shard_map/ppermute | solution.py:252
  90.2 0.1 compare_convert_fusion.2
  90.4 0.7 convert_bitcast_fusion.2
  91.1 0.7 convert_bitcast_fusion.3
  91.8 0.1 multiply_add_fusion.2
  91.8 2.5 %fusion.26 = f32[32,32,1024,1]{2,1,3,0:T(8,128)S(1)} fusion(bf16[32,32,8,128]{3,2,1,0:T(8,128)(2,1)S(1)} %convert_bitcast_fusion.3, f32[8,128]{1,0:T(8,128)S(1)} %get-tuple-element.73, f32[1024]{0:T(1024)S(1)} %iota_add_fusion), kind=kOutput, calls=%fused_computation.40 | convolution fusion | flops 2153775104 | bytes 6299648 | tf_op jit(solution)/shard_map/zlat,atv->zlv/dot_general | solution.py:233
  94.4 2.5 %fusion.28 = f32[32,32,1024,1]{2,1,3,0:T(8,128)S(1)} fusion(bf16[32,32,8,128]{3,2,1,0:T(8,128)(2,1)S(1)} %convert_bitcast_fusion.2, f32[8,128]{1,0:T(8,128)S(1)} %get-tuple-element.74, f32[1024]{0:T(1024)S(1)} %iota_add_fusion), kind=kOutput, calls=%fused_computation.41 | convolution fusion | flops 2153775104 | bytes 6299648 | tf_op jit(solution)/shard_map/zlat,atv->zlv/dot_general | solution.py:233
  96.9 1.9 %bitcast_add_fusion.1 = f32[32,32,1024]{2,1,0:T(8,128)S(1)} fusion(f32[32,32,1024,1]{2,1,3,0:T(8,128)S(1)} %fusion.28, f32[32,32,1024]{2,1,0:T(8,128)S(1)} %convolution_bitcast_fusion, f32[32,32,1024,1]{2,1,3,0:T(8,128)S(1)} %fusion.26), kind=kLoop, calls=%fused_computation.33 | loop fusion | flops 2097152 | bytes 16777216 | tf_op jit(solution)/shard_map/add | solution.py:255
  98.9 3.0 %collective-permute-done.5 = bf16[17,128,128]{2,1,0:T(8,128)(2,1)S(1)} collective-permute-done((bf16[17,128,128]{2,1,0:T(8,128)(2,1)S(1)}, bf16[17,128,128]{2,1,0:T(8,128)(2,1)S(1)}, u32[]{:S(2)}, u32[]{:S(2)}) %collective-permute-start.5) | collective-permute-done | bytes 557088 | tf_op jit(solution)/shard_map/ppermute | solution.py:253
  101.9 0.1 convert_reduce_fusion.1
  102.0 0.1 multiply_bitcast_fusion
  102.1 0.1 compare_convert_fusion
  102.2 0.1 multiply_add_fusion
  102.3 1.7 %convert_bitcast_fusion.1 = bf16[32,32,8,128]{3,2,1,0:T(8,128)(2,1)S(1)} fusion(bf16[17,128,128]{2,1,0:T(8,128)(2,1)S(1)} %collective-permute-done.5, bf16[16,128,128]{2,1,0:T(8,128)(2,1)} %collective-permute-done.4, bf16[256,128]{1,0:T(8,128)(2,1)S(1)} %compare_convert_fusion), kind=kOutput, calls=%fused_computation.56 | convolution fusion | flops 270008320 | bytes 3244032 | tf_op jit(solution)/shard_map/zpi,zit->zpt/dot_general | solution.py:229
  104.1 2.6 %broadcast_multiply_fusion = (f32[32,32,1024]{2,1,0:T(8,128)S(1)}, f32[32,32,1024,1]{2,1,3,0:T(8,128)S(1)}) fusion(f32[32]{0:T(128)S(1)} %copy-done.3, f32[32,32,1024]{2,1,0:T(8,128)S(1)} %bitcast_add_fusion.1, f32[8,128]{1,0:T(8,128)S(1)} %multiply_add_fusion, f32[1024]{0:T(1024)S(1)} %iota_add_fusion, bf16[32,32,8,128]{3,2,1,0:T(8,128)(2,1)S(1)} %convert_bitcast_fusion.1), kind=kOutput, calls=%fused_computation.63 | convolution fusion | flops 2155872256 | bytes 14688384 | tf_op jit(solution)/shard_map/zlat,atv->zlv/dot_general | solution.py:233
  106.7 10.6 %collective-permute-start.6 = (f32[1,32,1024]{2,1,0:T(8,128)S(1)}, f32[1,32,1024]{2,1,0:T(8,128)S(1)}, u32[]{:S(2)}, u32[]{:S(2)}) collective-permute-start(f32[1,32,1024]{2,1,0:T(8,128)S(1)} %get-tuple-element.67), channel_id=1, source_target_pairs={{0,4},{4,8},{8,12},{12,16},{16,20},{20,24},{24,28},{28,32},{32,36}... | collective-permute-start | bytes 393224 | tf_op jit(solution)/shard_map/ppermute | solution.py:25
  117.4 1.9 %collective-permute-start.7 = (f32[1,32,1024]{2,1,0:T(8,128)S(1)}, f32[1,32,1024]{2,1,0:T(8,128)S(1)}, u32[]{:S(2)}, u32[]{:S(2)}) collective-permute-start(f32[1,32,1024]{2,1,0:T(8,128)S(1)} %get-tuple-element.68), channel_id=1, source_target_pairs={{4,0},{8,4},{12,8},{16,12},{20,16},{24,20},{28,24},{32,28},{36,32}... | collective-permute-start | bytes 393224 | tf_op jit(solution)/shard_map/ppermute | solution.py:26
  119.3 6.5 %collective-permute-done.7 = f32[1,32,1024]{2,1,0:T(8,128)S(1)} collective-permute-done((f32[1,32,1024]{2,1,0:T(8,128)S(1)}, f32[1,32,1024]{2,1,0:T(8,128)S(1)}, u32[]{:S(2)}, u32[]{:S(2)}) %collective-permute-start.7) | collective-permute-done | bytes 131104 | tf_op jit(solution)/shard_map/ppermute | solution.py:26
  125.7 4.2 %fusion.17 = f32[32,32,1024]{2,1,0:T(8,128)} fusion(f32[32,32,1024]{2,1,0:T(8,128)S(1)} %div.89, f32[1,32,1024]{2,1,0:T(8,128)S(1)} %collective-permute-done.7, f32[32,32,1024]{2,1,0:T(8,128)S(1)} %get-tuple-element.77, f32[1,32,1024]{2,1,0:T(8,128)S(1)} %collective-permute-done.6, f32[32]{0:T(128)S(1)} %multiply_subtract_fusion, ...), kind=kLoop, calls=%fused_computation.23 | loop fusion | flops 7340032 | bytes 21233792 | tf_op jit(solution)/shard_map/mul | solution.py:261
  (30 shorter events, 0.4 us)
Async XLA Ops:
  0.0 26.4 %copy-start.2 = (s32[1,8]{1,0:T(1,128)S(1)}, s32[1,8]{1,0:T(1,128)}, u32[]{:S(2)}) copy-start(s32[1,8]{1,0:T(1,128)} %param.21) | copy-start | bytes 100
  0.0 27.1 %copy-start.3 = (f32[32]{0:T(128)S(1)}, f32[32]{0:T(128)}, u32[]{:S(2)}) copy-start(f32[32]{0:T(128)} %param.16) | copy-start | bytes 388
  1.0 27.6 %collective-permute-start = (f32[1,32,1024]{2,1,0:T(8,128)S(1)}, f32[1,32,1024]{2,1,0:T(8,128)S(1)}, u32[]{:S(2)}, u32[]{:S(2)}) collective-permute-start(f32[1,32,1024]{2,1,0:T(8,128)S(1)} %get-tuple-element.69), channel_id=1, source_target_pairs={{0,4},{4,8},{8,12},{12,16},{16,20},{20,24},{24,28},{28,32},{32,36}... | collective-permute-start | bytes 393224 | tf_op jit(solution)/shard_map/ppermute | solution.py:25
  5.0 23.6 %collective-permute-start.1 = (f32[1,32,1024]{2,1,0:T(8,128)S(1)}, f32[1,32,1024]{2,1,0:T(8,128)S(1)}, u32[]{:S(2)}, u32[]{:S(2)}) collective-permute-start(f32[1,32,1024]{2,1,0:T(8,128)S(1)} %get-tuple-element.70), channel_id=1, source_target_pairs={{4,0},{8,4},{12,8},{16,12},{20,16},{24,20},{28,24},{32,28},{36,32}... | collective-permute-start | bytes 393224 | tf_op jit(solution)/shard_map/ppermute | solution.py:26
  13.0 40.4 %all-to-all-start = ((bf16[64,2,4224]{2,1,0:T(2,128)(2,1)}), bf16[64,2,4224]{2,1,0:T(2,128)(2,1)S(1)}, u32[]{:S(2)}, u32[]{:S(2)}) async-start(bf16[64,2,4224]{2,1,0:T(2,128)(2,1)} %reshape.591), calls=%async_computation | async-start | bytes 2162688 | tf_op jit(solution)/shard_map/all_to_all | solution.py:197
  60.8 4.0 %copy-start = (f32[32,32,1024]{2,1,0:T(8,128)S(1)}, f32[32,32,1024]{2,1,0:T(8,128)}, u32[]{:S(2)}) copy-start(f32[32,32,1024]{2,1,0:T(8,128)} %param.14) | copy-start | bytes 12582916
  60.8 4.0 %copy-start.1 = (f32[32,32,1024]{2,1,0:T(8,128)S(1)}, f32[32,32,1024]{2,1,0:T(8,128)}, u32[]{:S(2)}) copy-start(f32[32,32,1024]{2,1,0:T(8,128)} %param.15) | copy-start | bytes 12582916
  62.0 24.4 %collective-permute-start.3 = (bf16[33,128,128]{2,1,0:T(8,128)(2,1)S(1)}, bf16[33,128,128]{2,1,0:T(8,128)(2,1)S(1)}, u32[]{:S(2)}, u32[]{:S(2)}) collective-permute-start(bf16[33,128,128]{2,1,0:T(8,128)(2,1)S(1)} %pad_maximum_fusion.4), channel_id=1, source_target_pairs={{0,3},{1,0},{2,1},{3,2},{4,7},{5,4},{6,5},{7,6},{8,11},{9,8},{10,9... | collective-permute-start | bytes 3244040 | tf_op jit(solution)/shard_map/ppermute | solution.py:245
  62.6 23.9 %collective-permute-start.2 = (bf16[33,128,128]{2,1,0:T(8,128)(2,1)S(1)}, bf16[33,128,128]{2,1,0:T(8,128)(2,1)S(1)}, u32[]{:S(2)}, u32[]{:S(2)}) collective-permute-start(bf16[33,128,128]{2,1,0:T(8,128)(2,1)S(1)} %pad_maximum_fusion.4), channel_id=1, source_target_pairs={{0,1},{1,2},{2,3},{3,0},{4,5},{5,6},{6,7},{7,4},{8,9},{9,10},{10,1... | collective-permute-start | bytes 3244040 | tf_op jit(solution)/shard_map/ppermute | solution.py:244
  87.8 11.1 %collective-permute-start.4 = (bf16[16,128,128]{2,1,0:T(8,128)(2,1)}, bf16[16,128,128]{2,1,0:T(8,128)(2,1)}, u32[]{:S(2)}, u32[]{:S(2)}) collective-permute-start(bf16[16,128,128]{2,1,0:T(8,128)(2,1)} %slice.166), channel_id=1, source_target_pairs={{0,1},{1,2},{2,3},{3,0},{4,5},{5,6},{6,7},{7,4},{8,9},{9,10},{10,1... | collective-permute-start | bytes 1572872 | tf_op jit(solution)/shard_map/ppermute | solution.py:252
  90.2 11.6 %collective-permute-start.5 = (bf16[17,128,128]{2,1,0:T(8,128)(2,1)S(1)}, bf16[17,128,128]{2,1,0:T(8,128)(2,1)S(1)}, u32[]{:S(2)}, u32[]{:S(2)}) collective-permute-start(bf16[17,128,128]{2,1,0:T(8,128)(2,1)S(1)} %slice.167), channel_id=1, source_target_pairs={{0,3},{1,0},{2,1},{3,2},{4,7},{5,4},{6,5},{7,6},{8,11},{9,8},{10,9... | collective-permute-start | bytes 1671176 | tf_op jit(solution)/shard_map/ppermute | solution.py:253
  106.7 12.6 %collective-permute-start.6 = (f32[1,32,1024]{2,1,0:T(8,128)S(1)}, f32[1,32,1024]{2,1,0:T(8,128)S(1)}, u32[]{:S(2)}, u32[]{:S(2)}) collective-permute-start(f32[1,32,1024]{2,1,0:T(8,128)S(1)} %get-tuple-element.67), channel_id=1, source_target_pairs={{0,4},{4,8},{8,12},{12,16},{16,20},{20,24},{24,28},{28,32},{32,36}... | collective-permute-start | bytes 393224 | tf_op jit(solution)/shard_map/ppermute | solution.py:25
  117.4 8.4 %collective-permute-start.7 = (f32[1,32,1024]{2,1,0:T(8,128)S(1)}, f32[1,32,1024]{2,1,0:T(8,128)S(1)}, u32[]{:S(2)}, u32[]{:S(2)}) collective-permute-start(f32[1,32,1024]{2,1,0:T(8,128)S(1)} %get-tuple-element.68), channel_id=1, source_target_pairs={{4,0},{8,4},{12,8},{16,12},{20,16},{24,20},{28,24},{32,28},{36,32}... | collective-permute-start | bytes 393224 | tf_op jit(solution)/shard_map/ppermute | solution.py:26

commit v14 on v10

--- a/solution.py
+++ b/solution.py
@@ -163,18 +163,22 @@
     activity, sensitivity, psf_width, measured, block_slab, block_line, block_angle, subset_views
 ):
     weight = psf_width[:, None, None]
-    padded = with_halo(activity, (("slab", 0),), 1)
-    blurred = ((1.0 - 2.0 * weight) * activity + weight * (padded[:-2] + padded[2:])).astype(
-        jnp.bfloat16
-    )
+    views = subset_views[0]
+    angle_total = views.shape[0]
+    column = jnp.arange(measured.shape[3], dtype=jnp.int32)
+    digits = jnp.concatenate([views // 16, views % 16])
+    fixed = jnp.zeros(column.shape, jnp.int32).at[1 : 1 + 2 * angle_total].set(digits)
+    fixed = fixed.astype(jnp.bfloat16)
+
+    def info_row(index_column):
+        return jnp.where(column[None, :] == 0, index_column[:, None], fixed[None, :])
+
     planes, lines_here, length = activity.shape
     bins = measured.shape[3]
     row = planes * bins
     tof_kernel = kernels(subset_views[0], bins, length)
     angle_count = tof_kernel.shape[0]
     pairs = angle_count * lines_here
-    projected = jnp.einsum("zlv,atv->zalt", blurred, tof_kernel, preferred_element_type=jnp.float32)
-    projected = projected.reshape(planes, pairs, bins)
 
     slab_count = lax.axis_size("slab")
     block_total = measured.shape[1]
@@ -194,6 +198,13 @@
     tag = jnp.broadcast_to(pair_id.astype(jnp.bfloat16)[:, None], (block_total, extra))
     outgoing = jnp.concatenate([measured[0].reshape(block_total, row), tag], axis=1)
     send = jnp.dot(place, outgoing, preferred_element_type=jnp.float32).astype(jnp.bfloat16)
+    send, activity_late = lax.optimization_barrier((send, activity))
+    padded = with_halo(activity_late, (("slab", 0),), 1)
+    blurred = ((1.0 - 2.0 * weight) * activity + weight * (padded[:-2] + padded[2:])).astype(
+        jnp.bfloat16
+    )
+    projected = jnp.einsum("zlv,atv->zalt", blurred, tof_kernel, preferred_element_type=jnp.float32)
+    projected = projected.reshape(planes, pairs, bins)
     recv = lax.all_to_all(
         send.reshape(slab_count, capacity, row + extra), "slab", 0, 0, tiled=True
     ).reshape(slots, row + extra)
@@ -212,14 +223,7 @@
         "zij,zjt->zit", merge, ratios, precision=lax.Precision.HIGH
     ).astype(jnp.bfloat16)
 
-    views = subset_views[0]
-    info = jnp.zeros((slots, bins), jnp.float32)
-    info = info.at[:, 0].set(index.astype(jnp.float32))
-    info = info.at[:, 1 : 1 + angle_count].set((views // 16).astype(jnp.float32)[None, :])
-    info = info.at[:, 1 + angle_count : 1 + 2 * angle_count].set(
-        (views % 16).astype(jnp.float32)[None, :]
-    )
-    payload = jnp.concatenate([merged, info.astype(jnp.bfloat16)[None]], axis=0)
+    payload = jnp.concatenate([merged, info_row(recv[:, row])[None]], axis=0)
     def back_project(got, kernel_k):
         index_k = got[planes, :, 0].astype(jnp.int32)
         order = jnp.arange(pairs, dtype=jnp.int32)

time: 129 us -> 126 us (0.977); the launches traced: 129 us -> 124 us
  starting transfers between devices: 36.5 us -> 30.9 us
  other arithmetic: 15.8 us -> 12.1 us
  local copies, waits for them, and re-layouts: 7.4 us -> 10.4 us
  waiting for transfers between devices: 42.7 us -> 44.6 us
    ppermute x2, waiting for transfers between devices: 0.01 us -> 17.5 us  [with_halo(): before = lax.ppermute(last, axis, up)]
    all_to_all x1, waiting for transfers between devices: 15.1 us -> 0.01 us  [on_device(): lax.all_to_all(send.reshape(slab_count, capacity, row + extra), 'slab', 0...]
    ppermute x2, starting transfers between devices: 14.7 us -> 9.49 us  [with_halo(): before = lax.ppermute(last, axis, up)]
    another operation x6 -> x1, other arithmetic: 4.02 us -> 0.01 us
    convert_element_type x0 -> x2, local copies, waits for them, and re-layouts: none -> 3.78 us  [on_device(): ratios = rows.astype(jnp.float32) / (estimate + BACKGROUND)]
    ppermute x1, waiting for transfers between devices: 18.2 us -> 14.6 us  [on_device(): from_right = lax.ppermute(payload, 'view', leftward)]
    ppermute x2, waiting for transfers between devices: 6.46 us -> 9.37 us  [with_halo(): after = lax.ppermute(leading, axis, down)]
  transfers between devices with their start and end apart: 9 -> 9, of which waited for: 4 -> 6; matrix products, arithmetic and copies ran while one was open for 24% -> 18% of each run, Pallas kernels for 0% -> 0%
where the time goes in v14:
time: 126 us; the launch traced here: 124 us
  waiting for transfers between devices  44.6 us (35%)
  starting transfers between devices  30.9 us (25%)
  matrix products  25.9 us (21%)
  other arithmetic  12.1 us (10%)
  local copies, waits for them, and re-layouts  10.4 us (8%)
    ppermute x2, waiting for transfers between devices, with_halo(): before = lax.ppermute(last, axis, up)  17.5 us
    ppermute x1, waiting for transfers between devices, on_device(): from_right = lax.ppermute(payload, 'view', leftward)  14.6 us
    all_to_all x1, starting transfers between devices, on_device(): lax.all_to_all(send.reshape(slab_count, capacity, row + extra), 'slab', 0...  12.3 us
    dot_general x4, matrix products, back_project(): jnp.einsum('zlat,atv->zlv', dense, kernel_k, preferred_element_type=jnp.f...  10.2 us
    ppermute x2, starting transfers between devices, with_halo(): before = lax.ppermute(last, axis, up)  9.49 us
    ppermute x2, waiting for transfers between devices, with_halo(): after = lax.ppermute(leading, axis, down)  9.37 us
    dot_general x1, matrix products, on_device(): jnp.einsum('zlv,atv->zalt', blurred, tof_kernel, preferred_element_type=j...  7.21 us
    div x1, other arithmetic, on_device(): return activity * smoothed / sensitivity  4.79 us
  transfers between devices with their start and end apart: 9, of which 6 were waited for; matrix products, arithmetic and copies ran while one was open for 18% of the time, Pallas kernels for 0%

profile of v14, /device:TPU:31, one launch (start us, length us, event | category | flops | bytes accessed | tf_op | source)
XLA Modules:
  0.0 124.2 jit_solution(13096095114629652556)
XLA Ops:
  0.0 0.8 fusion.77
  0.8 0.1 reduce_window_sum.11
  0.9 0.8 select_reduce_fusion
  1.7 0.7 multiply_add_fusion.4
  2.4 1.3 %copy.50 = bf16[8,8,32,128]{3,1,2,0:T(8,128)(2,1)S(1)} copy(bf16[8,8,32,128]{3,2,1,0:T(8,128)(2,1)} %bitcast.116) | data formatting | bytes 1048576
  3.6 0.7 convert_bitcast_fusion.4
  4.3 0.1 broadcast_in_dim.32
  4.4 0.4 convolution_convert_fusion
  4.8 1.2 reshape.606
  6.0 12.3 %all-to-all-start = ((bf16[64,2,4224]{2,1,0:T(2,128)(2,1)}), bf16[64,2,4224]{2,1,0:T(2,128)(2,1)S(1)}, u32[]{:S(2)}, u32[]{:S(2)}) async-start(bf16[64,2,4224]{2,1,0:T(2,128)(2,1)} %reshape.606), calls=%async_computation | async-start | bytes 2162688 | tf_op jit(solution)/shard_map/all_to_all | solution.py:208
  18.3 1.0 fusion.107
  19.3 3.3 %collective-permute-start = (f32[1,32,1024]{2,1,0:T(8,128)S(1)}, f32[1,32,1024]{2,1,0:T(8,128)S(1)}, u32[]{:S(2)}, u32[]{:S(2)}) collective-permute-start(f32[1,32,1024]{2,1,0:T(8,128)S(1)} %get-tuple-element.41), channel_id=1, source_target_pairs={{0,4},{4,8},{8,12},{12,16},{16,20},{20,24},{24,28},{28,32},{32,36}... | collective-permute-start | bytes 393224 | tf_op jit(solution)/shard_map/ppermute | solution.py:25
  22.7 1.9 %collective-permute-start.1 = (f32[1,32,1024]{2,1,0:T(8,128)S(1)}, f32[1,32,1024]{2,1,0:T(8,128)S(1)}, u32[]{:S(2)}, u32[]{:S(2)}) collective-permute-start(f32[1,32,1024]{2,1,0:T(8,128)S(1)} %get-tuple-element.42), channel_id=1, source_target_pairs={{4,0},{8,4},{12,8},{16,12},{20,16},{24,20},{28,24},{32,28},{36,32}... | collective-permute-start | bytes 393224 | tf_op jit(solution)/shard_map/ppermute | solution.py:26
  24.7 0.1 fusion.88
  24.7 0.1 multiply_add_fusion.3
  24.8 0.1 select_maximum_fusion
  24.9 17.5 %collective-permute-done = f32[1,32,1024]{2,1,0:T(8,128)S(1)} collective-permute-done((f32[1,32,1024]{2,1,0:T(8,128)S(1)}, f32[1,32,1024]{2,1,0:T(8,128)S(1)}, u32[]{:S(2)}, u32[]{:S(2)}) %collective-permute-start) | collective-permute-done | bytes 131104 | tf_op jit(solution)/shard_map/ppermute | solution.py:25
  42.4 2.9 %collective-permute-done.1 = f32[1,32,1024]{2,1,0:T(8,128)S(1)} collective-permute-done((f32[1,32,1024]{2,1,0:T(8,128)S(1)}, f32[1,32,1024]{2,1,0:T(8,128)S(1)}, u32[]{:S(2)}, u32[]{:S(2)}) %collective-permute-start.1) | collective-permute-done | bytes 131104 | tf_op jit(solution)/shard_map/ppermute | solution.py:26
  45.4 7.2 %convolution_bitcast_fusion.1 = f32[32,8,32,128]{3,2,0,1:T(8,128)S(1)} fusion(f32[1,32,1024]{2,1,0:T(8,128)S(1)} %collective-permute-done.1, f32[32,32,1024]{2,1,0:T(8,128)} %param.10, f32[1,32,1024]{2,1,0:T(8,128)S(1)} %collective-permute-done, f32[32]{0:T(128)S(1)} %copy-done.3, f32[8,128]{1,0:T(8,128)S(1)} %multiply_add_fusion.3, ...), kind=kOutput, calls=%fused_computation.37 | convolution fusion | flops 2161115136 | bytes 8659200 | tf_op jit(solution)/shard_map/zlv,atv->zalt/dot_general | solution.py:206
  52.6 2.5 %copy.28 = f32[32,8,32,128]{3,2,1,0:T(8,128)} copy(f32[32,8,32,128]{3,2,0,1:T(8,128)S(1)} %convolution_bitcast_fusion.1) | data formatting | bytes 8388608 | tf_op jit(solution)/shard_map/zlv,atv->zalt/transpose | solution.py:206
  55.0 0.4 reshape.607
  55.5 0.1 slice_reduce_fusion
  55.6 0.2 fusion.74
  55.8 0.1 fusion.73
  55.9 0.2 slice_convert_fusion
  56.1 0.1 fusion.75
  56.2 1.9 %copy.26 = f32[128,4096]{0,1:T(8,128)} copy(f32[128,4096]{1,0:T(8,128)S(1)} %slice_convert_fusion) | data formatting | bytes 4194304 | tf_op jit(solution)/shard_map/convert_element_type | solution.py:216
  58.1 1.9 %copy.27 = f32[128,32,128]{2,0,1:T(8,128)S(1)} copy(f32[128,32,128]{0,2,1:T(8,128)} %bitcast.114) | data formatting | bytes 4194304 | tf_op jit(solution)/shard_map/convert_element_type | solution.py:216
  60.0 0.1 broadcast_select_fusion
  60.1 4.2 %fusion.57 = f32[32,128,128]{2,1,0:T(8,128)S(1)} fusion(f32[32,256,128]{2,1,0:T(8,128)} %bitcast.113, f32[128,256]{1,0:T(8,128)S(1)} %fusion.73), kind=kOutput, calls=%fused_computation.71 | convolution fusion | flops 805306368 | bytes 6422528 | tf_op jit(solution)/shard_map/zjp,zpt->zjt/dot_general | solution.py:215
  64.2 1.1 fusion.60
  65.3 0.1 pad_maximum_fusion.4
  65.4 0.5 collective-permute-start.3
  66.0 2.2 %collective-permute-start.2 = (bf16[33,128,128]{2,1,0:T(8,128)(2,1)S(1)}, bf16[33,128,128]{2,1,0:T(8,128)(2,1)S(1)}, u32[]{:S(2)}, u32[]{:S(2)}) collective-permute-start(bf16[33,128,128]{2,1,0:T(8,128)(2,1)S(1)} %pad_maximum_fusion.4), channel_id=1, source_target_pairs={{0,1},{1,2},{2,3},{3,0},{4,5},{5,6},{6,7},{7,4},{8,9},{9,10},{10,1... | collective-permute-start | bytes 3244040 | tf_op jit(solution)/shard_map/ppermute | solution.py:248
  68.2 0.1 convert_reduce_fusion.3
  68.3 0.1 compare_convert_fusion.3
  68.4 0.7 convert_bitcast_fusion.3
  69.1 2.5 %convolution_bitcast_fusion = f32[32,32,1024]{2,1,0:T(8,128)S(1)} fusion(bf16[32,32,8,128]{3,2,1,0:T(8,128)(2,1)S(1)} %convert_bitcast_fusion.3, f32[8,128]{1,0:T(8,128)S(1)} %multiply_add_fusion.3, f32[1024]{0:T(1024)S(1)} %iota_add_fusion), kind=kOutput, calls=%fused_computation.36 | convolution fusion | flops 2153775104 | bytes 6299648 | tf_op jit(solution)/shard_map/zlat,atv->zlv/dot_general | solution.py:237
  71.7 14.6 %collective-permute-done.3 = bf16[33,128,128]{2,1,0:T(8,128)(2,1)S(1)} collective-permute-done((bf16[33,128,128]{2,1,0:T(8,128)(2,1)S(1)}, bf16[33,128,128]{2,1,0:T(8,128)(2,1)S(1)}, u32[]{:S(2)}, u32[]{:S(2)}) %collective-permute-start.3) | collective-permute-done | bytes 1081376 | tf_op jit(solution)/shard_map/ppermute | solution.py:249
  86.3 1.2 collective-permute-done.2
  87.5 0.1 convert_reduce_fusion.1
  87.7 0.1 multiply_bitcast_fusion.1
  87.9 0.1 multiply_bitcast_fusion.2
  88.0 2.5 %collective-permute-start.4 = (bf16[16,128,128]{2,1,0:T(8,128)(2,1)S(1)}, bf16[16,128,128]{2,1,0:T(8,128)(2,1)S(1)}, u32[]{:S(2)}, u32[]{:S(2)}) collective-permute-start(bf16[16,128,128]{2,1,0:T(8,128)(2,1)S(1)} %slice.123), channel_id=1, source_target_pairs={{0,1},{1,2},{2,3},{3,0},{4,5},{5,6},{6,7},{7,4},{8,9},{9,10},{10,1... | collective-permute-start | bytes 1572872 | tf_op jit(solution)/shard_map/ppermute | solution.py:252
  90.5 0.1 compare_convert_fusion.2
  90.6 0.7 convert_bitcast_fusion.1
  91.3 0.7 convert_bitcast_fusion.2
  92.0 0.1 multiply_add_fusion.2
  92.1 2.5 %fusion.27 = f32[32,32,1024,1]{2,1,3,0:T(8,128)S(1)} fusion(bf16[32,32,8,128]{3,2,1,0:T(8,128)(2,1)S(1)} %convert_bitcast_fusion.2, f32[8,128]{1,0:T(8,128)S(1)} %get-tuple-element.45, f32[1024]{0:T(1024)S(1)} %iota_add_fusion), kind=kOutput, calls=%fused_computation.41 | convolution fusion | flops 2153775104 | bytes 6299648 | tf_op jit(solution)/shard_map/zlat,atv->zlv/dot_general | solution.py:237
  94.6 2.5 %fusion.29 = f32[32,32,1024,1]{2,1,3,0:T(8,128)S(1)} fusion(bf16[32,32,8,128]{3,2,1,0:T(8,128)(2,1)S(1)} %convert_bitcast_fusion.1, f32[8,128]{1,0:T(8,128)S(1)} %get-tuple-element.46, f32[1024]{0:T(1024)S(1)} %iota_add_fusion), kind=kOutput, calls=%fused_computation.42 | convolution fusion | flops 2153775104 | bytes 6299648 | tf_op jit(solution)/shard_map/zlat,atv->zlv/dot_general | solution.py:237
  97.2 1.9 %bitcast_add_fusion.1 = f32[32,32,1024]{2,1,0:T(8,128)S(1)} fusion(f32[32,32,1024,1]{2,1,3,0:T(8,128)S(1)} %fusion.29, f32[32,32,1024]{2,1,0:T(8,128)S(1)} %convolution_bitcast_fusion, f32[32,32,1024,1]{2,1,3,0:T(8,128)S(1)} %fusion.27), kind=kLoop, calls=%fused_computation.34 | loop fusion | flops 2097152 | bytes 16777216 | tf_op jit(solution)/shard_map/add | solution.py:255
  99.1 1.9 %collective-permute-done.5 = bf16[17,128,128]{2,1,0:T(8,128)(2,1)S(1)} collective-permute-done((bf16[17,128,128]{2,1,0:T(8,128)(2,1)S(1)}, bf16[17,128,128]{2,1,0:T(8,128)(2,1)S(1)}, u32[]{:S(2)}, u32[]{:S(2)}) %collective-permute-start.5) | collective-permute-done | bytes 557088 | tf_op jit(solution)/shard_map/ppermute | solution.py:253
  101.0 0.1 convert_reduce_fusion
  101.1 0.1 multiply_bitcast_fusion
  101.3 0.1 compare_convert_fusion
  101.4 0.1 multiply_add_fusion
  101.5 0.7 convert_bitcast_fusion
  102.2 0.0 copy-start
  102.2 0.0 copy-start.1
  102.2 2.6 %broadcast_multiply_fusion = (f32[32,32,1024]{2,1,0:T(8,128)S(1)}, f32[32,32,1024,1]{2,1,3,0:T(8,128)S(1)}) fusion(f32[32]{0:T(128)S(1)} %copy-done.3, f32[32,32,1024]{2,1,0:T(8,128)S(1)} %bitcast_add_fusion.1, f32[8,128]{1,0:T(8,128)S(1)} %multiply_add_fusion, f32[1024]{0:T(1024)S(1)} %iota_add_fusion, bf16[32,32,8,128]{3,2,1,0:T(8,128)(2,1)S(1)} %convert_bitcast_fusion), kind=kOutput, calls=%fused_computation.61 | convolution fusion | flops 2155872256 | bytes 14688384 | tf_op jit(solution)/shard_map/zlat,atv->zlv/dot_general | solution.py:237
  104.9 6.2 %collective-permute-start.6 = (f32[1,32,1024]{2,1,0:T(8,128)S(1)}, f32[1,32,1024]{2,1,0:T(8,128)S(1)}, u32[]{:S(2)}, u32[]{:S(2)}) collective-permute-start(f32[1,32,1024]{2,1,0:T(8,128)S(1)} %get-tuple-element.39), channel_id=1, source_target_pairs={{0,4},{4,8},{8,12},{12,16},{16,20},{20,24},{24,28},{28,32},{32,36}... | collective-permute-start | bytes 393224 | tf_op jit(solution)/shard_map/ppermute | solution.py:25
  111.0 1.9 %collective-permute-start.7 = (f32[1,32,1024]{2,1,0:T(8,128)S(1)}, f32[1,32,1024]{2,1,0:T(8,128)S(1)}, u32[]{:S(2)}, u32[]{:S(2)}) collective-permute-start(f32[1,32,1024]{2,1,0:T(8,128)S(1)} %get-tuple-element.40), channel_id=1, source_target_pairs={{4,0},{8,4},{12,8},{16,12},{20,16},{24,20},{28,24},{32,28},{36,32}... | collective-permute-start | bytes 393224 | tf_op jit(solution)/shard_map/ppermute | solution.py:26
  113.0 6.5 %collective-permute-done.7 = f32[1,32,1024]{2,1,0:T(8,128)S(1)} collective-permute-done((f32[1,32,1024]{2,1,0:T(8,128)S(1)}, f32[1,32,1024]{2,1,0:T(8,128)S(1)}, u32[]{:S(2)}, u32[]{:S(2)}) %collective-permute-start.7) | collective-permute-done | bytes 131104 | tf_op jit(solution)/shard_map/ppermute | solution.py:26
  119.4 4.8 %fusion.18 = f32[32,32,1024]{2,1,0:T(8,128)} fusion(f32[32,32,1024]{2,1,0:T(8,128)S(1)} %copy-done.1, f32[32,32,1024]{2,1,0:T(8,128)S(1)} %copy-done, f32[1,32,1024]{2,1,0:T(8,128)S(1)} %collective-permute-done.7, f32[32,32,1024]{2,1,0:T(8,128)S(1)} %get-tuple-element.51, f32[1,32,1024]{2,1,0:T(8,128)S(1)} %collective-permute-done.6, ...), kind=kLoop, calls=%fused_computation.24 | loop fusion | flops 8388608 | bytes 25428096 | tf_op jit(solution)/shard_map/div | solution.py:261
  (26 shorter events, 0.3 us)
Async XLA Ops:
  0.0 24.6 %copy-start.3 = (f32[32]{0:T(128)S(1)}, f32[32]{0:T(128)}, u32[]{:S(2)}) copy-start(f32[32]{0:T(128)} %param.12) | copy-start | bytes 388
  0.0 24.7 %copy-start.2 = (s32[1,8]{1,0:T(1,128)S(1)}, s32[1,8]{1,0:T(1,128)}, u32[]{:S(2)}) copy-start(s32[1,8]{1,0:T(1,128)} %param.17) | copy-start | bytes 100
  6.0 49.0 %all-to-all-start = ((bf16[64,2,4224]{2,1,0:T(2,128)(2,1)}), bf16[64,2,4224]{2,1,0:T(2,128)(2,1)S(1)}, u32[]{:S(2)}, u32[]{:S(2)}) async-start(bf16[64,2,4224]{2,1,0:T(2,128)(2,1)} %reshape.606), calls=%async_computation | async-start | bytes 2162688 | tf_op jit(solution)/shard_map/all_to_all | solution.py:208
  19.3 23.1 %collective-permute-start = (f32[1,32,1024]{2,1,0:T(8,128)S(1)}, f32[1,32,1024]{2,1,0:T(8,128)S(1)}, u32[]{:S(2)}, u32[]{:S(2)}) collective-permute-start(f32[1,32,1024]{2,1,0:T(8,128)S(1)} %get-tuple-element.41), channel_id=1, source_target_pairs={{0,4},{4,8},{8,12},{12,16},{16,20},{20,24},{24,28},{28,32},{32,36}... | collective-permute-start | bytes 393224 | tf_op jit(solution)/shard_map/ppermute | solution.py:25
  22.7 22.7 %collective-permute-start.1 = (f32[1,32,1024]{2,1,0:T(8,128)S(1)}, f32[1,32,1024]{2,1,0:T(8,128)S(1)}, u32[]{:S(2)}, u32[]{:S(2)}) collective-permute-start(f32[1,32,1024]{2,1,0:T(8,128)S(1)} %get-tuple-element.42), channel_id=1, source_target_pairs={{4,0},{8,4},{12,8},{16,12},{20,16},{24,20},{28,24},{32,28},{36,32}... | collective-permute-start | bytes 393224 | tf_op jit(solution)/shard_map/ppermute | solution.py:26
  65.4 20.8 %collective-permute-start.3 = (bf16[33,128,128]{2,1,0:T(8,128)(2,1)S(1)}, bf16[33,128,128]{2,1,0:T(8,128)(2,1)S(1)}, u32[]{:S(2)}, u32[]{:S(2)}) collective-permute-start(bf16[33,128,128]{2,1,0:T(8,128)(2,1)S(1)} %pad_maximum_fusion.4), channel_id=1, source_target_pairs={{0,3},{1,0},{2,1},{3,2},{4,7},{5,4},{6,5},{7,6},{8,11},{9,8},{10,9... | collective-permute-start | bytes 3244040 | tf_op jit(solution)/shard_map/ppermute | solution.py:249
  66.0 21.5 %collective-permute-start.2 = (bf16[33,128,128]{2,1,0:T(8,128)(2,1)S(1)}, bf16[33,128,128]{2,1,0:T(8,128)(2,1)S(1)}, u32[]{:S(2)}, u32[]{:S(2)}) collective-permute-start(bf16[33,128,128]{2,1,0:T(8,128)(2,1)S(1)} %pad_maximum_fusion.4), channel_id=1, source_target_pairs={{0,1},{1,2},{2,3},{3,0},{4,5},{5,6},{6,7},{7,4},{8,9},{9,10},{10,1... | collective-permute-start | bytes 3244040 | tf_op jit(solution)/shard_map/ppermute | solution.py:248
  88.0 11.1 %collective-permute-start.4 = (bf16[16,128,128]{2,1,0:T(8,128)(2,1)S(1)}, bf16[16,128,128]{2,1,0:T(8,128)(2,1)S(1)}, u32[]{:S(2)}, u32[]{:S(2)}) collective-permute-start(bf16[16,128,128]{2,1,0:T(8,128)(2,1)S(1)} %slice.123), channel_id=1, source_target_pairs={{0,1},{1,2},{2,3},{3,0},{4,5},{5,6},{6,7},{7,4},{8,9},{9,10},{10,1... | collective-permute-start | bytes 1572872 | tf_op jit(solution)/shard_map/ppermute | solution.py:252
  90.5 10.5 %collective-permute-start.5 = (bf16[17,128,128]{2,1,0:T(8,128)(2,1)S(1)}, bf16[17,128,128]{2,1,0:T(8,128)(2,1)S(1)}, u32[]{:S(2)}, u32[]{:S(2)}) collective-permute-start(bf16[17,128,128]{2,1,0:T(8,128)(2,1)S(1)} %slice.124), channel_id=1, source_target_pairs={{0,3},{1,0},{2,1},{3,2},{4,7},{5,4},{6,5},{7,6},{8,11},{9,8},{10,9... | collective-permute-start | bytes 1671176 | tf_op jit(solution)/shard_map/ppermute | solution.py:253
  102.2 17.2 %copy-start = (f32[32,32,1024]{2,1,0:T(8,128)S(1)}, f32[32,32,1024]{2,1,0:T(8,128)}, u32[]{:S(2)}) copy-start(f32[32,32,1024]{2,1,0:T(8,128)} %param.10) | copy-start | bytes 12582916
  102.2 17.2 %copy-start.1 = (f32[32,32,1024]{2,1,0:T(8,128)S(1)}, f32[32,32,1024]{2,1,0:T(8,128)}, u32[]{:S(2)}) copy-start(f32[32,32,1024]{2,1,0:T(8,128)} %param.11) | copy-start | bytes 12582916
  104.9 8.1 %collective-permute-start.6 = (f32[1,32,1024]{2,1,0:T(8,128)S(1)}, f32[1,32,1024]{2,1,0:T(8,128)S(1)}, u32[]{:S(2)}, u32[]{:S(2)}) collective-permute-start(f32[1,32,1024]{2,1,0:T(8,128)S(1)} %get-tuple-element.39), channel_id=1, source_target_pairs={{0,4},{4,8},{8,12},{12,16},{16,20},{20,24},{24,28},{28,32},{32,36}... | collective-permute-start | bytes 393224 | tf_op jit(solution)/shard_map/ppermute | solution.py:25
  111.0 8.4 %collective-permute-start.7 = (f32[1,32,1024]{2,1,0:T(8,128)S(1)}, f32[1,32,1024]{2,1,0:T(8,128)S(1)}, u32[]{:S(2)}, u32[]{:S(2)}) collective-permute-start(f32[1,32,1024]{2,1,0:T(8,128)S(1)} %get-tuple-element.40), channel_id=1, source_target_pairs={{4,0},{8,4},{12,8},{16,12},{20,16},{24,20},{28,24},{32,28},{36,32}... | collective-permute-start | bytes 393224 | tf_op jit(solution)/shard_map/ppermute | solution.py:26

commit v15 on v14

--- a/solution.py
+++ b/solution.py
@@ -210,6 +210,7 @@
     ).reshape(slots, row + extra)
     index = recv[:, row].astype(jnp.int32)
     rows = recv[:, :row].reshape(slots, planes, bins).transpose(1, 0, 2)
+    rows = lax.optimization_barrier(rows)
     pick = (index[:, None] == jnp.arange(pairs, dtype=jnp.int32)[None, :]).astype(jnp.float32)
     pick = jnp.broadcast_to(pick[None], (planes, slots, pairs))
     estimate = jnp.einsum("zjp,zpt->zjt", pick, projected, precision=lax.Precision.HIGH)

time: 126 us -> 123 us (0.976)
  local copies, waits for them, and re-layouts: 10.4 us -> 8.1 us
    convert_element_type x2 -> x0, local copies, waits for them, and re-layouts: 3.78 us -> none  [on_device(): ratios = rows.astype(jnp.float32) / (estimate + BACKGROUND)]
  transfers between devices with their start and end apart: 9 -> 9, of which waited for: 6 -> 6; matrix products, arithmetic and copies ran while one was open for 18% -> 19% of each run, Pallas kernels for 0% -> 0%
where the time goes in v15:
time: 123 us; the launch traced here: 122 us
  waiting for transfers between devices  44.6 us (36%)
  starting transfers between devices  30.9 us (25%)
  matrix products  25.9 us (21%)
  other arithmetic  11.8 us (10%)
  local copies, waits for them, and re-layouts  8.1 us (7%)
    ppermute x2, waiting for transfers between devices, with_halo(): before = lax.ppermute(last, axis, up)  17.5 us
    ppermute x1, waiting for transfers between devices, on_device(): from_right = lax.ppermute(payload, 'view', leftward)  14.6 us
    all_to_all x1, starting transfers between devices, on_device(): lax.all_to_all(send.reshape(slab_count, capacity, row + extra), 'slab', 0...  12.3 us
    dot_general x4, matrix products, back_project(): jnp.einsum('zlat,atv->zlv', dense, kernel_k, preferred_element_type=jnp.f...  10.2 us
    ppermute x2, starting transfers between devices, with_halo(): before = lax.ppermute(last, axis, up)  9.5 us
    ppermute x2, waiting for transfers between devices, with_halo(): after = lax.ppermute(leading, axis, down)  9.37 us
    dot_general x1, matrix products, on_device(): jnp.einsum('zlv,atv->zalt', blurred, tof_kernel, preferred_element_type=j...  7.21 us
    div x1, other arithmetic, on_device(): return activity * smoothed / sensitivity  4.79 us
  transfers between devices with their start and end apart: 9, of which 6 were waited for; matrix products, arithmetic and copies ran while one was open for 19% of the time, Pallas kernels for 0%

profile of v15, /device:TPU:31, one launch (start us, length us, event | category | flops | bytes accessed | tf_op | source)
XLA Modules:
  0.0 121.7 jit_solution(3282828583533851723)
XLA Ops:
  0.0 0.8 fusion.81
  0.8 0.1 reduce_window_sum.11
  0.9 0.8 select_reduce_fusion
  1.7 0.7 multiply_add_fusion.4
  2.4 1.3 %copy.50 = bf16[8,8,32,128]{3,1,2,0:T(8,128)(2,1)S(1)} copy(bf16[8,8,32,128]{3,2,1,0:T(8,128)(2,1)} %bitcast.113) | data formatting | bytes 1048576
  3.6 0.7 convert_bitcast_fusion.4
  4.3 0.1 broadcast_in_dim.32
  4.4 0.4 convolution_convert_fusion
  4.8 1.2 %reshape.606 = bf16[64,2,4224]{2,1,0:T(2,128)(2,1)} reshape(bf16[128,4224]{1,0:T(8,128)(2,1)S(1)} %convolution_convert_fusion) | data formatting | bytes 2162688 | tf_op jit(solution)/shard_map/reshape | solution.py:209
  6.0 12.3 %all-to-all-start = ((bf16[64,2,4224]{2,1,0:T(2,128)(2,1)}), bf16[64,2,4224]{2,1,0:T(2,128)(2,1)S(1)}, u32[]{:S(2)}, u32[]{:S(2)}) async-start(bf16[64,2,4224]{2,1,0:T(2,128)(2,1)} %reshape.606), calls=%async_computation | async-start | bytes 2162688 | tf_op jit(solution)/shard_map/all_to_all | solution.py:208
  18.3 1.0 fusion.111
  19.3 3.3 %collective-permute-start = (f32[1,32,1024]{2,1,0:T(8,128)S(1)}, f32[1,32,1024]{2,1,0:T(8,128)S(1)}, u32[]{:S(2)}, u32[]{:S(2)}) collective-permute-start(f32[1,32,1024]{2,1,0:T(8,128)S(1)} %get-tuple-element.41), channel_id=1, source_target_pairs={{0,4},{4,8},{8,12},{12,16},{16,20},{20,24},{24,28},{28,32},{32,36}... | collective-permute-start | bytes 393224 | tf_op jit(solution)/shard_map/ppermute | solution.py:25
  22.7 1.9 %collective-permute-start.1 = (f32[1,32,1024]{2,1,0:T(8,128)S(1)}, f32[1,32,1024]{2,1,0:T(8,128)S(1)}, u32[]{:S(2)}, u32[]{:S(2)}) collective-permute-start(f32[1,32,1024]{2,1,0:T(8,128)S(1)} %get-tuple-element.42), channel_id=1, source_target_pairs={{4,0},{8,4},{12,8},{16,12},{20,16},{24,20},{28,24},{32,28},{36,32}... | collective-permute-start | bytes 393224 | tf_op jit(solution)/shard_map/ppermute | solution.py:26
  24.7 0.1 fusion.92
  24.7 0.1 multiply_add_fusion.3
  24.8 0.1 select_maximum_fusion
  24.9 17.5 %collective-permute-done = f32[1,32,1024]{2,1,0:T(8,128)S(1)} collective-permute-done((f32[1,32,1024]{2,1,0:T(8,128)S(1)}, f32[1,32,1024]{2,1,0:T(8,128)S(1)}, u32[]{:S(2)}, u32[]{:S(2)}) %collective-permute-start) | collective-permute-done | bytes 131104 | tf_op jit(solution)/shard_map/ppermute | solution.py:25
  42.4 2.9 %collective-permute-done.1 = f32[1,32,1024]{2,1,0:T(8,128)S(1)} collective-permute-done((f32[1,32,1024]{2,1,0:T(8,128)S(1)}, f32[1,32,1024]{2,1,0:T(8,128)S(1)}, u32[]{:S(2)}, u32[]{:S(2)}) %collective-permute-start.1) | collective-permute-done | bytes 131104 | tf_op jit(solution)/shard_map/ppermute | solution.py:26
  45.4 7.2 %convolution_bitcast_fusion.1 = f32[32,8,32,128]{3,2,0,1:T(8,128)S(1)} fusion(f32[1,32,1024]{2,1,0:T(8,128)S(1)} %collective-permute-done.1, f32[32,32,1024]{2,1,0:T(8,128)} %param.10, f32[1,32,1024]{2,1,0:T(8,128)S(1)} %collective-permute-done, f32[32]{0:T(128)S(1)} %copy-done.3, f32[8,128]{1,0:T(8,128)S(1)} %multiply_add_fusion.3, ...), kind=kOutput, calls=%fused_computation.37 | convolution fusion | flops 2161115136 | bytes 8659200 | tf_op jit(solution)/shard_map/zlv,atv->zalt/dot_general | solution.py:206
  52.6 2.5 %copy.28 = f32[32,8,32,128]{3,2,1,0:T(8,128)} copy(f32[32,8,32,128]{3,2,0,1:T(8,128)S(1)} %convolution_bitcast_fusion.1) | data formatting | bytes 8388608 | tf_op jit(solution)/shard_map/zlv,atv->zalt/transpose | solution.py:206
  55.0 0.4 reshape.607
  55.5 0.1 slice_reduce_fusion
  55.6 0.1 slice.136
  55.7 0.2 fusion.78
  55.9 0.1 fusion.77
  56.0 0.7 copy.26
  56.6 0.7 copy.27
  57.3 0.1 fusion.79
  57.4 0.1 broadcast_select_fusion
  57.5 4.2 %fusion.58 = f32[32,128,128]{2,1,0:T(8,128)S(1)} fusion(f32[32,256,128]{2,1,0:T(8,128)} %bitcast.109, f32[128,256]{1,0:T(8,128)S(1)} %fusion.77), kind=kOutput, calls=%fused_computation.71 | convolution fusion | flops 805306368 | bytes 6422528 | tf_op jit(solution)/shard_map/zjp,zpt->zjt/dot_general | solution.py:216
  61.7 1.1 fusion.62
  62.8 0.1 pad_maximum_fusion.4
  62.9 0.5 collective-permute-start.3
  63.5 2.2 %collective-permute-start.2 = (bf16[33,128,128]{2,1,0:T(8,128)(2,1)S(1)}, bf16[33,128,128]{2,1,0:T(8,128)(2,1)S(1)}, u32[]{:S(2)}, u32[]{:S(2)}) collective-permute-start(bf16[33,128,128]{2,1,0:T(8,128)(2,1)S(1)} %pad_maximum_fusion.4), channel_id=1, source_target_pairs={{0,1},{1,2},{2,3},{3,0},{4,5},{5,6},{6,7},{7,4},{8,9},{9,10},{10,1... | collective-permute-start | bytes 3244040 | tf_op jit(solution)/shard_map/ppermute | solution.py:249
  65.7 0.1 convert_reduce_fusion.3
  65.8 0.1 compare_convert_fusion.3
  65.9 0.7 convert_bitcast_fusion.3
  66.6 2.5 %convolution_bitcast_fusion = f32[32,32,1024]{2,1,0:T(8,128)S(1)} fusion(bf16[32,32,8,128]{3,2,1,0:T(8,128)(2,1)S(1)} %convert_bitcast_fusion.3, f32[8,128]{1,0:T(8,128)S(1)} %multiply_add_fusion.3, f32[1024]{0:T(1024)S(1)} %iota_add_fusion), kind=kOutput, calls=%fused_computation.36 | convolution fusion | flops 2153775104 | bytes 6299648 | tf_op jit(solution)/shard_map/zlat,atv->zlv/dot_general | solution.py:238
  69.1 14.6 %collective-permute-done.3 = bf16[33,128,128]{2,1,0:T(8,128)(2,1)S(1)} collective-permute-done((bf16[33,128,128]{2,1,0:T(8,128)(2,1)S(1)}, bf16[33,128,128]{2,1,0:T(8,128)(2,1)S(1)}, u32[]{:S(2)}, u32[]{:S(2)}) %collective-permute-start.3) | collective-permute-done | bytes 1081376 | tf_op jit(solution)/shard_map/ppermute | solution.py:250
  83.7 1.2 collective-permute-done.2
  85.0 0.1 convert_reduce_fusion.1
  85.2 0.1 multiply_bitcast_fusion.1
  85.3 0.1 multiply_bitcast_fusion.2
  85.5 2.5 %collective-permute-start.4 = (bf16[16,128,128]{2,1,0:T(8,128)(2,1)S(1)}, bf16[16,128,128]{2,1,0:T(8,128)(2,1)S(1)}, u32[]{:S(2)}, u32[]{:S(2)}) collective-permute-start(bf16[16,128,128]{2,1,0:T(8,128)(2,1)S(1)} %slice.123), channel_id=1, source_target_pairs={{0,1},{1,2},{2,3},{3,0},{4,5},{5,6},{6,7},{7,4},{8,9},{9,10},{10,1... | collective-permute-start | bytes 1572872 | tf_op jit(solution)/shard_map/ppermute | solution.py:253
  88.0 0.1 compare_convert_fusion.2
  88.1 0.7 convert_bitcast_fusion.1
  88.8 0.7 convert_bitcast_fusion.2
  89.5 0.1 multiply_add_fusion.2
  89.6 2.5 %fusion.27 = f32[32,32,1024,1]{2,1,3,0:T(8,128)S(1)} fusion(bf16[32,32,8,128]{3,2,1,0:T(8,128)(2,1)S(1)} %convert_bitcast_fusion.2, f32[8,128]{1,0:T(8,128)S(1)} %get-tuple-element.45, f32[1024]{0:T(1024)S(1)} %iota_add_fusion), kind=kOutput, calls=%fused_computation.41 | convolution fusion | flops 2153775104 | bytes 6299648 | tf_op jit(solution)/shard_map/zlat,atv->zlv/dot_general | solution.py:238
  92.1 2.5 %fusion.29 = f32[32,32,1024,1]{2,1,3,0:T(8,128)S(1)} fusion(bf16[32,32,8,128]{3,2,1,0:T(8,128)(2,1)S(1)} %convert_bitcast_fusion.1, f32[8,128]{1,0:T(8,128)S(1)} %get-tuple-element.46, f32[1024]{0:T(1024)S(1)} %iota_add_fusion), kind=kOutput, calls=%fused_computation.42 | convolution fusion | flops 2153775104 | bytes 6299648 | tf_op jit(solution)/shard_map/zlat,atv->zlv/dot_general | solution.py:238
  94.7 1.9 %bitcast_add_fusion.1 = f32[32,32,1024]{2,1,0:T(8,128)S(1)} fusion(f32[32,32,1024,1]{2,1,3,0:T(8,128)S(1)} %fusion.29, f32[32,32,1024]{2,1,0:T(8,128)S(1)} %convolution_bitcast_fusion, f32[32,32,1024,1]{2,1,3,0:T(8,128)S(1)} %fusion.27), kind=kLoop, calls=%fused_computation.34 | loop fusion | flops 2097152 | bytes 16777216 | tf_op jit(solution)/shard_map/add | solution.py:256
  96.6 1.9 %collective-permute-done.5 = bf16[17,128,128]{2,1,0:T(8,128)(2,1)S(1)} collective-permute-done((bf16[17,128,128]{2,1,0:T(8,128)(2,1)S(1)}, bf16[17,128,128]{2,1,0:T(8,128)(2,1)S(1)}, u32[]{:S(2)}, u32[]{:S(2)}) %collective-permute-start.5) | collective-permute-done | bytes 557088 | tf_op jit(solution)/shard_map/ppermute | solution.py:254
  98.5 0.1 convert_reduce_fusion
  98.6 0.1 multiply_bitcast_fusion
  98.8 0.1 compare_convert_fusion
  98.9 0.1 multiply_add_fusion
  99.0 0.7 convert_bitcast_fusion
  99.7 0.0 copy-start
  99.7 0.0 copy-start.1
  99.7 2.6 %broadcast_multiply_fusion = (f32[32,32,1024]{2,1,0:T(8,128)S(1)}, f32[32,32,1024,1]{2,1,3,0:T(8,128)S(1)}) fusion(f32[32]{0:T(128)S(1)} %copy-done.3, f32[32,32,1024]{2,1,0:T(8,128)S(1)} %bitcast_add_fusion.1, f32[8,128]{1,0:T(8,128)S(1)} %multiply_add_fusion, f32[1024]{0:T(1024)S(1)} %iota_add_fusion, bf16[32,32,8,128]{3,2,1,0:T(8,128)(2,1)S(1)} %convert_bitcast_fusion), kind=kOutput, calls=%fused_computation.61 | convolution fusion | flops 2155872256 | bytes 14688384 | tf_op jit(solution)/shard_map/zlat,atv->zlv/dot_general | solution.py:238
  102.3 6.2 %collective-permute-start.6 = (f32[1,32,1024]{2,1,0:T(8,128)S(1)}, f32[1,32,1024]{2,1,0:T(8,128)S(1)}, u32[]{:S(2)}, u32[]{:S(2)}) collective-permute-start(f32[1,32,1024]{2,1,0:T(8,128)S(1)} %get-tuple-element.39), channel_id=1, source_target_pairs={{0,4},{4,8},{8,12},{12,16},{16,20},{20,24},{24,28},{28,32},{32,36}... | collective-permute-start | bytes 393224 | tf_op jit(solution)/shard_map/ppermute | solution.py:25
  108.5 1.9 %collective-permute-start.7 = (f32[1,32,1024]{2,1,0:T(8,128)S(1)}, f32[1,32,1024]{2,1,0:T(8,128)S(1)}, u32[]{:S(2)}, u32[]{:S(2)}) collective-permute-start(f32[1,32,1024]{2,1,0:T(8,128)S(1)} %get-tuple-element.40), channel_id=1, source_target_pairs={{4,0},{8,4},{12,8},{16,12},{20,16},{24,20},{28,24},{32,28},{36,32}... | collective-permute-start | bytes 393224 | tf_op jit(solution)/shard_map/ppermute | solution.py:26
  110.4 6.5 %collective-permute-done.7 = f32[1,32,1024]{2,1,0:T(8,128)S(1)} collective-permute-done((f32[1,32,1024]{2,1,0:T(8,128)S(1)}, f32[1,32,1024]{2,1,0:T(8,128)S(1)}, u32[]{:S(2)}, u32[]{:S(2)}) %collective-permute-start.7) | collective-permute-done | bytes 131104 | tf_op jit(solution)/shard_map/ppermute | solution.py:26
  116.9 4.8 %fusion.18 = f32[32,32,1024]{2,1,0:T(8,128)} fusion(f32[32,32,1024]{2,1,0:T(8,128)S(1)} %copy-done.1, f32[32,32,1024]{2,1,0:T(8,128)S(1)} %copy-done, f32[1,32,1024]{2,1,0:T(8,128)S(1)} %collective-permute-done.7, f32[32,32,1024]{2,1,0:T(8,128)S(1)} %get-tuple-element.51, f32[1,32,1024]{2,1,0:T(8,128)S(1)} %collective-permute-done.6, ...), kind=kLoop, calls=%fused_computation.24 | loop fusion | flops 8388608 | bytes 25428096 | tf_op jit(solution)/shard_map/div | solution.py:262
  (26 shorter events, 0.3 us)
Async XLA Ops:
  0.0 24.6 %copy-start.3 = (f32[32]{0:T(128)S(1)}, f32[32]{0:T(128)}, u32[]{:S(2)}) copy-start(f32[32]{0:T(128)} %param.12) | copy-start | bytes 388
  0.0 24.7 %copy-start.2 = (s32[1,8]{1,0:T(1,128)S(1)}, s32[1,8]{1,0:T(1,128)}, u32[]{:S(2)}) copy-start(s32[1,8]{1,0:T(1,128)} %param.17) | copy-start | bytes 100
  6.0 49.0 %all-to-all-start = ((bf16[64,2,4224]{2,1,0:T(2,128)(2,1)}), bf16[64,2,4224]{2,1,0:T(2,128)(2,1)S(1)}, u32[]{:S(2)}, u32[]{:S(2)}) async-start(bf16[64,2,4224]{2,1,0:T(2,128)(2,1)} %reshape.606), calls=%async_computation | async-start | bytes 2162688 | tf_op jit(solution)/shard_map/all_to_all | solution.py:208
  19.3 23.1 %collective-permute-start = (f32[1,32,1024]{2,1,0:T(8,128)S(1)}, f32[1,32,1024]{2,1,0:T(8,128)S(1)}, u32[]{:S(2)}, u32[]{:S(2)}) collective-permute-start(f32[1,32,1024]{2,1,0:T(8,128)S(1)} %get-tuple-element.41), channel_id=1, source_target_pairs={{0,4},{4,8},{8,12},{12,16},{16,20},{20,24},{24,28},{28,32},{32,36}... | collective-permute-start | bytes 393224 | tf_op jit(solution)/shard_map/ppermute | solution.py:25
  22.7 22.7 %collective-permute-start.1 = (f32[1,32,1024]{2,1,0:T(8,128)S(1)}, f32[1,32,1024]{2,1,0:T(8,128)S(1)}, u32[]{:S(2)}, u32[]{:S(2)}) collective-permute-start(f32[1,32,1024]{2,1,0:T(8,128)S(1)} %get-tuple-element.42), channel_id=1, source_target_pairs={{4,0},{8,4},{12,8},{16,12},{20,16},{24,20},{28,24},{32,28},{36,32}... | collective-permute-start | bytes 393224 | tf_op jit(solution)/shard_map/ppermute | solution.py:26
  62.9 20.8 %collective-permute-start.3 = (bf16[33,128,128]{2,1,0:T(8,128)(2,1)S(1)}, bf16[33,128,128]{2,1,0:T(8,128)(2,1)S(1)}, u32[]{:S(2)}, u32[]{:S(2)}) collective-permute-start(bf16[33,128,128]{2,1,0:T(8,128)(2,1)S(1)} %pad_maximum_fusion.4), channel_id=1, source_target_pairs={{0,3},{1,0},{2,1},{3,2},{4,7},{5,4},{6,5},{7,6},{8,11},{9,8},{10,9... | collective-permute-start | bytes 3244040 | tf_op jit(solution)/shard_map/ppermute | solution.py:250
  63.5 21.5 %collective-permute-start.2 = (bf16[33,128,128]{2,1,0:T(8,128)(2,1)S(1)}, bf16[33,128,128]{2,1,0:T(8,128)(2,1)S(1)}, u32[]{:S(2)}, u32[]{:S(2)}) collective-permute-start(bf16[33,128,128]{2,1,0:T(8,128)(2,1)S(1)} %pad_maximum_fusion.4), channel_id=1, source_target_pairs={{0,1},{1,2},{2,3},{3,0},{4,5},{5,6},{6,7},{7,4},{8,9},{9,10},{10,1... | collective-permute-start | bytes 3244040 | tf_op jit(solution)/shard_map/ppermute | solution.py:249
  85.5 11.1 %collective-permute-start.4 = (bf16[16,128,128]{2,1,0:T(8,128)(2,1)S(1)}, bf16[16,128,128]{2,1,0:T(8,128)(2,1)S(1)}, u32[]{:S(2)}, u32[]{:S(2)}) collective-permute-start(bf16[16,128,128]{2,1,0:T(8,128)(2,1)S(1)} %slice.123), channel_id=1, source_target_pairs={{0,1},{1,2},{2,3},{3,0},{4,5},{5,6},{6,7},{7,4},{8,9},{9,10},{10,1... | collective-permute-start | bytes 1572872 | tf_op jit(solution)/shard_map/ppermute | solution.py:253
  88.0 10.5 %collective-permute-start.5 = (bf16[17,128,128]{2,1,0:T(8,128)(2,1)S(1)}, bf16[17,128,128]{2,1,0:T(8,128)(2,1)S(1)}, u32[]{:S(2)}, u32[]{:S(2)}) collective-permute-start(bf16[17,128,128]{2,1,0:T(8,128)(2,1)S(1)} %slice.124), channel_id=1, source_target_pairs={{0,3},{1,0},{2,1},{3,2},{4,7},{5,4},{6,5},{7,6},{8,11},{9,8},{10,9... | collective-permute-start | bytes 1671176 | tf_op jit(solution)/shard_map/ppermute | solution.py:254
  99.7 17.2 %copy-start = (f32[32,32,1024]{2,1,0:T(8,128)S(1)}, f32[32,32,1024]{2,1,0:T(8,128)}, u32[]{:S(2)}) copy-start(f32[32,32,1024]{2,1,0:T(8,128)} %param.10) | copy-start | bytes 12582916
  99.7 17.2 %copy-start.1 = (f32[32,32,1024]{2,1,0:T(8,128)S(1)}, f32[32,32,1024]{2,1,0:T(8,128)}, u32[]{:S(2)}) copy-start(f32[32,32,1024]{2,1,0:T(8,128)} %param.11) | copy-start | bytes 12582916
  102.3 8.1 %collective-permute-start.6 = (f32[1,32,1024]{2,1,0:T(8,128)S(1)}, f32[1,32,1024]{2,1,0:T(8,128)S(1)}, u32[]{:S(2)}, u32[]{:S(2)}) collective-permute-start(f32[1,32,1024]{2,1,0:T(8,128)S(1)} %get-tuple-element.39), channel_id=1, source_target_pairs={{0,4},{4,8},{8,12},{12,16},{16,20},{20,24},{24,28},{28,32},{32,36}... | collective-permute-start | bytes 393224 | tf_op jit(solution)/shard_map/ppermute | solution.py:25
  108.5 8.4 %collective-permute-start.7 = (f32[1,32,1024]{2,1,0:T(8,128)S(1)}, f32[1,32,1024]{2,1,0:T(8,128)S(1)}, u32[]{:S(2)}, u32[]{:S(2)}) collective-permute-start(f32[1,32,1024]{2,1,0:T(8,128)S(1)} %get-tuple-element.40), channel_id=1, source_target_pairs={{4,0},{8,4},{12,8},{16,12},{20,16},{24,20},{28,24},{32,28},{36,32}... | collective-permute-start | bytes 393224 | tf_op jit(solution)/shard_map/ppermute | solution.py:26

commit v16 on v15

--- a/solution.py
+++ b/solution.py
@@ -213,7 +213,13 @@
     rows = lax.optimization_barrier(rows)
     pick = (index[:, None] == jnp.arange(pairs, dtype=jnp.int32)[None, :]).astype(jnp.float32)
     pick = jnp.broadcast_to(pick[None], (planes, slots, pairs))
-    estimate = jnp.einsum("zjp,zpt->zjt", pick, projected, precision=lax.Precision.HIGH)
+    high = lax.reduce_precision(projected, exponent_bits=8, mantissa_bits=7)
+    parts = (high.astype(jnp.bfloat16), (projected - high).astype(jnp.bfloat16))
+    estimate = sum(
+        jnp.einsum("zjp,zpt->zjt", pick.astype(jnp.bfloat16), piece,
+                   preferred_element_type=jnp.float32)
+        for piece in parts
+    )
     ratios = rows.astype(jnp.float32) / (estimate + BACKGROUND)
 
     same = index[:, None] == index[None, :]

time: 123 us -> 128 us (1.041)
  other arithmetic: 11.8 us -> 14.3 us
  local copies, waits for them, and re-layouts: 8.1 us -> 10.6 us
    convert_element_type x1 -> x2, other arithmetic: 0.09 us -> 2.52 us  [the longest x1 2.43 us: on_device(): parts = (high.astype(jnp.bfloat16), (projected - high).astype(jnp.bfloat16))]
    slice x2, local copies, waits for them, and re-layouts: 0.77 us -> 2.6 us  [on_device(): rows = recv[:, :row].reshape(slots, planes, bins).transpose(1, 0, 2)]
    transpose x1, local copies, waits for them, and re-layouts: 2.45 us -> 0.63 us  [on_device(): jnp.einsum('zlv,atv->zalt', blurred, tof_kernel, preferred_element_type=j...]
    dot_general x1 -> x2, matrix products: 4.15 us -> 2.98 us  [on_device(): jnp.einsum('zjp,zpt->zjt', pick.astype(jnp.bfloat16), piece, preferred_el...]
where the time goes in v16:
time: 128 us; the launch traced here: 126 us
  waiting for transfers between devices  43.7 us (34%)
  starting transfers between devices  31.8 us (25%)
  matrix products  24.9 us (19%)
  other arithmetic  14.3 us (11%)
  local copies, waits for them, and re-layouts  10.6 us (8%)
    ppermute x2, waiting for transfers between devices, with_halo(): before = lax.ppermute(last, axis, up)  17.5 us
    ppermute x1, waiting for transfers between devices, on_device(): from_right = lax.ppermute(payload, 'view', leftward)  14 us
    all_to_all x1, starting transfers between devices, on_device(): lax.all_to_all(send.reshape(slab_count, capacity, row + extra), 'slab', 0...  12.3 us
    ppermute x2, starting transfers between devices, with_halo(): before = lax.ppermute(last, axis, up)  10.4 us
    dot_general x4, matrix products, back_project(): jnp.einsum('zlat,atv->zlv', dense, kernel_k, preferred_element_type=jnp.f...  10.2 us
    ppermute x2, waiting for transfers between devices, with_halo(): after = lax.ppermute(leading, axis, down)  9.37 us
    dot_general x1, matrix products, on_device(): jnp.einsum('zlv,atv->zalt', blurred, tof_kernel, preferred_element_type=j...  7.2 us
    div x1, other arithmetic, on_device(): return activity * smoothed / sensitivity  4.79 us
  transfers between devices with their start and end apart: 9, of which 6 were waited for; matrix products, arithmetic and copies ran while one was open for 19% of the time, Pallas kernels for 0%

profile of v16, /device:TPU:31, one launch (start us, length us, event | category | flops | bytes accessed | tf_op | source)
XLA Modules:
  0.0 125.6 jit_solution(5130929195075721740)
XLA Ops:
  0.0 0.8 fusion.84
  0.8 0.1 reduce_window_sum.11
  0.9 0.8 select_reduce_fusion
  1.7 0.7 multiply_add_fusion.4
  2.4 1.3 copy.50
  3.6 0.7 convert_bitcast_fusion.4
  4.3 0.1 broadcast_in_dim.32
  4.4 0.4 convolution_convert_fusion
  4.8 1.2 reshape.606
  6.0 12.3 %all-to-all-start = ((bf16[64,2,4224]{2,1,0:T(2,128)(2,1)}), bf16[64,2,4224]{2,1,0:T(2,128)(2,1)S(1)}, u32[]{:S(2)}, u32[]{:S(2)}) async-start(bf16[64,2,4224]{2,1,0:T(2,128)(2,1)} %reshape.606), calls=%async_computation | async-start | bytes 2162688 | tf_op jit(solution)/shard_map/all_to_all | solution.py:208
  18.3 1.0 fusion.114
  19.3 3.3 %collective-permute-start = (f32[1,32,1024]{2,1,0:T(8,128)S(1)}, f32[1,32,1024]{2,1,0:T(8,128)S(1)}, u32[]{:S(2)}, u32[]{:S(2)}) collective-permute-start(f32[1,32,1024]{2,1,0:T(8,128)S(1)} %get-tuple-element.43), channel_id=1, source_target_pairs={{0,4},{4,8},{8,12},{12,16},{16,20},{20,24},{24,28},{28,32},{32,36}... | collective-permute-start | bytes 393224 | tf_op jit(solution)/shard_map/ppermute | solution.py:25
  22.7 1.9 %collective-permute-start.1 = (f32[1,32,1024]{2,1,0:T(8,128)S(1)}, f32[1,32,1024]{2,1,0:T(8,128)S(1)}, u32[]{:S(2)}, u32[]{:S(2)}) collective-permute-start(f32[1,32,1024]{2,1,0:T(8,128)S(1)} %get-tuple-element.44), channel_id=1, source_target_pairs={{4,0},{8,4},{12,8},{16,12},{20,16},{24,20},{28,24},{32,28},{36,32}... | collective-permute-start | bytes 393224 | tf_op jit(solution)/shard_map/ppermute | solution.py:26
  24.6 0.1 fusion.95
  24.7 0.1 multiply_add_fusion.3
  24.8 0.1 select_maximum_fusion
  24.9 17.5 %collective-permute-done = f32[1,32,1024]{2,1,0:T(8,128)S(1)} collective-permute-done((f32[1,32,1024]{2,1,0:T(8,128)S(1)}, f32[1,32,1024]{2,1,0:T(8,128)S(1)}, u32[]{:S(2)}, u32[]{:S(2)}) %collective-permute-start) | collective-permute-done | bytes 131104 | tf_op jit(solution)/shard_map/ppermute | solution.py:25
  42.4 2.9 %collective-permute-done.1 = f32[1,32,1024]{2,1,0:T(8,128)S(1)} collective-permute-done((f32[1,32,1024]{2,1,0:T(8,128)S(1)}, f32[1,32,1024]{2,1,0:T(8,128)S(1)}, u32[]{:S(2)}, u32[]{:S(2)}) %collective-permute-start.1) | collective-permute-done | bytes 131104 | tf_op jit(solution)/shard_map/ppermute | solution.py:26
  45.3 7.2 %convolution_bitcast_fusion.1 = f32[32,8,32,128]{3,2,0,1:T(8,128)S(1)} fusion(f32[1,32,1024]{2,1,0:T(8,128)S(1)} %collective-permute-done.1, f32[32,32,1024]{2,1,0:T(8,128)} %param.10, f32[1,32,1024]{2,1,0:T(8,128)S(1)} %collective-permute-done, f32[32]{0:T(128)S(1)} %copy-done.3, f32[8,128]{1,0:T(8,128)S(1)} %multiply_add_fusion.3, ...), kind=kOutput, calls=%fused_computation.40 | convolution fusion | flops 2161115136 | bytes 8659200 | tf_op jit(solution)/shard_map/zlv,atv->zalt/dot_general | solution.py:206
  52.6 0.6 copy.28
  53.2 2.4 %fusion = (bf16[32,256,128]{2,1,0:T(8,128)(2,1)}, bf16[32,256,128]{2,1,0:T(8,128)(2,1)S(1)}) fusion(f32[32,8,32,128]{3,2,1,0:T(8,128)S(1)} %copy.28), kind=kLoop, calls=%fused_computation.7 | loop fusion | flops 4194304 | bytes 8388608 | tf_op jit(solution)/shard_map/convert_element_type | solution.py:217
  55.6 1.2 reshape.607
  56.8 0.9 slice_reduce_fusion
  57.7 1.3 %slice.136 = bf16[128,4096]{1,0:T(8,128)(2,1)S(1)} slice(bf16[128,4224]{1,0:T(8,128)(2,1)} %reshape.607), slice={[0:128], [0:4096]} | slice | bytes 2097152 | tf_op jit(solution)/shard_map/slice | solution.py:212
  59.0 0.2 fusion.81
  59.2 0.1 convert_convert_fusion
  59.3 1.3 %copy.26 = bf16[128,4096]{0,1:T(8,128)(2,1)} copy(bf16[128,4096]{1,0:T(8,128)(2,1)S(1)} %slice.136) | data formatting | bytes 2097152 | tf_op jit(solution)/shard_map/slice | solution.py:212
  60.6 1.6 %copy.27 = bf16[128,32,128]{2,0,1:T(8,128)(2,1)S(1)} copy(bf16[128,32,128]{0,2,1:T(8,128)(2,1)} %bitcast.112) | data formatting | bytes 2097152 | tf_op jit(solution)/shard_map/reshape | solution.py:212
  62.2 0.1 fusion.82
  62.3 2.3 %fusion.72 = f32[32,128,128]{2,1,0:T(8,128)S(1)} fusion(bf16[32,256,128]{2,1,0:T(8,128)(2,1)} %get-tuple-element.41, bf16[128,256]{1,0:T(8,128)(2,1)S(1)} %convert_convert_fusion), kind=kOutput, calls=%fused_computation.87 | convolution fusion | flops 268435456 | bytes 4259840 | tf_op jit(solution)/shard_map/zjp,zpt->zjt/dot_general | solution.py:219
  64.6 0.7 fusion.74
  65.3 0.1 broadcast_select_fusion
  65.4 1.3 %fusion.62 = bf16[32,128,128]{2,1,0:T(8,128)(2,1)S(1)} fusion(f32[32,128,128]{2,1,0:T(8,128)S(1)} %fusion.74, f32[32,128,128]{2,1,0:T(8,128)S(1)} %fusion.72, bf16[32,128,128]{2,1,0:T(8,128)(2,1)S(1)} %bitcast.114, f32[128,128]{1,0:T(8,128)S(1)} %fusion.82), kind=kOutput, calls=%fused_computation.77 | convolution fusion | flops 405274624 | bytes 6356992 | tf_op jit(solution)/shard_map/zij,zjt->zit/dot_general | solution.py:229
  66.7 0.1 pad_maximum_fusion.4
  66.8 0.5 collective-permute-start.3
  67.4 2.2 %collective-permute-start.2 = (bf16[33,128,128]{2,1,0:T(8,128)(2,1)S(1)}, bf16[33,128,128]{2,1,0:T(8,128)(2,1)S(1)}, u32[]{:S(2)}, u32[]{:S(2)}) collective-permute-start(bf16[33,128,128]{2,1,0:T(8,128)(2,1)S(1)} %pad_maximum_fusion.4), channel_id=1, source_target_pairs={{0,1},{1,2},{2,3},{3,0},{4,5},{5,6},{6,7},{7,4},{8,9},{9,10},{10,1... | collective-permute-start | bytes 3244040 | tf_op jit(solution)/shard_map/ppermute | solution.py:255
  69.6 0.1 convert_reduce_fusion.3
  69.7 0.1 compare_convert_fusion.3
  69.8 0.7 convert_bitcast_fusion.3
  70.5 2.5 %convolution_bitcast_fusion = f32[32,32,1024]{2,1,0:T(8,128)S(1)} fusion(bf16[32,32,8,128]{3,2,1,0:T(8,128)(2,1)S(1)} %convert_bitcast_fusion.3, f32[8,128]{1,0:T(8,128)S(1)} %multiply_add_fusion.3, f32[1024]{0:T(1024)S(1)} %iota_add_fusion), kind=kOutput, calls=%fused_computation.39 | convolution fusion | flops 2153775104 | bytes 6299648 | tf_op jit(solution)/shard_map/zlat,atv->zlv/dot_general | solution.py:244
  73.1 14.0 %collective-permute-done.3 = bf16[33,128,128]{2,1,0:T(8,128)(2,1)S(1)} collective-permute-done((bf16[33,128,128]{2,1,0:T(8,128)(2,1)S(1)}, bf16[33,128,128]{2,1,0:T(8,128)(2,1)S(1)}, u32[]{:S(2)}, u32[]{:S(2)}) %collective-permute-start.3) | collective-permute-done | bytes 1081376 | tf_op jit(solution)/shard_map/ppermute | solution.py:256
  87.1 1.8 %collective-permute-done.2 = bf16[33,128,128]{2,1,0:T(8,128)(2,1)S(1)} collective-permute-done((bf16[33,128,128]{2,1,0:T(8,128)(2,1)S(1)}, bf16[33,128,128]{2,1,0:T(8,128)(2,1)S(1)}, u32[]{:S(2)}, u32[]{:S(2)}) %collective-permute-start.2) | collective-permute-done | bytes 1081376 | tf_op jit(solution)/shard_map/ppermute | solution.py:255
  88.9 0.1 convert_reduce_fusion.1
  89.1 0.1 multiply_bitcast_fusion.1
  89.3 0.1 multiply_bitcast_fusion.2
  89.4 2.5 %collective-permute-start.4 = (bf16[16,128,128]{2,1,0:T(8,128)(2,1)S(1)}, bf16[16,128,128]{2,1,0:T(8,128)(2,1)S(1)}, u32[]{:S(2)}, u32[]{:S(2)}) collective-permute-start(bf16[16,128,128]{2,1,0:T(8,128)(2,1)S(1)} %slice.123), channel_id=1, source_target_pairs={{0,1},{1,2},{2,3},{3,0},{4,5},{5,6},{6,7},{7,4},{8,9},{9,10},{10,1... | collective-permute-start | bytes 1572872 | tf_op jit(solution)/shard_map/ppermute | solution.py:259
  91.9 0.1 compare_convert_fusion.2
  92.0 0.7 convert_bitcast_fusion.1
  92.7 0.7 convert_bitcast_fusion.2
  93.4 0.1 multiply_add_fusion.2
  93.5 2.5 %fusion.28 = f32[32,32,1024,1]{2,1,3,0:T(8,128)S(1)} fusion(bf16[32,32,8,128]{3,2,1,0:T(8,128)(2,1)S(1)} %convert_bitcast_fusion.2, f32[8,128]{1,0:T(8,128)S(1)} %get-tuple-element.47, f32[1024]{0:T(1024)S(1)} %iota_add_fusion), kind=kOutput, calls=%fused_computation.44 | convolution fusion | flops 2153775104 | bytes 6299648 | tf_op jit(solution)/shard_map/zlat,atv->zlv/dot_general | solution.py:244
  96.1 2.5 %fusion.30 = f32[32,32,1024,1]{2,1,3,0:T(8,128)S(1)} fusion(bf16[32,32,8,128]{3,2,1,0:T(8,128)(2,1)S(1)} %convert_bitcast_fusion.1, f32[8,128]{1,0:T(8,128)S(1)} %get-tuple-element.48, f32[1024]{0:T(1024)S(1)} %iota_add_fusion), kind=kOutput, calls=%fused_computation.45 | convolution fusion | flops 2153775104 | bytes 6299648 | tf_op jit(solution)/shard_map/zlat,atv->zlv/dot_general | solution.py:244
  98.6 1.9 %bitcast_add_fusion.1 = f32[32,32,1024]{2,1,0:T(8,128)S(1)} fusion(f32[32,32,1024,1]{2,1,3,0:T(8,128)S(1)} %fusion.30, f32[32,32,1024]{2,1,0:T(8,128)S(1)} %convolution_bitcast_fusion, f32[32,32,1024,1]{2,1,3,0:T(8,128)S(1)} %fusion.28), kind=kLoop, calls=%fused_computation.37 | loop fusion | flops 2097152 | bytes 16777216 | tf_op jit(solution)/shard_map/add | solution.py:262
  100.6 0.9 collective-permute-done.5
  101.5 0.1 convert_reduce_fusion
  101.6 0.1 multiply_bitcast_fusion
  101.8 0.1 compare_convert_fusion
  101.9 0.1 multiply_add_fusion
  102.0 0.7 convert_bitcast_fusion
  102.7 2.6 %broadcast_multiply_fusion = (f32[32,32,1024]{2,1,0:T(8,128)S(1)}, f32[32,32,1024,1]{2,1,3,0:T(8,128)S(1)}) fusion(f32[32]{0:T(128)S(1)} %copy-done.3, f32[32,32,1024]{2,1,0:T(8,128)S(1)} %bitcast_add_fusion.1, f32[8,128]{1,0:T(8,128)S(1)} %multiply_add_fusion, f32[1024]{0:T(1024)S(1)} %iota_add_fusion, bf16[32,32,8,128]{3,2,1,0:T(8,128)(2,1)S(1)} %convert_bitcast_fusion), kind=kOutput, calls=%fused_computation.65 | convolution fusion | flops 2155872256 | bytes 14688384 | tf_op jit(solution)/shard_map/zlat,atv->zlv/dot_general | solution.py:244
  105.3 7.1 %collective-permute-start.6 = (f32[1,32,1024]{2,1,0:T(8,128)S(1)}, f32[1,32,1024]{2,1,0:T(8,128)S(1)}, u32[]{:S(2)}, u32[]{:S(2)}) collective-permute-start(f32[1,32,1024]{2,1,0:T(8,128)S(1)} %get-tuple-element.39), channel_id=1, source_target_pairs={{0,4},{4,8},{8,12},{12,16},{16,20},{20,24},{24,28},{28,32},{32,36}... | collective-permute-start | bytes 393224 | tf_op jit(solution)/shard_map/ppermute | solution.py:25
  112.4 1.9 %collective-permute-start.7 = (f32[1,32,1024]{2,1,0:T(8,128)S(1)}, f32[1,32,1024]{2,1,0:T(8,128)S(1)}, u32[]{:S(2)}, u32[]{:S(2)}) collective-permute-start(f32[1,32,1024]{2,1,0:T(8,128)S(1)} %get-tuple-element.40), channel_id=1, source_target_pairs={{4,0},{8,4},{12,8},{16,12},{20,16},{24,20},{28,24},{32,28},{36,32}... | collective-permute-start | bytes 393224 | tf_op jit(solution)/shard_map/ppermute | solution.py:26
  114.4 6.5 %collective-permute-done.7 = f32[1,32,1024]{2,1,0:T(8,128)S(1)} collective-permute-done((f32[1,32,1024]{2,1,0:T(8,128)S(1)}, f32[1,32,1024]{2,1,0:T(8,128)S(1)}, u32[]{:S(2)}, u32[]{:S(2)}) %collective-permute-start.7) | collective-permute-done | bytes 131104 | tf_op jit(solution)/shard_map/ppermute | solution.py:26
  120.8 4.8 %fusion.19 = f32[32,32,1024]{2,1,0:T(8,128)} fusion(f32[32,32,1024]{2,1,0:T(8,128)S(1)} %copy-done.1, f32[32,32,1024]{2,1,0:T(8,128)S(1)} %copy-done, f32[1,32,1024]{2,1,0:T(8,128)S(1)} %collective-permute-done.7, f32[32,32,1024]{2,1,0:T(8,128)S(1)} %get-tuple-element.53, f32[1,32,1024]{2,1,0:T(8,128)S(1)} %collective-permute-done.6, ...), kind=kLoop, calls=%fused_computation.27 | loop fusion | flops 8388608 | bytes 25428096 | tf_op jit(solution)/shard_map/div | solution.py:268
  (28 shorter events, 0.3 us)
Async XLA Ops:
  0.0 24.6 %copy-start.2 = (s32[1,8]{1,0:T(1,128)S(1)}, s32[1,8]{1,0:T(1,128)}, u32[]{:S(2)}) copy-start(s32[1,8]{1,0:T(1,128)} %param.17) | copy-start | bytes 100
  0.0 24.7 %copy-start.3 = (f32[32]{0:T(128)S(1)}, f32[32]{0:T(128)}, u32[]{:S(2)}) copy-start(f32[32]{0:T(128)} %param.12) | copy-start | bytes 388
  6.0 49.6 %all-to-all-start = ((bf16[64,2,4224]{2,1,0:T(2,128)(2,1)}), bf16[64,2,4224]{2,1,0:T(2,128)(2,1)S(1)}, u32[]{:S(2)}, u32[]{:S(2)}) async-start(bf16[64,2,4224]{2,1,0:T(2,128)(2,1)} %reshape.606), calls=%async_computation | async-start | bytes 2162688 | tf_op jit(solution)/shard_map/all_to_all | solution.py:208
  19.3 23.1 %collective-permute-start = (f32[1,32,1024]{2,1,0:T(8,128)S(1)}, f32[1,32,1024]{2,1,0:T(8,128)S(1)}, u32[]{:S(2)}, u32[]{:S(2)}) collective-permute-start(f32[1,32,1024]{2,1,0:T(8,128)S(1)} %get-tuple-element.43), channel_id=1, source_target_pairs={{0,4},{4,8},{8,12},{12,16},{16,20},{20,24},{24,28},{28,32},{32,36}... | collective-permute-start | bytes 393224 | tf_op jit(solution)/shard_map/ppermute | solution.py:25
  22.7 22.7 %collective-permute-start.1 = (f32[1,32,1024]{2,1,0:T(8,128)S(1)}, f32[1,32,1024]{2,1,0:T(8,128)S(1)}, u32[]{:S(2)}, u32[]{:S(2)}) collective-permute-start(f32[1,32,1024]{2,1,0:T(8,128)S(1)} %get-tuple-element.44), channel_id=1, source_target_pairs={{4,0},{8,4},{12,8},{16,12},{20,16},{24,20},{28,24},{32,28},{36,32}... | collective-permute-start | bytes 393224 | tf_op jit(solution)/shard_map/ppermute | solution.py:26
  66.8 20.2 %collective-permute-start.3 = (bf16[33,128,128]{2,1,0:T(8,128)(2,1)S(1)}, bf16[33,128,128]{2,1,0:T(8,128)(2,1)S(1)}, u32[]{:S(2)}, u32[]{:S(2)}) collective-permute-start(bf16[33,128,128]{2,1,0:T(8,128)(2,1)S(1)} %pad_maximum_fusion.4), channel_id=1, source_target_pairs={{0,3},{1,0},{2,1},{3,2},{4,7},{5,4},{6,5},{7,6},{8,11},{9,8},{10,9... | collective-permute-start | bytes 3244040 | tf_op jit(solution)/shard_map/ppermute | solution.py:256
  67.4 21.5 %collective-permute-start.2 = (bf16[33,128,128]{2,1,0:T(8,128)(2,1)S(1)}, bf16[33,128,128]{2,1,0:T(8,128)(2,1)S(1)}, u32[]{:S(2)}, u32[]{:S(2)}) collective-permute-start(bf16[33,128,128]{2,1,0:T(8,128)(2,1)S(1)} %pad_maximum_fusion.4), channel_id=1, source_target_pairs={{0,1},{1,2},{2,3},{3,0},{4,5},{5,6},{6,7},{7,4},{8,9},{9,10},{10,1... | collective-permute-start | bytes 3244040 | tf_op jit(solution)/shard_map/ppermute | solution.py:255
  89.4 11.1 %collective-permute-start.4 = (bf16[16,128,128]{2,1,0:T(8,128)(2,1)S(1)}, bf16[16,128,128]{2,1,0:T(8,128)(2,1)S(1)}, u32[]{:S(2)}, u32[]{:S(2)}) collective-permute-start(bf16[16,128,128]{2,1,0:T(8,128)(2,1)S(1)} %slice.123), channel_id=1, source_target_pairs={{0,1},{1,2},{2,3},{3,0},{4,5},{5,6},{6,7},{7,4},{8,9},{9,10},{10,1... | collective-permute-start | bytes 1572872 | tf_op jit(solution)/shard_map/ppermute | solution.py:259
  91.9 9.6 %collective-permute-start.5 = (bf16[17,128,128]{2,1,0:T(8,128)(2,1)S(1)}, bf16[17,128,128]{2,1,0:T(8,128)(2,1)S(1)}, u32[]{:S(2)}, u32[]{:S(2)}) collective-permute-start(bf16[17,128,128]{2,1,0:T(8,128)(2,1)S(1)} %slice.124), channel_id=1, source_target_pairs={{0,3},{1,0},{2,1},{3,2},{4,7},{5,4},{6,5},{7,6},{8,11},{9,8},{10,9... | collective-permute-start | bytes 1671176 | tf_op jit(solution)/shard_map/ppermute | solution.py:260
  102.7 18.1 %copy-start = (f32[32,32,1024]{2,1,0:T(8,128)S(1)}, f32[32,32,1024]{2,1,0:T(8,128)}, u32[]{:S(2)}) copy-start(f32[32,32,1024]{2,1,0:T(8,128)} %param.10) | copy-start | bytes 12582916
  102.7 18.1 %copy-start.1 = (f32[32,32,1024]{2,1,0:T(8,128)S(1)}, f32[32,32,1024]{2,1,0:T(8,128)}, u32[]{:S(2)}) copy-start(f32[32,32,1024]{2,1,0:T(8,128)} %param.11) | copy-start | bytes 12582916
  105.3 9.0 %collective-permute-start.6 = (f32[1,32,1024]{2,1,0:T(8,128)S(1)}, f32[1,32,1024]{2,1,0:T(8,128)S(1)}, u32[]{:S(2)}, u32[]{:S(2)}) collective-permute-start(f32[1,32,1024]{2,1,0:T(8,128)S(1)} %get-tuple-element.39), channel_id=1, source_target_pairs={{0,4},{4,8},{8,12},{12,16},{16,20},{20,24},{24,28},{28,32},{32,36}... | collective-permute-start | bytes 393224 | tf_op jit(solution)/shard_map/ppermute | solution.py:25
  112.4 8.4 %collective-permute-start.7 = (f32[1,32,1024]{2,1,0:T(8,128)S(1)}, f32[1,32,1024]{2,1,0:T(8,128)S(1)}, u32[]{:S(2)}, u32[]{:S(2)}) collective-permute-start(f32[1,32,1024]{2,1,0:T(8,128)S(1)} %get-tuple-element.40), channel_id=1, source_target_pairs={{4,0},{8,4},{12,8},{16,12},{20,16},{24,20},{28,24},{32,28},{36,32}... | collective-permute-start | bytes 393224 | tf_op jit(solution)/shard_map/ppermute | solution.py:26

commit v17 on v14

--- a/solution.py
+++ b/solution.py
@@ -209,19 +209,17 @@
         send.reshape(slab_count, capacity, row + extra), "slab", 0, 0, tiled=True
     ).reshape(slots, row + extra)
     index = recv[:, row].astype(jnp.int32)
-    rows = recv[:, :row].reshape(slots, planes, bins).transpose(1, 0, 2)
-    pick = (index[:, None] == jnp.arange(pairs, dtype=jnp.int32)[None, :]).astype(jnp.float32)
-    pick = jnp.broadcast_to(pick[None], (planes, slots, pairs))
-    estimate = jnp.einsum("zjp,zpt->zjt", pick, projected, precision=lax.Precision.HIGH)
-    ratios = rows.astype(jnp.float32) / (estimate + BACKGROUND)
+    rows = recv[:, :row].reshape(slots, planes, bins)
+    by_pair = projected.transpose(1, 0, 2)
+    estimate = by_pair[index]
+    ratios = (rows.astype(jnp.float32) / (estimate + BACKGROUND)).reshape(slots, row)
 
     same = index[:, None] == index[None, :]
     earlier = jnp.arange(slots)[None, :] < jnp.arange(slots)[:, None]
     first = ~jnp.any(same & earlier, axis=1)
-    merge = jnp.broadcast_to((same & first[:, None]).astype(jnp.float32)[None], (planes, slots, slots))
-    merged = jnp.einsum(
-        "zij,zjt->zit", merge, ratios, precision=lax.Precision.HIGH
-    ).astype(jnp.bfloat16)
+    merge = (same & first[:, None]).astype(jnp.float32)
+    merged = jnp.dot(merge, ratios, precision=lax.Precision.HIGH).astype(jnp.bfloat16)
+    merged = merged.reshape(slots, planes, bins).transpose(1, 0, 2)
 
     payload = jnp.concatenate([merged, info_row(recv[:, row])[None]], axis=0)
     def back_project(got, kernel_k):

time: 126 us -> 125 us (level)
  the two profiles are of different devices: /device:TPU:31 before, /device:TPU:103 now
where the time goes in v17:
time: 125 us; the launch traced here: 124 us
  waiting for transfers between devices  45.1 us (36%)
  starting transfers between devices  31.7 us (25%)
  matrix products  22.7 us (18%)
  local copies, waits for them, and re-layouts  12.2 us (10%)
  other arithmetic  12 us (10%)
    ppermute x2, waiting for transfers between devices, with_halo(): before = lax.ppermute(last, axis, up)  17.1 us
    ppermute x1, waiting for transfers between devices, on_device(): from_right = lax.ppermute(payload, 'view', leftward)  11.8 us
    ppermute x2, starting transfers between devices, with_halo(): before = lax.ppermute(last, axis, up)  11.3 us
    all_to_all x1, starting transfers between devices, on_device(): lax.all_to_all(send.reshape(slab_count, capacity, row + extra), 'slab', 0...  11 us
    ppermute x2, waiting for transfers between devices, with_halo(): after = lax.ppermute(leading, axis, down)  10.6 us
    dot_general x4, matrix products, back_project(): jnp.einsum('zlat,atv->zlv', dense, kernel_k, preferred_element_type=jnp.f...  10.2 us
    dot_general x1, matrix products, on_device(): jnp.einsum('zlv,atv->zalt', blurred, tof_kernel, preferred_element_type=j...  7.21 us
    ppermute x1, waiting for transfers between devices, on_device(): from_left = lax.ppermute(payload, 'view', rightward)  5.61 us
  transfers between devices with their start and end apart: 9, of which 5 were waited for; matrix products, arithmetic and copies ran while one was open for 20% of the time, Pallas kernels for 0%

profile of v17, /device:TPU:103, one launch (start us, length us, event | category | flops | bytes accessed | tf_op | source)
XLA Modules:
  0.0 124.2 jit_solution(3931543531220952563)
XLA Ops:
  0.0 0.8 fusion.74
  0.8 0.1 reduce_window_sum.11
  0.9 0.8 select_reduce_fusion
  1.7 0.7 multiply_add_fusion.4
  2.4 1.3 %copy.66 = bf16[8,8,32,128]{3,1,2,0:T(8,128)(2,1)S(1)} copy(bf16[8,8,32,128]{3,2,1,0:T(8,128)(2,1)} %bitcast.129) | data formatting | bytes 1048576
  3.6 0.7 convert_bitcast_fusion.4
  4.3 0.1 broadcast_in_dim.28
  4.4 0.4 convolution_convert_fusion
  4.8 1.2 %reshape.547 = bf16[64,2,4224]{2,1,0:T(2,128)(2,1)} reshape(bf16[128,4224]{1,0:T(8,128)(2,1)S(1)} %convolution_convert_fusion) | data formatting | bytes 2162688 | tf_op jit(solution)/shard_map/reshape | solution.py:209
  6.1 11.0 %all-to-all-start = ((bf16[64,2,4224]{2,1,0:T(2,128)(2,1)}), bf16[64,2,4224]{2,1,0:T(2,128)(2,1)S(1)}, u32[]{:S(2)}, u32[]{:S(2)}) async-start(bf16[64,2,4224]{2,1,0:T(2,128)(2,1)} %reshape.547), calls=%async_computation | async-start | bytes 2162688 | tf_op jit(solution)/shard_map/all_to_all | solution.py:208
  17.1 1.0 fusion.105
  18.0 4.6 %collective-permute-start = (f32[1,32,1024]{2,1,0:T(8,128)S(1)}, f32[1,32,1024]{2,1,0:T(8,128)S(1)}, u32[]{:S(2)}, u32[]{:S(2)}) collective-permute-start(f32[1,32,1024]{2,1,0:T(8,128)S(1)} %get-tuple-element.43), channel_id=1, source_target_pairs={{0,4},{4,8},{8,12},{12,16},{16,20},{20,24},{24,28},{28,32},{32,36}... | collective-permute-start | bytes 393224 | tf_op jit(solution)/shard_map/ppermute | solution.py:25
  22.6 1.9 %collective-permute-start.1 = (f32[1,32,1024]{2,1,0:T(8,128)S(1)}, f32[1,32,1024]{2,1,0:T(8,128)S(1)}, u32[]{:S(2)}, u32[]{:S(2)}) collective-permute-start(f32[1,32,1024]{2,1,0:T(8,128)S(1)} %get-tuple-element.44), channel_id=1, source_target_pairs={{4,0},{8,4},{12,8},{16,12},{20,16},{24,20},{28,24},{32,28},{36,32}... | collective-permute-start | bytes 393224 | tf_op jit(solution)/shard_map/ppermute | solution.py:26
  24.6 0.1 fusion.87
  24.7 0.1 multiply_add_fusion.3
  24.8 0.1 select_maximum_fusion
  24.8 17.1 %collective-permute-done = f32[1,32,1024]{2,1,0:T(8,128)S(1)} collective-permute-done((f32[1,32,1024]{2,1,0:T(8,128)S(1)}, f32[1,32,1024]{2,1,0:T(8,128)S(1)}, u32[]{:S(2)}, u32[]{:S(2)}) %collective-permute-start) | collective-permute-done | bytes 131104 | tf_op jit(solution)/shard_map/ppermute | solution.py:25
  42.0 2.9 %collective-permute-done.1 = f32[1,32,1024]{2,1,0:T(8,128)S(1)} collective-permute-done((f32[1,32,1024]{2,1,0:T(8,128)S(1)}, f32[1,32,1024]{2,1,0:T(8,128)S(1)}, u32[]{:S(2)}, u32[]{:S(2)}) %collective-permute-start.1) | collective-permute-done | bytes 131104 | tf_op jit(solution)/shard_map/ppermute | solution.py:26
  44.9 7.2 %convolution_bitcast_fusion.1 = f32[32,8,32,128]{3,2,0,1:T(8,128)S(1)} fusion(f32[1,32,1024]{2,1,0:T(8,128)S(1)} %collective-permute-done.1, f32[32,32,1024]{2,1,0:T(8,128)} %param.10, f32[1,32,1024]{2,1,0:T(8,128)S(1)} %collective-permute-done, f32[32]{0:T(128)S(1)} %copy-done.3, f32[8,128]{1,0:T(8,128)S(1)} %multiply_add_fusion.3, ...), kind=kOutput, calls=%fused_computation.40 | convolution fusion | flops 2161115136 | bytes 8659200 | tf_op jit(solution)/shard_map/zlv,atv->zalt/dot_general | solution.py:206
  52.1 0.4 copy.29
  52.6 4.4 %copy.64 = f32[32,256,128]{2,0,1:T(8,128)} copy(f32[32,256,128]{2,1,0:T(8,128)S(1)} %bitcast.124) | data formatting | bytes 8388608 | tf_op jit(solution)/shard_map/reshape | solution.py:207
  57.0 0.0 all-to-all-done
  57.0 0.4 reshape.548
  57.5 0.1 slice_reduce_fusion
  57.6 0.1 convert_reduce_fusion
  57.7 0.2 fusion.71
  57.9 2.9 %gather_fusion = f32[128,32,128]{2,1,0:T(8,128)S(1)} fusion(f32[256,32,128]{2,1,0:T(8,128)} %bitcast.125, s32[1024]{0:T(1024)S(1)} %pad_clamp_fusion), kind=kCustom, calls=%fused_computation | custom fusion | bytes 4194816 | tf_op jit(solution)/shard_map/gather | solution.py:214
  60.8 0.2 broadcast_add_fusion
  61.1 2.0 %fusion.58 = bf16[16,32,8,128]{3,2,1,0:T(8,128)(2,1)S(1)} fusion(f32[16,8,32,128]{3,2,1,0:T(8,128)S(1)} %bitcast.127, bf16[128,4224]{1,0:T(8,128)(2,1)S(1)} %reshape.548, s32[128]{0:T(128)S(1)} %convert_element_type.180, s32[128]{0:T(128)S(1)} %get-tuple-element.33, pred[128]{0:T(512)(128)(4,1)S(1)} %not.7), kind=kOutput, calls=%fused_computation.75 | convolution fusion | flops 404258816 | bytes 4195840 | tf_op jit(solution)/shard_map/dot_general | solution.py:221
  63.1 0.3 copy.65
  63.4 0.1 broadcast_select_fusion
  63.5 0.1 pad_maximum_fusion.4
  63.6 2.8 %collective-permute-start.3 = (bf16[33,128,128]{2,1,0:T(8,128)(2,1)S(1)}, bf16[33,128,128]{2,1,0:T(8,128)(2,1)S(1)}, u32[]{:S(2)}, u32[]{:S(2)}) collective-permute-start(bf16[33,128,128]{2,1,0:T(8,128)(2,1)S(1)} %pad_maximum_fusion.4), channel_id=1, source_target_pairs={{0,3},{1,0},{2,1},{3,2},{4,7},{5,4},{6,5},{7,6},{8,11},{9,8},{10,9... | collective-permute-start | bytes 3244040 | tf_op jit(solution)/shard_map/ppermute | solution.py:247
  66.4 0.0 collective-permute-start.2
  66.4 0.1 convert_reduce_fusion.4
  66.5 0.1 compare_convert_fusion.3
  66.6 0.7 convert_bitcast_fusion.3
  67.3 2.5 %convolution_bitcast_fusion = f32[32,32,1024]{2,1,0:T(8,128)S(1)} fusion(bf16[32,32,8,128]{3,2,1,0:T(8,128)(2,1)S(1)} %convert_bitcast_fusion.3, f32[8,128]{1,0:T(8,128)S(1)} %multiply_add_fusion.3, f32[1024]{0:T(1024)S(1)} %iota_add_fusion), kind=kOutput, calls=%fused_computation.39 | convolution fusion | flops 2153775104 | bytes 6299648 | tf_op jit(solution)/shard_map/zlat,atv->zlv/dot_general | solution.py:235
  69.9 11.8 %collective-permute-done.3 = bf16[33,128,128]{2,1,0:T(8,128)(2,1)S(1)} collective-permute-done((bf16[33,128,128]{2,1,0:T(8,128)(2,1)S(1)}, bf16[33,128,128]{2,1,0:T(8,128)(2,1)S(1)}, u32[]{:S(2)}, u32[]{:S(2)}) %collective-permute-start.3) | collective-permute-done | bytes 1081376 | tf_op jit(solution)/shard_map/ppermute | solution.py:247
  81.7 5.6 %collective-permute-done.2 = bf16[33,128,128]{2,1,0:T(8,128)(2,1)S(1)} collective-permute-done((bf16[33,128,128]{2,1,0:T(8,128)(2,1)S(1)}, bf16[33,128,128]{2,1,0:T(8,128)(2,1)S(1)}, u32[]{:S(2)}, u32[]{:S(2)}) %collective-permute-start.2) | collective-permute-done | bytes 1081376 | tf_op jit(solution)/shard_map/ppermute | solution.py:246
  87.3 0.1 convert_reduce_fusion.2
  87.5 0.1 multiply_bitcast_fusion.1
  87.6 0.1 multiply_bitcast_fusion.2
  87.8 0.1 collective-permute-start.4
  87.9 2.7 %collective-permute-start.5 = (bf16[17,128,128]{2,1,0:T(8,128)(2,1)S(1)}, bf16[17,128,128]{2,1,0:T(8,128)(2,1)S(1)}, u32[]{:S(2)}, u32[]{:S(2)}) collective-permute-start(bf16[17,128,128]{2,1,0:T(8,128)(2,1)S(1)} %slice.124), channel_id=1, source_target_pairs={{0,3},{1,0},{2,1},{3,2},{4,7},{5,4},{6,5},{7,6},{8,11},{9,8},{10,9... | collective-permute-start | bytes 1671176 | tf_op jit(solution)/shard_map/ppermute | solution.py:251
  90.6 0.1 compare_convert_fusion.2
  90.7 0.7 convert_bitcast_fusion.1
  91.4 0.7 convert_bitcast_fusion.2
  92.1 0.1 multiply_add_fusion.2
  92.2 2.5 %fusion.27 = f32[32,32,1024,1]{2,1,3,0:T(8,128)S(1)} fusion(bf16[32,32,8,128]{3,2,1,0:T(8,128)(2,1)S(1)} %convert_bitcast_fusion.2, f32[8,128]{1,0:T(8,128)S(1)} %get-tuple-element.47, f32[1024]{0:T(1024)S(1)} %iota_add_fusion), kind=kOutput, calls=%fused_computation.44 | convolution fusion | flops 2153775104 | bytes 6299648 | tf_op jit(solution)/shard_map/zlat,atv->zlv/dot_general | solution.py:235
  94.7 2.5 %fusion.29 = f32[32,32,1024,1]{2,1,3,0:T(8,128)S(1)} fusion(bf16[32,32,8,128]{3,2,1,0:T(8,128)(2,1)S(1)} %convert_bitcast_fusion.1, f32[8,128]{1,0:T(8,128)S(1)} %get-tuple-element.48, f32[1024]{0:T(1024)S(1)} %iota_add_fusion), kind=kOutput, calls=%fused_computation.45 | convolution fusion | flops 2153775104 | bytes 6299648 | tf_op jit(solution)/shard_map/zlat,atv->zlv/dot_general | solution.py:235
  97.2 1.9 %bitcast_add_fusion.1 = f32[32,32,1024]{2,1,0:T(8,128)S(1)} fusion(f32[32,32,1024,1]{2,1,3,0:T(8,128)S(1)} %fusion.29, f32[32,32,1024]{2,1,0:T(8,128)S(1)} %convolution_bitcast_fusion, f32[32,32,1024,1]{2,1,3,0:T(8,128)S(1)} %fusion.27), kind=kLoop, calls=%fused_computation.36 | loop fusion | flops 2097152 | bytes 16777216 | tf_op jit(solution)/shard_map/add | solution.py:253
  99.2 0.1 convert_reduce_fusion.1
  99.3 0.1 multiply_bitcast_fusion
  99.5 0.1 compare_convert_fusion
  99.6 0.1 multiply_add_fusion
  99.7 0.7 convert_bitcast_fusion
  100.4 0.0 copy-start
  100.4 0.0 copy-start.1
  100.4 2.6 %broadcast_multiply_fusion = (f32[32,32,1024]{2,1,0:T(8,128)S(1)}, f32[32,32,1024,1]{2,1,3,0:T(8,128)S(1)}) fusion(f32[32]{0:T(128)S(1)} %copy-done.3, f32[32,32,1024]{2,1,0:T(8,128)S(1)} %bitcast_add_fusion.1, f32[8,128]{1,0:T(8,128)S(1)} %multiply_add_fusion, f32[1024]{0:T(1024)S(1)} %iota_add_fusion, bf16[32,32,8,128]{3,2,1,0:T(8,128)(2,1)S(1)} %convert_bitcast_fusion), kind=kOutput, calls=%fused_computation.63 | convolution fusion | flops 2155872256 | bytes 14688384 | tf_op jit(solution)/shard_map/zlat,atv->zlv/dot_general | solution.py:235
  103.1 6.7 %collective-permute-start.6 = (f32[1,32,1024]{2,1,0:T(8,128)S(1)}, f32[1,32,1024]{2,1,0:T(8,128)S(1)}, u32[]{:S(2)}, u32[]{:S(2)}) collective-permute-start(f32[1,32,1024]{2,1,0:T(8,128)S(1)} %get-tuple-element.41), channel_id=1, source_target_pairs={{0,4},{4,8},{8,12},{12,16},{16,20},{20,24},{24,28},{28,32},{32,36}... | collective-permute-start | bytes 393224 | tf_op jit(solution)/shard_map/ppermute | solution.py:25
  109.8 1.9 %collective-permute-start.7 = (f32[1,32,1024]{2,1,0:T(8,128)S(1)}, f32[1,32,1024]{2,1,0:T(8,128)S(1)}, u32[]{:S(2)}, u32[]{:S(2)}) collective-permute-start(f32[1,32,1024]{2,1,0:T(8,128)S(1)} %get-tuple-element.42), channel_id=1, source_target_pairs={{4,0},{8,4},{12,8},{16,12},{20,16},{24,20},{28,24},{32,28},{36,32}... | collective-permute-start | bytes 393224 | tf_op jit(solution)/shard_map/ppermute | solution.py:26
  111.7 7.7 %collective-permute-done.7 = f32[1,32,1024]{2,1,0:T(8,128)S(1)} collective-permute-done((f32[1,32,1024]{2,1,0:T(8,128)S(1)}, f32[1,32,1024]{2,1,0:T(8,128)S(1)}, u32[]{:S(2)}, u32[]{:S(2)}) %collective-permute-start.7) | collective-permute-done | bytes 131104 | tf_op jit(solution)/shard_map/ppermute | solution.py:26
  119.4 4.8 %fusion.18 = f32[32,32,1024]{2,1,0:T(8,128)} fusion(f32[32,32,1024]{2,1,0:T(8,128)S(1)} %copy-done.1, f32[32,32,1024]{2,1,0:T(8,128)S(1)} %copy-done, f32[1,32,1024]{2,1,0:T(8,128)S(1)} %collective-permute-done.7, f32[32,32,1024]{2,1,0:T(8,128)S(1)} %get-tuple-element.53, f32[1,32,1024]{2,1,0:T(8,128)S(1)} %collective-permute-done.6, ...), kind=kLoop, calls=%fused_computation.26 | loop fusion | flops 8388608 | bytes 25428096 | tf_op jit(solution)/shard_map/div | solution.py:259
  (26 shorter events, 0.3 us)
Async XLA Ops:
  0.0 24.6 %copy-start.3 = (f32[32]{0:T(128)S(1)}, f32[32]{0:T(128)}, u32[]{:S(2)}) copy-start(f32[32]{0:T(128)} %param.12) | copy-start | bytes 388
  0.0 24.6 %copy-start.2 = (s32[1,8]{1,0:T(1,128)S(1)}, s32[1,8]{1,0:T(1,128)}, u32[]{:S(2)}) copy-start(s32[1,8]{1,0:T(1,128)} %param.17) | copy-start | bytes 100
  6.1 51.0 %all-to-all-start = ((bf16[64,2,4224]{2,1,0:T(2,128)(2,1)}), bf16[64,2,4224]{2,1,0:T(2,128)(2,1)S(1)}, u32[]{:S(2)}, u32[]{:S(2)}) async-start(bf16[64,2,4224]{2,1,0:T(2,128)(2,1)} %reshape.547), calls=%async_computation | async-start | bytes 2162688 | tf_op jit(solution)/shard_map/all_to_all | solution.py:208
  18.0 23.9 %collective-permute-start = (f32[1,32,1024]{2,1,0:T(8,128)S(1)}, f32[1,32,1024]{2,1,0:T(8,128)S(1)}, u32[]{:S(2)}, u32[]{:S(2)}) collective-permute-start(f32[1,32,1024]{2,1,0:T(8,128)S(1)} %get-tuple-element.43), channel_id=1, source_target_pairs={{0,4},{4,8},{8,12},{12,16},{16,20},{20,24},{24,28},{28,32},{32,36}... | collective-permute-start | bytes 393224 | tf_op jit(solution)/shard_map/ppermute | solution.py:25
  22.6 22.3 %collective-permute-start.1 = (f32[1,32,1024]{2,1,0:T(8,128)S(1)}, f32[1,32,1024]{2,1,0:T(8,128)S(1)}, u32[]{:S(2)}, u32[]{:S(2)}) collective-permute-start(f32[1,32,1024]{2,1,0:T(8,128)S(1)} %get-tuple-element.44), channel_id=1, source_target_pairs={{4,0},{8,4},{12,8},{16,12},{20,16},{24,20},{28,24},{32,28},{36,32}... | collective-permute-start | bytes 393224 | tf_op jit(solution)/shard_map/ppermute | solution.py:26
  63.6 18.1 %collective-permute-start.3 = (bf16[33,128,128]{2,1,0:T(8,128)(2,1)S(1)}, bf16[33,128,128]{2,1,0:T(8,128)(2,1)S(1)}, u32[]{:S(2)}, u32[]{:S(2)}) collective-permute-start(bf16[33,128,128]{2,1,0:T(8,128)(2,1)S(1)} %pad_maximum_fusion.4), channel_id=1, source_target_pairs={{0,3},{1,0},{2,1},{3,2},{4,7},{5,4},{6,5},{7,6},{8,11},{9,8},{10,9... | collective-permute-start | bytes 3244040 | tf_op jit(solution)/shard_map/ppermute | solution.py:247
  66.4 20.8 %collective-permute-start.2 = (bf16[33,128,128]{2,1,0:T(8,128)(2,1)S(1)}, bf16[33,128,128]{2,1,0:T(8,128)(2,1)S(1)}, u32[]{:S(2)}, u32[]{:S(2)}) collective-permute-start(bf16[33,128,128]{2,1,0:T(8,128)(2,1)S(1)} %pad_maximum_fusion.4), channel_id=1, source_target_pairs={{0,1},{1,2},{2,3},{3,0},{4,5},{5,6},{6,7},{7,4},{8,9},{9,10},{10,1... | collective-permute-start | bytes 3244040 | tf_op jit(solution)/shard_map/ppermute | solution.py:246
  87.8 11.4 %collective-permute-start.4 = (bf16[16,128,128]{2,1,0:T(8,128)(2,1)S(1)}, bf16[16,128,128]{2,1,0:T(8,128)(2,1)S(1)}, u32[]{:S(2)}, u32[]{:S(2)}) collective-permute-start(bf16[16,128,128]{2,1,0:T(8,128)(2,1)S(1)} %slice.123), channel_id=1, source_target_pairs={{0,1},{1,2},{2,3},{3,0},{4,5},{5,6},{6,7},{7,4},{8,9},{9,10},{10,1... | collective-permute-start | bytes 1572872 | tf_op jit(solution)/shard_map/ppermute | solution.py:250
  87.9 11.3 %collective-permute-start.5 = (bf16[17,128,128]{2,1,0:T(8,128)(2,1)S(1)}, bf16[17,128,128]{2,1,0:T(8,128)(2,1)S(1)}, u32[]{:S(2)}, u32[]{:S(2)}) collective-permute-start(bf16[17,128,128]{2,1,0:T(8,128)(2,1)S(1)} %slice.124), channel_id=1, source_target_pairs={{0,3},{1,0},{2,1},{3,2},{4,7},{5,4},{6,5},{7,6},{8,11},{9,8},{10,9... | collective-permute-start | bytes 1671176 | tf_op jit(solution)/shard_map/ppermute | solution.py:251
  100.4 19.0 %copy-start = (f32[32,32,1024]{2,1,0:T(8,128)S(1)}, f32[32,32,1024]{2,1,0:T(8,128)}, u32[]{:S(2)}) copy-start(f32[32,32,1024]{2,1,0:T(8,128)} %param.10) | copy-start | bytes 12582916
  100.4 19.0 %copy-start.1 = (f32[32,32,1024]{2,1,0:T(8,128)S(1)}, f32[32,32,1024]{2,1,0:T(8,128)}, u32[]{:S(2)}) copy-start(f32[32,32,1024]{2,1,0:T(8,128)} %param.11) | copy-start | bytes 12582916
  103.1 8.7 %collective-permute-start.6 = (f32[1,32,1024]{2,1,0:T(8,128)S(1)}, f32[1,32,1024]{2,1,0:T(8,128)S(1)}, u32[]{:S(2)}, u32[]{:S(2)}) collective-permute-start(f32[1,32,1024]{2,1,0:T(8,128)S(1)} %get-tuple-element.41), channel_id=1, source_target_pairs={{0,4},{4,8},{8,12},{12,16},{16,20},{20,24},{24,28},{28,32},{32,36}... | collective-permute-start | bytes 393224 | tf_op jit(solution)/shard_map/ppermute | solution.py:25
  109.8 9.6 %collective-permute-start.7 = (f32[1,32,1024]{2,1,0:T(8,128)S(1)}, f32[1,32,1024]{2,1,0:T(8,128)S(1)}, u32[]{:S(2)}, u32[]{:S(2)}) collective-permute-start(f32[1,32,1024]{2,1,0:T(8,128)S(1)} %get-tuple-element.42), channel_id=1, source_target_pairs={{4,0},{8,4},{12,8},{16,12},{20,16},{24,20},{28,24},{32,28},{36,32}... | collective-permute-start | bytes 393224 | tf_op jit(solution)/shard_map/ppermute | solution.py:26

commit v18 on v15

--- a/solution.py
+++ b/solution.py
@@ -197,7 +197,10 @@
     extra = 128
     tag = jnp.broadcast_to(pair_id.astype(jnp.bfloat16)[:, None], (block_total, extra))
     outgoing = jnp.concatenate([measured[0].reshape(block_total, row), tag], axis=1)
-    send = jnp.dot(place, outgoing, preferred_element_type=jnp.float32).astype(jnp.bfloat16)
+    send = jnp.concatenate(
+        [jnp.dot(place[k::capacity], outgoing, preferred_element_type=jnp.float32)
+         for k in range(capacity)], axis=1,
+    ).astype(jnp.bfloat16)
     send, activity_late = lax.optimization_barrier((send, activity))
     padded = with_halo(activity_late, (("slab", 0),), 1)
     blurred = ((1.0 - 2.0 * weight) * activity + weight * (padded[:-2] + padded[2:])).astype(
@@ -205,9 +208,10 @@
     )
     projected = jnp.einsum("zlv,atv->zalt", blurred, tof_kernel, preferred_element_type=jnp.float32)
     projected = projected.reshape(planes, pairs, bins)
-    recv = lax.all_to_all(
-        send.reshape(slab_count, capacity, row + extra), "slab", 0, 0, tiled=True
-    ).reshape(slots, row + extra)
+    recv = lax.all_to_all(send, "slab", 0, 0, tiled=True)
+    recv = jnp.concatenate(
+        [recv[:, k * (row + extra) : (k + 1) * (row + extra)] for k in range(capacity)], axis=0
+    )
     index = recv[:, row].astype(jnp.int32)
     rows = recv[:, :row].reshape(slots, planes, bins).transpose(1, 0, 2)
     rows = lax.optimization_barrier(rows)

time: 123 us -> 126 us (1.024)
  other arithmetic: 11.8 us -> 13.6 us
    unnamed x9 -> x12, local copies, waits for them, and re-layouts: 1.27 us -> 3.45 us
    reshape x2 -> x0, local copies, waits for them, and re-layouts: 1.67 us -> none  [the longest x1 1.24 us: on_device(): send.reshape(slab_count, capacity, row + extra)]
    all_to_all x0 -> x1, other arithmetic: none -> 1.47 us  [on_device(): recv = lax.all_to_all(send, 'slab', 0, 0, tiled=True)]
  transfers between devices with their start and end apart: 9 -> 9, of which waited for: 6 -> 6; matrix products, arithmetic and copies ran while one was open for 19% -> 18% of each run, Pallas kernels for 0% -> 0%
where the time goes in v18:
time: 126 us; the launch traced here: 125 us
  waiting for transfers between devices  44.6 us (35%)
  starting transfers between devices  30.8 us (24%)
  matrix products  26.1 us (21%)
  other arithmetic  13.6 us (11%)
  local copies, waits for them, and re-layouts  9.05 us (7%)
    ppermute x2, waiting for transfers between devices, with_halo(): before = lax.ppermute(last, axis, up)  17.5 us
    ppermute x1, waiting for transfers between devices, on_device(): from_right = lax.ppermute(payload, 'view', leftward)  14.6 us
    all_to_all x1, starting transfers between devices, on_device(): recv = lax.all_to_all(send, 'slab', 0, 0, tiled=True)  12.3 us
    dot_general x4, matrix products, back_project(): jnp.einsum('zlat,atv->zlv', dense, kernel_k, preferred_element_type=jnp.f...  10.2 us
    ppermute x2, starting transfers between devices, with_halo(): before = lax.ppermute(last, axis, up)  9.48 us
    ppermute x2, waiting for transfers between devices, with_halo(): after = lax.ppermute(leading, axis, down)  9.37 us
    dot_general x1, matrix products, on_device(): jnp.einsum('zlv,atv->zalt', blurred, tof_kernel, preferred_element_type=j...  7.2 us
    div x1, other arithmetic, on_device(): return activity * smoothed / sensitivity  4.79 us
  transfers between devices with their start and end apart: 9, of which 6 were waited for; matrix products, arithmetic and copies ran while one was open for 18% of the time, Pallas kernels for 0%

profile of v18, /device:TPU:31, one launch (start us, length us, event | category | flops | bytes accessed | tf_op | source)
XLA Modules:
  0.0 124.6 jit_solution(7019345765381477126)
XLA Ops:
  0.0 0.7 fusion.77
  0.7 0.1 reduce_window_sum.11
  0.8 0.8 select_reduce_fusion
  1.7 0.7 multiply_add_fusion.4
  2.4 1.3 %copy.54 = bf16[8,8,32,128]{3,1,2,0:T(8,128)(2,1)S(1)} copy(bf16[8,8,32,128]{3,2,1,0:T(8,128)(2,1)} %bitcast.122) | data formatting | bytes 1048576
  3.7 0.7 convert_bitcast_fusion.4
  4.4 0.1 broadcast_in_dim.32
  4.4 0.3 convolution_convert_fusion
  4.7 0.3 convolution_convert_fusion.1
  5.1 0.5 broadcast.628
  5.7 1.5 %reduce.12 = bf16[64,8448]{1,0:T(8,128)(2,1)S(1)} reduce(bf16[64,1,8448]{2,0,1:T(8,128)(2,1)S(1)} %bitcast.118, bf16[]{:T(256)} %broadcast.628), dimensions={1}, to_apply=%copy.26.reduce_sub_computation | reduce | bytes 2162690 | tf_op jit(solution)/shard_map/all_to_all | solution.py:211
  7.1 1.2 reshape.668
  8.3 12.3 %all-to-all-start = ((bf16[64,2,4224]{2,1,0:T(2,128)(2,1)}), bf16[64,2,4224]{2,1,0:T(2,128)(2,1)S(1)}, u32[]{:S(2)}, u32[]{:S(2)}) async-start(bf16[64,2,4224]{2,1,0:T(2,128)(2,1)} %reshape.668), calls=%async_computation | async-start | bytes 2162688 | tf_op jit(solution)/shard_map/all_to_all | solution.py:211
  20.6 1.0 fusion.108
  21.6 3.3 %collective-permute-start = (f32[1,32,1024]{2,1,0:T(8,128)S(1)}, f32[1,32,1024]{2,1,0:T(8,128)S(1)}, u32[]{:S(2)}, u32[]{:S(2)}) collective-permute-start(f32[1,32,1024]{2,1,0:T(8,128)S(1)} %get-tuple-element.41), channel_id=1, source_target_pairs={{0,4},{4,8},{8,12},{12,16},{16,20},{20,24},{24,28},{28,32},{32,36}... | collective-permute-start | bytes 393224 | tf_op jit(solution)/shard_map/ppermute | solution.py:25
  24.9 1.9 %collective-permute-start.1 = (f32[1,32,1024]{2,1,0:T(8,128)S(1)}, f32[1,32,1024]{2,1,0:T(8,128)S(1)}, u32[]{:S(2)}, u32[]{:S(2)}) collective-permute-start(f32[1,32,1024]{2,1,0:T(8,128)S(1)} %get-tuple-element.42), channel_id=1, source_target_pairs={{4,0},{8,4},{12,8},{16,12},{20,16},{24,20},{28,24},{32,28},{36,32}... | collective-permute-start | bytes 393224 | tf_op jit(solution)/shard_map/ppermute | solution.py:26
  27.0 0.1 select_maximum_fusion
  27.1 17.5 %collective-permute-done = f32[1,32,1024]{2,1,0:T(8,128)S(1)} collective-permute-done((f32[1,32,1024]{2,1,0:T(8,128)S(1)}, f32[1,32,1024]{2,1,0:T(8,128)S(1)}, u32[]{:S(2)}, u32[]{:S(2)}) %collective-permute-start) | collective-permute-done | bytes 131104 | tf_op jit(solution)/shard_map/ppermute | solution.py:25
  44.7 2.9 %collective-permute-done.1 = f32[1,32,1024]{2,1,0:T(8,128)S(1)} collective-permute-done((f32[1,32,1024]{2,1,0:T(8,128)S(1)}, f32[1,32,1024]{2,1,0:T(8,128)S(1)}, u32[]{:S(2)}, u32[]{:S(2)}) %collective-permute-start.1) | collective-permute-done | bytes 131104 | tf_op jit(solution)/shard_map/ppermute | solution.py:26
  47.6 7.2 %convolution_bitcast_fusion.1 = f32[32,8,32,128]{3,2,0,1:T(8,128)S(1)} fusion(f32[1,32,1024]{2,1,0:T(8,128)S(1)} %collective-permute-done.1, f32[32,32,1024]{2,1,0:T(8,128)} %param.10, f32[1,32,1024]{2,1,0:T(8,128)S(1)} %collective-permute-done, f32[32]{0:T(128)S(1)} %copy-done.3, f32[8,128]{1,0:T(8,128)S(1)} %multiply_add_fusion.3, ...), kind=kOutput, calls=%fused_computation.38 | convolution fusion | flops 2161115136 | bytes 8659200 | tf_op jit(solution)/shard_map/zlv,atv->zalt/dot_general | solution.py:209
  54.8 2.5 %copy.29 = f32[32,8,32,128]{3,2,1,0:T(8,128)} copy(f32[32,8,32,128]{3,2,0,1:T(8,128)S(1)} %convolution_bitcast_fusion.1) | data formatting | bytes 8388608 | tf_op jit(solution)/shard_map/zlv,atv->zalt/transpose | solution.py:209
  57.2 0.9 reshape.669
  58.2 0.1 copy.53
  58.3 0.1 fusion.109
  58.4 0.1 maximum_reduce_fusion
  58.5 0.1 pad_maximum_fusion.8
  58.6 0.2 fusion.75
  58.8 0.1 fusion.74
  58.9 0.7 copy.27
  59.5 0.7 copy.28
  60.2 0.1 fusion.76
  60.3 0.1 broadcast_select_fusion
  60.4 4.2 %fusion.58 = f32[32,128,128]{2,1,0:T(8,128)S(1)} fusion(f32[32,256,128]{2,1,0:T(8,128)} %bitcast.115, f32[128,256]{1,0:T(8,128)S(1)} %fusion.74), kind=kOutput, calls=%fused_computation.72 | convolution fusion | flops 805306368 | bytes 6422528 | tf_op jit(solution)/shard_map/zjp,zpt->zjt/dot_general | solution.py:220
  64.6 1.1 fusion.62
  65.7 0.1 pad_maximum_fusion.5
  65.8 0.5 collective-permute-start.3
  66.4 2.2 %collective-permute-start.2 = (bf16[33,128,128]{2,1,0:T(8,128)(2,1)S(1)}, bf16[33,128,128]{2,1,0:T(8,128)(2,1)S(1)}, u32[]{:S(2)}, u32[]{:S(2)}) collective-permute-start(bf16[33,128,128]{2,1,0:T(8,128)(2,1)S(1)} %pad_maximum_fusion.5), channel_id=1, source_target_pairs={{0,1},{1,2},{2,3},{3,0},{4,5},{5,6},{6,7},{7,4},{8,9},{9,10},{10,1... | collective-permute-start | bytes 3244040 | tf_op jit(solution)/shard_map/ppermute | solution.py:253
  68.6 0.1 convert_reduce_fusion.3
  68.7 0.1 compare_convert_fusion.3
  68.8 0.7 convert_bitcast_fusion.3
  69.5 2.5 %convolution_bitcast_fusion = f32[32,32,1024]{2,1,0:T(8,128)S(1)} fusion(bf16[32,32,8,128]{3,2,1,0:T(8,128)(2,1)S(1)} %convert_bitcast_fusion.3, f32[8,128]{1,0:T(8,128)S(1)} %multiply_add_fusion.3, f32[1024]{0:T(1024)S(1)} %iota_add_fusion), kind=kOutput, calls=%fused_computation.37 | convolution fusion | flops 2153775104 | bytes 6299648 | tf_op jit(solution)/shard_map/zlat,atv->zlv/dot_general | solution.py:242
  72.0 14.6 %collective-permute-done.3 = bf16[33,128,128]{2,1,0:T(8,128)(2,1)S(1)} collective-permute-done((bf16[33,128,128]{2,1,0:T(8,128)(2,1)S(1)}, bf16[33,128,128]{2,1,0:T(8,128)(2,1)S(1)}, u32[]{:S(2)}, u32[]{:S(2)}) %collective-permute-start.3) | collective-permute-done | bytes 1081376 | tf_op jit(solution)/shard_map/ppermute | solution.py:254
  86.7 1.2 collective-permute-done.2
  87.9 0.1 convert_reduce_fusion.1
  88.1 0.1 multiply_bitcast_fusion.1
  88.2 0.1 multiply_bitcast_fusion.2
  88.4 2.5 %collective-permute-start.4 = (bf16[16,128,128]{2,1,0:T(8,128)(2,1)S(1)}, bf16[16,128,128]{2,1,0:T(8,128)(2,1)S(1)}, u32[]{:S(2)}, u32[]{:S(2)}) collective-permute-start(bf16[16,128,128]{2,1,0:T(8,128)(2,1)S(1)} %slice.139), channel_id=1, source_target_pairs={{0,1},{1,2},{2,3},{3,0},{4,5},{5,6},{6,7},{7,4},{8,9},{9,10},{10,1... | collective-permute-start | bytes 1572872 | tf_op jit(solution)/shard_map/ppermute | solution.py:257
  90.9 0.1 compare_convert_fusion.2
  91.0 0.7 convert_bitcast_fusion.1
  91.7 0.7 convert_bitcast_fusion.2
  92.4 0.1 multiply_add_fusion.2
  92.5 2.5 %fusion.27 = f32[32,32,1024,1]{2,1,3,0:T(8,128)S(1)} fusion(bf16[32,32,8,128]{3,2,1,0:T(8,128)(2,1)S(1)} %convert_bitcast_fusion.2, f32[8,128]{1,0:T(8,128)S(1)} %get-tuple-element.47, f32[1024]{0:T(1024)S(1)} %iota_add_fusion), kind=kOutput, calls=%fused_computation.42 | convolution fusion | flops 2153775104 | bytes 6299648 | tf_op jit(solution)/shard_map/zlat,atv->zlv/dot_general | solution.py:242
  95.0 2.5 %fusion.29 = f32[32,32,1024,1]{2,1,3,0:T(8,128)S(1)} fusion(bf16[32,32,8,128]{3,2,1,0:T(8,128)(2,1)S(1)} %convert_bitcast_fusion.1, f32[8,128]{1,0:T(8,128)S(1)} %get-tuple-element.48, f32[1024]{0:T(1024)S(1)} %iota_add_fusion), kind=kOutput, calls=%fused_computation.43 | convolution fusion | flops 2153775104 | bytes 6299648 | tf_op jit(solution)/shard_map/zlat,atv->zlv/dot_general | solution.py:242
  97.6 1.9 %bitcast_add_fusion.1 = f32[32,32,1024]{2,1,0:T(8,128)S(1)} fusion(f32[32,32,1024,1]{2,1,3,0:T(8,128)S(1)} %fusion.29, f32[32,32,1024]{2,1,0:T(8,128)S(1)} %convolution_bitcast_fusion, f32[32,32,1024,1]{2,1,3,0:T(8,128)S(1)} %fusion.27), kind=kLoop, calls=%fused_computation.35 | loop fusion | flops 2097152 | bytes 16777216 | tf_op jit(solution)/shard_map/add | solution.py:260
  99.5 1.9 %collective-permute-done.5 = bf16[17,128,128]{2,1,0:T(8,128)(2,1)S(1)} collective-permute-done((bf16[17,128,128]{2,1,0:T(8,128)(2,1)S(1)}, bf16[17,128,128]{2,1,0:T(8,128)(2,1)S(1)}, u32[]{:S(2)}, u32[]{:S(2)}) %collective-permute-start.5) | collective-permute-done | bytes 557088 | tf_op jit(solution)/shard_map/ppermute | solution.py:258
  101.4 0.1 convert_reduce_fusion
  101.5 0.1 multiply_bitcast_fusion
  101.7 0.1 compare_convert_fusion
  101.9 0.7 convert_bitcast_fusion
  102.6 2.6 %broadcast_multiply_fusion = (f32[32,32,1024]{2,1,0:T(8,128)S(1)}, f32[32,32,1024,1]{2,1,3,0:T(8,128)S(1)}) fusion(f32[32]{0:T(128)S(1)} %copy-done.3, f32[32,32,1024]{2,1,0:T(8,128)S(1)} %bitcast_add_fusion.1, f32[8,128]{1,0:T(8,128)S(1)} %multiply_add_fusion, f32[1024]{0:T(1024)S(1)} %iota_add_fusion, bf16[32,32,8,128]{3,2,1,0:T(8,128)(2,1)S(1)} %convert_bitcast_fusion), kind=kOutput, calls=%fused_computation.62 | convolution fusion | flops 2155872256 | bytes 14688384 | tf_op jit(solution)/shard_map/zlat,atv->zlv/dot_general | solution.py:242
  105.3 6.1 %collective-permute-start.6 = (f32[1,32,1024]{2,1,0:T(8,128)S(1)}, f32[1,32,1024]{2,1,0:T(8,128)S(1)}, u32[]{:S(2)}, u32[]{:S(2)}) collective-permute-start(f32[1,32,1024]{2,1,0:T(8,128)S(1)} %get-tuple-element.39), channel_id=1, source_target_pairs={{0,4},{4,8},{8,12},{12,16},{16,20},{20,24},{24,28},{28,32},{32,36}... | collective-permute-start | bytes 393224 | tf_op jit(solution)/shard_map/ppermute | solution.py:25
  111.4 1.9 %collective-permute-start.7 = (f32[1,32,1024]{2,1,0:T(8,128)S(1)}, f32[1,32,1024]{2,1,0:T(8,128)S(1)}, u32[]{:S(2)}, u32[]{:S(2)}) collective-permute-start(f32[1,32,1024]{2,1,0:T(8,128)S(1)} %get-tuple-element.40), channel_id=1, source_target_pairs={{4,0},{8,4},{12,8},{16,12},{20,16},{24,20},{28,24},{32,28},{36,32}... | collective-permute-start | bytes 393224 | tf_op jit(solution)/shard_map/ppermute | solution.py:26
  113.3 6.5 %collective-permute-done.7 = f32[1,32,1024]{2,1,0:T(8,128)S(1)} collective-permute-done((f32[1,32,1024]{2,1,0:T(8,128)S(1)}, f32[1,32,1024]{2,1,0:T(8,128)S(1)}, u32[]{:S(2)}, u32[]{:S(2)}) %collective-permute-start.7) | collective-permute-done | bytes 131104 | tf_op jit(solution)/shard_map/ppermute | solution.py:26
  119.8 4.8 %fusion.18 = f32[32,32,1024]{2,1,0:T(8,128)} fusion(f32[32,32,1024]{2,1,0:T(8,128)S(1)} %copy-done.1, f32[32,32,1024]{2,1,0:T(8,128)S(1)} %copy-done, f32[1,32,1024]{2,1,0:T(8,128)S(1)} %collective-permute-done.7, f32[32,32,1024]{2,1,0:T(8,128)S(1)} %get-tuple-element.53, f32[1,32,1024]{2,1,0:T(8,128)S(1)} %collective-permute-done.6, ...), kind=kLoop, calls=%fused_computation.25 | loop fusion | flops 8388608 | bytes 25428096 | tf_op jit(solution)/shard_map/div | solution.py:266
  (35 shorter events, 0.7 us)
Async XLA Ops:
  5.0 21.8 %copy-start.3 = (f32[32]{0:T(128)S(1)}, f32[32]{0:T(128)}, u32[]{:S(2)}) copy-start(f32[32]{0:T(128)} %param.12) | copy-start | bytes 388
  5.0 21.8 %copy-start.2 = (s32[1,8]{1,0:T(1,128)S(1)}, s32[1,8]{1,0:T(1,128)}, u32[]{:S(2)}) copy-start(s32[1,8]{1,0:T(1,128)} %param.17) | copy-start | bytes 100
  8.3 49.0 %all-to-all-start = ((bf16[64,2,4224]{2,1,0:T(2,128)(2,1)}), bf16[64,2,4224]{2,1,0:T(2,128)(2,1)S(1)}, u32[]{:S(2)}, u32[]{:S(2)}) async-start(bf16[64,2,4224]{2,1,0:T(2,128)(2,1)} %reshape.668), calls=%async_computation | async-start | bytes 2162688 | tf_op jit(solution)/shard_map/all_to_all | solution.py:211
  21.6 23.1 %collective-permute-start = (f32[1,32,1024]{2,1,0:T(8,128)S(1)}, f32[1,32,1024]{2,1,0:T(8,128)S(1)}, u32[]{:S(2)}, u32[]{:S(2)}) collective-permute-start(f32[1,32,1024]{2,1,0:T(8,128)S(1)} %get-tuple-element.41), channel_id=1, source_target_pairs={{0,4},{4,8},{8,12},{12,16},{16,20},{20,24},{24,28},{28,32},{32,36}... | collective-permute-start | bytes 393224 | tf_op jit(solution)/shard_map/ppermute | solution.py:25
  24.9 22.7 %collective-permute-start.1 = (f32[1,32,1024]{2,1,0:T(8,128)S(1)}, f32[1,32,1024]{2,1,0:T(8,128)S(1)}, u32[]{:S(2)}, u32[]{:S(2)}) collective-permute-start(f32[1,32,1024]{2,1,0:T(8,128)S(1)} %get-tuple-element.42), channel_id=1, source_target_pairs={{4,0},{8,4},{12,8},{16,12},{20,16},{24,20},{28,24},{32,28},{36,32}... | collective-permute-start | bytes 393224 | tf_op jit(solution)/shard_map/ppermute | solution.py:26
  65.8 20.8 %collective-permute-start.3 = (bf16[33,128,128]{2,1,0:T(8,128)(2,1)S(1)}, bf16[33,128,128]{2,1,0:T(8,128)(2,1)S(1)}, u32[]{:S(2)}, u32[]{:S(2)}) collective-permute-start(bf16[33,128,128]{2,1,0:T(8,128)(2,1)S(1)} %pad_maximum_fusion.5), channel_id=1, source_target_pairs={{0,3},{1,0},{2,1},{3,2},{4,7},{5,4},{6,5},{7,6},{8,11},{9,8},{10,9... | collective-permute-start | bytes 3244040 | tf_op jit(solution)/shard_map/ppermute | solution.py:254
  66.4 21.5 %collective-permute-start.2 = (bf16[33,128,128]{2,1,0:T(8,128)(2,1)S(1)}, bf16[33,128,128]{2,1,0:T(8,128)(2,1)S(1)}, u32[]{:S(2)}, u32[]{:S(2)}) collective-permute-start(bf16[33,128,128]{2,1,0:T(8,128)(2,1)S(1)} %pad_maximum_fusion.5), channel_id=1, source_target_pairs={{0,1},{1,2},{2,3},{3,0},{4,5},{5,6},{6,7},{7,4},{8,9},{9,10},{10,1... | collective-permute-start | bytes 3244040 | tf_op jit(solution)/shard_map/ppermute | solution.py:253
  88.4 11.1 %collective-permute-start.4 = (bf16[16,128,128]{2,1,0:T(8,128)(2,1)S(1)}, bf16[16,128,128]{2,1,0:T(8,128)(2,1)S(1)}, u32[]{:S(2)}, u32[]{:S(2)}) collective-permute-start(bf16[16,128,128]{2,1,0:T(8,128)(2,1)S(1)} %slice.139), channel_id=1, source_target_pairs={{0,1},{1,2},{2,3},{3,0},{4,5},{5,6},{6,7},{7,4},{8,9},{9,10},{10,1... | collective-permute-start | bytes 1572872 | tf_op jit(solution)/shard_map/ppermute | solution.py:257
  90.9 10.5 %collective-permute-start.5 = (bf16[17,128,128]{2,1,0:T(8,128)(2,1)S(1)}, bf16[17,128,128]{2,1,0:T(8,128)(2,1)S(1)}, u32[]{:S(2)}, u32[]{:S(2)}) collective-permute-start(bf16[17,128,128]{2,1,0:T(8,128)(2,1)S(1)} %slice.140), channel_id=1, source_target_pairs={{0,3},{1,0},{2,1},{3,2},{4,7},{5,4},{6,5},{7,6},{8,11},{9,8},{10,9... | collective-permute-start | bytes 1671176 | tf_op jit(solution)/shard_map/ppermute | solution.py:258
  102.6 17.2 %copy-start = (f32[32,32,1024]{2,1,0:T(8,128)S(1)}, f32[32,32,1024]{2,1,0:T(8,128)}, u32[]{:S(2)}) copy-start(f32[32,32,1024]{2,1,0:T(8,128)} %param.10) | copy-start | bytes 12582916
  102.6 17.2 %copy-start.1 = (f32[32,32,1024]{2,1,0:T(8,128)S(1)}, f32[32,32,1024]{2,1,0:T(8,128)}, u32[]{:S(2)}) copy-start(f32[32,32,1024]{2,1,0:T(8,128)} %param.11) | copy-start | bytes 12582916
  105.3 8.1 %collective-permute-start.6 = (f32[1,32,1024]{2,1,0:T(8,128)S(1)}, f32[1,32,1024]{2,1,0:T(8,128)S(1)}, u32[]{:S(2)}, u32[]{:S(2)}) collective-permute-start(f32[1,32,1024]{2,1,0:T(8,128)S(1)} %get-tuple-element.39), channel_id=1, source_target_pairs={{0,4},{4,8},{8,12},{12,16},{16,20},{20,24},{24,28},{28,32},{32,36}... | collective-permute-start | bytes 393224 | tf_op jit(solution)/shard_map/ppermute | solution.py:25
  111.4 8.4 %collective-permute-start.7 = (f32[1,32,1024]{2,1,0:T(8,128)S(1)}, f32[1,32,1024]{2,1,0:T(8,128)S(1)}, u32[]{:S(2)}, u32[]{:S(2)}) collective-permute-start(f32[1,32,1024]{2,1,0:T(8,128)S(1)} %get-tuple-element.40), channel_id=1, source_target_pairs={{4,0},{8,4},{12,8},{16,12},{20,16},{24,20},{28,24},{32,28},{36,32}... | collective-permute-start | bytes 393224 | tf_op jit(solution)/shard_map/ppermute | solution.py:26
